TPU v7x, 256 devices: a whole 4x4x8 slice. The times are simulated.
256 devices in a mesh: row: 8 (over x, core), col: 32 (over y, z).
Axes of the slice: x: 4, y: 4, z: 8, core: 2. Of those that a mesh axis runs over, the one named last changes fastest.
Arguments:
- frames: bfloat16 [3072, 4096], P('row', 'col'), may hold values from -6 to 6
- gain: float32 [4096], replicated, may hold values from 0.3 to 10
- w_value: bfloat16 [4096, 4096], P('row', 'col'), may hold values from -0.09375 to 0.09375
- w_gate: bfloat16 [4096, 4096], P('row', 'col'), may hold values from -0.09375 to 0.09375
- kernel: float32 [31, 4096], P(None, 'col'), may hold values from -1.5 to 1.5
- bias: float32 [4096], P('col'), may hold values from -3 to 3
- w_out: bfloat16 [4096, 4096], P('row', 'col'), may hold values from -0.09375 to 0.09375
- grad_out: bfloat16 [3072, 4096], P('row', 'col'), may hold values from -6 to 6
Outputs:
- encoded: bfloat16 [3072, 4096], P('row', 'col')
- input_grad: bfloat16 [3072, 4096], P('row', 'col')
- grad_value: float32 [4096, 4096], P('row', 'col')
- grad_gate: float32 [4096, 4096], P('row', 'col')
- grad_kernel: float32 [31, 4096], P(None, 'col')
- grad_bias: float32 [4096], P('col')
- grad_out_weight: float32 [4096, 4096], P('row', 'col')
- grad_gain: float32 [4096], P('col')
All inputs are finite; a program needn't handle non-finite values.
Results may differ from a plain program's by a relative error of at most 0.035.
Values may be sent and summed in bfloat16 or wider, within the bound.
No kernel may reach another device: no remote copies, remote signals or barrier semaphores. Data moves between devices by JAX's collectives and lax.ppermute only.
A program may use at most 128 MiB of HBM per device.

v0:
```python
import jax
import jax.numpy as jnp
from jax import lax
from jax.sharding import PartitionSpec as P

K = 31
LEN = 2048


epsilon = 1e-05


def extended(block, sides, width):
    for axis, dim in sides:
        count = lax.axis_size(axis)
        forward = [(i, i + 1) for i in range(count - 1)]
        backward = [(target, source) for source, target in forward]
        low = lax.ppermute(
            lax.slice_in_dim(block, block.shape[dim] - width, None, axis=dim), axis, forward
        )
        high = lax.ppermute(lax.slice_in_dim(block, 0, width, axis=dim), axis, backward)
        block = jnp.concatenate([low, block, high], axis=dim)
    return block


def tap_masks(positions):
    offsets = jnp.arange(K, dtype=jnp.int32) - K // 2
    placed = (positions % LEN)[None, :] + offsets[:, None]
    return ((placed >= 0) & (placed < LEN)).astype(jnp.float32)


def contract_rows(left, right):
    return lax.dot_general(
        left, right, (((0,), (0,)), ((), ())), preferred_element_type=jnp.float32
    )


def contract_cols(left, right):
    return lax.dot_general(
        left, right, (((1,), (1,)), ((), ())), preferred_element_type=jnp.float32
    )


def shards(frames, gain, w_value, w_gate, kernel, bias, w_out, grad_out):
    row_count = frames.shape[0]
    col_count = frames.shape[1]
    chan_count = w_value.shape[1]
    width = col_count * lax.axis_size("col")
    half_width = K // 2
    row_start = lax.axis_index("row") * row_count
    col_start = lax.axis_index("col") * col_count
    local_gain = lax.dynamic_slice_in_dim(gain, col_start, col_count, 0)
    wide = frames.astype(jnp.float32)
    sum_row, square_sum = lax.psum((jnp.sum(wide, axis=1), jnp.sum(wide * wide, axis=1)), "col")
    mean_row = sum_row / width
    inv_std = lax.rsqrt(square_sum / width - mean_row * mean_row + epsilon)
    centred = (wide - mean_row[:, None]) * inv_std[:, None]
    normed = lax.all_gather(
        (centred * local_gain[None, :]).astype(jnp.bfloat16), "col", axis=1, tiled=True
    )
    value_full, gate_full = (
        lax.all_gather(w_value, "row", axis=0, tiled=True),
        lax.all_gather(w_gate, "row", axis=0, tiled=True),
    )
    value_pre = jnp.dot(normed, value_full, preferred_element_type=jnp.float32)
    gate_pre = jnp.dot(normed, gate_full, preferred_element_type=jnp.float32)
    gate_sig = jax.nn.sigmoid(gate_pre)
    gated = (value_pre * gate_sig).astype(jnp.bfloat16)
    padded_glu = extended(gated, (("row", 0),), half_width).astype(jnp.float32)
    local_masks = tap_masks(row_start + jnp.arange(row_count, dtype=jnp.int32))
    conv_pre = jnp.zeros((row_count, chan_count), jnp.float32) + bias[None, :]
    for tap_index in range(K):
        conv_pre = (
            conv_pre
            + kernel[tap_index][None, :]
            * local_masks[tap_index][:, None]
            * padded_glu[tap_index : tap_index + row_count]
        )
    conv_sig = jax.nn.sigmoid(conv_pre)
    activated = (conv_pre * conv_sig).astype(jnp.bfloat16)
    act_full = lax.all_gather(activated, "col", axis=1, tiled=True)
    out_full = lax.all_gather(w_out, "row", axis=0, tiled=True)
    encoded = (
        frames.astype(jnp.float32) + jnp.dot(act_full, out_full, preferred_element_type=jnp.float32)
    ).astype(jnp.bfloat16)
    act_terms = contract_cols(grad_out, out_full)
    act_grad = lax.psum_scatter(
        act_terms.astype(jnp.bfloat16), "col", scatter_dimension=1, tiled=True
    ).astype(jnp.float32)
    grad_out_weight = lax.psum_scatter(
        contract_rows(act_full, grad_out).astype(jnp.bfloat16),
        "row",
        scatter_dimension=0,
        tiled=True,
    ).astype(jnp.float32)
    conv_grad = (act_grad * conv_sig * (1.0 + conv_pre * (1.0 - conv_sig))).astype(jnp.bfloat16)
    conv_wide = conv_grad.astype(jnp.float32)
    padded_grad = extended(conv_grad, (("row", 0),), half_width).astype(jnp.float32)
    outer_masks = tap_masks(
        row_start - half_width + jnp.arange(row_count + 2 * half_width, dtype=jnp.int32)
    )
    glu_grad = jnp.zeros((row_count, chan_count), jnp.float32)
    kernel_rows = []
    for tap_index in range(K):
        begin = 2 * half_width - tap_index
        glu_grad = (
            glu_grad
            + kernel[tap_index][None, :]
            * outer_masks[tap_index, begin : begin + row_count][:, None]
            * padded_grad[begin : begin + row_count]
        )
        kernel_rows.append(
            jnp.sum(
                local_masks[tap_index][:, None]
                * conv_wide
                * padded_glu[tap_index : tap_index + row_count],
                axis=0,
            )
        )
    kernel_term = jnp.stack(kernel_rows)
    bias_term = jnp.sum(conv_wide, axis=0)
    grad_kernel, grad_bias = lax.psum((kernel_term, bias_term), "row")
    value_grad = (glu_grad * gate_sig).astype(jnp.bfloat16)
    gate_grad = (glu_grad * value_pre * gate_sig * (1.0 - gate_sig)).astype(jnp.bfloat16)
    both_grads = jnp.concatenate([value_grad, gate_grad], axis=1)
    in_weight = lax.psum_scatter(
        contract_rows(normed, both_grads).astype(jnp.bfloat16),
        "row",
        scatter_dimension=0,
        tiled=True,
    ).astype(jnp.float32)
    grad_value = in_weight[:, :chan_count]
    grad_gate = in_weight[:, chan_count:]
    norm_terms = contract_cols(value_grad, value_full) + contract_cols(gate_grad, gate_full)
    normed_grad = lax.psum_scatter(
        norm_terms.astype(jnp.bfloat16), "col", scatter_dimension=1, tiled=True
    ).astype(jnp.float32)
    hat_grad = normed_grad * local_gain[None, :]
    first_sum, second_sum = lax.psum(
        (jnp.sum(hat_grad, axis=1), jnp.sum(hat_grad * centred, axis=1)), "col"
    )
    input_grad = (
        grad_out.astype(jnp.float32)
        + inv_std[:, None]
        * (hat_grad - first_sum[:, None] / width - centred * (second_sum / width)[:, None])
    ).astype(jnp.bfloat16)
    gain_term = jnp.sum(normed_grad * centred, axis=0)
    grad_gain = lax.psum(gain_term, "row")
    return (
        encoded,
        input_grad,
        grad_value,
        grad_gate,
        grad_kernel,
        grad_bias,
        grad_out_weight,
        grad_gain,
    )


def solution(mesh):
    placed = (
        P("row", "col"),
        P(),
        P("row", "col"),
        P("row", "col"),
        P(None, "col"),
        P("col"),
        P("row", "col"),
        P("row", "col"),
    )
    return jax.shard_map(
        shards,
        mesh=mesh,
        in_specs=placed,
        out_specs=(
            P("row", "col"),
            P("row", "col"),
            P("row", "col"),
            P("row", "col"),
            P(None, "col"),
            P("col"),
            P("row", "col"),
            P("col"),
        ),
        check_vma=False,
    )
```

profile of v0, /device:TPU:6, one launch (start us, length us, event | category | flops | bytes accessed | tf_op | source)
XLA Modules:
  0.0 862.0 jit_solution(822775014375690964)
XLA Ops:
  10.5 77.9 %all-reduce.1 = (f32[384]{0:T(512)S(1)}, f32[384]{0:T(512)S(1)}) all-reduce(f32[384]{0:T(512)S(1)} %get-tuple-element.44, f32[384]{0:T(512)S(1)} %get-tuple-element.43), channel_id=1, replica_groups=mesh['row'=8,'col'=32] {'col'}, use_global_device_ids=true, to_apply=%region_3.0 | all-reduce | flops 768 | bytes 6144 | tf_op jit(solution)/shard_map/psum | solution.py:54
  89.1 1.7 fusion.16
  91.5 2.3 convolution_convert_fusion
  93.7 2.8 copy.16
  98.7 64.5 %all-gather.6.cloned.1.call-done = bf16[384,4096]{1,0:T(8,128)(2,1)} async-done(((bf16[384,128]{1,0:T(8,128)(2,1)}), bf16[384,4096]{1,0:T(8,128)(2,1)}) %all-gather.6.cloned.1.call-update) | async-done | bytes 3145744 | tf_op jit(solution)/shard_map/all_gather | solution.py:58
  163.1 3.3 fusion.2
  166.4 23.0 %all-gather.8.cloned.1.call-done = bf16[4096,128]{1,0:T(8,128)(2,1)} async-done(((bf16[512,128]{1,0:T(8,128)(2,1)}), bf16[4096,128]{1,0:T(8,128)(2,1)}) %all-gather.8.cloned.1.call-update) | async-done | bytes 1048592 | tf_op jit(solution)/shard_map/all_gather | solution.py:62
  189.4 2.9 multiply_convert_fusion.4
  192.3 2.1 collective-permute-start
  194.4 3.4 collective-permute-start.1
  198.0 1.1 collective-permute-done.1
  199.2 215.0 %reduce-scatter.13.cloned.1.call-done = bf16[128,384]{1,0:T(8,128)(2,1)} async-done(((bf16[4096,384]{1,0:T(8,128)(2,1)}), bf16[128,384]{1,0:T(8,128)(2,1)}) %reduce-scatter.13.cloned.1.call-update) | async-done | bytes 98320
  415.6 4.1 fusion.75
  420.9 1.9 collective-permute-start.2
  422.8 3.6 collective-permute-start.3
  426.6 1.2 collective-permute-done.3
  428.1 3.1 multiply_convert_fusion
  431.2 2.6 convolution_convert_fusion.1
  436.1 2.9 copy.18
  439.3 58.1 %all-gather.12.cloned.1.call-done = bf16[384,4096]{1,0:T(8,128)(2,1)} async-done(((bf16[384,128]{1,0:T(8,128)(2,1)}), bf16[384,4096]{1,0:T(8,128)(2,1)}) %all-gather.12.cloned.1.call-update) | async-done | bytes 3145744 | tf_op jit(solution)/shard_map/all_gather | solution.py:81
  497.4 3.9 convolution_convert_fusion.2
  501.3 1.7 fusion.73
  503.1 1.9 fusion.77
  504.9 1.9 fusion.79
  506.8 3.0 stack.127
  509.8 23.5 %reduce-scatter.9.cloned.1.call-done = bf16[512,256]{1,0:T(8,128)(2,1)} async-done(((bf16[4096,256]{1,0:T(8,128)(2,1)}), bf16[512,256]{1,0:T(8,128)(2,1)}) %reduce-scatter.9.cloned.1.call-update) | async-done | bytes 262160 | tf_op jit(solution)/shard_map/reduce_scatter | solution.py:126
  533.3 1.8 fusion.121
  535.1 2.9 fusion.3
  537.9 221.4 %reduce-scatter.15.cloned.1.call-done = bf16[128,384]{1,0:T(8,128)(2,1)} async-done(((bf16[4096,384]{1,0:T(8,128)(2,1)}), bf16[128,384]{1,0:T(8,128)(2,1)}) %reduce-scatter.15.cloned.1.call-update) | async-done | bytes 98320
  760.7 72.2 %all-reduce = (f32[384]{0:T(512)S(1)}, f32[384]{0:T(512)S(1)}) all-reduce(f32[384]{0:T(512)S(1)} %get-tuple-element.40, f32[384]{0:T(512)S(1)} %get-tuple-element.41), channel_id=1, replica_groups=mesh['row'=8,'col'=32] {'col'}, use_global_device_ids=true, to_apply=%region_9.10 | all-reduce | flops 768 | bytes 6144 | tf_op jit(solution)/shard_map/psum | solution.py:139
  832.9 20.0 %all-reduce.2 = (f32[31,128]{1,0:T(8,128)}, f32[128]{0:T(128)}, f32[128]{0:T(128)}) all-reduce(f32[31,128]{1,0:T(8,128)S(1)} %stack.127, f32[128]{0:T(128)S(1)} %copy-done.71, f32[128]{0:T(128)S(1)} %get-tuple-element.39), channel_id=1, replica_groups=mesh['row'=8,'col'=32] {'row'}, use_global_device_ids=true, to_apply=%region_42.43 | all-reduce | flops 4224 | bytes 33792 | tf_op jit(solution)/shard_map/psum | solution.py:122
  853.8 1.6 convert_element_type.92
  (194 shorter events, 13.9 us)
Async XLA Ops:
  7.2 84.3 %all-gather.14.cloned.1.call-start = ((), (), s32[]{:S(2)}) async-start(), calls=%async_computation.8 | async-start | bytes 1179648 | tf_op jit(solution)/shard_map/all_gather | solution.py:82
  7.9 90.7 %all-gather.10.cloned.1.call-start = ((), (), s32[]{:S(2)}) async-start(), calls=%async_computation.6 | async-start | bytes 1179648 | tf_op jit(solution)/shard_map/all_gather | solution.py:63
  8.7 154.5 %all-gather.6.cloned.1.call-start = ((), (), s32[]{:S(2)}) async-start(), calls=%async_computation.4 | async-start | bytes 3244032 | tf_op jit(solution)/shard_map/all_gather | solution.py:58
  90.8 98.6 %all-gather.8.cloned.1.call-start = ((), (), s32[]{:S(2)}) async-start(), calls=%async_computation.5 | async-start | bytes 1179648 | tf_op jit(solution)/shard_map/all_gather | solution.py:62
  91.4 322.8 %reduce-scatter.13.cloned.1.call-start = ((), (), s32[]{:S(2)}) async-start(), calls=%async_computation.11 | async-start | bytes 3244032
  96.5 400.8 %all-gather.12.cloned.1.call-start = ((), (), s32[]{:S(2)}) async-start(), calls=%async_computation.7 | async-start | bytes 3244032 | tf_op jit(solution)/shard_map/all_gather | solution.py:81
  97.2 318.0 %copy-start.13 = (f32[384]{0:T(512)}, f32[384]{0:T(512)S(1)}, u32[]{:S(2)}) copy-start(f32[384]{0:T(512)S(1)} %get-tuple-element.77) | copy-start | bytes 4612
  97.2 318.0 %copy-start.14 = (f32[384]{0:T(512)}, f32[384]{0:T(512)S(1)}, u32[]{:S(2)}) copy-start(f32[384]{0:T(512)S(1)} %get-tuple-element.78) | copy-start | bytes 4612
  97.2 318.0 %copy-start.15 = (f32[384]{0:T(512)}, f32[384]{0:T(512)S(1)}, u32[]{:S(2)}) copy-start(f32[384]{0:T(512)S(1)} %get-tuple-element.91) | copy-start | bytes 4612
  97.3 318.0 %copy-start.16 = (f32[384]{0:T(512)}, f32[384]{0:T(512)S(1)}, u32[]{:S(2)}) copy-start(f32[384]{0:T(512)S(1)} %get-tuple-element.92) | copy-start | bytes 4612
  97.3 318.0 %copy-start.17 = (f32[384]{0:T(512)}, f32[384]{0:T(512)S(1)}, u32[]{:S(2)}) copy-start(f32[384]{0:T(512)S(1)} %get-tuple-element.93) | copy-start | bytes 4612
  97.3 318.0 %copy-start.18 = (f32[384]{0:T(512)}, f32[384]{0:T(512)S(1)}, u32[]{:S(2)}) copy-start(f32[384]{0:T(512)S(1)} %get-tuple-element.94) | copy-start | bytes 4612
  97.3 318.0 %copy-start.19 = (f32[384]{0:T(512)}, f32[384]{0:T(512)S(1)}, u32[]{:S(2)}) copy-start(f32[384]{0:T(512)S(1)} %get-tuple-element.76) | copy-start | bytes 4612
  97.3 318.0 %copy-start.20 = (f32[384]{0:T(512)}, f32[384]{0:T(512)S(1)}, u32[]{:S(2)}) copy-start(f32[384]{0:T(512)S(1)} %get-tuple-element.80) | copy-start | bytes 4612
  97.3 318.0 %copy-start.21 = (f32[384]{0:T(512)}, f32[384]{0:T(512)S(1)}, u32[]{:S(2)}) copy-start(f32[384]{0:T(512)S(1)} %get-tuple-element.81) | copy-start | bytes 4612
  97.3 318.0 %copy-start.22 = (f32[384]{0:T(512)}, f32[384]{0:T(512)S(1)}, u32[]{:S(2)}) copy-start(f32[384]{0:T(512)S(1)} %get-tuple-element.82) | copy-start | bytes 4612
  97.9 317.4 %copy-start.38 = (f32[128]{0:T(128)}, f32[128]{0:T(128)S(1)}, u32[]{:S(2)}) copy-start(f32[128]{0:T(128)S(1)} %get-tuple-element.143) | copy-start | bytes 1540
  97.9 317.4 %copy-start.39 = (f32[128]{0:T(128)}, f32[128]{0:T(128)S(1)}, u32[]{:S(2)}) copy-start(f32[128]{0:T(128)S(1)} %get-tuple-element.144) | copy-start | bytes 1540
  97.9 317.4 %copy-start.40 = (f32[128]{0:T(128)}, f32[128]{0:T(128)S(1)}, u32[]{:S(2)}) copy-start(f32[128]{0:T(128)S(1)} %get-tuple-element.145) | copy-start | bytes 1540
  97.9 317.4 %copy-start.41 = (f32[128]{0:T(128)}, f32[128]{0:T(128)S(1)}, u32[]{:S(2)}) copy-start(f32[128]{0:T(128)S(1)} %get-tuple-element.146) | copy-start | bytes 1540
  97.9 317.4 %copy-start.42 = (f32[128]{0:T(128)}, f32[128]{0:T(128)S(1)}, u32[]{:S(2)}) copy-start(f32[128]{0:T(128)S(1)} %get-tuple-element.147) | copy-start | bytes 1540
  192.3 5.8 collective-permute-start
  194.4 4.7 collective-permute-start.1
  420.5 112.7 %reduce-scatter.9.cloned.1.call-start = ((), (), s32[]{:S(2)}) async-start(), calls=%async_computation.9 | async-start | bytes 2359296 | tf_op jit(solution)/shard_map/reduce_scatter | solution.py:126
  420.9 5.7 collective-permute-start.2
  422.8 5.0 collective-permute-start.3
  433.9 325.5 %reduce-scatter.15.cloned.1.call-start = ((), (), s32[]{:S(2)}) async-start(), calls=%async_computation.12 | async-start | bytes 3244032
  439.1 414.8 %reduce-scatter.11.cloned.1.call-start = ((), (), s32[]{:S(2)}) async-start(), calls=%async_computation.10 | async-start | bytes 1179648 | tf_op jit(solution)/shard_map/reduce_scatter | solution.py:90
  506.8 253.6 %copy-start.12 = (f32[384]{0:T(512)S(1)}, f32[384]{0:T(512)}, u32[]{:S(2)}) copy-start(f32[384]{0:T(512)} %copy-done.11) | copy-start | bytes 4612
  506.8 253.6 %copy-start.37 = (f32[128]{0:T(128)S(1)}, f32[128]{0:T(128)}, u32[]{:S(2)}) copy-start(f32[128]{0:T(128)} %copy-done.36) | copy-start | bytes 1540
  506.8 326.1 %copy-start.71 = (f32[128]{0:T(128)S(1)}, f32[128]{0:T(128)}, u32[]{:S(2)}) copy-start(f32[128]{0:T(128)} %get-tuple-element.42) | copy-start | bytes 1540
  506.8 346.1 %copy-start.7 = (bf16[384,128]{1,0:T(8,128)(2,1)S(1)}, bf16[384,128]{1,0:T(8,128)(2,1)}, u32[]{:S(2)}) copy-start(bf16[384,128]{1,0:T(8,128)(2,1)} %param.15) | copy-start | bytes 294916
  (53 other events, 3499.5 us)
Sparse Core Ops, SparseCore 0:
  9.9 27.2 all-gather.13
  39.0 25.7 all-gather.9
  90.9 72.1 all-gather.5
  164.8 24.5 all-gather.7
  193.1 221.0 reduce-scatter.12
  420.7 76.6 all-gather.11
  500.1 33.1 reduce-scatter.8
  537.6 221.6 reduce-scatter.14
  761.9 29.8 reduce-scatter.10
where the time goes:
time: 865 us; the launch traced here: 862 us
  waiting for transfers between devices  610 us (71%)
  blocking collectives  170 us (20%)
  matrix products  19.8 us (2%)
  other arithmetic  19.2 us (2%)
  local copies, waits for them, and re-layouts  16.5 us (2%)
  between operations  15 us (2%)
  starting transfers between devices  11.7 us (1%)
    unnamed x11, waiting for transfers between devices  438 us
    psum x1, blocking collectives, shards(): lax.psum((jnp.sum(wide, axis=1), jnp.sum(wide * wide, axis=1)), 'col')  77.9 us
    psum x1, blocking collectives, shards(): lax.psum((jnp.sum(hat_grad, axis=1), jnp.sum(hat_grad * centred, axis=1))...  72.2 us
    all_gather x1, waiting for transfers between devices, shards(): lax.all_gather((centred * local_gain[None, :]).astype(jnp.bfloat16), 'col...  64.5 us
    all_gather x1, waiting for transfers between devices, shards(): act_full = lax.all_gather(activated, 'col', axis=1, tiled=True)  58.1 us
    reduce_scatter x1, waiting for transfers between devices, shards(): lax.psum_scatter(contract_rows(normed, both_grads).astype(jnp.bfloat16),...  23.5 us
    all_gather x1, waiting for transfers between devices, shards(): lax.all_gather(w_value, 'row', axis=0, tiled=True)  23 us
    psum x1, blocking collectives, shards(): grad_kernel, grad_bias = lax.psum((kernel_term, bias_term), 'row')  20 us
  transfers between devices with their start and end apart: 13, of which 8 were waited for; matrix products, arithmetic and copies ran while one was open for 5% of the time, Pallas kernels for 0%

commit v1 on v0

v1 whole, which is shorter than its diff:
```python
import jax
import jax.numpy as jnp
from jax import lax
from jax.sharding import Mesh, PartitionSpec as P

K = 31
LEN = 2048
HALF = K // 2
NX, NK, NY, NZ = 4, 2, 4, 8
ROW = ("x", "k")
COL = ("y", "z")


epsilon = 1e-05


def extended(block, width):
    count = NX * NK
    forward = [(i, i + 1) for i in range(count - 1)]
    backward = [(target, source) for source, target in forward]
    low = lax.ppermute(block[-width:], ROW, forward)
    high = lax.ppermute(block[:width], ROW, backward)
    return jnp.concatenate([low, block, high], axis=0)


def tap_masks(positions):
    offsets = jnp.arange(K, dtype=jnp.int32) - HALF
    placed = (positions % LEN)[None, :] + offsets[:, None]
    return ((placed >= 0) & (placed < LEN)).astype(jnp.float32)


def dot(left, right, dims):
    return lax.dot_general(left, right, (dims, ((), ())), preferred_element_type=jnp.float32)


def swap_xy(block):
    return lax.ppermute(
        block, ("x", "y"), [(a * NY + b, b * NY + a) for a in range(NX) for b in range(NY)]
    )


def scatter_sum(parts, axis):
    moved = lax.all_to_all(parts.astype(jnp.bfloat16), axis, 0, 0, tiled=True)
    return jnp.sum(moved.astype(jnp.float32), axis=0)


def shards(frames, gain, w_value, w_gate, kernel, bias, w_out, grad_out):
    bf16 = jnp.bfloat16
    rows, cols = frames.shape
    width = cols * NY * NZ
    quarter = cols * NZ
    row_start = (lax.axis_index("x") * NK + lax.axis_index("k")) * rows
    y_index = lax.axis_index("y")
    col_start = (y_index * NZ + lax.axis_index("z")) * cols
    local_gain = lax.dynamic_slice_in_dim(gain, col_start, cols, 0)
    quarter_gain = lax.dynamic_slice_in_dim(gain, y_index * quarter, quarter, 0)

    vg_own = swap_xy(jnp.concatenate([w_value, w_gate], axis=1))
    out_own = swap_xy(w_out)
    vg_full = lax.all_gather(vg_own, ROW, axis=0, tiled=True).reshape(NY, quarter, 2 * cols)
    out_full = lax.all_gather(out_own, ROW, axis=0, tiled=True).reshape(NY, quarter, cols)

    frames_q = lax.all_gather(frames, "z", axis=1, tiled=True)
    wide_q = frames_q.astype(jnp.float32)
    sums = lax.psum(jnp.stack([jnp.sum(wide_q, axis=1), jnp.sum(wide_q * wide_q, axis=1)]), "y")
    mean_row = sums[0] / width
    inv_std = lax.rsqrt(sums[1] / width - mean_row * mean_row + epsilon)
    centred_q = (wide_q - mean_row[:, None]) * inv_std[:, None]
    normed_q = (centred_q * quarter_gain[None, :]).astype(bf16)
    wide = frames.astype(jnp.float32)
    centred = (wide - mean_row[:, None]) * inv_std[:, None]

    pre_parts = jnp.stack([dot(normed_q, vg_full[i], ((1,), (0,))) for i in range(NY)])
    pre = scatter_sum(pre_parts, "y")
    value_pre = pre[:, :cols]
    gate_pre = pre[:, cols:]
    gate_sig = jax.nn.sigmoid(gate_pre)
    gated = (value_pre * gate_sig).astype(bf16)

    padded_glu = extended(gated, HALF).astype(jnp.float32)
    local_masks = tap_masks(row_start + jnp.arange(rows, dtype=jnp.int32))
    conv_pre = jnp.zeros((rows, cols), jnp.float32) + bias[None, :]
    for tap in range(K):
        conv_pre = (
            conv_pre
            + kernel[tap][None, :] * local_masks[tap][:, None] * padded_glu[tap : tap + rows]
        )
    conv_sig = jax.nn.sigmoid(conv_pre)
    activated = (conv_pre * conv_sig).astype(bf16)

    grad_full = lax.all_gather(grad_out, "y", axis=0, tiled=False)
    act_terms = sum(dot(grad_full[i], out_full[i], ((1,), (1,))) for i in range(NY))
    act_parts = act_terms.reshape(rows, NZ, cols).transpose(1, 0, 2)
    act_grad = scatter_sum(act_parts, "z")

    act_q = lax.all_gather(activated, "z", axis=1, tiled=True)
    enc_parts = jnp.stack([dot(act_q, out_full[i], ((1,), (0,))) for i in range(NY)])
    encoded = (wide + scatter_sum(enc_parts, "y")).astype(bf16)
    out_weight_parts = jnp.stack([dot(act_q, grad_full[i], ((0,), (0,))) for i in range(NY)])
    grad_out_weight = swap_xy(
        lax.psum_scatter(
            out_weight_parts.astype(bf16).reshape(NY * quarter, cols),
            ROW,
            scatter_dimension=0,
            tiled=True,
        )
    ).astype(jnp.float32)

    conv_grad = (act_grad * conv_sig * (1.0 + conv_pre * (1.0 - conv_sig))).astype(bf16)
    conv_wide = conv_grad.astype(jnp.float32)
    padded_grad = extended(conv_grad, HALF).astype(jnp.float32)
    outer_masks = tap_masks(row_start - HALF + jnp.arange(rows + 2 * HALF, dtype=jnp.int32))
    glu_grad = jnp.zeros((rows, cols), jnp.float32)
    kernel_rows = []
    for tap in range(K):
        begin = 2 * HALF - tap
        glu_grad = (
            glu_grad
            + kernel[tap][None, :]
            * outer_masks[tap, begin : begin + rows][:, None]
            * padded_grad[begin : begin + rows]
        )
        kernel_rows.append(
            jnp.sum(
                local_masks[tap][:, None] * conv_wide * padded_glu[tap : tap + rows],
                axis=0,
            )
        )
    kernel_term = jnp.stack(kernel_rows)
    bias_term = jnp.sum(conv_wide, axis=0)

    value_grad = (glu_grad * gate_sig).astype(bf16)
    gate_grad = (glu_grad * value_pre * gate_sig * (1.0 - gate_sig)).astype(bf16)
    vg_grads = lax.all_gather(
        jnp.concatenate([value_grad, gate_grad], axis=1), "y", axis=0, tiled=False
    )
    weight_parts = jnp.stack([dot(normed_q, vg_grads[i], ((0,), (0,))) for i in range(NY)])
    in_weight = swap_xy(
        lax.psum_scatter(
            weight_parts.astype(bf16).reshape(NY * quarter, 2 * cols),
            ROW,
            scatter_dimension=0,
            tiled=True,
        )
    ).astype(jnp.float32)
    grad_value = in_weight[:, :cols]
    grad_gate = in_weight[:, cols:]

    norm_terms = sum(dot(vg_grads[i], vg_full[i], ((1,), (1,))) for i in range(NY))
    hat_terms = norm_terms * quarter_gain[None, :]
    hat_sums = jnp.stack([jnp.sum(hat_terms, axis=1), jnp.sum(hat_terms * centred_q, axis=1)])
    hat_sums = lax.psum(lax.psum(hat_sums, "y"), "z") / width
    norm_parts = norm_terms.reshape(rows, NZ, cols).transpose(1, 0, 2)
    normed_grad = scatter_sum(norm_parts, "z")
    hat_grad = normed_grad * local_gain[None, :]
    input_grad = (
        grad_out.astype(jnp.float32)
        + inv_std[:, None] * (hat_grad - hat_sums[0][:, None] - centred * hat_sums[1][:, None])
    ).astype(bf16)
    gain_term = jnp.sum(normed_grad * centred, axis=0)
    grad_kernel, grad_bias, grad_gain = lax.psum((kernel_term, bias_term, gain_term), ROW)
    return (
        encoded,
        input_grad,
        grad_value,
        grad_gate,
        grad_kernel,
        grad_bias,
        grad_out_weight,
        grad_gain,
    )


def solution(mesh):
    fine = Mesh(mesh.devices.reshape(NX, NK, NY, NZ), ("x", "k", "y", "z"))
    both = P(ROW, COL)
    return jax.shard_map(
        shards,
        mesh=fine,
        in_specs=(both, P(), both, both, P(None, COL), P(COL), both, both),
        out_specs=(both, both, both, both, P(None, COL), P(COL), both, P(COL)),
        check_vma=False,
    )
```

time: 865 us -> 287 us (0.33)
  the two profiles are of different devices: /device:TPU:6 before, /device:TPU:24 now
where the time goes in v1:
time: 287 us; the launch traced here: 286 us
  blocking collectives  141 us (49%)
  starting transfers between devices  47.3 us (16%)
  waiting for transfers between devices  38.3 us (13%)
  other arithmetic  19.2 us (7%)
  matrix products  15.7 us (5%)
  between operations  15.1 us (5%)
  local copies, waits for them, and re-layouts  10 us (3%)
    all_gather x1, blocking collectives, shards(): frames_q = lax.all_gather(frames, 'z', axis=1, tiled=True)  30.7 us
    psum x1, blocking collectives, shards(): lax.psum((kernel_term, bias_term, gain_term), ROW)  27.7 us
    psum x2, blocking collectives, shards(): hat_sums = lax.psum(lax.psum(hat_sums, 'y'), 'z') / width  24.8 us
    all_to_all x4, starting transfers between devices, scatter_sum(): moved = lax.all_to_all(parts.astype(jnp.bfloat16), axis, 0, 0, tiled=True)  23.8 us
    all_gather x1, blocking collectives, shards(): act_q = lax.all_gather(activated, 'z', axis=1, tiled=True)  23.6 us
    ppermute x4, waiting for transfers between devices, swap_xy(): lax.ppermute(block, ('x', 'y'), [(a * NY + b, b * NY + a) for a in range(...  22.6 us
    ppermute x4, starting transfers between devices, swap_xy(): lax.ppermute(block, ('x', 'y'), [(a * NY + b, b * NY + a) for a in range(...  18.3 us
    dot_general x24, matrix products, dot(): lax.dot_general(left, right, (dims, ((), ())), preferred_element_type=jnp...  15.7 us
  transfers between devices with their start and end apart: 16, of which 5 were waited for; matrix products, arithmetic and copies ran while one was open for 9% of the time, Pallas kernels for 0%

profile of v1, /device:TPU:24, one launch (start us, length us, event | category | flops | bytes accessed | tf_op | source)
XLA Modules:
  0.0 286.4 jit_solution(14856642492126005355)
XLA Ops:
  7.2 4.3 %collective-permute-start.3 = (bf16[512,128]{1,0:T(8,128)(2,1)}, bf16[512,128]{1,0:T(8,128)(2,1)S(1)}, u32[]{:S(2)}, u32[]{:S(2)}) collective-permute-start(bf16[512,128]{1,0:T(8,128)(2,1)} %param.14), channel_id=1, source_target_pairs={{0,0},{8,64},{16,128},{24,192},{64,8},{72,72},{80,136},{88,200},{1... | collective-permute-start | bytes 393224 | tf_op jit(solution)/shard_map/ppermute | solution.py:37
  11.6 9.1 %collective-permute-done.3 = bf16[512,128]{1,0:T(8,128)(2,1)S(1)} collective-permute-done((bf16[512,128]{1,0:T(8,128)(2,1)}, bf16[512,128]{1,0:T(8,128)(2,1)S(1)}, u32[]{:S(2)}, u32[]{:S(2)}) %collective-permute-start.3) | collective-permute-done | bytes 131104 | tf_op jit(solution)/shard_map/ppermute | solution.py:37
  22.4 4.3 %collective-permute-start = (bf16[512,256]{1,0:T(8,128)(2,1)S(1)}, bf16[512,256]{1,0:T(8,128)(2,1)S(1)}, u32[]{:S(2)}, u32[]{:S(2)}) collective-permute-start(bf16[512,256]{1,0:T(8,128)(2,1)S(1)} %pad_maximum_fusion.4), channel_id=1, source_target_pairs={{0,0},{8,64},{16,128},{24,192},{64,8},{72,72},{80,136},{88,200},{1... | collective-permute-start | bytes 786440 | tf_op jit(solution)/shard_map/ppermute | solution.py:37
  26.8 13.4 %collective-permute-done = bf16[512,256]{1,0:T(8,128)(2,1)S(1)} collective-permute-done((bf16[512,256]{1,0:T(8,128)(2,1)S(1)}, bf16[512,256]{1,0:T(8,128)(2,1)S(1)}, u32[]{:S(2)}, u32[]{:S(2)}) %collective-permute-start) | collective-permute-done | bytes 262176 | tf_op jit(solution)/shard_map/ppermute | solution.py:37
  40.9 30.7 %all_gather.24 = bf16[384,1024]{1,0:T(8,128)(2,1)S(1)} all-gather(bf16[384,128]{1,0:T(8,128)(2,1)} %param.8), channel_id=1, replica_groups=mesh['x'=4,'k'=2,'y'=4,'z'=8] {'z'}, dimensions={1}, use_global_device_ids=true | all-gather | bytes 884736 | tf_op jit(solution)/shard_map/all_gather | solution.py:63
  72.6 7.5 %psum.42 = f32[2,384]{1,0:T(2,128)S(1)} all-reduce(f32[2,384]{1,0:T(2,128)S(1)} %pad_maximum_fusion.6), channel_id=1, replica_groups=mesh['x'=4,'k'=2,'y'=4,'z'=8] {'y'}, use_global_device_ids=true, to_apply=%region_2.0 | all-reduce | flops 768 | bytes 6144 | tf_op jit(solution)/shard_map/psum | solution.py:65
  82.2 12.8 %all-gather = bf16[1536,128]{1,0:T(8,128)(2,1)S(1)} all-gather(bf16[384,128]{1,0:T(8,128)(2,1)S(1)} %copy-done.11), channel_id=2, replica_groups=mesh['x'=4,'k'=2,'y'=4,'z'=8] {'y'}, dimensions={0}, use_global_device_ids=true | all-gather | bytes 491520 | tf_op jit(solution)/shard_map/all_gather | solution.py:91
  95.3 1.5 fusion.42
  96.9 1.6 fusion.14
  98.4 1.4 fusion.15
  101.7 7.4 %all-to-all-start = ((bf16[4,384,256]{2,1,0:T(8,128)(2,1)}), bf16[4,384,256]{2,1,0:T(8,128)(2,1)}, u32[]{:S(2)}, u32[]{:S(2)}) async-start(bf16[4,384,256]{2,1,0:T(8,128)(2,1)} %pad_maximum_fusion.2), calls=%async_computation | async-start | bytes 1572864 | tf_op jit(solution)/shard_map/all_to_all | solution.py:43
  109.0 1.3 fusion.45
  112.3 4.3 %all-to-all-done = bf16[4,384,256]{2,1,0:T(8,128)(2,1)} async-done(((bf16[4,384,256]{2,1,0:T(8,128)(2,1)}), bf16[4,384,256]{2,1,0:T(8,128)(2,1)}, u32[]{:S(2)}, u32[]{:S(2)}) %all-to-all-start) | async-done | bytes 786464 | tf_op jit(solution)/shard_map/all_to_all | solution.py:43
  116.5 4.5 %all-to-all-start.2 = ((bf16[8,384,128]{2,1,0:T(8,128)(2,1)}), bf16[8,384,128]{2,1,0:T(8,128)(2,1)S(1)}, u32[]{:S(2)}, u32[]{:S(2)}) async-start(bf16[8,384,128]{2,1,0:T(8,128)(2,1)} %bitcast.158), calls=%async_computation.2 | async-start | bytes 1572864 | tf_op jit(solution)/shard_map/all_to_all | solution.py:43
  124.9 1.3 collective-permute-start.1
  126.2 1.3 collective-permute-start.2
  127.5 9.7 %all-to-all-done.2 = bf16[8,384,128]{2,1,0:T(8,128)(2,1)S(1)} async-done(((bf16[8,384,128]{2,1,0:T(8,128)(2,1)}), bf16[8,384,128]{2,1,0:T(8,128)(2,1)S(1)}, u32[]{:S(2)}, u32[]{:S(2)}) %all-to-all-start.2) | async-done | bytes 786464 | tf_op jit(solution)/shard_map/all_to_all | solution.py:43
  137.7 4.1 %fusion.117 = (f32[128]{0:T(128)}, f32[128]{0:T(128)}, f32[128]{0:T(128)}, f32[128]{0:T(128)}, f32[128]{0:T(128)}, /*index=5*/f32[128]{0:T(128)}, f32[128]{0:T(1...) fusion(f32[414,128]{1,0:T(8,128)S(1)} %maximum_convert_fusion, ...), kind=kLoop, calls=%fused_computation.181 | loop fusion | flops 6388608 | bytes 6654976 | tf_op jit(solution)/shard_map/reduce_sum | solution.py:124
  143.1 1.3 collective-permute-start.5
  144.6 1.6 collective-permute-done.5
  146.3 3.4 %multiply_convert_fusion.1 = (bf16[384,128]{1,0:T(8,128)(2,1)S(1)}, f32[384,128]{1,0:T(8,128)S(1)}) fusion(f32[384,256]{1,0:T(8,128)S(1)} %convert_reduce_fusion.4, f32[414,128]{1,0:T(8,128)S(1)} %maximum_convert_fusion.1, f32[384]{0:T(512)S(1)} %get-tuple-element.45, f32[128]{0:T(128)} %get-tuple-element.156, f32[384]{0:T(512)S(1)} %copy-done.46, ...), kind=kLoop, calls=%fused_computation.253 | loop fusion | flops 4767744 | bytes 6649856 | tf_op jit(solution)/shard_map/convert_element_type | solution.py:132
  149.9 13.7 %all-gather.1 = bf16[1536,256]{1,0:T(8,128)(2,1)S(1)} all-gather(bf16[384,256]{1,0:T(8,128)(2,1)S(1)} %pad_maximum_fusion.5), channel_id=3, replica_groups=mesh['x'=4,'k'=2,'y'=4,'z'=8] {'y'}, dimensions={0}, use_global_device_ids=true | all-gather | bytes 983040 | tf_op jit(solution)/shard_map/all_gather | solution.py:134
  165.5 1.6 pad_maximum_fusion
  167.1 23.6 %all_gather.26 = bf16[384,1024]{1,0:T(8,128)(2,1)S(1)} all-gather(bf16[384,128]{1,0:T(8,128)(2,1)S(1)} %multiply_convert_fusion.3), channel_id=1, replica_groups=mesh['x'=4,'k'=2,'y'=4,'z'=8] {'z'}, dimensions={1}, use_global_device_ids=true | all-gather | bytes 884736 | tf_op jit(solution)/shard_map/all_gather | solution.py:96
  193.1 7.2 %all-to-all-start.1 = ((bf16[4,384,128]{2,1,0:T(8,128)(2,1)}), bf16[4,384,128]{2,1,0:T(8,128)(2,1)S(1)}, u32[]{:S(2)}, u32[]{:S(2)}) async-start(bf16[4,384,128]{2,1,0:T(8,128)(2,1)} %pad_maximum_fusion.3), calls=%async_computation.1 | async-start | bytes 786432 | tf_op jit(solution)/shard_map/all_to_all | solution.py:43
  203.3 1.6 fusion.31
  207.8 4.7 %all-to-all-start.3 = ((bf16[8,384,128]{2,1,0:T(8,128)(2,1)}), bf16[8,384,128]{2,1,0:T(8,128)(2,1)S(1)}, u32[]{:S(2)}, u32[]{:S(2)}) async-start(bf16[8,384,128]{2,1,0:T(8,128)(2,1)} %bitcast.156), calls=%async_computation.3 | async-start | bytes 1572864 | tf_op jit(solution)/shard_map/all_to_all | solution.py:43
  215.0 7.5 %psum.43 = f32[2,384]{1,0:T(2,128)S(1)} all-reduce(f32[2,384]{1,0:T(2,128)S(1)} %pad_maximum_fusion.7), channel_id=1, replica_groups=mesh['x'=4,'k'=2,'y'=4,'z'=8] {'y'}, use_global_device_ids=true, to_apply=%region_9.10 | all-reduce | flops 768 | bytes 6144 | tf_op jit(solution)/shard_map/psum | solution.py:152
  222.4 17.4 %psum.44 = f32[2,384]{1,0:T(2,128)S(1)} all-reduce(f32[2,384]{1,0:T(2,128)S(1)} %psum.43), channel_id=1, replica_groups=mesh['x'=4,'k'=2,'y'=4,'z'=8] {'z'}, use_global_device_ids=true, to_apply=%region_10.11 | all-reduce | flops 768 | bytes 6144 | tf_op jit(solution)/shard_map/psum | solution.py:152
  239.9 7.7 %collective-permute-start.6 = (bf16[512,256]{1,0:T(8,128)(2,1)}, bf16[512,256]{1,0:T(8,128)(2,1)S(1)}, u32[]{:S(2)}, u32[]{:S(2)}) collective-permute-start(bf16[512,256]{1,0:T(8,128)(2,1)} %reduce-scatter.3.cloned.1.call-done), channel_id=1, source_target_pairs={{0,0},{8,64},{16,128},{24,192},{64,8},{72,72},{80,136},{88,200},{1... | collective-permute-start | bytes 786440 | tf_op jit(solution)/shard_map/ppermute | solution.py:37
  247.8 1.9 collective-permute-start.7
  250.6 27.7 %all-reduce = (f32[31,128]{1,0:T(8,128)}, f32[128]{0:T(128)}, f32[128]{0:T(128)}) all-reduce(f32[31,128]{1,0:T(8,128)S(1)} %stack.246, f32[128]{0:T(128)S(1)} %get-tuple-element.43, f32[128]{0:T(128)S(1)} %get-tuple-element.118), channel_id=1, replica_groups=mesh['x'=4,'k'=2,'y'=4,'z'=8] {'x','k'}, use_global_device_ids=true, to_apply=%region_43.44 | all-reduce | flops 4224 | bytes 33792 | tf_op jit(solution)/shard_map/psum | solution.py:161
  (225 shorter events, 30.1 us)
Async XLA Ops:
  7.2 75.0 %copy-start.11 = (bf16[384,128]{1,0:T(8,128)(2,1)S(1)}, bf16[384,128]{1,0:T(8,128)(2,1)}, u32[]{:S(2)}) copy-start(bf16[384,128]{1,0:T(8,128)(2,1)} %param.15) | copy-start | bytes 294916
  7.2 88.1 %all-gather.7.cloned.1.call-start = ((), (), s32[]{:S(2)}) async-start(), calls=%async_computation.7 | async-start | bytes 1179648 | tf_op jit(solution)/shard_map/all_gather | solution.py:61
  7.2 13.5 %collective-permute-start.3 = (bf16[512,128]{1,0:T(8,128)(2,1)}, bf16[512,128]{1,0:T(8,128)(2,1)S(1)}, u32[]{:S(2)}, u32[]{:S(2)}) collective-permute-start(bf16[512,128]{1,0:T(8,128)(2,1)} %param.14), channel_id=1, source_target_pairs={{0,0},{8,64},{16,128},{24,192},{64,8},{72,72},{80,136},{88,200},{1... | collective-permute-start | bytes 393224 | tf_op jit(solution)/shard_map/ppermute | solution.py:37
  21.4 75.5 %all-gather.5.cloned.1.call-start = ((), (), s32[]{:S(2)}) async-start(), calls=%async_computation.6 | async-start | bytes 2359296 | tf_op jit(solution)/shard_map/all_gather | solution.py:60
  22.4 17.7 %collective-permute-start = (bf16[512,256]{1,0:T(8,128)(2,1)S(1)}, bf16[512,256]{1,0:T(8,128)(2,1)S(1)}, u32[]{:S(2)}, u32[]{:S(2)}) collective-permute-start(bf16[512,256]{1,0:T(8,128)(2,1)S(1)} %pad_maximum_fusion.4), channel_id=1, source_target_pairs={{0,0},{8,64},{16,128},{24,192},{64,8},{72,72},{80,136},{88,200},{1... | collective-permute-start | bytes 786440 | tf_op jit(solution)/shard_map/ppermute | solution.py:37
  101.7 14.9 %all-to-all-start = ((bf16[4,384,256]{2,1,0:T(8,128)(2,1)}), bf16[4,384,256]{2,1,0:T(8,128)(2,1)}, u32[]{:S(2)}, u32[]{:S(2)}) async-start(bf16[4,384,256]{2,1,0:T(8,128)(2,1)} %pad_maximum_fusion.2), calls=%async_computation | async-start | bytes 1572864 | tf_op jit(solution)/shard_map/all_to_all | solution.py:43
  116.5 20.6 %all-to-all-start.2 = ((bf16[8,384,128]{2,1,0:T(8,128)(2,1)}), bf16[8,384,128]{2,1,0:T(8,128)(2,1)S(1)}, u32[]{:S(2)}, u32[]{:S(2)}) async-start(bf16[8,384,128]{2,1,0:T(8,128)(2,1)} %bitcast.158), calls=%async_computation.2 | async-start | bytes 1572864 | tf_op jit(solution)/shard_map/all_to_all | solution.py:43
  121.0 118.9 %reduce-scatter.3.cloned.1.call-start = ((), (), s32[]{:S(2)}) async-start(), calls=%async_computation.8 | async-start | bytes 2359296 | tf_op jit(solution)/shard_map/reduce_scatter | solution.py:139
  121.9 15.4 %copy-start.18 = (f32[384]{0:T(512)S(1)}, f32[384]{0:T(512)}, u32[]{:S(2)}) copy-start(f32[384]{0:T(512)} %get-tuple-element.92) | copy-start | bytes 4612
  122.0 15.4 %copy-start.19 = (f32[384]{0:T(512)S(1)}, f32[384]{0:T(512)}, u32[]{:S(2)}) copy-start(f32[384]{0:T(512)} %get-tuple-element.93) | copy-start | bytes 4612
  122.0 15.4 %copy-start.20 = (f32[384]{0:T(512)S(1)}, f32[384]{0:T(512)}, u32[]{:S(2)}) copy-start(f32[384]{0:T(512)} %get-tuple-element.75) | copy-start | bytes 4612
  122.0 15.4 %copy-start.21 = (f32[384]{0:T(512)S(1)}, f32[384]{0:T(512)}, u32[]{:S(2)}) copy-start(f32[384]{0:T(512)} %get-tuple-element.79) | copy-start | bytes 4612
  122.0 15.4 %copy-start.22 = (f32[384]{0:T(512)S(1)}, f32[384]{0:T(512)}, u32[]{:S(2)}) copy-start(f32[384]{0:T(512)} %get-tuple-element.80) | copy-start | bytes 4612
  122.0 15.4 %copy-start.23 = (f32[384]{0:T(512)S(1)}, f32[384]{0:T(512)}, u32[]{:S(2)}) copy-start(f32[384]{0:T(512)} %get-tuple-element.81) | copy-start | bytes 4612
  122.0 15.4 %copy-start.24 = (f32[384]{0:T(512)S(1)}, f32[384]{0:T(512)}, u32[]{:S(2)}) copy-start(f32[384]{0:T(512)} %get-tuple-element.94) | copy-start | bytes 4612
  122.0 15.4 %copy-start.25 = (f32[384]{0:T(512)S(1)}, f32[384]{0:T(512)}, u32[]{:S(2)}) copy-start(f32[384]{0:T(512)} %get-tuple-element.99) | copy-start | bytes 4612
  122.0 15.4 %copy-start.26 = (f32[384]{0:T(512)S(1)}, f32[384]{0:T(512)}, u32[]{:S(2)}) copy-start(f32[384]{0:T(512)} %get-tuple-element.100) | copy-start | bytes 4612
  122.0 15.4 %copy-start.27 = (f32[384]{0:T(512)S(1)}, f32[384]{0:T(512)}, u32[]{:S(2)}) copy-start(f32[384]{0:T(512)} %get-tuple-element.101) | copy-start | bytes 4612
  122.0 15.4 %copy-start.28 = (f32[384]{0:T(512)S(1)}, f32[384]{0:T(512)}, u32[]{:S(2)}) copy-start(f32[384]{0:T(512)} %get-tuple-element.102) | copy-start | bytes 4612
  122.1 15.4 %copy-start.29 = (f32[384]{0:T(512)S(1)}, f32[384]{0:T(512)}, u32[]{:S(2)}) copy-start(f32[384]{0:T(512)} %get-tuple-element.103) | copy-start | bytes 4612
  122.1 15.4 %copy-start.30 = (f32[384]{0:T(512)S(1)}, f32[384]{0:T(512)}, u32[]{:S(2)}) copy-start(f32[384]{0:T(512)} %get-tuple-element.104) | copy-start | bytes 4612
  124.9 12.4 %collective-permute-start.1 = (bf16[15,128]{1,0:T(8,128)(2,1)S(1)}, bf16[15,128]{1,0:T(8,128)(2,1)S(1)}, u32[]{:S(2)}, u32[]{:S(2)}) collective-permute-start(bf16[15,128]{1,0:T(8,128)(2,1)S(1)} %get-tuple-element.125), channel_id=1, source_target_pairs={{0,32},{32,64},{64,96},{96,128},{128,160},{160,192},{192,224},{1,3... | collective-permute-start | bytes 11528 | tf_op jit(solution)/shard_map/ppermute | solution.py:21
  126.2 11.1 %collective-permute-start.2 = (bf16[15,128]{1,0:T(8,128)(2,1)S(1)}, bf16[15,128]{1,0:T(8,128)(2,1)S(1)}, u32[]{:S(2)}, u32[]{:S(2)}) collective-permute-start(bf16[15,128]{1,0:T(8,128)(2,1)S(1)} %get-tuple-element.126), channel_id=1, source_target_pairs={{32,0},{64,32},{96,64},{128,96},{160,128},{192,160},{224,192},{33,... | collective-permute-start | bytes 11528 | tf_op jit(solution)/shard_map/ppermute | solution.py:22
  141.9 2.7 collective-permute-start.4
  143.1 3.1 %collective-permute-start.5 = (bf16[15,128]{1,0:T(8,128)(2,1)S(1)}, bf16[15,128]{1,0:T(8,128)(2,1)S(1)}, u32[]{:S(2)}, u32[]{:S(2)}) collective-permute-start(bf16[15,128]{1,0:T(8,128)(2,1)S(1)} %get-tuple-element.124), channel_id=1, source_target_pairs={{32,0},{64,32},{96,64},{128,96},{160,128},{192,160},{224,192},{33,... | collective-permute-start | bytes 11528 | tf_op jit(solution)/shard_map/ppermute | solution.py:22
  193.1 14.7 %all-to-all-start.1 = ((bf16[4,384,128]{2,1,0:T(8,128)(2,1)}), bf16[4,384,128]{2,1,0:T(8,128)(2,1)S(1)}, u32[]{:S(2)}, u32[]{:S(2)}) async-start(bf16[4,384,128]{2,1,0:T(8,128)(2,1)} %pad_maximum_fusion.3), calls=%async_computation.1 | async-start | bytes 786432 | tf_op jit(solution)/shard_map/all_to_all | solution.py:43
  200.3 47.5 %reduce-scatter.5.cloned.1.call-start = ((), (), s32[]{:S(2)}) async-start(), calls=%async_computation.9 | async-start | bytes 1179648 | tf_op jit(solution)/shard_map/reduce_scatter | solution.py:101
  207.8 39.8 %all-to-all-start.3 = ((bf16[8,384,128]{2,1,0:T(8,128)(2,1)}), bf16[8,384,128]{2,1,0:T(8,128)(2,1)S(1)}, u32[]{:S(2)}, u32[]{:S(2)}) async-start(bf16[8,384,128]{2,1,0:T(8,128)(2,1)} %bitcast.156), calls=%async_computation.3 | async-start | bytes 1572864 | tf_op jit(solution)/shard_map/all_to_all | solution.py:43
  214.2 35.5 %copy-start.10 = (bf16[384,128]{1,0:T(8,128)(2,1)S(1)}, bf16[384,128]{1,0:T(8,128)(2,1)}, u32[]{:S(2)}) copy-start(bf16[384,128]{1,0:T(8,128)(2,1)} %param.8) | copy-start | bytes 294916
  214.2 35.5 %copy-start.12 = (bf16[384,128]{1,0:T(8,128)(2,1)S(1)}, bf16[384,128]{1,0:T(8,128)(2,1)}, u32[]{:S(2)}) copy-start(bf16[384,128]{1,0:T(8,128)(2,1)} %param.15) | copy-start | bytes 294916
  239.9 39.1 %collective-permute-start.6 = (bf16[512,256]{1,0:T(8,128)(2,1)}, bf16[512,256]{1,0:T(8,128)(2,1)S(1)}, u32[]{:S(2)}, u32[]{:S(2)}) collective-permute-start(bf16[512,256]{1,0:T(8,128)(2,1)} %reduce-scatter.3.cloned.1.call-done), channel_id=1, source_target_pairs={{0,0},{8,64},{16,128},{24,192},{64,8},{72,72},{80,136},{88,200},{1... | collective-permute-start | bytes 786440 | tf_op jit(solution)/shard_map/ppermute | solution.py:37
  247.8 30.6 %collective-permute-start.7 = (bf16[512,128]{1,0:T(8,128)(2,1)}, bf16[512,128]{1,0:T(8,128)(2,1)S(1)}, u32[]{:S(2)}, u32[]{:S(2)}) collective-permute-start(bf16[512,128]{1,0:T(8,128)(2,1)} %reduce-scatter.5.cloned.1.call-done), channel_id=1, source_target_pairs={{0,0},{8,64},{16,128},{24,192},{64,8},{72,72},{80,136},{88,200},{1... | collective-permute-start | bytes 393224 | tf_op jit(solution)/shard_map/ppermute | solution.py:37
  (52 other events, 455.5 us)
Sparse Core Ops, SparseCore 0:
  21.5 25.9 all-gather.6
  49.9 28.0 all-gather.4
  167.2 33.6 reduce-scatter.2
  203.3 33.4 reduce-scatter.4

commit v2 on v1

v2 whole, which is shorter than its diff:
```python
import jax
import jax.numpy as jnp
from jax import lax
from jax.sharding import Mesh, PartitionSpec as P

K = 31
LEN = 2048
HALF = K // 2
NX, NK, NY, NZ = 4, 2, 4, 8
ROW = ("x", "k")
COL = ("y", "z")
TIME = ("y", "k")


epsilon = 1e-05


def extended(block, width):
    place = [k * NY + y for y in range(NY) for k in range(NK)]
    forward = list(zip(place[:-1], place[1:]))
    backward = [(target, source) for source, target in forward]
    low = lax.ppermute(block[-width:], ("k", "y"), forward)
    high = lax.ppermute(block[:width], ("k", "y"), backward)
    return jnp.concatenate([low, block, high], axis=0)


def tap_masks(positions):
    offsets = jnp.arange(K, dtype=jnp.int32) - HALF
    placed = (positions % LEN)[None, :] + offsets[:, None]
    return ((placed >= 0) & (placed < LEN)).astype(jnp.float32)


def dot(left, right, dims):
    return lax.dot_general(left, right, (dims, ((), ())), preferred_element_type=jnp.float32)


def swap_xy(block):
    return lax.ppermute(
        block, ("x", "y"), [(a * NY + b, b * NY + a) for a in range(NX) for b in range(NY)]
    )


def exchange(parts, axis):
    return lax.all_to_all(parts, axis, 0, 0, tiled=True)


def gathered(block, axis, count):
    return exchange(jnp.broadcast_to(block[None], (count,) + block.shape), axis)


def pieces(value):
    out = []
    for _ in range(3):
        piece = lax.reduce_precision(value, 8, 7)
        out.append(piece.astype(jnp.bfloat16))
        value = value - piece
    return jnp.stack(out)


def rows_of(value, lanes, count):
    flat = pieces(value).reshape(-1)
    flat = jnp.pad(flat, (0, count * lanes - flat.shape[0]))
    return flat.reshape(count, lanes)


def from_rows(rows, shape):
    size = 1
    for extent in shape:
        size = size * extent
    total = jnp.sum(rows.astype(jnp.float32), axis=0).reshape(-1)[: 3 * size]
    return jnp.sum(total.reshape((3,) + shape), axis=0)


def shards(frames, gain, w_value, w_gate, kernel, bias, w_out, grad_out):
    bf16 = jnp.bfloat16
    rows, cols = frames.shape
    width = cols * NX * NZ
    quarter = cols * NZ
    x_index = lax.axis_index("x")
    k_index = lax.axis_index("k")
    row_start = (lax.axis_index("y") * NK + k_index) * rows
    col_start = (x_index * NZ + lax.axis_index("z")) * cols
    local_gain = lax.dynamic_slice_in_dim(gain, col_start, cols, 0)
    quarter_gain = lax.dynamic_slice_in_dim(gain, x_index * quarter, quarter, 0)

    swapped = swap_xy(jnp.concatenate([frames, grad_out], axis=1))
    frames = swapped[:, :cols]
    grad_out = swapped[:, cols:]
    taps = swap_xy(jnp.concatenate([kernel, bias[None, :]], axis=0))
    kernel = taps[:K]
    bias = taps[K]

    vg_own = jnp.concatenate([w_value, w_gate], axis=1)
    vg_full = lax.all_gather(vg_own, TIME, axis=0, tiled=True).reshape(NY, quarter, 2 * cols)
    out_full = lax.all_gather(w_out, TIME, axis=0, tiled=True).reshape(NY, quarter, cols)

    frames_q = gathered(frames, "z", NZ).transpose(1, 0, 2).reshape(rows, quarter)
    grad_full = gathered(grad_out, "x", NX)
    wide_q = frames_q.astype(jnp.float32)
    sums = lax.psum(jnp.stack([jnp.sum(wide_q, axis=1), jnp.sum(wide_q * wide_q, axis=1)]), "x")
    mean_row = sums[0] / width
    inv_std = lax.rsqrt(sums[1] / width - mean_row * mean_row + epsilon)
    centred_q = (wide_q - mean_row[:, None]) * inv_std[:, None]
    normed_q = (centred_q * quarter_gain[None, :]).astype(bf16)
    wide = frames.astype(jnp.float32)
    centred = (wide - mean_row[:, None]) * inv_std[:, None]

    unit_terms = jnp.sum(vg_full.astype(jnp.float32) * quarter_gain[None, :, None], axis=1)
    pre_parts = []
    for i in range(NX):
        main = dot(normed_q, vg_full[i], ((1,), (0,))).astype(bf16)
        pre_parts.append(jnp.concatenate([main, rows_of(unit_terms[i], 2 * cols, 16)], axis=0))
    pre_moved = exchange(jnp.stack(pre_parts), "x")
    unit = from_rows(pre_moved[:, rows:], (2 * cols,))
    pre = jnp.sum(pre_moved[:, :rows].astype(jnp.float32), axis=0)
    value_pre = pre[:, :cols]
    gate_pre = pre[:, cols:]
    gate_sig = jax.nn.sigmoid(gate_pre)
    gated = (value_pre * gate_sig).astype(bf16)

    padded_glu = extended(gated, HALF).astype(jnp.float32)
    local_masks = tap_masks(row_start + jnp.arange(rows, dtype=jnp.int32))
    conv_pre = jnp.zeros((rows, cols), jnp.float32) + bias[None, :]
    for tap in range(K):
        conv_pre = (
            conv_pre
            + kernel[tap][None, :] * local_masks[tap][:, None] * padded_glu[tap : tap + rows]
        )
    conv_sig = jax.nn.sigmoid(conv_pre)
    activated = (conv_pre * conv_sig).astype(bf16)

    act_terms = sum(dot(grad_full[i], out_full[i], ((1,), (1,))) for i in range(NX))
    act_parts = act_terms.astype(bf16).reshape(rows, NZ, cols).transpose(1, 0, 2)
    act_grad = jnp.sum(exchange(act_parts, "z").astype(jnp.float32), axis=0)

    conv_grad = (act_grad * conv_sig * (1.0 + conv_pre * (1.0 - conv_sig))).astype(bf16)
    conv_wide = conv_grad.astype(jnp.float32)
    padded_grad = extended(conv_grad, HALF).astype(jnp.float32)
    outer_masks = tap_masks(row_start - HALF + jnp.arange(rows + 2 * HALF, dtype=jnp.int32))
    glu_grad = jnp.zeros((rows, cols), jnp.float32)
    kernel_rows = []
    for tap in range(K):
        begin = 2 * HALF - tap
        glu_grad = (
            glu_grad
            + kernel[tap][None, :]
            * outer_masks[tap, begin : begin + rows][:, None]
            * padded_grad[begin : begin + rows]
        )
        kernel_rows.append(
            jnp.sum(
                local_masks[tap][:, None] * conv_wide * padded_glu[tap : tap + rows],
                axis=0,
            )
        )
    bias_term = jnp.sum(conv_wide, axis=0)

    value_grad = (glu_grad * gate_sig).astype(bf16)
    gate_grad = (glu_grad * value_pre * gate_sig * (1.0 - gate_sig)).astype(bf16)
    vg_grad = jnp.concatenate([value_grad, gate_grad], axis=1)
    vg_wide = vg_grad.astype(jnp.float32)
    hat_terms = jnp.stack(
        [jnp.sum(vg_wide * unit[None, :], axis=1), jnp.sum(vg_wide * pre, axis=1)]
    )
    vg_moved = gathered(
        jnp.concatenate([vg_grad, rows_of(hat_terms, 2 * cols, 16)], axis=0), "x", NX
    )
    vg_grads = vg_moved[:, :rows]
    hat_part = from_rows(vg_moved[:, rows:], (2, rows))

    weight_parts = jnp.stack([dot(normed_q, vg_grads[i], ((0,), (0,))) for i in range(NX)])
    weight_parts = weight_parts.astype(bf16).reshape(NY, NK, quarter // NK, 2 * cols)
    kept = lax.dynamic_index_in_dim(weight_parts, k_index, 1, keepdims=False)
    given = lax.dynamic_index_in_dim(weight_parts, 1 - k_index, 1, keepdims=False)
    taken = lax.ppermute(given, "k", [(0, 1), (1, 0)])
    both = (kept.astype(jnp.float32) + taken.astype(jnp.float32)).astype(bf16)
    in_weight = jnp.sum(exchange(both, "y").astype(jnp.float32), axis=0)
    grad_value = in_weight[:, :cols]
    grad_gate = in_weight[:, cols:]

    norm_terms = sum(dot(vg_grads[i], vg_full[i], ((1,), (1,))) for i in range(NX))
    norm_parts = norm_terms.astype(bf16).reshape(rows, NZ, cols).transpose(1, 0, 2)
    hat_rows = jnp.broadcast_to(rows_of(hat_part, cols, 32)[None], (NZ, 32, cols))
    norm_moved = exchange(jnp.concatenate([norm_parts, hat_rows], axis=1), "z")
    hat_sums = from_rows(norm_moved[:, rows:], (2, rows)) / width
    normed_grad = jnp.sum(norm_moved[:, :rows].astype(jnp.float32), axis=0)
    hat_grad = normed_grad * local_gain[None, :]
    input_grad = (
        grad_out.astype(jnp.float32)
        + inv_std[:, None] * (hat_grad - hat_sums[0][:, None] - centred * hat_sums[1][:, None])
    ).astype(bf16)
    input_grad = swap_xy(input_grad)

    act_q = gathered(activated, "z", NZ).transpose(1, 0, 2).reshape(rows, quarter)
    out_weight_parts = jnp.stack([dot(act_q, grad_full[i], ((0,), (0,))) for i in range(NX)])
    grad_out_weight = lax.psum_scatter(
        out_weight_parts.astype(bf16).reshape(NY * quarter, cols),
        TIME,
        scatter_dimension=0,
        tiled=True,
    ).astype(jnp.float32)
    enc_parts = jnp.stack([dot(act_q, out_full[i], ((1,), (0,))) for i in range(NX)]).astype(bf16)
    enc_sum = jnp.sum(exchange(enc_parts, "x").astype(jnp.float32), axis=0)
    encoded = swap_xy((wide + enc_sum).astype(bf16))

    gain_term = jnp.sum(normed_grad * centred, axis=0)
    small = jnp.stack(kernel_rows + [bias_term, gain_term])
    small = small + lax.ppermute(small, "k", [(0, 1), (1, 0)])
    arrived = []
    for shift in range(NX):
        route = [
            (a * NY + b, ((b + shift) % NX) * NY + a) for a in range(NX) for b in range(NY)
        ]
        arrived.append(lax.ppermute(small, ("x", "y"), route))
    small = sum(arrived)
    return (
        encoded,
        input_grad,
        grad_value,
        grad_gate,
        small[:K],
        small[K],
        grad_out_weight,
        small[K + 1],
    )


def solution(mesh):
    fine = Mesh(mesh.devices.reshape(NX, NK, NY, NZ), ("x", "k", "y", "z"))
    both = P(ROW, COL)
    return jax.shard_map(
        shards,
        mesh=fine,
        in_specs=(both, P(), both, both, P(None, COL), P(COL), both, both),
        out_specs=(both, both, both, both, P(None, COL), P(COL), both, P(COL)),
        check_vma=False,
    )
```

time: 287 us -> 276 us (0.962)
  the two profiles are of different devices: /device:TPU:24 before, /device:TPU:6 now
where the time goes in v2:
time: 276 us; the launch traced here: 274 us
  starting transfers between devices  91.5 us (33%)
  waiting for transfers between devices  82.4 us (30%)
  other arithmetic  34.1 us (12%)
  matrix products  22.3 us (8%)
  local copies, waits for them, and re-layouts  20.8 us (8%)
  between operations  15.7 us (6%)
  blocking collectives  7.48 us (3%)
    all_to_all x9, waiting for transfers between devices, exchange(): return lax.all_to_all(parts, axis, 0, 0, tiled=True)  62.4 us
    all_to_all x9, starting transfers between devices, exchange(): return lax.all_to_all(parts, axis, 0, 0, tiled=True)  51.6 us
    dot_general x24, matrix products, dot(): lax.dot_general(left, right, (dims, ((), ())), preferred_element_type=jnp...  22.3 us
    ppermute x4, starting transfers between devices, swap_xy(): lax.ppermute(block, ('x', 'y'), [(a * NY + b, b * NY + a) for a in range(...  18.8 us
    ppermute x4, waiting for transfers between devices, swap_xy(): lax.ppermute(block, ('x', 'y'), [(a * NY + b, b * NY + a) for a in range(...  14.5 us
    ppermute x4, starting transfers between devices, shards(): arrived.append(lax.ppermute(small, ('x', 'y'), route))  12.2 us
    reduce_sum x4, other arithmetic, shards(): jnp.sum(local_masks[tap][:, None] * conv_wide * padded_glu[tap:tap + rows...  7.74 us
    psum x1, blocking collectives, shards(): lax.psum(jnp.stack([jnp.sum(wide_q, axis=1), jnp.sum(wide_q * wide_q, axi...  7.48 us
  transfers between devices with their start and end apart: 26, of which 13 were waited for; matrix products, arithmetic and copies ran while one was open for 23% of the time, Pallas kernels for 0%

profile of v2, /device:TPU:6, one launch (start us, length us, event | category | flops | bytes accessed | tf_op | source)
XLA Modules:
  0.0 274.3 jit_solution(14298450669366844797)
XLA Ops:
  8.9 4.8 %collective-permute-start = (bf16[384,256]{1,0:T(8,128)(2,1)S(1)}, bf16[384,256]{1,0:T(8,128)(2,1)S(1)}, u32[]{:S(2)}, u32[]{:S(2)}) collective-permute-start(bf16[384,256]{1,0:T(8,128)(2,1)S(1)} %pad_maximum_fusion.7), channel_id=1, source_target_pairs={{0,0},{8,64},{16,128},{24,192},{64,8},{72,72},{80,136},{88,200},{1... | collective-permute-start | bytes 589832 | tf_op jit(solution)/shard_map/ppermute | solution.py:38
  15.5 9.5 %collective-permute-done = bf16[384,256]{1,0:T(8,128)(2,1)S(1)} collective-permute-done((bf16[384,256]{1,0:T(8,128)(2,1)S(1)}, bf16[384,256]{1,0:T(8,128)(2,1)S(1)}, u32[]{:S(2)}, u32[]{:S(2)}) %collective-permute-start) | collective-permute-done | bytes 196640 | tf_op jit(solution)/shard_map/ppermute | solution.py:38
  26.1 8.5 %all-to-all-start = ((bf16[8,384,128]{1,2,0:T(8,128)(2,1)}), bf16[8,384,128]{1,2,0:T(8,128)(2,1)S(1)}, u32[]{:S(2)}, u32[]{:S(2)}) async-start(bf16[8,384,128]{1,2,0:T(8,128)(2,1)} %broadcast_in_dim.15), calls=%async_computation | async-start | bytes 1572864 | tf_op jit(solution)/shard_map/all_to_all | solution.py:44
  35.2 4.8 %collective-permute-start.1 = (f32[32,128]{1,0:T(8,128)}, f32[32,128]{1,0:T(8,128)}, u32[]{:S(2)}, u32[]{:S(2)}) collective-permute-start(f32[32,128]{1,0:T(8,128)} %pad_maximum_fusion.9), channel_id=1, source_target_pairs={{0,0},{8,64},{16,128},{24,192},{64,8},{72,72},{80,136},{88,200},{1... | collective-permute-start | bytes 49160 | tf_op jit(solution)/shard_map/ppermute | solution.py:38
  43.8 13.1 %all-to-all-done = bf16[8,384,128]{1,2,0:T(8,128)(2,1)S(1)} async-done(((bf16[8,384,128]{1,2,0:T(8,128)(2,1)}), bf16[8,384,128]{1,2,0:T(8,128)(2,1)S(1)}, u32[]{:S(2)}, u32[]{:S(2)}) %all-to-all-start) | async-done | bytes 786464 | tf_op jit(solution)/shard_map/all_to_all | solution.py:44
  57.6 4.5 %all-to-all-start.4 = ((bf16[4,384,128]{2,1,0:T(8,128)(2,1)}), bf16[4,384,128]{2,1,0:T(8,128)(2,1)S(1)}, u32[]{:S(2)}, u32[]{:S(2)}) async-start(bf16[4,384,128]{2,1,0:T(8,128)(2,1)} %broadcast_in_dim.17), calls=%async_computation.4 | async-start | bytes 786432 | tf_op jit(solution)/shard_map/all_to_all | solution.py:44
  62.4 7.5 %psum.7 = f32[2,384]{1,0:T(2,128)S(1)} all-reduce(f32[2,384]{1,0:T(2,128)S(1)} %pad_maximum_fusion.12), channel_id=1, replica_groups=mesh['x'=4,'k'=2,'y'=4,'z'=8] {'x'}, use_global_device_ids=true, to_apply=%region_2.0 | all-reduce | flops 768 | bytes 6144 | tf_op jit(solution)/shard_map/psum | solution.py:100
  74.7 4.2 %all-to-all-start.5 = ((bf16[8,384,128]{2,1,0:T(8,128)(2,1)}), bf16[8,384,128]{2,1,0:T(8,128)(2,1)}, u32[]{:S(2)}, u32[]{:S(2)}) async-start(bf16[8,384,128]{2,1,0:T(8,128)(2,1)} %bitcast.245), calls=%async_computation.5 | async-start | bytes 1572864 | tf_op jit(solution)/shard_map/all_to_all | solution.py:44
  79.0 2.2 fusion
  85.5 14.2 %all-to-all-done.5 = bf16[8,384,128]{2,1,0:T(8,128)(2,1)} async-done(((bf16[8,384,128]{2,1,0:T(8,128)(2,1)}), bf16[8,384,128]{2,1,0:T(8,128)(2,1)}, u32[]{:S(2)}, u32[]{:S(2)}) %all-to-all-start.5) | async-done | bytes 786464 | tf_op jit(solution)/shard_map/all_to_all | solution.py:44
  99.8 6.5 %all-to-all-start.1 = ((bf16[4,400,256]{2,1,0:T(8,128)(2,1)}), bf16[4,400,256]{2,1,0:T(8,128)(2,1)S(1)}, u32[]{:S(2)}, u32[]{:S(2)}) async-start(bf16[4,400,256]{2,1,0:T(8,128)(2,1)} %pad_maximum_fusion.3), calls=%async_computation.1 | async-start | bytes 1638400 | tf_op jit(solution)/shard_map/all_to_all | solution.py:44
  118.9 3.9 %fusion.109 = (f32[128]{0:T(128)}, f32[128]{0:T(128)}, f32[128]{0:T(128)}, f32[128]{0:T(128)}, f32[128]{0:T(128)}, /*index=5*/f32[128]{0:T(128)}, f32[128]{0:T(1...) fusion(f32[414,128]{1,0:T(8,128)S(1)} %maximum_convert_fusion, ...), kind=kLoop, calls=%fused_computation.188 | loop fusion | flops 6388608 | bytes 6654976 | tf_op jit(solution)/shard_map/reduce_sum | solution.py:151
  122.8 4.0 %collective-permute-start.5 = (bf16[15,128]{1,0:T(8,128)(2,1)S(1)}, bf16[15,128]{1,0:T(8,128)(2,1)S(1)}, u32[]{:S(2)}, u32[]{:S(2)}) collective-permute-start(bf16[15,128]{1,0:T(8,128)(2,1)S(1)} %get-tuple-element.121), channel_id=1, source_target_pairs={{0,32},{32,8},{8,40},{40,16},{16,48},{48,24},{24,56},{1,33},{33,9}... | collective-permute-start | bytes 11528 | tf_op jit(solution)/shard_map/ppermute | solution.py:22
  130.0 3.2 %multiply_convert_fusion.2 = (bf16[384,128]{1,0:T(8,128)(2,1)S(1)}, f32[384,128]{1,0:T(8,128)S(1)}) fusion(f32[384,256]{1,0:T(8,128)S(1)} %convert_reduce_fusion.4, f32[414,128]{1,0:T(8,128)S(1)} %maximum_convert_fusion.1, f32[384]{0:T(512)S(1)} %copy-done.36, f32[128]{0:T(128)S(1)} %get-tuple-element.128, f32[384]{0:T(512)S(1)} %copy-done.37, ...), kind=kLoop, calls=%fused_computation.269 | loop fusion | flops 4767744 | bytes 6649856 | tf_op jit(solution)/shard_map/convert_element_type | solution.py:158
  134.6 5.5 %all-to-all-start.6 = ((bf16[4,400,256]{2,1,0:T(8,128)(2,1)}), bf16[4,400,256]{2,1,0:T(8,128)(2,1)S(1)}, u32[]{:S(2)}, u32[]{:S(2)}) async-start(bf16[4,400,256]{2,1,0:T(8,128)(2,1)} %broadcast_in_dim.18), calls=%async_computation.6 | async-start | bytes 1638400 | tf_op jit(solution)/shard_map/all_to_all | solution.py:44
  143.1 8.1 %all-to-all-done.6 = bf16[4,400,256]{2,1,0:T(8,128)(2,1)S(1)} async-done(((bf16[4,400,256]{2,1,0:T(8,128)(2,1)}), bf16[4,400,256]{2,1,0:T(8,128)(2,1)S(1)}, u32[]{:S(2)}, u32[]{:S(2)}) %all-to-all-start.6) | async-done | bytes 819232 | tf_op jit(solution)/shard_map/all_to_all | solution.py:44
  152.2 3.7 %all-to-all-start.2 = ((bf16[8,384,128]{1,2,0:T(8,128)(2,1)}), bf16[8,384,128]{1,2,0:T(8,128)(2,1)S(1)}, u32[]{:S(2)}, u32[]{:S(2)}) async-start(bf16[8,384,128]{1,2,0:T(8,128)(2,1)} %broadcast_in_dim.16), calls=%async_computation.2 | async-start | bytes 1572864 | tf_op jit(solution)/shard_map/all_to_all | solution.py:44
  170.0 8.1 %all-to-all-done.2 = bf16[8,384,128]{1,2,0:T(8,128)(2,1)S(1)} async-done(((bf16[8,384,128]{1,2,0:T(8,128)(2,1)}), bf16[8,384,128]{1,2,0:T(8,128)(2,1)S(1)}, u32[]{:S(2)}, u32[]{:S(2)}) %all-to-all-start.2) | async-done | bytes 786464 | tf_op jit(solution)/shard_map/all_to_all | solution.py:44
  182.6 6.1 %all-to-all-start.3 = ((bf16[4,384,128]{2,1,0:T(8,128)(2,1)}), bf16[4,384,128]{2,1,0:T(8,128)(2,1)}, u32[]{:S(2)}, u32[]{:S(2)}) async-start(bf16[4,384,128]{2,1,0:T(8,128)(2,1)} %pad_maximum_fusion.4), calls=%async_computation.3 | async-start | bytes 786432 | tf_op jit(solution)/shard_map/all_to_all | solution.py:44
  188.7 2.8 %fusion.6 = bf16[48,8,8,128]{3,2,1,0:T(8,128)(2,1)S(1)} fusion(f32[384,1024]{1,0:T(8,128)} %fusion.21, f32[384,1024]{1,0:T(8,128)} %fusion.27, f32[384,1024]{1,0:T(8,128)} %fusion.24, bf16[4096,256]{1,0:T(8,128)(2,1)S(1)} %copy-done.1, bf16[4,400,256]{2,1,0:T(8,128)(2,1)} %copy-done.4), kind=kOutput, calls=%fused_computation.50 | convolution fusion | flops 202899456 | bytes 6225920 | tf_op jit(solution)/shard_map/dot_general | solution.py:34
  192.7 2.7 all-to-all-done.3
  195.4 4.2 %all-to-all-start.7 = ((bf16[8,416,128]{2,1,0:T(8,128)(2,1)}), bf16[8,416,128]{2,1,0:T(8,128)(2,1)}, u32[]{:S(2)}, u32[]{:S(2)}) async-start(bf16[8,416,128]{2,1,0:T(8,128)(2,1)} %pad_maximum_fusion.2), calls=%async_computation.7 | async-start | bytes 1703936 | tf_op jit(solution)/shard_map/all_to_all | solution.py:44
  205.1 2.5 fusion.1
  209.0 14.8 %all-to-all-done.7 = bf16[8,416,128]{2,1,0:T(8,128)(2,1)} async-done(((bf16[8,416,128]{2,1,0:T(8,128)(2,1)}), bf16[8,416,128]{2,1,0:T(8,128)(2,1)}, u32[]{:S(2)}, u32[]{:S(2)}) %all-to-all-start.7) | async-done | bytes 852000 | tf_op jit(solution)/shard_map/all_to_all | solution.py:44
  223.8 8.3 %all-to-all-start.8 = ((bf16[4,512,256]{2,1,0:T(8,128)(2,1)}), bf16[4,512,256]{2,1,0:T(8,128)(2,1)S(1)}, u32[]{:S(2)}, u32[]{:S(2)}) async-start(bf16[4,512,256]{2,1,0:T(8,128)(2,1)} %fusion.1), calls=%async_computation.8 | async-start | bytes 2097152 | tf_op jit(solution)/shard_map/all_to_all | solution.py:44
  236.3 3.2 %collective-permute-start.13 = (f32[33,128]{1,0:T(8,128)S(1)}, f32[33,128]{1,0:T(8,128)S(1)}, u32[]{:S(2)}, u32[]{:S(2)}) collective-permute-start(f32[33,128]{1,0:T(8,128)S(1)} %add.451), channel_id=1, source_target_pairs={{0,192},{8,0},{16,64},{24,128},{64,200},{72,8},{80,72},{88,136},{1... | collective-permute-start | bytes 50696 | tf_op jit(solution)/shard_map/ppermute | solution.py:214
  239.9 4.1 %collective-permute-start.11 = (f32[33,128]{1,0:T(8,128)S(1)}, f32[33,128]{1,0:T(8,128)S(1)}, u32[]{:S(2)}, u32[]{:S(2)}) collective-permute-start(f32[33,128]{1,0:T(8,128)S(1)} %add.451), channel_id=1, source_target_pairs={{0,64},{8,128},{16,192},{24,0},{64,72},{72,136},{80,200},{88,8},{1... | collective-permute-start | bytes 50696 | tf_op jit(solution)/shard_map/ppermute | solution.py:214
  243.9 4.6 %collective-permute-start.10 = (f32[33,128]{1,0:T(8,128)S(1)}, f32[33,128]{1,0:T(8,128)S(1)}, u32[]{:S(2)}, u32[]{:S(2)}) collective-permute-start(f32[33,128]{1,0:T(8,128)S(1)} %add.451), channel_id=1, source_target_pairs={{0,0},{8,64},{16,128},{24,192},{64,8},{72,72},{80,136},{88,200},{1... | collective-permute-start | bytes 50696 | tf_op jit(solution)/shard_map/ppermute | solution.py:214
  248.5 4.6 %collective-permute-start.7 = (bf16[384,128]{1,0:T(8,128)(2,1)S(1)}, bf16[384,128]{1,0:T(8,128)(2,1)S(1)}, u32[]{:S(2)}, u32[]{:S(2)}) collective-permute-start(bf16[384,128]{1,0:T(8,128)(2,1)S(1)} %get-tuple-element.117), channel_id=1, source_target_pairs={{0,0},{8,64},{16,128},{24,192},{64,8},{72,72},{80,136},{88,200},{1... | collective-permute-start | bytes 294920 | tf_op jit(solution)/shard_map/ppermute | solution.py:38
  253.1 4.6 %collective-permute-start.4 = (bf16[384,128]{1,0:T(8,128)(2,1)S(1)}, bf16[384,128]{1,0:T(8,128)(2,1)S(1)}, u32[]{:S(2)}, u32[]{:S(2)}) collective-permute-start(bf16[384,128]{1,0:T(8,128)(2,1)S(1)} %get-tuple-element.118), channel_id=1, source_target_pairs={{0,0},{8,64},{16,128},{24,192},{64,8},{72,72},{80,136},{88,200},{1... | collective-permute-start | bytes 294920 | tf_op jit(solution)/shard_map/ppermute | solution.py:38
  258.9 2.0 collective-permute-done.7
  260.9 3.0 %collective-permute-done.4 = bf16[384,128]{1,0:T(8,128)(2,1)S(1)} collective-permute-done((bf16[384,128]{1,0:T(8,128)(2,1)S(1)}, bf16[384,128]{1,0:T(8,128)(2,1)S(1)}, u32[]{:S(2)}, u32[]{:S(2)}) %collective-permute-start.4) | collective-permute-done | bytes 98336 | tf_op jit(solution)/shard_map/ppermute | solution.py:38
  (337 shorter events, 74.7 us)
Async XLA Ops:
  7.2 64.0 %all-gather.5.cloned.1.call-start = ((), (), s32[]{:S(2)}) async-start(), calls=%async_computation.11 | async-start | bytes 1179648 | tf_op jit(solution)/shard_map/all_gather | solution.py:95
  7.9 71.1 %all-gather.3.cloned.1.call-start = ((), (), s32[]{:S(2)}) async-start(), calls=%async_computation.10 | async-start | bytes 2359296 | tf_op jit(solution)/shard_map/all_gather | solution.py:94
  8.9 16.1 %collective-permute-start = (bf16[384,256]{1,0:T(8,128)(2,1)S(1)}, bf16[384,256]{1,0:T(8,128)(2,1)S(1)}, u32[]{:S(2)}, u32[]{:S(2)}) collective-permute-start(bf16[384,256]{1,0:T(8,128)(2,1)S(1)} %pad_maximum_fusion.7), channel_id=1, source_target_pairs={{0,0},{8,64},{16,128},{24,192},{64,8},{72,72},{80,136},{88,200},{1... | collective-permute-start | bytes 589832 | tf_op jit(solution)/shard_map/ppermute | solution.py:38
  26.1 30.7 %all-to-all-start = ((bf16[8,384,128]{1,2,0:T(8,128)(2,1)}), bf16[8,384,128]{1,2,0:T(8,128)(2,1)S(1)}, u32[]{:S(2)}, u32[]{:S(2)}) async-start(bf16[8,384,128]{1,2,0:T(8,128)(2,1)} %broadcast_in_dim.15), calls=%async_computation | async-start | bytes 1572864 | tf_op jit(solution)/shard_map/all_to_all | solution.py:44
  35.2 73.7 %collective-permute-start.1 = (f32[32,128]{1,0:T(8,128)}, f32[32,128]{1,0:T(8,128)}, u32[]{:S(2)}, u32[]{:S(2)}) collective-permute-start(f32[32,128]{1,0:T(8,128)} %pad_maximum_fusion.9), channel_id=1, source_target_pairs={{0,0},{8,64},{16,128},{24,192},{64,8},{72,72},{80,136},{88,200},{1... | collective-permute-start | bytes 49160 | tf_op jit(solution)/shard_map/ppermute | solution.py:38
  57.6 13.5 %all-to-all-start.4 = ((bf16[4,384,128]{2,1,0:T(8,128)(2,1)}), bf16[4,384,128]{2,1,0:T(8,128)(2,1)S(1)}, u32[]{:S(2)}, u32[]{:S(2)}) async-start(bf16[4,384,128]{2,1,0:T(8,128)(2,1)} %broadcast_in_dim.17), calls=%async_computation.4 | async-start | bytes 786432 | tf_op jit(solution)/shard_map/all_to_all | solution.py:44
  74.7 25.0 %all-to-all-start.5 = ((bf16[8,384,128]{2,1,0:T(8,128)(2,1)}), bf16[8,384,128]{2,1,0:T(8,128)(2,1)}, u32[]{:S(2)}, u32[]{:S(2)}) async-start(bf16[8,384,128]{2,1,0:T(8,128)(2,1)} %bitcast.245), calls=%async_computation.5 | async-start | bytes 1572864 | tf_op jit(solution)/shard_map/all_to_all | solution.py:44
  99.8 14.1 %all-to-all-start.1 = ((bf16[4,400,256]{2,1,0:T(8,128)(2,1)}), bf16[4,400,256]{2,1,0:T(8,128)(2,1)S(1)}, u32[]{:S(2)}, u32[]{:S(2)}) async-start(bf16[4,400,256]{2,1,0:T(8,128)(2,1)} %pad_maximum_fusion.3), calls=%async_computation.1 | async-start | bytes 1638400 | tf_op jit(solution)/shard_map/all_to_all | solution.py:44
  114.1 2.6 collective-permute-start.2
  115.4 3.1 %collective-permute-start.3 = (bf16[15,128]{1,0:T(8,128)(2,1)S(1)}, bf16[15,128]{1,0:T(8,128)(2,1)S(1)}, u32[]{:S(2)}, u32[]{:S(2)}) collective-permute-start(bf16[15,128]{1,0:T(8,128)(2,1)S(1)} %get-tuple-element.124), channel_id=1, source_target_pairs={{32,0},{8,32},{40,8},{16,40},{48,16},{24,48},{56,24},{33,1},{9,33}... | collective-permute-start | bytes 11528 | tf_op jit(solution)/shard_map/ppermute | solution.py:23
  122.8 5.3 %collective-permute-start.5 = (bf16[15,128]{1,0:T(8,128)(2,1)S(1)}, bf16[15,128]{1,0:T(8,128)(2,1)S(1)}, u32[]{:S(2)}, u32[]{:S(2)}) collective-permute-start(bf16[15,128]{1,0:T(8,128)(2,1)S(1)} %get-tuple-element.121), channel_id=1, source_target_pairs={{0,32},{32,8},{8,40},{40,16},{16,48},{48,24},{24,56},{1,33},{33,9}... | collective-permute-start | bytes 11528 | tf_op jit(solution)/shard_map/ppermute | solution.py:22
  126.8 3.1 %collective-permute-start.6 = (bf16[15,128]{1,0:T(8,128)(2,1)S(1)}, bf16[15,128]{1,0:T(8,128)(2,1)S(1)}, u32[]{:S(2)}, u32[]{:S(2)}) collective-permute-start(bf16[15,128]{1,0:T(8,128)(2,1)S(1)} %get-tuple-element.122), channel_id=1, source_target_pairs={{32,0},{8,32},{40,8},{16,40},{48,16},{24,48},{56,24},{33,1},{9,33}... | collective-permute-start | bytes 11528 | tf_op jit(solution)/shard_map/ppermute | solution.py:23
  134.6 16.6 %all-to-all-start.6 = ((bf16[4,400,256]{2,1,0:T(8,128)(2,1)}), bf16[4,400,256]{2,1,0:T(8,128)(2,1)S(1)}, u32[]{:S(2)}, u32[]{:S(2)}) async-start(bf16[4,400,256]{2,1,0:T(8,128)(2,1)} %broadcast_in_dim.18), calls=%async_computation.6 | async-start | bytes 1638400 | tf_op jit(solution)/shard_map/all_to_all | solution.py:44
  152.2 25.9 %all-to-all-start.2 = ((bf16[8,384,128]{1,2,0:T(8,128)(2,1)}), bf16[8,384,128]{1,2,0:T(8,128)(2,1)S(1)}, u32[]{:S(2)}, u32[]{:S(2)}) async-start(bf16[8,384,128]{1,2,0:T(8,128)(2,1)} %broadcast_in_dim.16), calls=%async_computation.2 | async-start | bytes 1572864 | tf_op jit(solution)/shard_map/all_to_all | solution.py:44
  163.5 40.8 %collective-permute-start.8 = (bf16[4,512,256]{2,1,0:T(8,128)(2,1)}, bf16[4,512,256]{2,1,0:T(8,128)(2,1)}, u32[]{:S(2)}, u32[]{:S(2)}) collective-permute-start(bf16[4,512,256]{2,1,0:T(8,128)(2,1)} %dynamic-slice_bitcast_fusion), channel_id=1, source_target_pairs={{0,32},{32,0},{1,33},{33,1},{2,34},{34,2},{3,35},{35,3},{4,36},{36... | collective-permute-start | bytes 3145736 | tf_op jit(solution)/shard_map/ppermute | solution.py:175
  182.6 12.8 %all-to-all-start.3 = ((bf16[4,384,128]{2,1,0:T(8,128)(2,1)}), bf16[4,384,128]{2,1,0:T(8,128)(2,1)}, u32[]{:S(2)}, u32[]{:S(2)}) async-start(bf16[4,384,128]{2,1,0:T(8,128)(2,1)} %pad_maximum_fusion.4), calls=%async_computation.3 | async-start | bytes 786432 | tf_op jit(solution)/shard_map/all_to_all | solution.py:44
  195.4 28.4 %all-to-all-start.7 = ((bf16[8,416,128]{2,1,0:T(8,128)(2,1)}), bf16[8,416,128]{2,1,0:T(8,128)(2,1)}, u32[]{:S(2)}, u32[]{:S(2)}) async-start(bf16[8,416,128]{2,1,0:T(8,128)(2,1)} %pad_maximum_fusion.2), calls=%async_computation.7 | async-start | bytes 1703936 | tf_op jit(solution)/shard_map/all_to_all | solution.py:44
  199.6 65.3 %reduce-scatter.2.cloned.1.call-start = ((), (), s32[]{:S(2)}) async-start(), calls=%async_computation.12 | async-start | bytes 1179648 | tf_op jit(solution)/shard_map/reduce_scatter | solution.py:196
  208.7 25.9 %copy-start.60 = (f32[128]{0:T(128)S(1)}, f32[128]{0:T(128)}, u32[]{:S(2)}) copy-start(f32[128]{0:T(128)} %get-tuple-element.28) | copy-start | bytes 1540
  208.7 25.9 %copy-start.61 = (f32[128]{0:T(128)S(1)}, f32[128]{0:T(128)}, u32[]{:S(2)}) copy-start(f32[128]{0:T(128)} %get-tuple-element.29) | copy-start | bytes 1540
  208.8 25.9 %copy-start.62 = (f32[128]{0:T(128)S(1)}, f32[128]{0:T(128)}, u32[]{:S(2)}) copy-start(f32[128]{0:T(128)} %get-tuple-element.30) | copy-start | bytes 1540
  208.8 25.9 %copy-start.63 = (f32[128]{0:T(128)S(1)}, f32[128]{0:T(128)}, u32[]{:S(2)}) copy-start(f32[128]{0:T(128)} %get-tuple-element.31) | copy-start | bytes 1540
  208.8 25.9 %copy-start.64 = (f32[128]{0:T(128)S(1)}, f32[128]{0:T(128)}, u32[]{:S(2)}) copy-start(f32[128]{0:T(128)} %get-tuple-element.32) | copy-start | bytes 1540
  208.8 25.9 %copy-start.65 = (f32[128]{0:T(128)S(1)}, f32[128]{0:T(128)}, u32[]{:S(2)}) copy-start(f32[128]{0:T(128)} %get-tuple-element.33) | copy-start | bytes 1540
  223.8 40.1 %all-to-all-start.8 = ((bf16[4,512,256]{2,1,0:T(8,128)(2,1)}), bf16[4,512,256]{2,1,0:T(8,128)(2,1)S(1)}, u32[]{:S(2)}, u32[]{:S(2)}) async-start(bf16[4,512,256]{2,1,0:T(8,128)(2,1)} %fusion.1), calls=%async_computation.8 | async-start | bytes 2097152 | tf_op jit(solution)/shard_map/all_to_all | solution.py:44
  235.0 1.3 collective-permute-start.9
  236.3 16.8 %collective-permute-start.13 = (f32[33,128]{1,0:T(8,128)S(1)}, f32[33,128]{1,0:T(8,128)S(1)}, u32[]{:S(2)}, u32[]{:S(2)}) collective-permute-start(f32[33,128]{1,0:T(8,128)S(1)} %add.451), channel_id=1, source_target_pairs={{0,192},{8,0},{16,64},{24,128},{64,200},{72,8},{80,72},{88,136},{1... | collective-permute-start | bytes 50696 | tf_op jit(solution)/shard_map/ppermute | solution.py:214
  239.5 18.2 %collective-permute-start.12 = (f32[33,128]{1,0:T(8,128)S(1)}, f32[33,128]{1,0:T(8,128)S(1)}, u32[]{:S(2)}, u32[]{:S(2)}) collective-permute-start(f32[33,128]{1,0:T(8,128)S(1)} %add.451), channel_id=1, source_target_pairs={{0,128},{8,192},{16,0},{24,64},{64,136},{72,200},{80,8},{88,72},{1... | collective-permute-start | bytes 50696 | tf_op jit(solution)/shard_map/ppermute | solution.py:214
  239.9 17.9 %collective-permute-start.11 = (f32[33,128]{1,0:T(8,128)S(1)}, f32[33,128]{1,0:T(8,128)S(1)}, u32[]{:S(2)}, u32[]{:S(2)}) collective-permute-start(f32[33,128]{1,0:T(8,128)S(1)} %add.451), channel_id=1, source_target_pairs={{0,64},{8,128},{16,192},{24,0},{64,72},{72,136},{80,200},{88,8},{1... | collective-permute-start | bytes 50696 | tf_op jit(solution)/shard_map/ppermute | solution.py:214
  243.9 13.8 %collective-permute-start.10 = (f32[33,128]{1,0:T(8,128)S(1)}, f32[33,128]{1,0:T(8,128)S(1)}, u32[]{:S(2)}, u32[]{:S(2)}) collective-permute-start(f32[33,128]{1,0:T(8,128)S(1)} %add.451), channel_id=1, source_target_pairs={{0,0},{8,64},{16,128},{24,192},{64,8},{72,72},{80,136},{88,200},{1... | collective-permute-start | bytes 50696 | tf_op jit(solution)/shard_map/ppermute | solution.py:214
  248.5 12.4 %collective-permute-start.7 = (bf16[384,128]{1,0:T(8,128)(2,1)S(1)}, bf16[384,128]{1,0:T(8,128)(2,1)S(1)}, u32[]{:S(2)}, u32[]{:S(2)}) collective-permute-start(bf16[384,128]{1,0:T(8,128)(2,1)S(1)} %get-tuple-element.117), channel_id=1, source_target_pairs={{0,0},{8,64},{16,128},{24,192},{64,8},{72,72},{80,136},{88,200},{1... | collective-permute-start | bytes 294920 | tf_op jit(solution)/shard_map/ppermute | solution.py:38
  253.1 10.8 %collective-permute-start.4 = (bf16[384,128]{1,0:T(8,128)(2,1)S(1)}, bf16[384,128]{1,0:T(8,128)(2,1)S(1)}, u32[]{:S(2)}, u32[]{:S(2)}) collective-permute-start(bf16[384,128]{1,0:T(8,128)(2,1)S(1)} %get-tuple-element.118), channel_id=1, source_target_pairs={{0,0},{8,64},{16,128},{24,192},{64,8},{72,72},{80,136},{88,200},{1... | collective-permute-start | bytes 294920 | tf_op jit(solution)/shard_map/ppermute | solution.py:38
  (82 other events, 1069.1 us)
Sparse Core Ops, SparseCore 0:
  9.9 28.8 all-gather.4
  41.2 27.6 all-gather.2
  204.5 46.0 reduce-scatter.1

commit v3 on v1

v3 whole, which is shorter than its diff:
```python
import jax
import jax.numpy as jnp
from jax import lax
from jax.experimental import pallas as pl
from jax.experimental.pallas import tpu as pltpu
from jax.sharding import Mesh, PartitionSpec as P

K = 31
LEN = 2048
HALF = K // 2
NX, NK, NY, NZ = 4, 2, 4, 8
ROW = ("x", "k")
COL = ("y", "z")
TIME = ("y", "k")
ROWS = 384
COLS = 128
QUARTER = COLS * NZ
WIDTH = QUARTER * NX
EDGE = 32

epsilon = 1e-05
f32 = jnp.float32
bf16 = jnp.bfloat16


def dot(left, right, left_dim, right_dim):
    return lax.dot_general(
        left, right, (((left_dim,), (right_dim,)), ((), ())), preferred_element_type=f32
    )


def split3(value):
    high = value.astype(bf16)
    rest = value - high.astype(f32)
    middle = rest.astype(bf16)
    low = (rest - middle.astype(f32)).astype(bf16)
    return high, middle, low


def one_hot():
    lane = lax.broadcasted_iota(jnp.int32, (16, 128), 1)
    row = lax.broadcasted_iota(jnp.int32, (16, 128), 0)
    return jnp.where(lane == row, 1.0, 0.0).astype(bf16)


def columns_to_rows(first, second):
    lane = lax.broadcasted_iota(jnp.int32, (first.shape[0], 128), 1)
    grid = jnp.zeros((first.shape[0], 128), f32)
    for j, piece in enumerate(split3(first) + split3(second)):
        grid = jnp.where(lane == j, piece.astype(f32), grid)
    return dot(one_hot(), grid.astype(bf16), 1, 1)


def rows_to_columns(rows):
    grid = dot(rows, one_hot(), 0, 0)
    first = grid[:, 0:1] + grid[:, 1:2] + grid[:, 2:3]
    second = grid[:, 3:4] + grid[:, 4:5] + grid[:, 5:6]
    return first, second


def stacked_rows(values):
    row = lax.broadcasted_iota(jnp.int32, (16, values[0].shape[1]), 0)
    out = jnp.zeros((16, values[0].shape[1]), f32)
    for j, value in enumerate(values):
        out = jnp.where(row == j, value.astype(f32), out)
    return out


def call(body, out_shape, args, smem=(), scratch=()):
    specs = [
        pl.BlockSpec(memory_space=pltpu.SMEM if i in smem else pltpu.VMEM)
        for i in range(len(args))
    ]
    many = isinstance(out_shape, (list, tuple))
    out_specs = [pl.BlockSpec(memory_space=pltpu.VMEM) for _ in out_shape] if many else (
        pl.BlockSpec(memory_space=pltpu.VMEM)
    )
    return pl.pallas_call(
        body,
        out_shape=out_shape,
        in_specs=specs,
        out_specs=out_specs,
        scratch_shapes=list(scratch),
        compiler_params=pltpu.CompilerParams(vmem_limit_bytes=48 * 1024 * 1024),
    )(*args)


def shape(dims, kind):
    return jax.ShapeDtypeStruct(dims, kind)


def project_kernel(frames_ref, gain_ref, gain_rows_ref, weight_ref, out_ref, left_ref):
    total = jnp.zeros((ROWS, 1), f32)
    square = jnp.zeros((ROWS, 1), f32)
    for i in range(NZ):
        wide = frames_ref[i].astype(f32)
        total = total + jnp.sum(wide, axis=1, keepdims=True)
        square = square + jnp.sum(wide * wide, axis=1, keepdims=True)
    mean = total / QUARTER
    for i in range(NZ):
        cut = pl.ds(i * COLS, COLS)
        scaled = (frames_ref[i].astype(f32) - mean) * gain_ref[0:1, cut]
        left_ref[:, cut] = scaled.astype(bf16)
    sums = columns_to_rows(total, square).astype(bf16)
    for i in range(NX):
        weight = weight_ref[pl.ds(i * QUARTER, QUARTER), 0 : 2 * COLS]
        out_ref[i, 0:ROWS, :] = dot(left_ref[...], weight, 1, 0).astype(bf16)
        unit = jnp.sum(dot(gain_rows_ref[...], weight, 1, 0), axis=0, keepdims=True)
        out_ref[i, ROWS : ROWS + 16, :] = stacked_rows(split3(unit)).astype(bf16)
        out_ref[i, ROWS + 16 : ROWS + 32, :] = sums[:, 0:256]
        out_ref[i, ROWS + 32 : ROWS + 48, 0:128] = sums[:, 256:384]
        out_ref[i, ROWS + 32 : ROWS + 48, 128:256] = jnp.zeros((16, 128), bf16)


def gate_kernel(parts_ref, pre_ref, gated_ref, unit_ref, stat_ref):
    totals, squares, units = [], [], []
    for i in range(NX):
        rows = jnp.concatenate(
            [parts_ref[i, ROWS + 16 : ROWS + 32, :], parts_ref[i, ROWS + 32 : ROWS + 48, 0:128]],
            axis=1,
        )
        first, second = rows_to_columns(rows)
        totals.append(first)
        squares.append(second)
        pieces = parts_ref[i, ROWS : ROWS + 16, :].astype(f32)
        units.append(jnp.sum(pieces, axis=0, keepdims=True))
    mean = sum(totals) / WIDTH
    inv_std = lax.rsqrt(sum(squares) / WIDTH - mean * mean + epsilon)
    pre = jnp.zeros((ROWS, 2 * COLS), f32)
    for i in range(NX):
        pre = pre + parts_ref[i, 0:ROWS, :].astype(f32)
        pre = pre + (totals[i] / QUARTER - mean) * units[i]
    pre = pre * inv_std
    pre_ref[...] = pre
    gated_ref[...] = (pre[:, 0:COLS] * jax.nn.sigmoid(pre[:, COLS:])).astype(bf16)
    unit_ref[...] = jnp.broadcast_to(sum(units), (8, 2 * COLS))
    lane = lax.broadcasted_iota(jnp.int32, (ROWS, 128), 1)
    stat_ref[...] = jnp.where(lane == 0, mean, inv_std)


def act_kernel(place_ref, g0_ref, g1_ref, g2_ref, g3_ref, weight_ref, out_ref):
    total = jnp.zeros((ROWS, QUARTER), f32)
    for j, grad_ref in enumerate((g0_ref, g1_ref, g2_ref, g3_ref)):
        start = pl.multiple_of(place_ref[j] * QUARTER, QUARTER)
        weight = weight_ref[pl.ds(start, QUARTER), 2 * COLS : 3 * COLS]
        total = total + dot(grad_ref[...], weight, 1, 1)
    for i in range(NZ):
        out_ref[pl.ds(i * ROWS, ROWS), :] = total[:, i * COLS : (i + 1) * COLS].astype(bf16)


def conv_kernel(
    place_ref,
    gated_ref,
    low_ref,
    high_ref,
    act_ref,
    act_low_ref,
    act_high_ref,
    taps_ref,
    pre_ref,
    unit_ref,
    activated_ref,
    message_ref,
    small_ref,
    wide_ref,
    grad_ref,
    glu_ref,
    sums_ref,
    masked_ref,
    masked_grad_ref,
):
    border = place_ref[0]
    wide_ref[0:EDGE, :] = low_ref[...].astype(f32)
    wide_ref[EDGE : EDGE + ROWS, :] = gated_ref[...].astype(f32)
    wide_ref[EDGE + ROWS :, :] = high_ref[...].astype(f32)
    sums_ref[...] = jnp.zeros((K + 1, 8, COLS), f32)
    bias = taps_ref[K : K + 1, :]
    chunks = [(-16, 16), (0, 128), (128, 128), (256, 128), (ROWS, 16)]

    def same_clip(start, count):
        row = lax.broadcasted_iota(jnp.int32, (count + 32, COLS), 0) + (start - 16)
        inside = (row < border).astype(jnp.int32)
        own = jnp.where(start < border, 1, 0)
        return inside == own

    for start, count in chunks:
        here = wide_ref[pl.ds(start - 16 + EDGE, count + 32), :]
        masked_ref[0 : count + 32, :] = jnp.where(same_clip(start, count), here, 0.0)
        conv = jnp.broadcast_to(bias, (count, COLS))
        for tap in range(K):
            conv = conv + taps_ref[tap : tap + 1, :] * masked_ref[1 + tap : 1 + tap + count, :]
        sig = jax.nn.sigmoid(conv)
        if start < 0:
            act = act_low_ref[...]
        elif start < ROWS:
            act = act_ref[pl.ds(start, count), :]
        else:
            act = act_high_ref[...]
        grad = (act.astype(f32) * sig * (1.0 + conv * (1.0 - sig))).astype(bf16).astype(f32)
        grad_ref[pl.ds(start + 16, count), :] = grad
        if 0 <= start < ROWS:
            activated_ref[pl.ds(start, count), :] = (conv * sig).astype(bf16)
            for tap in range(K):
                product = grad * masked_ref[1 + tap : 1 + tap + count, :]
                sums_ref[tap] += jnp.sum(product.reshape(count // 8, 8, COLS), axis=0)
            sums_ref[K] += jnp.sum(grad.reshape(count // 8, 8, COLS), axis=0)
    activated_ref[ROWS:, :] = jnp.zeros((activated_ref.shape[0] - ROWS, COLS), bf16)
    small_ref[...] = jnp.sum(sums_ref[...], axis=1)

    for start, count in chunks[1:4]:
        here = grad_ref[pl.ds(start, count + 32), :]
        masked_grad_ref[...] = jnp.where(same_clip(start, count), here, 0.0)
        glu = jnp.zeros((count, COLS), f32)
        for tap in range(K):
            glu = glu + taps_ref[tap : tap + 1, :] * masked_grad_ref[31 - tap : 31 - tap + count, :]
        glu_ref[pl.ds(start, count), :] = glu

    glu = glu_ref[...]
    value_pre = pre_ref[:, 0:COLS]
    gate_pre = pre_ref[:, COLS:]
    gate_sig = jax.nn.sigmoid(gate_pre)
    value_grad = (glu * gate_sig).astype(bf16)
    gate_grad = (glu * value_pre * gate_sig * (1.0 - gate_sig)).astype(bf16)
    message_ref[0:ROWS, 0:COLS] = value_grad
    message_ref[0:ROWS, COLS:] = gate_grad
    value_wide = value_grad.astype(f32)
    gate_wide = gate_grad.astype(f32)
    first = jnp.sum(
        value_wide * unit_ref[0:1, 0:COLS] + gate_wide * unit_ref[0:1, COLS:],
        axis=1,
        keepdims=True,
    )
    second = jnp.sum(value_wide * value_pre + gate_wide * gate_pre, axis=1, keepdims=True)
    rows = columns_to_rows(first, second).astype(bf16)
    message_ref[ROWS : ROWS + 16, :] = rows[:, 0:256]
    message_ref[ROWS + 16 : ROWS + 32, 0:128] = rows[:, 256:384]
    message_ref[ROWS + 16 : ROWS + 32, 128:256] = jnp.zeros((16, 128), bf16)


def norm_kernel(grads_ref, weight_ref, out_ref):
    total = jnp.zeros((ROWS, QUARTER), f32)
    rows = jnp.zeros((16, ROWS), f32)
    for i in range(NX):
        weight = weight_ref[pl.ds(i * QUARTER, QUARTER), 0 : 2 * COLS]
        total = total + dot(grads_ref[i, 0:ROWS, :], weight, 1, 1)
        here = jnp.concatenate(
            [grads_ref[i, ROWS : ROWS + 16, :], grads_ref[i, ROWS + 16 : ROWS + 32, 0:128]], axis=1
        )
        rows = rows + here.astype(f32)
    first = rows[0:1] + rows[1:2] + rows[2:3]
    second = rows[3:4] + rows[4:5] + rows[5:6]
    sums = stacked_rows(split3(first) + split3(second)).astype(bf16)
    for i in range(NZ):
        out_ref[i, 0:ROWS, :] = total[:, i * COLS : (i + 1) * COLS].astype(bf16)
        for j in range(3):
            out_ref[i, ROWS + 16 * j : ROWS + 16 * j + 16, :] = sums[:, j * 128 : (j + 1) * 128]


def weight_kernel(
    place_ref, frames_ref, gain_ref, stat_ref, grads_ref, kept_ref, given_ref, left_ref, right_ref
):
    mean = stat_ref[:, 0:1]
    inv_std = stat_ref[:, 1:2]
    half = QUARTER // NK
    for i in range(NZ):
        scaled = (frames_ref[i].astype(f32) - mean) * inv_std * gain_ref[0:1, pl.ds(i * COLS, COLS)]
        left_ref[i * COLS // half, :, pl.ds(i * COLS % half, COLS)] = scaled.astype(bf16)
    for i in range(NX):
        right_ref[:, pl.ds(i * 2 * COLS, 2 * COLS)] = grads_ref[i, 0:ROWS, :]
    core = place_ref[1]
    for out_ref, which in ((given_ref, 1 - core), (kept_ref, core)):
        out = dot(left_ref[which], right_ref[...], 0, 0).astype(bf16)
        for i in range(NX):
            out_ref[i] = out[:, i * 2 * COLS : (i + 1) * 2 * COLS]


def out_kernel(
    place_ref, act_ref, g0_ref, g1_ref, g2_ref, g3_ref, weight_ref, enc_ref, grad_ref, left_ref
):
    for i in range(NZ):
        left_ref[:, pl.ds(i * COLS, COLS)] = act_ref[i, 0:ROWS, :]
    left = left_ref[...]
    for i in range(NX):
        weight = weight_ref[pl.ds(i * QUARTER, QUARTER), 2 * COLS : 3 * COLS]
        enc_ref[i] = dot(left, weight, 1, 0).astype(bf16)
    for j, right_ref in enumerate((g0_ref, g1_ref, g2_ref, g3_ref)):
        start = pl.multiple_of(place_ref[j] * QUARTER, QUARTER)
        grad_ref[pl.ds(start, QUARTER), :] = dot(left, right_ref[...], 0, 0).astype(bf16)


def input_kernel(parts_ref, frames_ref, grad_ref, stat_ref, gain_ref, out_ref, small_ref):
    normed_grad = jnp.zeros((ROWS, COLS), f32)
    rows = jnp.zeros((16, ROWS), f32)
    for i in range(NZ):
        normed_grad = normed_grad + parts_ref[i, 0:ROWS, :].astype(f32)
        here = [parts_ref[i, ROWS + 16 * j : ROWS + 16 * j + 16, :] for j in range(3)]
        rows = rows + jnp.concatenate(here, axis=1).astype(f32)
    first = rows[0:1] + rows[1:2] + rows[2:3]
    second = rows[3:4] + rows[4:5] + rows[5:6]
    sums = stacked_rows(split3(first) + split3(second)).astype(bf16)
    first, second = rows_to_columns(sums)
    mean = stat_ref[:, 0:1]
    inv_std = stat_ref[:, 1:2]
    centred = (frames_ref[...].astype(f32) - mean) * inv_std
    hat = normed_grad * gain_ref[0:1, :]
    out = grad_ref[...].astype(f32) + inv_std * (hat - first / WIDTH - centred * (second / WIDTH))
    out_ref[...] = out.astype(bf16)
    gain_term = jnp.sum(normed_grad * centred, axis=0, keepdims=True)
    small_ref[...] = jnp.broadcast_to(gain_term, (8, COLS))


def swap_xy(block):
    return lax.ppermute(
        block, ("x", "y"), [(a * NY + b, b * NY + a) for a in range(NX) for b in range(NY)]
    )


def neighbours(block, width):
    place = [k * NY + y for y in range(NY) for k in range(NK)]
    forward = list(zip(place[:-1], place[1:]))
    backward = [(target, source) for source, target in forward]
    low = lax.ppermute(block[-width:], ("k", "y"), forward)
    high = lax.ppermute(block[:width], ("k", "y"), backward)
    return low, high


def exchange(parts, axis):
    return lax.all_to_all(parts, axis, 0, 0, tiled=True)


def gathered(block, axis, count):
    return exchange(jnp.broadcast_to(block[None], (count,) + block.shape), axis)


def shifted(block, axis, count, shift):
    return lax.ppermute(block, axis, [(i, (i + shift) % count) for i in range(count)])


def spread(block, axis, count):
    return [block] + [shifted(block, axis, count, j) for j in range(1, count)]


def taken(parts, axis, count):
    index = lax.axis_index(axis)
    total = lax.dynamic_index_in_dim(parts, index, 0, keepdims=False).astype(f32)
    for j in range(1, count):
        part = lax.dynamic_index_in_dim(parts, (index + j) % count, 0, keepdims=False)
        total = total + shifted(part, axis, count, j).astype(f32)
    return total


def after(value, *others):
    return lax.optimization_barrier((value,) + others)[0]


def shards(frames, gain, w_value, w_gate, kernel, bias, w_out, grad_out):
    x_index = lax.axis_index("x")
    k_index = lax.axis_index("k")
    row_start = (lax.axis_index("y") * NK + k_index) * ROWS
    col_start = (x_index * NZ + lax.axis_index("z")) * COLS
    local_gain = lax.dynamic_slice_in_dim(gain, col_start, COLS, 0)[None]
    quarter_gain = lax.dynamic_slice_in_dim(gain, x_index * QUARTER, QUARTER, 0)[None]
    high = lax.reduce_precision(quarter_gain, 8, 7)
    middle = lax.reduce_precision(quarter_gain - high, 8, 7)
    low = quarter_gain - high - middle
    gain_rows = jnp.pad(jnp.concatenate([high, middle, low], axis=0), ((0, 13), (0, 0)))
    gain_rows = gain_rows.astype(bf16)
    order = (x_index + NX - jnp.arange(NX, dtype=jnp.int32)) % NX
    place = jnp.stack([LEN - row_start, k_index]).astype(jnp.int32)

    weights = lax.all_gather(
        jnp.concatenate([w_value, w_gate, w_out], axis=1), TIME, axis=0, tiled=True
    )

    frames = swap_xy(frames)
    frames_z = gathered(frames, "z", NZ)
    grad_out = swap_xy(after(grad_out, frames))
    grads = spread(grad_out, "x", NX)
    taps = swap_xy(jnp.concatenate([kernel, bias[None, :]], axis=0))

    pre_parts = call(
        project_kernel,
        shape((NX, ROWS + 48, 2 * COLS), bf16),
        (frames_z, quarter_gain, gain_rows, weights),
        scratch=[pltpu.VMEM((ROWS, QUARTER), bf16)],
    )
    pre_moved = exchange(pre_parts, "x")
    act_parts = call(
        act_kernel, shape((NZ * ROWS, COLS), bf16), (order, *grads, weights), smem=(0,)
    )
    act_grad = lax.psum_scatter(act_parts, "z", scatter_dimension=0, tiled=True)
    pre, gated, unit, stat = call(
        gate_kernel,
        [
            shape((ROWS, 2 * COLS), f32),
            shape((ROWS, COLS), bf16),
            shape((8, 2 * COLS), f32),
            shape((ROWS, 128), f32),
        ],
        (pre_moved,),
    )
    gated_low, gated_high = neighbours(gated, EDGE)
    act_low, act_high = neighbours(act_grad, 16)
    activated, message, small = call(
        conv_kernel,
        [
            shape((512, COLS), bf16),
            shape((ROWS + 32, 2 * COLS), bf16),
            shape((K + 1, COLS), f32),
        ],
        (
            place,
            gated,
            gated_low,
            gated_high,
            act_grad,
            act_low,
            act_high,
            taps,
            pre,
            unit,
        ),
        smem=(0,),
        scratch=[
            pltpu.VMEM((ROWS + 2 * EDGE, COLS), f32),
            pltpu.VMEM((ROWS + 32, COLS), f32),
            pltpu.VMEM((ROWS, COLS), f32),
            pltpu.VMEM((K + 1, 8, COLS), f32),
            pltpu.VMEM((160, COLS), f32),
            pltpu.VMEM((160, COLS), f32),
        ],
    )

    vg_grads = gathered(message, "x", NX)
    act_wide = lax.all_gather(activated, "z", axis=0, tiled=False)
    norm_parts = call(norm_kernel, shape((NZ, ROWS + 48, COLS), bf16), (vg_grads, weights))
    norm_moved = exchange(norm_parts, "z")
    kept, given = call(
        weight_kernel,
        [shape((NY, QUARTER // NK, 2 * COLS), bf16) for _ in range(2)],
        (place, frames_z, quarter_gain, stat, vg_grads),
        smem=(0,),
        scratch=[
            pltpu.VMEM((NK, ROWS, QUARTER // NK), bf16),
            pltpu.VMEM((ROWS, NX * 2 * COLS), bf16),
        ],
    )
    other = lax.ppermute(given, "k", [(0, 1), (1, 0)])
    both = (kept.astype(f32) + other.astype(f32)).astype(bf16)
    in_weight = taken(both, "y", NY)

    enc_parts, out_weight_parts = call(
        out_kernel,
        [shape((NX, ROWS, COLS), bf16), shape((NY * QUARTER, COLS), bf16)],
        (order, act_wide, *grads, weights),
        smem=(0,),
        scratch=[pltpu.VMEM((ROWS, QUARTER), bf16)],
    )
    grad_out_weight = lax.psum_scatter(
        out_weight_parts, TIME, scatter_dimension=0, tiled=True
    ).astype(f32)
    enc_sum = taken(enc_parts, "x", NX)
    encoded = swap_xy((frames.astype(f32) + enc_sum).astype(bf16))

    input_grad, gain_term = call(
        input_kernel,
        [shape((ROWS, COLS), bf16), shape((8, COLS), f32)],
        (norm_moved, frames, grad_out, stat, local_gain),
    )
    input_grad = swap_xy(input_grad)

    small = jnp.concatenate([small, gain_term], axis=0)
    small = small + lax.ppermute(small, "k", [(0, 1), (1, 0)])
    arrived = []
    for shift in range(NX):
        route = [
            (a * NY + b, ((b + shift) % NX) * NY + a) for a in range(NX) for b in range(NY)
        ]
        arrived.append(lax.ppermute(small, ("x", "y"), route))
    small = sum(arrived)
    return (
        encoded,
        input_grad,
        in_weight[:, :COLS],
        in_weight[:, COLS:],
        small[:K],
        small[K],
        grad_out_weight,
        small[K + 1],
    )


def solution(mesh):
    fine = Mesh(mesh.devices.reshape(NX, NK, NY, NZ), ("x", "k", "y", "z"))
    both = P(ROW, COL)
    return jax.shard_map(
        shards,
        mesh=fine,
        in_specs=(both, P(), both, both, P(None, COL), P(COL), both, both),
        out_specs=(both, both, both, both, P(None, COL), P(COL), both, P(COL)),
        check_vma=False,
    )
```

time: 287 us -> 220 us (0.77)
  the two profiles are of different devices: /device:TPU:24 before, /device:TPU:6 now
where the time goes in v3:
time: 220 us; the launch traced here: 219 us
  starting transfers between devices  71.7 us (33%)
  waiting for transfers between devices  63.7 us (29%)
  local copies, waits for them, and re-layouts  27.5 us (12%)
  Pallas kernels  18.3 us (8%)
  blocking collectives  15.8 us (7%)
  between operations  14.3 us (6%)
  other arithmetic  7.54 us (3%)
    ppermute x5, starting transfers between devices, swap_xy(): lax.ppermute(block, ('x', 'y'), [(a * NY + b, b * NY + a) for a in range(...  22.1 us
    unnamed x65, local copies, waits for them, and re-layouts  21.4 us
    ppermute x5, waiting for transfers between devices, swap_xy(): lax.ppermute(block, ('x', 'y'), [(a * NY + b, b * NY + a) for a in range(...  20.1 us
    pallas_call x8, Pallas kernels, call(): pl.pallas_call(body, out_shape=out_shape, in_specs=specs, out_specs=out_s...  18.3 us
    all_to_all x3, starting transfers between devices, exchange(): return lax.all_to_all(parts, axis, 0, 0, tiled=True)  18 us
    all_to_all x1, blocking collectives, exchange(): return lax.all_to_all(parts, axis, 0, 0, tiled=True)  15.8 us
    all_gather x1, waiting for transfers between devices, shards(): act_wide = lax.all_gather(activated, 'z', axis=0, tiled=False)  14.8 us
    ppermute x9, starting transfers between devices, shifted(): lax.ppermute(block, axis, [(i, (i + shift) % count) for i in range(count)])  13.9 us
  transfers between devices with their start and end apart: 31, of which 12 were waited for; matrix products, arithmetic and copies ran while one was open for 5% of the time, Pallas kernels for 7%

profile of v3, /device:TPU:6, one launch (start us, length us, event | category | flops | bytes accessed | tf_op | source)
XLA Modules:
  0.0 218.8 jit_solution(15852589813217222218)
XLA Ops:
  9.1 4.8 %collective-permute-start = (bf16[384,128]{1,0:T(8,128)(2,1)}, bf16[384,128]{1,0:T(8,128)(2,1)S(1)}, u32[]{:S(2)}, u32[]{:S(2)}) collective-permute-start(bf16[384,128]{1,0:T(8,128)(2,1)} %param.8), channel_id=1, source_target_pairs={{0,0},{8,64},{16,128},{24,192},{64,8},{72,72},{80,136},{88,200},{1... | collective-permute-start | bytes 294920 | tf_op jit(solution)/shard_map/ppermute | solution.py:313
  13.9 7.3 %collective-permute-done.frames_ref = bf16[384,128]{1,0:T(8,128)(2,1)S(1)} collective-permute-done((bf16[384,128]{1,0:T(8,128)(2,1)}, bf16[384,128]{1,0:T(8,128)(2,1)S(1)}, u32[]{:S(2)}, u32[]{:S(2)}) %collective-permute-start) | collective-permute-done | bytes 98336 | tf_op jit(solution)/shard_map/ppermute | solution.py:313
  22.2 8.5 %all-to-all-start = ((bf16[8,384,128]{2,1,0:T(8,128)(2,1)}), bf16[8,384,128]{2,1,0:T(8,128)(2,1)}, u32[]{:S(2)}, u32[]{:S(2)}) async-start(bf16[8,384,128]{2,1,0:T(8,128)(2,1)} %broadcast_in_dim.10), calls=%async_computation | async-start | bytes 1572864 | tf_op jit(solution)/shard_map/all_to_all | solution.py:328
  30.8 4.8 %collective-permute-start.3 = (bf16[384,128]{1,0:T(8,128)(2,1)S(1)}, bf16[384,128]{1,0:T(8,128)(2,1)S(1)}, u32[]{:S(2)}, u32[]{:S(2)}) collective-permute-start(bf16[384,128]{1,0:T(8,128)(2,1)S(1)} %copy-done.30), channel_id=1, source_target_pairs={{0,0},{8,64},{16,128},{24,192},{64,8},{72,72},{80,136},{88,200},{1... | collective-permute-start | bytes 294920 | tf_op jit(solution)/shard_map/ppermute | solution.py:313
  35.5 6.1 %collective-permute-done.3.g0_ref.grad_ref = bf16[384,128]{1,0:T(8,128)(2,1)S(1)} collective-permute-done((bf16[384,128]{1,0:T(8,128)(2,1)S(1)}, bf16[384,128]{1,0:T(8,128)(2,1)S(1)}, u32[]{:S(2)}, u32[]{:S(2)}) %collective-permute-start.3) | collective-permute-done | bytes 98336 | tf_op jit(solution)/shard_map/ppermute | solution.py:313
  41.7 2.5 %collective-permute-start.5 = (bf16[384,128]{1,0:T(8,128)(2,1)S(1)}, bf16[384,128]{1,0:T(8,128)(2,1)S(1)}, u32[]{:S(2)}, u32[]{:S(2)}) collective-permute-start(bf16[384,128]{1,0:T(8,128)(2,1)S(1)} %collective-permute-done.3.g0_ref.grad_ref), channel_id=1, source_target_pairs={{0,128},{64,192},{128,0},{192,64},{1,129},{65,193},{129,1},{193,65... | collective-permute-start | bytes 294920 | tf_op jit(solution)/shard_map/ppermute | solution.py:336
  44.2 2.1 collective-permute-done.4.g1_ref
  47.8 2.2 %collective-permute-done.6.g3_ref = bf16[384,128]{1,0:T(8,128)(2,1)S(1)} collective-permute-done((bf16[384,128]{1,0:T(8,128)(2,1)S(1)}, bf16[384,128]{1,0:T(8,128)(2,1)S(1)}, u32[]{:S(2)}, u32[]{:S(2)}) %collective-permute-start.6) | collective-permute-done | bytes 98336 | tf_op jit(solution)/shard_map/ppermute | solution.py:336
  50.7 1.9 copy-done
  57.2 3.3 %shard_map.143 = bf16[4,432,256]{2,1,0:T(8,128)(2,1)S(1)} custom-call(bf16[8,384,128]{2,1,0:T(8,128)(2,1)} %all-to-all-done.frames_ref, f32[1,1024]{1,0:T(1,128)S(1)} %bitcast.30, bf16[16,1024]{1,0:T(8,128)(2,1)S(1)} %fusion.10.gain_rows_ref, bf16[4096,384]{1,0:T(8,128)(2,1)S(1)} %copy-done.1), custom_call_target="tpu_custom_call" | custom-call | tf_op jit(solution)/shard_map/pallas_call | solution.py:78
  61.5 5.1 %all-to-all-start.1 = ((bf16[4,432,256]{2,1,0:T(8,128)(2,1)}), bf16[4,432,256]{2,1,0:T(8,128)(2,1)}, u32[]{:S(2)}, u32[]{:S(2)}) async-start(bf16[4,432,256]{2,1,0:T(8,128)(2,1)} %copy-done.3), calls=%async_computation.1 | async-start | bytes 1769472 | tf_op jit(solution)/shard_map/all_to_all | solution.py:328
  67.2 3.6 %collective-permute-start.9 = (f32[32,128]{1,0:T(8,128)}, f32[32,128]{1,0:T(8,128)}, u32[]{:S(2)}, u32[]{:S(2)}) collective-permute-start(f32[32,128]{1,0:T(8,128)} %pad_maximum_fusion.1), channel_id=1, source_target_pairs={{0,0},{8,64},{16,128},{24,192},{64,8},{72,72},{80,136},{88,200},{1... | collective-permute-start | bytes 49160 | tf_op jit(solution)/shard_map/ppermute | solution.py:313
  70.8 3.8 %all-to-all-done.1.parts_ref = bf16[4,432,256]{2,1,0:T(8,128)(2,1)} async-done(((bf16[4,432,256]{2,1,0:T(8,128)(2,1)}), bf16[4,432,256]{2,1,0:T(8,128)(2,1)}, u32[]{:S(2)}, u32[]{:S(2)}) %all-to-all-start.1) | async-done | bytes 884768 | tf_op jit(solution)/shard_map/all_to_all | solution.py:328
  74.6 2.3 %shard_map.144 = (f32[384,256]{1,0:T(8,128)S(1)}, bf16[384,128]{1,0:T(8,128)(2,1)S(1)}, f32[8,256]{1,0:T(8,128)S(1)}, f32[384,128]{1,0:T(8,128)S(1)}) custom-call(bf16[4,432,256]{2,1,0:T(8,128)(2,1)} %all-to-all-done.1.parts_ref), custom_call_target="tpu_custom_call" | custom-call | tf_op jit(solution)/shard_map/pallas_call | solution.py:78
  79.0 1.9 collective-permute-start.1
  82.2 12.3 %reduce-scatter.3.cloned.1.call-done.act_ref = bf16[384,128]{1,0:T(8,128)(2,1)} async-done(((bf16[3072,128]{1,0:T(8,128)(2,1)}), bf16[384,128]{1,0:T(8,128)(2,1)}) %reduce-scatter.3.cloned.1.call-update) | async-done | bytes 98320 | tf_op jit(solution)/shard_map/reduce_scatter | solution.py:391
  97.9 3.3 %collective-permute-done.8.act_high_ref = bf16[16,128]{1,0:T(8,128)(2,1)S(1)} collective-permute-done((bf16[16,128]{1,0:T(8,128)(2,1)S(1)}, bf16[16,128]{1,0:T(8,128)(2,1)S(1)}, u32[]{:S(2)}, u32[]{:S(2)}) %collective-permute-start.8) | collective-permute-done | bytes 4128 | tf_op jit(solution)/shard_map/ppermute | solution.py:323
  104.0 2.8 %shard_map.146 = (bf16[512,128]{1,0:T(8,128)(2,1)S(1)}, bf16[416,256]{1,0:T(8,128)(2,1)S(1)}, f32[32,128]{1,0:T(8,128)S(1)}) custom-call(s32[2]{0:T(128)S(1)} %pad_add_fusion.place_ref, bf16[384,128]{1,0:T(8,128)(2,1)S(1)} %copy-done.21, bf16[32,128]{1,0:T(8,128)(2,1)} %collective-permute-done.1.low_ref, bf16[32,128]{1,0:T(8,128)(2,1)} %collective-permute-done.2.high_ref, ...), custom_call_target="tpu_custom_call" | custom-call | tf_op jit(solution)/shard_map/pallas_call | solution.py:78
  109.8 15.8 %all_to_all.20.grads_ref = bf16[4,416,256]{2,1,0:T(8,128)(2,1)S(1)} all-to-all(bf16[4,416,256]{2,1,0:T(8,128)(2,1)S(1)} %broadcast_in_dim.24), channel_id=1, replica_groups=mesh['x'=4,'k'=2,'y'=4,'z'=8] {'x'}, dimensions={0} | all-to-all | bytes 1703936 | tf_op jit(solution)/shard_map/all_to_all | solution.py:328
  125.6 3.2 %shard_map.150 = (bf16[4,512,256]{2,1,0:T(8,128)(2,1)S(1)}, bf16[4,512,256]{2,1,0:T(8,128)(2,1)}) custom-call(s32[2]{0:T(128)S(1)} %pad_add_fusion.place_ref, bf16[8,384,128]{2,1,0:T(8,128)(2,1)} %all-to-all-done.frames_ref, f32[1,1024]{1,0:T(1,128)S(1)} %bitcast.31, f32[384,128]{1,0:T(8,128)S(1)} %get-tuple-element.29.stat_ref, ...), custom_call_target="tpu_custom_call" | custom-call | tf_op jit(solution)/shard_map/pallas_call | solution.py:78
  132.7 4.4 %all-to-all-start.3 = ((bf16[8,432,128]{2,1,0:T(8,128)(2,1)}), bf16[8,432,128]{2,1,0:T(8,128)(2,1)}, u32[]{:S(2)}, u32[]{:S(2)}) async-start(bf16[8,432,128]{2,1,0:T(8,128)(2,1)} %copy-done.2), calls=%async_computation.4 | async-start | bytes 1769472 | tf_op jit(solution)/shard_map/all_to_all | solution.py:328
  137.2 14.8 %all-gather.6.cloned.1.call-done = bf16[4096,128]{1,0:T(8,128)(2,1)} async-done(((bf16[512,128]{1,0:T(8,128)(2,1)}), bf16[4096,128]{1,0:T(8,128)(2,1)}) %all-gather.6.cloned.1.call-update) | async-done | bytes 1048592 | tf_op jit(solution)/shard_map/all_gather | solution.py:435
  156.5 2.4 %shard_map.147 = (bf16[4,384,128]{2,1,0:T(8,128)(2,1)S(1)}, bf16[4096,128]{1,0:T(8,128)(2,1)S(1)}) custom-call(s32[4]{0:T(128)S(1)} %copy-done.27, bf16[8,512,128]{2,1,0:T(8,128)(2,1)S(1)} %bitcast.29, bf16[384,128]{1,0:T(8,128)(2,1)S(1)} %collective-permute-done.3.g0_ref.grad_ref, bf16[384,128]{1,0:T(8,128)(2,1)S(1)} %copy-done.13, ...), custom_call_target="tpu_custom_call" | custom-call | tf_op jit(solution)/shard_map/pallas_call | solution.py:78
  165.4 2.5 %collective-permute-start.10 = (bf16[384,128]{1,0:T(8,128)(2,1)S(1)}, bf16[384,128]{1,0:T(8,128)(2,1)S(1)}, u32[]{:S(2)}, u32[]{:S(2)}) collective-permute-start(bf16[384,128]{1,0:T(8,128)(2,1)S(1)} %get-tuple-element.43), channel_id=1, source_target_pairs={{0,64},{64,128},{128,192},{192,0},{1,65},{65,129},{129,193},{193,1... | collective-permute-start | bytes 294920 | tf_op jit(solution)/shard_map/ppermute | solution.py:336
  168.0 5.8 %collective-permute-start.18 = (bf16[512,256]{1,0:T(8,128)(2,1)S(1)}, bf16[512,256]{1,0:T(8,128)(2,1)S(1)}, u32[]{:S(2)}, u32[]{:S(2)}) collective-permute-start(bf16[512,256]{1,0:T(8,128)(2,1)S(1)} %get-tuple-element.39), channel_id=1, source_target_pairs={{0,24},{8,0},{16,8},{24,16},{1,25},{9,1},{17,9},{25,17},{2,26},{10... | collective-permute-start | bytes 786440 | tf_op jit(solution)/shard_map/ppermute | solution.py:336
  175.5 7.1 %collective-permute-start.13 = (bf16[384,128]{1,0:T(8,128)(2,1)}, bf16[384,128]{1,0:T(8,128)(2,1)S(1)}, u32[]{:S(2)}, u32[]{:S(2)}) collective-permute-start(bf16[384,128]{1,0:T(8,128)(2,1)} %fusion.5), channel_id=1, source_target_pairs={{0,0},{8,64},{16,128},{24,192},{64,8},{72,72},{80,136},{88,200},{1... | collective-permute-start | bytes 294920 | tf_op jit(solution)/shard_map/ppermute | solution.py:313
  184.4 2.7 %collective-permute-done.16 = bf16[512,256]{1,0:T(8,128)(2,1)S(1)} collective-permute-done((bf16[512,256]{1,0:T(8,128)(2,1)S(1)}, bf16[512,256]{1,0:T(8,128)(2,1)S(1)}, u32[]{:S(2)}, u32[]{:S(2)}) %collective-permute-start.16) | collective-permute-done | bytes 262176 | tf_op jit(solution)/shard_map/ppermute | solution.py:336
  187.3 2.3 %collective-permute-start.22 = (f32[40,128]{1,0:T(8,128)S(1)}, f32[40,128]{1,0:T(8,128)S(1)}, u32[]{:S(2)}, u32[]{:S(2)}) collective-permute-start(f32[40,128]{1,0:T(8,128)S(1)} %add.157), channel_id=1, source_target_pairs={{0,128},{8,192},{16,0},{24,64},{64,136},{72,200},{80,8},{88,72},{1... | collective-permute-start | bytes 61448 | tf_op jit(solution)/shard_map/ppermute | solution.py:479
  189.6 4.5 %collective-permute-start.20 = (f32[40,128]{1,0:T(8,128)S(1)}, f32[40,128]{1,0:T(8,128)S(1)}, u32[]{:S(2)}, u32[]{:S(2)}) collective-permute-start(f32[40,128]{1,0:T(8,128)S(1)} %add.157), channel_id=1, source_target_pairs={{0,0},{8,64},{16,128},{24,192},{64,8},{72,72},{80,136},{88,200},{1... | collective-permute-start | bytes 61448 | tf_op jit(solution)/shard_map/ppermute | solution.py:479
  194.1 3.9 %collective-permute-start.21 = (f32[40,128]{1,0:T(8,128)S(1)}, f32[40,128]{1,0:T(8,128)S(1)}, u32[]{:S(2)}, u32[]{:S(2)}) collective-permute-start(f32[40,128]{1,0:T(8,128)S(1)} %add.157), channel_id=1, source_target_pairs={{0,64},{8,128},{16,192},{24,0},{64,72},{72,136},{80,200},{88,8},{1... | collective-permute-start | bytes 61448 | tf_op jit(solution)/shard_map/ppermute | solution.py:479
  198.8 1.9 collective-permute-start.14
  202.7 6.7 %collective-permute-done.14 = bf16[384,128]{1,0:T(8,128)(2,1)S(1)} collective-permute-done((bf16[384,128]{1,0:T(8,128)(2,1)S(1)}, bf16[384,128]{1,0:T(8,128)(2,1)S(1)}, u32[]{:S(2)}, u32[]{:S(2)}) %collective-permute-start.14) | collective-permute-done | bytes 98336 | tf_op jit(solution)/shard_map/ppermute | solution.py:313
  (135 shorter events, 47.8 us)
Async XLA Ops:
  7.2 23.6 %copy-start.30 = (bf16[384,128]{1,0:T(8,128)(2,1)S(1)}, bf16[384,128]{1,0:T(8,128)(2,1)}, u32[]{:S(2)}) copy-start(bf16[384,128]{1,0:T(8,128)(2,1)} %param.15) | copy-start | bytes 294916
  7.2 43.5 %all-gather.4.cloned.1.call-start = ((), (), s32[]{:S(2)}) async-start(), calls=%async_computation.6 | async-start | bytes 3538944 | tf_op jit(solution)/shard_map/all_gather | solution.py:371
  9.1 12.1 %collective-permute-start = (bf16[384,128]{1,0:T(8,128)(2,1)}, bf16[384,128]{1,0:T(8,128)(2,1)S(1)}, u32[]{:S(2)}, u32[]{:S(2)}) collective-permute-start(bf16[384,128]{1,0:T(8,128)(2,1)} %param.8), channel_id=1, source_target_pairs={{0,0},{8,64},{16,128},{24,192},{64,8},{72,72},{80,136},{88,200},{1... | collective-permute-start | bytes 294920 | tf_op jit(solution)/shard_map/ppermute | solution.py:313
  22.2 34.9 %all-to-all-start = ((bf16[8,384,128]{2,1,0:T(8,128)(2,1)}), bf16[8,384,128]{2,1,0:T(8,128)(2,1)}, u32[]{:S(2)}, u32[]{:S(2)}) async-start(bf16[8,384,128]{2,1,0:T(8,128)(2,1)} %broadcast_in_dim.10), calls=%async_computation | async-start | bytes 1572864 | tf_op jit(solution)/shard_map/all_to_all | solution.py:328
  30.7 63.8 %reduce-scatter.3.cloned.1.call-start = ((), (), s32[]{:S(2)}) async-start(), calls=%async_computation.7 | async-start | bytes 884736 | tf_op jit(solution)/shard_map/reduce_scatter | solution.py:391
  30.8 10.9 %collective-permute-start.3 = (bf16[384,128]{1,0:T(8,128)(2,1)S(1)}, bf16[384,128]{1,0:T(8,128)(2,1)S(1)}, u32[]{:S(2)}, u32[]{:S(2)}) collective-permute-start(bf16[384,128]{1,0:T(8,128)(2,1)S(1)} %copy-done.30), channel_id=1, source_target_pairs={{0,0},{8,64},{16,128},{24,192},{64,8},{72,72},{80,136},{88,200},{1... | collective-permute-start | bytes 294920 | tf_op jit(solution)/shard_map/ppermute | solution.py:313
  41.6 4.6 %collective-permute-start.4 = (bf16[384,128]{1,0:T(8,128)(2,1)S(1)}, bf16[384,128]{1,0:T(8,128)(2,1)S(1)}, u32[]{:S(2)}, u32[]{:S(2)}) collective-permute-start(bf16[384,128]{1,0:T(8,128)(2,1)S(1)} %collective-permute-done.3.g0_ref.grad_ref), channel_id=1, source_target_pairs={{0,64},{64,128},{128,192},{192,0},{1,65},{65,129},{129,193},{193,1... | collective-permute-start | bytes 294920 | tf_op jit(solution)/shard_map/ppermute | solution.py:336
  41.7 6.1 %collective-permute-start.5 = (bf16[384,128]{1,0:T(8,128)(2,1)S(1)}, bf16[384,128]{1,0:T(8,128)(2,1)S(1)}, u32[]{:S(2)}, u32[]{:S(2)}) collective-permute-start(bf16[384,128]{1,0:T(8,128)(2,1)S(1)} %collective-permute-done.3.g0_ref.grad_ref), channel_id=1, source_target_pairs={{0,128},{64,192},{128,0},{192,64},{1,129},{65,193},{129,1},{193,65... | collective-permute-start | bytes 294920 | tf_op jit(solution)/shard_map/ppermute | solution.py:336
  44.2 5.8 %collective-permute-start.6 = (bf16[384,128]{1,0:T(8,128)(2,1)S(1)}, bf16[384,128]{1,0:T(8,128)(2,1)S(1)}, u32[]{:S(2)}, u32[]{:S(2)}) collective-permute-start(bf16[384,128]{1,0:T(8,128)(2,1)S(1)} %collective-permute-done.3.g0_ref.grad_ref), channel_id=1, source_target_pairs={{0,192},{64,0},{128,64},{192,128},{1,193},{65,1},{129,65},{193,129... | collective-permute-start | bytes 294920 | tf_op jit(solution)/shard_map/ppermute | solution.py:336
  61.5 13.2 %all-to-all-start.1 = ((bf16[4,432,256]{2,1,0:T(8,128)(2,1)}), bf16[4,432,256]{2,1,0:T(8,128)(2,1)}, u32[]{:S(2)}, u32[]{:S(2)}) async-start(bf16[4,432,256]{2,1,0:T(8,128)(2,1)} %copy-done.3), calls=%async_computation.1 | async-start | bytes 1769472 | tf_op jit(solution)/shard_map/all_to_all | solution.py:328
  66.6 85.3 %all-gather.6.cloned.1.call-start = ((), (), s32[]{:S(2)}) async-start(), calls=%async_computation.9 | async-start | bytes 1179648 | tf_op jit(solution)/shard_map/all_gather | solution.py:435
  67.2 30.6 %collective-permute-start.9 = (f32[32,128]{1,0:T(8,128)}, f32[32,128]{1,0:T(8,128)}, u32[]{:S(2)}, u32[]{:S(2)}) collective-permute-start(f32[32,128]{1,0:T(8,128)} %pad_maximum_fusion.1), channel_id=1, source_target_pairs={{0,0},{8,64},{16,128},{24,192},{64,8},{72,72},{80,136},{88,200},{1... | collective-permute-start | bytes 49160 | tf_op jit(solution)/shard_map/ppermute | solution.py:313
  79.0 18.8 %collective-permute-start.1 = (bf16[32,128]{1,0:T(8,128)(2,1)}, bf16[32,128]{1,0:T(8,128)(2,1)}, u32[]{:S(2)}, u32[]{:S(2)}) collective-permute-start(bf16[32,128]{1,0:T(8,128)(2,1)} %get-tuple-element.49), channel_id=1, source_target_pairs={{0,32},{32,8},{8,40},{40,16},{16,48},{48,24},{24,56},{1,33},{33,9}... | collective-permute-start | bytes 24584 | tf_op jit(solution)/shard_map/ppermute | solution.py:322
  80.9 17.0 %collective-permute-start.2 = (bf16[32,128]{1,0:T(8,128)(2,1)}, bf16[32,128]{1,0:T(8,128)(2,1)}, u32[]{:S(2)}, u32[]{:S(2)}) collective-permute-start(bf16[32,128]{1,0:T(8,128)(2,1)} %get-tuple-element.48), channel_id=1, source_target_pairs={{32,0},{8,32},{40,8},{16,40},{48,16},{24,48},{56,24},{33,1},{9,33}... | collective-permute-start | bytes 24584 | tf_op jit(solution)/shard_map/ppermute | solution.py:323
  95.2 2.7 %collective-permute-start.7 = (bf16[16,128]{1,0:T(8,128)(2,1)S(1)}, bf16[16,128]{1,0:T(8,128)(2,1)S(1)}, u32[]{:S(2)}, u32[]{:S(2)}) collective-permute-start(bf16[16,128]{1,0:T(8,128)(2,1)S(1)} %get-tuple-element.47), channel_id=1, source_target_pairs={{0,32},{32,8},{8,40},{40,16},{16,48},{48,24},{24,56},{1,33},{33,9}... | collective-permute-start | bytes 12296 | tf_op jit(solution)/shard_map/ppermute | solution.py:322
  96.5 4.7 %collective-permute-start.8 = (bf16[16,128]{1,0:T(8,128)(2,1)S(1)}, bf16[16,128]{1,0:T(8,128)(2,1)S(1)}, u32[]{:S(2)}, u32[]{:S(2)}) collective-permute-start(bf16[16,128]{1,0:T(8,128)(2,1)S(1)} %get-tuple-element.46), channel_id=1, source_target_pairs={{32,0},{8,32},{40,8},{16,40},{48,16},{24,48},{56,24},{33,1},{9,33}... | collective-permute-start | bytes 12296 | tf_op jit(solution)/shard_map/ppermute | solution.py:323
  129.8 31.7 %collective-permute-start.15 = (bf16[4,512,256]{2,1,0:T(8,128)(2,1)}, bf16[4,512,256]{2,1,0:T(8,128)(2,1)}, u32[]{:S(2)}, u32[]{:S(2)}) collective-permute-start(bf16[4,512,256]{2,1,0:T(8,128)(2,1)} %get-tuple-element.32), channel_id=1, source_target_pairs={{0,32},{32,0},{1,33},{33,1},{2,34},{34,2},{3,35},{35,3},{4,36},{36... | collective-permute-start | bytes 3145736 | tf_op jit(solution)/shard_map/ppermute | solution.py:448
  132.7 49.9 %all-to-all-start.3 = ((bf16[8,432,128]{2,1,0:T(8,128)(2,1)}), bf16[8,432,128]{2,1,0:T(8,128)(2,1)}, u32[]{:S(2)}, u32[]{:S(2)}) async-start(bf16[8,432,128]{2,1,0:T(8,128)(2,1)} %copy-done.2), calls=%async_computation.4 | async-start | bytes 1769472 | tf_op jit(solution)/shard_map/all_to_all | solution.py:328
  137.1 72.2 %reduce-scatter.5.cloned.1.call-start = ((), (), s32[]{:S(2)}) async-start(), calls=%async_computation.8 | async-start | bytes 1179648 | tf_op jit(solution)/shard_map/reduce_scatter | solution.py:459
  163.4 10.5 %collective-permute-start.12 = (bf16[384,128]{1,0:T(8,128)(2,1)S(1)}, bf16[384,128]{1,0:T(8,128)(2,1)S(1)}, u32[]{:S(2)}, u32[]{:S(2)}) collective-permute-start(bf16[384,128]{1,0:T(8,128)(2,1)S(1)} %get-tuple-element.44), channel_id=1, source_target_pairs={{0,192},{64,0},{128,64},{192,128},{1,193},{65,1},{129,65},{193,129... | collective-permute-start | bytes 294920 | tf_op jit(solution)/shard_map/ppermute | solution.py:336
  164.3 10.5 %collective-permute-start.11 = (bf16[384,128]{1,0:T(8,128)(2,1)S(1)}, bf16[384,128]{1,0:T(8,128)(2,1)S(1)}, u32[]{:S(2)}, u32[]{:S(2)}) collective-permute-start(bf16[384,128]{1,0:T(8,128)(2,1)S(1)} %get-tuple-element.45), channel_id=1, source_target_pairs={{0,128},{64,192},{128,0},{192,64},{1,129},{65,193},{129,1},{193,65... | collective-permute-start | bytes 294920 | tf_op jit(solution)/shard_map/ppermute | solution.py:336
  165.4 9.4 %collective-permute-start.10 = (bf16[384,128]{1,0:T(8,128)(2,1)S(1)}, bf16[384,128]{1,0:T(8,128)(2,1)S(1)}, u32[]{:S(2)}, u32[]{:S(2)}) collective-permute-start(bf16[384,128]{1,0:T(8,128)(2,1)S(1)} %get-tuple-element.43), channel_id=1, source_target_pairs={{0,64},{64,128},{128,192},{192,0},{1,65},{65,129},{129,193},{193,1... | collective-permute-start | bytes 294920 | tf_op jit(solution)/shard_map/ppermute | solution.py:336
  168.0 16.4 %collective-permute-start.18 = (bf16[512,256]{1,0:T(8,128)(2,1)S(1)}, bf16[512,256]{1,0:T(8,128)(2,1)S(1)}, u32[]{:S(2)}, u32[]{:S(2)}) collective-permute-start(bf16[512,256]{1,0:T(8,128)(2,1)S(1)} %get-tuple-element.39), channel_id=1, source_target_pairs={{0,24},{8,0},{16,8},{24,16},{1,25},{9,1},{17,9},{25,17},{2,26},{10... | collective-permute-start | bytes 786440 | tf_op jit(solution)/shard_map/ppermute | solution.py:336
  173.8 10.6 %collective-permute-start.17 = (bf16[512,256]{1,0:T(8,128)(2,1)S(1)}, bf16[512,256]{1,0:T(8,128)(2,1)S(1)}, u32[]{:S(2)}, u32[]{:S(2)}) collective-permute-start(bf16[512,256]{1,0:T(8,128)(2,1)S(1)} %get-tuple-element.40), channel_id=1, source_target_pairs={{0,16},{8,24},{16,0},{24,8},{1,17},{9,25},{17,1},{25,9},{2,18},{10... | collective-permute-start | bytes 786440 | tf_op jit(solution)/shard_map/ppermute | solution.py:336
  173.8 13.3 %collective-permute-start.16 = (bf16[512,256]{1,0:T(8,128)(2,1)S(1)}, bf16[512,256]{1,0:T(8,128)(2,1)S(1)}, u32[]{:S(2)}, u32[]{:S(2)}) collective-permute-start(bf16[512,256]{1,0:T(8,128)(2,1)S(1)} %get-tuple-element.38), channel_id=1, source_target_pairs={{0,8},{8,16},{16,24},{24,0},{1,9},{9,17},{17,25},{25,1},{2,10},{10... | collective-permute-start | bytes 786440 | tf_op jit(solution)/shard_map/ppermute | solution.py:336
  175.5 23.3 %collective-permute-start.13 = (bf16[384,128]{1,0:T(8,128)(2,1)}, bf16[384,128]{1,0:T(8,128)(2,1)S(1)}, u32[]{:S(2)}, u32[]{:S(2)}) collective-permute-start(bf16[384,128]{1,0:T(8,128)(2,1)} %fusion.5), channel_id=1, source_target_pairs={{0,0},{8,64},{16,128},{24,192},{64,8},{72,72},{80,136},{88,200},{1... | collective-permute-start | bytes 294920 | tf_op jit(solution)/shard_map/ppermute | solution.py:313
  184.3 2.9 %collective-permute-start.19 = (f32[40,128]{1,0:T(8,128)S(1)}, f32[40,128]{1,0:T(8,128)S(1)}, u32[]{:S(2)}, u32[]{:S(2)}) collective-permute-start(f32[40,128]{1,0:T(8,128)S(1)} %constant_dynamic-update-slice_fusion), channel_id=1, source_target_pairs={{0,32},{32,0},{1,33},{33,1},{2,34},{34,2},{3,35},{35,3},{4,36},{36... | collective-permute-start | bytes 61448 | tf_op jit(solution)/shard_map/ppermute | solution.py:473
  187.2 13.5 %collective-permute-start.23 = (f32[40,128]{1,0:T(8,128)S(1)}, f32[40,128]{1,0:T(8,128)S(1)}, u32[]{:S(2)}, u32[]{:S(2)}) collective-permute-start(f32[40,128]{1,0:T(8,128)S(1)} %add.157), channel_id=1, source_target_pairs={{0,192},{8,0},{16,64},{24,128},{64,200},{72,8},{80,72},{88,136},{1... | collective-permute-start | bytes 61448 | tf_op jit(solution)/shard_map/ppermute | solution.py:479
  187.3 13.4 %collective-permute-start.22 = (f32[40,128]{1,0:T(8,128)S(1)}, f32[40,128]{1,0:T(8,128)S(1)}, u32[]{:S(2)}, u32[]{:S(2)}) collective-permute-start(f32[40,128]{1,0:T(8,128)S(1)} %add.157), channel_id=1, source_target_pairs={{0,128},{8,192},{16,0},{24,64},{64,136},{72,200},{80,8},{88,72},{1... | collective-permute-start | bytes 61448 | tf_op jit(solution)/shard_map/ppermute | solution.py:479
  189.6 11.2 %collective-permute-start.20 = (f32[40,128]{1,0:T(8,128)S(1)}, f32[40,128]{1,0:T(8,128)S(1)}, u32[]{:S(2)}, u32[]{:S(2)}) collective-permute-start(f32[40,128]{1,0:T(8,128)S(1)} %add.157), channel_id=1, source_target_pairs={{0,0},{8,64},{16,128},{24,192},{64,8},{72,72},{80,136},{88,200},{1... | collective-permute-start | bytes 61448 | tf_op jit(solution)/shard_map/ppermute | solution.py:479
  194.1 7.5 %collective-permute-start.21 = (f32[40,128]{1,0:T(8,128)S(1)}, f32[40,128]{1,0:T(8,128)S(1)}, u32[]{:S(2)}, u32[]{:S(2)}) collective-permute-start(f32[40,128]{1,0:T(8,128)S(1)} %add.157), channel_id=1, source_target_pairs={{0,64},{8,128},{16,192},{24,0},{64,72},{72,136},{80,200},{88,8},{1... | collective-permute-start | bytes 61448 | tf_op jit(solution)/shard_map/ppermute | solution.py:479
  198.8 10.5 %collective-permute-start.14 = (bf16[384,128]{1,0:T(8,128)(2,1)S(1)}, bf16[384,128]{1,0:T(8,128)(2,1)S(1)}, u32[]{:S(2)}, u32[]{:S(2)}) collective-permute-start(bf16[384,128]{1,0:T(8,128)(2,1)S(1)} %get-tuple-element.30), channel_id=1, source_target_pairs={{0,0},{8,64},{16,128},{24,192},{64,8},{72,72},{80,136},{88,200},{1... | collective-permute-start | bytes 294920 | tf_op jit(solution)/shard_map/ppermute | solution.py:313
  (30 other events, 66.3 us)
Sparse Core Ops, SparseCore 0:
  9.8 35.3 all-gather.3
  56.5 37.9 reduce-scatter.2
  108.9 43.0 all-gather.5
  160.8 39.0 reduce-scatter.4

commit v4 on v3

--- a/solution.py
+++ b/solution.py
@@ -68,18 +68,13 @@
 
 def call(body, out_shape, args, smem=(), scratch=()):
     specs = [
-        pl.BlockSpec(memory_space=pltpu.SMEM if i in smem else pltpu.VMEM)
+        pl.BlockSpec(memory_space=pltpu.SMEM) if i in smem else pl.BlockSpec()
         for i in range(len(args))
     ]
-    many = isinstance(out_shape, (list, tuple))
-    out_specs = [pl.BlockSpec(memory_space=pltpu.VMEM) for _ in out_shape] if many else (
-        pl.BlockSpec(memory_space=pltpu.VMEM)
-    )
     return pl.pallas_call(
         body,
         out_shape=out_shape,
         in_specs=specs,
-        out_specs=out_specs,
         scratch_shapes=list(scratch),
         compiler_params=pltpu.CompilerParams(vmem_limit_bytes=48 * 1024 * 1024),
     )(*args)
@@ -89,7 +84,8 @@
     return jax.ShapeDtypeStruct(dims, kind)
 
 
-def project_kernel(frames_ref, gain_ref, gain_rows_ref, weight_ref, out_ref, left_ref):
+def project_kernel(place_ref, frames_ref, gain_ref, gain_rows_ref, weight_ref, *refs):
+    left_ref = refs[NX]
     total = jnp.zeros((ROWS, 1), f32)
     square = jnp.zeros((ROWS, 1), f32)
     for i in range(NZ):
@@ -102,33 +98,34 @@
         scaled = (frames_ref[i].astype(f32) - mean) * gain_ref[0:1, cut]
         left_ref[:, cut] = scaled.astype(bf16)
     sums = columns_to_rows(total, square).astype(bf16)
-    for i in range(NX):
-        weight = weight_ref[pl.ds(i * QUARTER, QUARTER), 0 : 2 * COLS]
-        out_ref[i, 0:ROWS, :] = dot(left_ref[...], weight, 1, 0).astype(bf16)
+    for j, out_ref in enumerate(refs[:NX]):
+        start = pl.multiple_of(place_ref[4 + j] * QUARTER, QUARTER)
+        weight = weight_ref[pl.ds(start, QUARTER), 0 : 2 * COLS]
+        out_ref[0:ROWS, :] = dot(left_ref[...], weight, 1, 0).astype(bf16)
         unit = jnp.sum(dot(gain_rows_ref[...], weight, 1, 0), axis=0, keepdims=True)
-        out_ref[i, ROWS : ROWS + 16, :] = stacked_rows(split3(unit)).astype(bf16)
-        out_ref[i, ROWS + 16 : ROWS + 32, :] = sums[:, 0:256]
-        out_ref[i, ROWS + 32 : ROWS + 48, 0:128] = sums[:, 256:384]
-        out_ref[i, ROWS + 32 : ROWS + 48, 128:256] = jnp.zeros((16, 128), bf16)
-
-
-def gate_kernel(parts_ref, pre_ref, gated_ref, unit_ref, stat_ref):
+        out_ref[ROWS : ROWS + 16, :] = stacked_rows(split3(unit)).astype(bf16)
+        out_ref[ROWS + 16 : ROWS + 32, :] = sums[:, 0:256]
+        out_ref[ROWS + 32 : ROWS + 48, 0:128] = sums[:, 256:384]
+        out_ref[ROWS + 32 : ROWS + 48, 128:256] = jnp.zeros((16, 128), bf16)
+
+
+def gate_kernel(p0_ref, p1_ref, p2_ref, p3_ref, pre_ref, gated_ref, unit_ref, stat_ref):
+    parts = (p0_ref, p1_ref, p2_ref, p3_ref)
     totals, squares, units = [], [], []
-    for i in range(NX):
+    for part_ref in parts:
         rows = jnp.concatenate(
-            [parts_ref[i, ROWS + 16 : ROWS + 32, :], parts_ref[i, ROWS + 32 : ROWS + 48, 0:128]],
-            axis=1,
+            [part_ref[ROWS + 16 : ROWS + 32, :], part_ref[ROWS + 32 : ROWS + 48, 0:128]], axis=1
         )
         first, second = rows_to_columns(rows)
         totals.append(first)
         squares.append(second)
-        pieces = parts_ref[i, ROWS : ROWS + 16, :].astype(f32)
+        pieces = part_ref[ROWS : ROWS + 16, :].astype(f32)
         units.append(jnp.sum(pieces, axis=0, keepdims=True))
     mean = sum(totals) / WIDTH
     inv_std = lax.rsqrt(sum(squares) / WIDTH - mean * mean + epsilon)
     pre = jnp.zeros((ROWS, 2 * COLS), f32)
-    for i in range(NX):
-        pre = pre + parts_ref[i, 0:ROWS, :].astype(f32)
+    for i, part_ref in enumerate(parts):
+        pre = pre + part_ref[0:ROWS, :].astype(f32)
         pre = pre + (totals[i] / QUARTER - mean) * units[i]
     pre = pre * inv_std
     pre_ref[...] = pre
@@ -145,10 +142,59 @@
         weight = weight_ref[pl.ds(start, QUARTER), 2 * COLS : 3 * COLS]
         total = total + dot(grad_ref[...], weight, 1, 1)
     for i in range(NZ):
-        out_ref[pl.ds(i * ROWS, ROWS), :] = total[:, i * COLS : (i + 1) * COLS].astype(bf16)
-
-
-def conv_kernel(
+        out_ref[i] = total[:, i * COLS : (i + 1) * COLS].astype(bf16)
+
+
+def sum_kernel(parts_ref, out_ref):
+    total = jnp.zeros((ROWS, COLS), f32)
+    for i in range(NZ):
+        total = total + parts_ref[i].astype(f32)
+    out_ref[...] = total.astype(bf16)
+
+
+CHUNKS = [(-16, 16), (0, 128), (128, 128), (256, 128), (ROWS, 16)]
+
+
+def same_clip(border, start, count):
+    row = lax.broadcasted_iota(jnp.int32, (count + 32, COLS), 0) + (start - 16)
+    inside = (row < border).astype(jnp.int32)
+    own = jnp.where(start < border, 1, 0)
+    return inside == own
+
+
+def fill_wide(wide_ref, gated_ref, low_ref, high_ref):
+    wide_ref[0:EDGE, :] = low_ref[...].astype(f32)
+    wide_ref[EDGE : EDGE + ROWS, :] = gated_ref[...].astype(f32)
+    wide_ref[EDGE + ROWS :, :] = high_ref[...].astype(f32)
+
+
+def forward_kernel(
+    place_ref,
+    gated_ref,
+    low_ref,
+    high_ref,
+    taps_ref,
+    activated_ref,
+    slope_ref,
+    wide_ref,
+    masked_ref,
+):
+    border = place_ref[0]
+    fill_wide(wide_ref, gated_ref, low_ref, high_ref)
+    bias = taps_ref[K : K + 1, :]
+    for start, count in CHUNKS:
+        here = wide_ref[pl.ds(start - 16 + EDGE, count + 32), :]
+        masked_ref[0 : count + 32, :] = jnp.where(same_clip(border, start, count), here, 0.0)
+        conv = jnp.broadcast_to(bias, (count, COLS))
+        for tap in range(K):
+            conv = conv + taps_ref[tap : tap + 1, :] * masked_ref[1 + tap : 1 + tap + count, :]
+        sig = jax.nn.sigmoid(conv)
+        slope_ref[pl.ds(start + 16, count), :] = sig * (1.0 + conv * (1.0 - sig))
+        if 0 <= start < ROWS:
+            activated_ref[pl.ds(start, count), :] = (conv * sig).astype(bf16)
+
+
+def backward_kernel(
     place_ref,
     gated_ref,
     low_ref,
@@ -156,10 +202,10 @@
     act_ref,
     act_low_ref,
     act_high_ref,
+    slope_ref,
     taps_ref,
     pre_ref,
     unit_ref,
-    activated_ref,
     message_ref,
     small_ref,
     wide_ref,
@@ -170,46 +216,30 @@
     masked_grad_ref,
 ):
     border = place_ref[0]
-    wide_ref[0:EDGE, :] = low_ref[...].astype(f32)
-    wide_ref[EDGE : EDGE + ROWS, :] = gated_ref[...].astype(f32)
-    wide_ref[EDGE + ROWS :, :] = high_ref[...].astype(f32)
+    fill_wide(wide_ref, gated_ref, low_ref, high_ref)
     sums_ref[...] = jnp.zeros((K + 1, 8, COLS), f32)
-    bias = taps_ref[K : K + 1, :]
-    chunks = [(-16, 16), (0, 128), (128, 128), (256, 128), (ROWS, 16)]
-
-    def same_clip(start, count):
-        row = lax.broadcasted_iota(jnp.int32, (count + 32, COLS), 0) + (start - 16)
-        inside = (row < border).astype(jnp.int32)
-        own = jnp.where(start < border, 1, 0)
-        return inside == own
-
-    for start, count in chunks:
-        here = wide_ref[pl.ds(start - 16 + EDGE, count + 32), :]
-        masked_ref[0 : count + 32, :] = jnp.where(same_clip(start, count), here, 0.0)
-        conv = jnp.broadcast_to(bias, (count, COLS))
-        for tap in range(K):
-            conv = conv + taps_ref[tap : tap + 1, :] * masked_ref[1 + tap : 1 + tap + count, :]
-        sig = jax.nn.sigmoid(conv)
+    for start, count in CHUNKS:
         if start < 0:
             act = act_low_ref[...]
         elif start < ROWS:
             act = act_ref[pl.ds(start, count), :]
         else:
             act = act_high_ref[...]
-        grad = (act.astype(f32) * sig * (1.0 + conv * (1.0 - sig))).astype(bf16).astype(f32)
+        grad = act.astype(f32) * slope_ref[pl.ds(start + 16, count), :]
+        grad = grad.astype(bf16).astype(f32)
         grad_ref[pl.ds(start + 16, count), :] = grad
         if 0 <= start < ROWS:
-            activated_ref[pl.ds(start, count), :] = (conv * sig).astype(bf16)
+            here = wide_ref[pl.ds(start - 16 + EDGE, count + 32), :]
+            masked_ref[...] = jnp.where(same_clip(border, start, count), here, 0.0)
             for tap in range(K):
                 product = grad * masked_ref[1 + tap : 1 + tap + count, :]
                 sums_ref[tap] += jnp.sum(product.reshape(count // 8, 8, COLS), axis=0)
             sums_ref[K] += jnp.sum(grad.reshape(count // 8, 8, COLS), axis=0)
-    activated_ref[ROWS:, :] = jnp.zeros((activated_ref.shape[0] - ROWS, COLS), bf16)
     small_ref[...] = jnp.sum(sums_ref[...], axis=1)
 
-    for start, count in chunks[1:4]:
+    for start, count in CHUNKS[1:4]:
         here = grad_ref[pl.ds(start, count + 32), :]
-        masked_grad_ref[...] = jnp.where(same_clip(start, count), here, 0.0)
+        masked_grad_ref[...] = jnp.where(same_clip(border, start, count), here, 0.0)
         glu = jnp.zeros((count, COLS), f32)
         for tap in range(K):
             glu = glu + taps_ref[tap : tap + 1, :] * masked_grad_ref[31 - tap : 31 - tap + count, :]
@@ -237,14 +267,15 @@
     message_ref[ROWS + 16 : ROWS + 32, 128:256] = jnp.zeros((16, 128), bf16)
 
 
-def norm_kernel(grads_ref, weight_ref, out_ref):
+def norm_kernel(place_ref, g0_ref, g1_ref, g2_ref, g3_ref, weight_ref, out_ref):
     total = jnp.zeros((ROWS, QUARTER), f32)
     rows = jnp.zeros((16, ROWS), f32)
-    for i in range(NX):
-        weight = weight_ref[pl.ds(i * QUARTER, QUARTER), 0 : 2 * COLS]
-        total = total + dot(grads_ref[i, 0:ROWS, :], weight, 1, 1)
+    for j, grad_ref in enumerate((g0_ref, g1_ref, g2_ref, g3_ref)):
+        start = pl.multiple_of(place_ref[j] * QUARTER, QUARTER)
+        weight = weight_ref[pl.ds(start, QUARTER), 0 : 2 * COLS]
+        total = total + dot(grad_ref[0:ROWS, :], weight, 1, 1)
         here = jnp.concatenate(
-            [grads_ref[i, ROWS : ROWS + 16, :], grads_ref[i, ROWS + 16 : ROWS + 32, 0:128]], axis=1
+            [grad_ref[ROWS : ROWS + 16, :], grad_ref[ROWS + 16 : ROWS + 32, 0:128]], axis=1
         )
         rows = rows + here.astype(f32)
     first = rows[0:1] + rows[1:2] + rows[2:3]
@@ -257,35 +288,55 @@
 
 
 def weight_kernel(
-    place_ref, frames_ref, gain_ref, stat_ref, grads_ref, kept_ref, given_ref, left_ref, right_ref
+    place_ref,
+    frames_ref,
+    gain_ref,
+    stat_ref,
+    g0_ref,
+    g1_ref,
+    g2_ref,
+    g3_ref,
+    out_ref,
+    left_ref,
 ):
     mean = stat_ref[:, 0:1]
     inv_std = stat_ref[:, 1:2]
+    for i in range(NZ):
+        cut = pl.ds(i * COLS, COLS)
+        scaled = (frames_ref[i].astype(f32) - mean) * inv_std * gain_ref[0:1, cut]
+        left_ref[:, cut] = scaled.astype(bf16)
+    for j, grad_ref in enumerate((g0_ref, g1_ref, g2_ref, g3_ref)):
+        start = pl.multiple_of(place_ref[j] * QUARTER, QUARTER)
+        out = dot(left_ref[...], grad_ref[0:ROWS, :], 0, 0)
+        out_ref[pl.ds(start, QUARTER), :] = out.astype(bf16)
+
+
+def out_kernel(place_ref, act_ref, g0_ref, g1_ref, g2_ref, g3_ref, weight_ref, *refs):
+    enc_refs = refs[:NX]
+    kept_ref, given_ref, left_ref, grad_ref = refs[NX:]
     half = QUARTER // NK
     for i in range(NZ):
-        scaled = (frames_ref[i].astype(f32) - mean) * inv_std * gain_ref[0:1, pl.ds(i * COLS, COLS)]
-        left_ref[i * COLS // half, :, pl.ds(i * COLS % half, COLS)] = scaled.astype(bf16)
-    for i in range(NX):
-        right_ref[:, pl.ds(i * 2 * COLS, 2 * COLS)] = grads_ref[i, 0:ROWS, :]
-    core = place_ref[1]
+        left_ref[i * COLS // half, :, pl.ds(i * COLS % half, COLS)] = act_ref[i, 0:ROWS, :]
+    for j, enc_ref in enumerate(enc_refs):
+        total = jnp.zeros((ROWS, COLS), f32)
+        for h in range(NK):
+            start = pl.multiple_of(place_ref[4 + j] * QUARTER + h * half, half)
+            weight = weight_ref[pl.ds(start, half), 2 * COLS : 3 * COLS]
+            total = total + dot(left_ref[h], weight, 1, 0)
+        enc_ref[...] = total.astype(bf16)
+    for i in range(NY):
+        source = place_ref[10 + i]
+        for j, right_ref in enumerate((g0_ref, g1_ref, g2_ref, g3_ref)):
+
+            @pl.when(source == j)
+            def _(right_ref=right_ref, i=i):
+                grad_ref[:, i * COLS : (i + 1) * COLS] = right_ref[...]
+
+    core = place_ref[9]
     for out_ref, which in ((given_ref, 1 - core), (kept_ref, core)):
-        out = dot(left_ref[which], right_ref[...], 0, 0).astype(bf16)
-        for i in range(NX):
-            out_ref[i] = out[:, i * 2 * COLS : (i + 1) * 2 * COLS]
-
-
-def out_kernel(
-    place_ref, act_ref, g0_ref, g1_ref, g2_ref, g3_ref, weight_ref, enc_ref, grad_ref, left_ref
-):
-    for i in range(NZ):
-        left_ref[:, pl.ds(i * COLS, COLS)] = act_ref[i, 0:ROWS, :]
-    left = left_ref[...]
-    for i in range(NX):
-        weight = weight_ref[pl.ds(i * QUARTER, QUARTER), 2 * COLS : 3 * COLS]
-        enc_ref[i] = dot(left, weight, 1, 0).astype(bf16)
-    for j, right_ref in enumerate((g0_ref, g1_ref, g2_ref, g3_ref)):
-        start = pl.multiple_of(place_ref[j] * QUARTER, QUARTER)
-        grad_ref[pl.ds(start, QUARTER), :] = dot(left, right_ref[...], 0, 0).astype(bf16)
+        out = dot(left_ref[which], grad_ref[...], 0, 0).astype(bf16)
+        for i in range(NY):
+            out_ref[i] = out[:, i * COLS : (i + 1) * COLS]
 
 
 def input_kernel(parts_ref, frames_ref, grad_ref, stat_ref, gain_ref, out_ref, small_ref):
@@ -340,15 +391,6 @@
     return [block] + [shifted(block, axis, count, j) for j in range(1, count)]
 
 
-def taken(parts, axis, count):
-    index = lax.axis_index(axis)
-    total = lax.dynamic_index_in_dim(parts, index, 0, keepdims=False).astype(f32)
-    for j in range(1, count):
-        part = lax.dynamic_index_in_dim(parts, (index + j) % count, 0, keepdims=False)
-        total = total + shifted(part, axis, count, j).astype(f32)
-    return total
-
-
 def after(value, *others):
     return lax.optimization_barrier((value,) + others)[0]
 
@@ -365,8 +407,14 @@
     low = quarter_gain - high - middle
     gain_rows = jnp.pad(jnp.concatenate([high, middle, low], axis=0), ((0, 13), (0, 0)))
     gain_rows = gain_rows.astype(bf16)
-    order = (x_index + NX - jnp.arange(NX, dtype=jnp.int32)) % NX
-    place = jnp.stack([LEN - row_start, k_index]).astype(jnp.int32)
+    y_index = lax.axis_index("y")
+    steps = jnp.arange(NX, dtype=jnp.int32)
+    below = (x_index + NX - steps) % NX
+    above = (x_index + steps) % NX
+    distance = (x_index + 2 * NX - (y_index + steps) % NY) % NX
+    edges = jnp.stack([LEN - row_start, k_index]).astype(jnp.int32)
+    place = jnp.concatenate([below, above, edges, distance]).astype(jnp.int32)
+    border = place[8:9]
 
     weights = lax.all_gather(
         jnp.concatenate([w_value, w_gate, w_out], axis=1), TIME, axis=0, tiled=True
@@ -376,19 +424,21 @@
     frames_z = gathered(frames, "z", NZ)
     grad_out = swap_xy(after(grad_out, frames))
     grads = spread(grad_out, "x", NX)
-    taps = swap_xy(jnp.concatenate([kernel, bias[None, :]], axis=0))
+    taps = swap_xy(after(jnp.concatenate([kernel, bias[None, :]], axis=0), grads[1]))
 
     pre_parts = call(
         project_kernel,
-        shape((NX, ROWS + 48, 2 * COLS), bf16),
-        (frames_z, quarter_gain, gain_rows, weights),
+        [shape((ROWS + 48, 2 * COLS), bf16) for _ in range(NX)],
+        (place, frames_z, quarter_gain, gain_rows, weights),
+        smem=(0,),
         scratch=[pltpu.VMEM((ROWS, QUARTER), bf16)],
     )
-    pre_moved = exchange(pre_parts, "x")
+    pre_moved = [pre_parts[0]] + [shifted(pre_parts[j], "x", NX, j) for j in range(1, NX)]
+    held = lax.optimization_barrier((grads, pre_parts[0]))[0]
     act_parts = call(
-        act_kernel, shape((NZ * ROWS, COLS), bf16), (order, *grads, weights), smem=(0,)
-    )
-    act_grad = lax.psum_scatter(act_parts, "z", scatter_dimension=0, tiled=True)
+        act_kernel, shape((NZ, ROWS, COLS), bf16), (place, *held, weights), smem=(0,)
+    )
+    act_grad = call(sum_kernel, shape((ROWS, COLS), bf16), (exchange(act_parts, "z"),))
     pre, gated, unit, stat = call(
         gate_kernel,
         [
@@ -397,25 +447,33 @@
             shape((8, 2 * COLS), f32),
             shape((ROWS, 128), f32),
         ],
-        (pre_moved,),
+        tuple(pre_moved),
     )
     gated_low, gated_high = neighbours(gated, EDGE)
     act_low, act_high = neighbours(act_grad, 16)
-    activated, message, small = call(
-        conv_kernel,
-        [
-            shape((512, COLS), bf16),
-            shape((ROWS + 32, 2 * COLS), bf16),
-            shape((K + 1, COLS), f32),
+    activated, slope = call(
+        forward_kernel,
+        [shape((ROWS, COLS), bf16), shape((ROWS + 32, COLS), f32)],
+        (border, gated, gated_low, gated_high, taps),
+        smem=(0,),
+        scratch=[
+            pltpu.VMEM((ROWS + 2 * EDGE, COLS), f32),
+            pltpu.VMEM((160, COLS), f32),
         ],
+    )
+    act_z = gathered(activated, "z", NZ)
+    message, small = call(
+        backward_kernel,
+        [shape((ROWS + 32, 2 * COLS), bf16), shape((K + 1, COLS), f32)],
         (
-            place,
+            border,
             gated,
             gated_low,
             gated_high,
             act_grad,
             act_low,
             act_high,
+            slope,
             taps,
             pre,
             unit,
@@ -431,35 +489,46 @@
         ],
     )
 
-    vg_grads = gathered(message, "x", NX)
-    act_wide = lax.all_gather(activated, "z", axis=0, tiled=False)
-    norm_parts = call(norm_kernel, shape((NZ, ROWS + 48, COLS), bf16), (vg_grads, weights))
+    vg_grads = spread(message, "x", NX)
+    norm_parts = call(
+        norm_kernel,
+        shape((NZ, ROWS + 48, COLS), bf16),
+        (place, *vg_grads, weights),
+        smem=(0,),
+    )
     norm_moved = exchange(norm_parts, "z")
-    kept, given = call(
+    held = lax.optimization_barrier((vg_grads, norm_parts))[0]
+    weight_parts = call(
         weight_kernel,
-        [shape((NY, QUARTER // NK, 2 * COLS), bf16) for _ in range(2)],
-        (place, frames_z, quarter_gain, stat, vg_grads),
+        shape((NY * QUARTER, 2 * COLS), bf16),
+        (place, frames_z, quarter_gain, stat, *held),
+        smem=(0,),
+        scratch=[pltpu.VMEM((ROWS, QUARTER), bf16)],
+    )
+    in_weight = lax.psum_scatter(
+        weight_parts, TIME, scatter_dimension=0, tiled=True
+    ).astype(f32)
+
+    out_parts = call(
+        out_kernel,
+        [shape((ROWS, COLS), bf16) for _ in range(NX)]
+        + [shape((NY, QUARTER // NK, COLS), bf16) for _ in range(2)],
+        (place, after(act_z, norm_parts), *grads, weights),
         smem=(0,),
         scratch=[
             pltpu.VMEM((NK, ROWS, QUARTER // NK), bf16),
-            pltpu.VMEM((ROWS, NX * 2 * COLS), bf16),
+            pltpu.VMEM((ROWS, NY * COLS), bf16),
         ],
     )
+    kept, given = out_parts[NX:]
     other = lax.ppermute(given, "k", [(0, 1), (1, 0)])
-    both = (kept.astype(f32) + other.astype(f32)).astype(bf16)
-    in_weight = taken(both, "y", NY)
-
-    enc_parts, out_weight_parts = call(
-        out_kernel,
-        [shape((NX, ROWS, COLS), bf16), shape((NY * QUARTER, COLS), bf16)],
-        (order, act_wide, *grads, weights),
-        smem=(0,),
-        scratch=[pltpu.VMEM((ROWS, QUARTER), bf16)],
-    )
-    grad_out_weight = lax.psum_scatter(
-        out_weight_parts, TIME, scatter_dimension=0, tiled=True
-    ).astype(f32)
-    enc_sum = taken(enc_parts, "x", NX)
+    both = [(kept[i].astype(f32) + other[i].astype(f32)) for i in range(NY)]
+    grad_out_weight = both[0]
+    for i in range(1, NY):
+        grad_out_weight = grad_out_weight + shifted(both[i].astype(bf16), "y", NY, i).astype(f32)
+    enc_sum = out_parts[0].astype(f32)
+    for j in range(1, NX):
+        enc_sum = enc_sum + shifted(out_parts[j], "x", NX, j).astype(f32)
     encoded = swap_xy((frames.astype(f32) + enc_sum).astype(bf16))
 
     input_grad, gain_term = call(

time: 220 us -> 230 us (1.045)
  waiting for transfers between devices: 63.7 us -> 45.4 us
  blocking collectives: 15.8 us -> 29.9 us
  starting transfers between devices: 71.7 us -> 79.1 us
  local copies, waits for them, and re-layouts: 27.5 us -> 31 us
    all_gather x1 -> x0, waiting for transfers between devices: 14.8 us -> none  [shards(): act_wide = lax.all_gather(activated, 'z', axis=0, tiled=False)]
    all_to_all x1, blocking collectives: 15.8 us -> 29.9 us  [exchange(): return lax.all_to_all(parts, axis, 0, 0, tiled=True)]
    reduce_scatter x2 -> x1, waiting for transfers between devices: 12.3 us -> 0.01 us  [shards(): lax.psum_scatter(weight_parts, TIME, scatter_dimension=0, tiled=True)]
    ppermute x9 -> x15, waiting for transfers between devices: 8.51 us -> 20 us  [shifted(): lax.ppermute(block, axis, [(i, (i + shift) % count) for i in range(count)])]
    ppermute x5, starting transfers between devices: 22.1 us -> 28.9 us  [swap_xy(): lax.ppermute(block, ('x', 'y'), [(a * NY + b, b * NY + a) for a in range(...]
    unnamed x65 -> x73, local copies, waits for them, and re-layouts: 21.4 us -> 24.6 us
    ppermute x2, starting transfers between devices: 3.15 us -> 6.01 us  [neighbours(): low = lax.ppermute(block[-width:], ('k', 'y'), forward)]
    ppermute x2, waiting for transfers between devices: 3.33 us -> 0.72 us  [neighbours(): high = lax.ppermute(block[:width], ('k', 'y'), backward)]
  transfers between devices with their start and end apart: 31 -> 35, of which waited for: 12 -> 14; matrix products, arithmetic and copies ran while one was open for 5% -> 5% of each run, Pallas kernels for 7% -> 5%
where the time goes in v4:
time: 230 us; the launch traced here: 228 us
  starting transfers between devices  79.1 us (34%)
  waiting for transfers between devices  45.4 us (20%)
  local copies, waits for them, and re-layouts  31 us (13%)
  blocking collectives  29.9 us (13%)
  Pallas kernels  19.4 us (8%)
  between operations  14.6 us (6%)
  other arithmetic  8.36 us (4%)
    all_to_all x1, blocking collectives, exchange(): return lax.all_to_all(parts, axis, 0, 0, tiled=True)  29.9 us
    ppermute x5, starting transfers between devices, swap_xy(): lax.ppermute(block, ('x', 'y'), [(a * NY + b, b * NY + a) for a in range(...  28.9 us
    unnamed x73, local copies, waits for them, and re-layouts  24.6 us
    ppermute x15, waiting for transfers between devices, shifted(): lax.ppermute(block, axis, [(i, (i + shift) % count) for i in range(count)])  20 us
    pallas_call x10, Pallas kernels, call(): pl.pallas_call(body, out_shape=out_shape, in_specs=specs, scratch_shapes=...  19.4 us
    ppermute x5, waiting for transfers between devices, swap_xy(): lax.ppermute(block, ('x', 'y'), [(a * NY + b, b * NY + a) for a in range(...  17.7 us
    all_to_all x3, starting transfers between devices, exchange(): return lax.all_to_all(parts, axis, 0, 0, tiled=True)  16.9 us
    ppermute x15, starting transfers between devices, shifted(): lax.ppermute(block, axis, [(i, (i + shift) % count) for i in range(count)])  14.8 us
  transfers between devices with their start and end apart: 35, of which 14 were waited for; matrix products, arithmetic and copies ran while one was open for 5% of the time, Pallas kernels for 5%

profile of v4, /device:TPU:6, one launch (start us, length us, event | category | flops | bytes accessed | tf_op | source)
XLA Modules:
  0.0 227.7 jit_solution(121878283834336496)
XLA Ops:
  7.2 1.8 pad_maximum_fusion
  9.1 4.8 %collective-permute-start = (bf16[384,128]{1,0:T(8,128)(2,1)}, bf16[384,128]{1,0:T(8,128)(2,1)S(1)}, u32[]{:S(2)}, u32[]{:S(2)}) collective-permute-start(bf16[384,128]{1,0:T(8,128)(2,1)} %param.8), channel_id=1, source_target_pairs={{0,0},{8,64},{16,128},{24,192},{64,8},{72,72},{80,136},{88,200},{1... | collective-permute-start | bytes 294920 | tf_op jit(solution)/shard_map/ppermute | solution.py:364
  13.9 7.3 %collective-permute-done.frames_ref = bf16[384,128]{1,0:T(8,128)(2,1)S(1)} collective-permute-done((bf16[384,128]{1,0:T(8,128)(2,1)}, bf16[384,128]{1,0:T(8,128)(2,1)S(1)}, u32[]{:S(2)}, u32[]{:S(2)}) %collective-permute-start) | collective-permute-done | bytes 98336 | tf_op jit(solution)/shard_map/ppermute | solution.py:364
  22.2 8.5 %all-to-all-start = ((bf16[8,384,128]{2,1,0:T(8,128)(2,1)}), bf16[8,384,128]{2,1,0:T(8,128)(2,1)S(1)}, u32[]{:S(2)}, u32[]{:S(2)}) async-start(bf16[8,384,128]{2,1,0:T(8,128)(2,1)} %broadcast_in_dim.10), calls=%async_computation | async-start | bytes 1572864 | tf_op jit(solution)/shard_map/all_to_all | solution.py:379
  31.5 4.8 %collective-permute-start.6 = (bf16[384,128]{1,0:T(8,128)(2,1)S(1)}, bf16[384,128]{1,0:T(8,128)(2,1)S(1)}, u32[]{:S(2)}, u32[]{:S(2)}) collective-permute-start(bf16[384,128]{1,0:T(8,128)(2,1)S(1)} %copy-done.34), channel_id=1, source_target_pairs={{0,0},{8,64},{16,128},{24,192},{64,8},{72,72},{80,136},{88,200},{1... | collective-permute-start | bytes 294920 | tf_op jit(solution)/shard_map/ppermute | solution.py:364
  36.3 6.0 %collective-permute-done.6.g0_ref.grad_ref = bf16[384,128]{1,0:T(8,128)(2,1)S(1)} collective-permute-done((bf16[384,128]{1,0:T(8,128)(2,1)S(1)}, bf16[384,128]{1,0:T(8,128)(2,1)S(1)}, u32[]{:S(2)}, u32[]{:S(2)}) %collective-permute-start.6) | collective-permute-done | bytes 98336 | tf_op jit(solution)/shard_map/ppermute | solution.py:364
  42.4 2.0 collective-permute-start.10
  45.5 5.1 %all-to-all-done.frames_ref = bf16[8,384,128]{2,1,0:T(8,128)(2,1)S(1)} async-done(((bf16[8,384,128]{2,1,0:T(8,128)(2,1)}), bf16[8,384,128]{2,1,0:T(8,128)(2,1)S(1)}, u32[]{:S(2)}, u32[]{:S(2)}) %all-to-all-start) | async-done | bytes 786464 | tf_op jit(solution)/shard_map/all_to_all | solution.py:379
  51.5 1.9 copy-done
  55.3 2.7 %shard_map.143 = (bf16[432,256]{1,0:T(8,128)(2,1)S(1)}, bf16[432,256]{1,0:T(8,128)(2,1)S(1)}, bf16[432,256]{1,0:T(8,128)(2,1)S(1)}, bf16[432,256]{1,0:T(8,128)(2,1)S(1)}) custom-call(s32[14]{0:T(128)S(1)} %concatenate.16.place_ref, bf16[8,384,128]{2,1,0:T(8,128)(2,1)S(1)} %copy-done.4, f32[1,1024]{1,0:T(1,128)S(1)} %bitcast.22, ...), custom_call_target="tpu_custom_call" | custom-call | tf_op jit(solution)/shard_map/pallas_call | solution.py:74
  60.8 1.9 shard_map.146
  63.6 4.2 %all-to-all-start.2 = ((bf16[8,384,128]{2,1,0:T(8,128)(2,1)}), bf16[8,384,128]{2,1,0:T(8,128)(2,1)}, u32[]{:S(2)}, u32[]{:S(2)}) async-start(bf16[8,384,128]{2,1,0:T(8,128)(2,1)} %copy-done.7), calls=%async_computation.2 | async-start | bytes 1572864 | tf_op jit(solution)/shard_map/all_to_all | solution.py:379
  68.6 3.9 %collective-permute-start.2 = (bf16[432,256]{1,0:T(8,128)(2,1)}, bf16[432,256]{1,0:T(8,128)(2,1)S(1)}, u32[]{:S(2)}, u32[]{:S(2)}) collective-permute-start(bf16[432,256]{1,0:T(8,128)(2,1)} %copy-done.28), channel_id=1, source_target_pairs={{0,128},{64,192},{128,0},{192,64},{1,129},{65,193},{129,1},{193,65... | collective-permute-start | bytes 663560 | tf_op jit(solution)/shard_map/ppermute | solution.py:387
  73.8 6.4 %collective-permute-start.8 = (f32[32,128]{1,0:T(8,128)}, f32[32,128]{1,0:T(8,128)}, u32[]{:S(2)}, u32[]{:S(2)}) collective-permute-start(f32[32,128]{1,0:T(8,128)} %pad_maximum_fusion.1), channel_id=1, source_target_pairs={{0,0},{8,64},{16,128},{24,192},{64,8},{72,72},{80,136},{88,200},{1... | collective-permute-start | bytes 49160 | tf_op jit(solution)/shard_map/ppermute | solution.py:364
  89.3 4.7 %collective-permute-start.11 = (bf16[16,128]{1,0:T(8,128)(2,1)S(1)}, bf16[16,128]{1,0:T(8,128)(2,1)S(1)}, u32[]{:S(2)}, u32[]{:S(2)}) collective-permute-start(bf16[16,128]{1,0:T(8,128)(2,1)S(1)} %get-tuple-element.78), channel_id=1, source_target_pairs={{0,32},{32,8},{8,40},{40,16},{16,48},{48,24},{24,56},{1,33},{33,9}... | collective-permute-start | bytes 12296 | tf_op jit(solution)/shard_map/ppermute | solution.py:373
  100.9 2.2 shard_map.148
  105.3 4.6 %collective-permute-done.13.g1_ref = bf16[416,256]{1,0:T(8,128)(2,1)S(1)} collective-permute-done((bf16[416,256]{1,0:T(8,128)(2,1)S(1)}, bf16[416,256]{1,0:T(8,128)(2,1)S(1)}, u32[]{:S(2)}, u32[]{:S(2)}) %collective-permute-start.13) | collective-permute-done | bytes 213024 | tf_op jit(solution)/shard_map/ppermute | solution.py:387
  109.9 3.0 %collective-permute-done.14.g2_ref = bf16[416,256]{1,0:T(8,128)(2,1)S(1)} collective-permute-done((bf16[416,256]{1,0:T(8,128)(2,1)S(1)}, bf16[416,256]{1,0:T(8,128)(2,1)S(1)}, u32[]{:S(2)}, u32[]{:S(2)}) %collective-permute-start.14) | collective-permute-done | bytes 213024 | tf_op jit(solution)/shard_map/ppermute | solution.py:387
  112.9 5.5 %collective-permute-done.15.g3_ref = bf16[416,256]{1,0:T(8,128)(2,1)S(1)} collective-permute-done((bf16[416,256]{1,0:T(8,128)(2,1)S(1)}, bf16[416,256]{1,0:T(8,128)(2,1)S(1)}, u32[]{:S(2)}, u32[]{:S(2)}) %collective-permute-start.15) | collective-permute-done | bytes 213024 | tf_op jit(solution)/shard_map/ppermute | solution.py:387
  121.0 2.3 %shard_map.152 = bf16[4096,256]{1,0:T(8,128)(2,1)S(1)} custom-call(s32[14]{0:T(128)S(1)} %concatenate.16.place_ref, bf16[8,384,128]{2,1,0:T(8,128)(2,1)S(1)} %copy-done.5, f32[1,1024]{1,0:T(1,128)S(1)} %bitcast.23, f32[384,128]{1,0:T(8,128)S(1)} %get-tuple-element.60.stat_ref, bf16[416,256]{1,0:T(8,128)(2,1)S(1)} %get-tuple-element.62.g0_ref, ...), custom_call_target="tpu_custom_call" | custom-call | tf_op jit(solution)/shard_map/pallas_call | solution.py:74
  125.6 29.9 %all_to_all.20.act_ref = bf16[8,384,128]{2,1,0:T(8,128)(2,1)} all-to-all(bf16[8,384,128]{2,1,0:T(8,128)(2,1)S(1)} %broadcast_in_dim.24), channel_id=1, replica_groups=mesh['x'=4,'k'=2,'y'=4,'z'=8] {'z'}, dimensions={0} | all-to-all | bytes 1572864 | tf_op jit(solution)/shard_map/all_to_all | solution.py:379
  155.6 4.2 %all-to-all-start.3 = ((bf16[8,432,128]{2,1,0:T(8,128)(2,1)}), bf16[8,432,128]{2,1,0:T(8,128)(2,1)}, u32[]{:S(2)}, u32[]{:S(2)}) async-start(bf16[8,432,128]{2,1,0:T(8,128)(2,1)} %copy-done.6), calls=%async_computation.3 | async-start | bytes 1769472 | tf_op jit(solution)/shard_map/all_to_all | solution.py:379
  162.7 3.3 %shard_map.150 = (bf16[384,128]{1,0:T(8,128)(2,1)S(1)}, bf16[384,128]{1,0:T(8,128)(2,1)S(1)}, bf16[384,128]{1,0:T(8,128)(2,1)S(1)}, bf16[384,128]{1,0:T(8,128)(2...) custom-call(s32[14]{0:T(128)S(1)} %concatenate.16.place_ref, bf16[8,384,128]{2,1,0:T(8,128)(2,1)S(1)} %copy-done.8, ...), custom_call_target="tpu_custom_call" | custom-call | tf_op jit(solution)/shard_map/pallas_call | solution.py:74
  172.9 3.1 %collective-permute-done.16 = bf16[384,128]{1,0:T(8,128)(2,1)S(1)} collective-permute-done((bf16[384,128]{1,0:T(8,128)(2,1)}, bf16[384,128]{1,0:T(8,128)(2,1)S(1)}, u32[]{:S(2)}, u32[]{:S(2)}) %collective-permute-start.16) | collective-permute-done | bytes 98336 | tf_op jit(solution)/shard_map/ppermute | solution.py:387
  177.4 1.9 collective-permute-done.18
  180.3 8.2 %collective-permute-start.19 = (bf16[384,128]{1,0:T(8,128)(2,1)S(1)}, bf16[384,128]{1,0:T(8,128)(2,1)S(1)}, u32[]{:S(2)}, u32[]{:S(2)}) collective-permute-start(bf16[384,128]{1,0:T(8,128)(2,1)S(1)} %add_convert_fusion.3), channel_id=1, source_target_pairs={{0,0},{8,64},{16,128},{24,192},{64,8},{72,72},{80,136},{88,200},{1... | collective-permute-start | bytes 294920 | tf_op jit(solution)/shard_map/ppermute | solution.py:364
  190.4 2.6 %collective-permute-start.29 = (bf16[512,128]{1,0:T(8,128)(2,1)S(1)}, bf16[512,128]{1,0:T(8,128)(2,1)S(1)}, u32[]{:S(2)}, u32[]{:S(2)}) collective-permute-start(bf16[512,128]{1,0:T(8,128)(2,1)S(1)} %get-tuple-element.73), channel_id=1, source_target_pairs={{0,24},{8,0},{16,8},{24,16},{1,25},{9,1},{17,9},{25,17},{2,26},{10... | collective-permute-start | bytes 393224 | tf_op jit(solution)/shard_map/ppermute | solution.py:387
  196.0 4.8 %collective-permute-start.22 = (f32[40,128]{1,0:T(8,128)S(1)}, f32[40,128]{1,0:T(8,128)S(1)}, u32[]{:S(2)}, u32[]{:S(2)}) collective-permute-start(f32[40,128]{1,0:T(8,128)S(1)} %add.121), channel_id=1, source_target_pairs={{0,0},{8,64},{16,128},{24,192},{64,8},{72,72},{80,136},{88,200},{1... | collective-permute-start | bytes 61448 | tf_op jit(solution)/shard_map/ppermute | solution.py:548
  200.8 3.1 %collective-permute-start.23 = (f32[40,128]{1,0:T(8,128)S(1)}, f32[40,128]{1,0:T(8,128)S(1)}, u32[]{:S(2)}, u32[]{:S(2)}) collective-permute-start(f32[40,128]{1,0:T(8,128)S(1)} %add.121), channel_id=1, source_target_pairs={{0,64},{8,128},{16,192},{24,0},{64,72},{72,136},{80,200},{88,8},{1... | collective-permute-start | bytes 61448 | tf_op jit(solution)/shard_map/ppermute | solution.py:548
  203.9 1.9 collective-permute-start.24
  207.5 4.7 %collective-permute-start.20 = (bf16[384,128]{1,0:T(8,128)(2,1)S(1)}, bf16[384,128]{1,0:T(8,128)(2,1)S(1)}, u32[]{:S(2)}, u32[]{:S(2)}) collective-permute-start(bf16[384,128]{1,0:T(8,128)(2,1)S(1)} %get-tuple-element.61), channel_id=1, source_target_pairs={{0,0},{8,64},{16,128},{24,192},{64,8},{72,72},{80,136},{88,200},{1... | collective-permute-start | bytes 294920 | tf_op jit(solution)/shard_map/ppermute | solution.py:364
  213.4 4.4 %collective-permute-done.20 = bf16[384,128]{1,0:T(8,128)(2,1)S(1)} collective-permute-done((bf16[384,128]{1,0:T(8,128)(2,1)S(1)}, bf16[384,128]{1,0:T(8,128)(2,1)S(1)}, u32[]{:S(2)}, u32[]{:S(2)}) %collective-permute-start.20) | collective-permute-done | bytes 98336 | tf_op jit(solution)/shard_map/ppermute | solution.py:364
  (149 shorter events, 57.4 us)
Async XLA Ops:
  7.2 44.3 %all-gather.2.cloned.1.call-start = ((), (), s32[]{:S(2)}) async-start(), calls=%async_computation.5 | async-start | bytes 3538944 | tf_op jit(solution)/shard_map/all_gather | solution.py:419
  9.1 12.1 %collective-permute-start = (bf16[384,128]{1,0:T(8,128)(2,1)}, bf16[384,128]{1,0:T(8,128)(2,1)S(1)}, u32[]{:S(2)}, u32[]{:S(2)}) collective-permute-start(bf16[384,128]{1,0:T(8,128)(2,1)} %param.8), channel_id=1, source_target_pairs={{0,0},{8,64},{16,128},{24,192},{64,8},{72,72},{80,136},{88,200},{1... | collective-permute-start | bytes 294920 | tf_op jit(solution)/shard_map/ppermute | solution.py:364
  22.2 28.4 %all-to-all-start = ((bf16[8,384,128]{2,1,0:T(8,128)(2,1)}), bf16[8,384,128]{2,1,0:T(8,128)(2,1)S(1)}, u32[]{:S(2)}, u32[]{:S(2)}) async-start(bf16[8,384,128]{2,1,0:T(8,128)(2,1)} %broadcast_in_dim.10), calls=%async_computation | async-start | bytes 1572864 | tf_op jit(solution)/shard_map/all_to_all | solution.py:379
  31.5 10.9 %collective-permute-start.6 = (bf16[384,128]{1,0:T(8,128)(2,1)S(1)}, bf16[384,128]{1,0:T(8,128)(2,1)S(1)}, u32[]{:S(2)}, u32[]{:S(2)}) collective-permute-start(bf16[384,128]{1,0:T(8,128)(2,1)S(1)} %copy-done.34), channel_id=1, source_target_pairs={{0,0},{8,64},{16,128},{24,192},{64,8},{72,72},{80,136},{88,200},{1... | collective-permute-start | bytes 294920 | tf_op jit(solution)/shard_map/ppermute | solution.py:364
  42.4 18.4 %collective-permute-start.7 = (bf16[384,128]{1,0:T(8,128)(2,1)S(1)}, bf16[384,128]{1,0:T(8,128)(2,1)S(1)}, u32[]{:S(2)}, u32[]{:S(2)}) collective-permute-start(bf16[384,128]{1,0:T(8,128)(2,1)S(1)} %collective-permute-done.6.g0_ref.grad_ref), channel_id=1, source_target_pairs={{0,64},{64,128},{128,192},{192,0},{1,65},{65,129},{129,193},{193,1... | collective-permute-start | bytes 294920 | tf_op jit(solution)/shard_map/ppermute | solution.py:387
  42.4 18.4 %collective-permute-start.10 = (bf16[384,128]{1,0:T(8,128)(2,1)S(1)}, bf16[384,128]{1,0:T(8,128)(2,1)S(1)}, u32[]{:S(2)}, u32[]{:S(2)}) collective-permute-start(bf16[384,128]{1,0:T(8,128)(2,1)S(1)} %collective-permute-done.6.g0_ref.grad_ref), channel_id=1, source_target_pairs={{0,192},{64,0},{128,64},{192,128},{1,193},{65,1},{129,65},{193,129... | collective-permute-start | bytes 294920 | tf_op jit(solution)/shard_map/ppermute | solution.py:387
  44.4 16.4 %collective-permute-start.9 = (bf16[384,128]{1,0:T(8,128)(2,1)S(1)}, bf16[384,128]{1,0:T(8,128)(2,1)}, u32[]{:S(2)}, u32[]{:S(2)}) collective-permute-start(bf16[384,128]{1,0:T(8,128)(2,1)S(1)} %collective-permute-done.6.g0_ref.grad_ref), channel_id=1, source_target_pairs={{0,128},{64,192},{128,0},{192,64},{1,129},{65,193},{129,1},{193,65... | collective-permute-start | bytes 294920 | tf_op jit(solution)/shard_map/ppermute | solution.py:387
  63.6 24.4 %all-to-all-start.2 = ((bf16[8,384,128]{2,1,0:T(8,128)(2,1)}), bf16[8,384,128]{2,1,0:T(8,128)(2,1)}, u32[]{:S(2)}, u32[]{:S(2)}) async-start(bf16[8,384,128]{2,1,0:T(8,128)(2,1)} %copy-done.7), calls=%async_computation.2 | async-start | bytes 1572864 | tf_op jit(solution)/shard_map/all_to_all | solution.py:379
  67.8 150.0 %reduce-scatter.2.cloned.1.call-start = ((), (), s32[]{:S(2)}) async-start(), calls=%async_computation.6 | async-start | bytes 2359296 | tf_op jit(solution)/shard_map/reduce_scatter | solution.py:508
  67.9 12.3 %collective-permute-start.1 = (bf16[432,256]{1,0:T(8,128)(2,1)}, bf16[432,256]{1,0:T(8,128)(2,1)S(1)}, u32[]{:S(2)}, u32[]{:S(2)}) collective-permute-start(bf16[432,256]{1,0:T(8,128)(2,1)} %copy-done.29), channel_id=1, source_target_pairs={{0,64},{64,128},{128,192},{192,0},{1,65},{65,129},{129,193},{193,1... | collective-permute-start | bytes 663560 | tf_op jit(solution)/shard_map/ppermute | solution.py:387
  68.6 11.6 %collective-permute-start.2 = (bf16[432,256]{1,0:T(8,128)(2,1)}, bf16[432,256]{1,0:T(8,128)(2,1)S(1)}, u32[]{:S(2)}, u32[]{:S(2)}) collective-permute-start(bf16[432,256]{1,0:T(8,128)(2,1)} %copy-done.28), channel_id=1, source_target_pairs={{0,128},{64,192},{128,0},{192,64},{1,129},{65,193},{129,1},{193,65... | collective-permute-start | bytes 663560 | tf_op jit(solution)/shard_map/ppermute | solution.py:387
  72.5 8.2 %collective-permute-start.3 = (bf16[432,256]{1,0:T(8,128)(2,1)}, bf16[432,256]{1,0:T(8,128)(2,1)S(1)}, u32[]{:S(2)}, u32[]{:S(2)}) collective-permute-start(bf16[432,256]{1,0:T(8,128)(2,1)} %copy-done.27), channel_id=1, source_target_pairs={{0,192},{64,0},{128,64},{192,128},{1,193},{65,1},{129,65},{193,129... | collective-permute-start | bytes 663560 | tf_op jit(solution)/shard_map/ppermute | solution.py:387
  73.8 21.5 %collective-permute-start.8 = (f32[32,128]{1,0:T(8,128)}, f32[32,128]{1,0:T(8,128)}, u32[]{:S(2)}, u32[]{:S(2)}) collective-permute-start(f32[32,128]{1,0:T(8,128)} %pad_maximum_fusion.1), channel_id=1, source_target_pairs={{0,0},{8,64},{16,128},{24,192},{64,8},{72,72},{80,136},{88,200},{1... | collective-permute-start | bytes 49160 | tf_op jit(solution)/shard_map/ppermute | solution.py:364
  84.8 10.6 %collective-permute-start.4 = (bf16[32,128]{1,0:T(8,128)(2,1)}, bf16[32,128]{1,0:T(8,128)(2,1)S(1)}, u32[]{:S(2)}, u32[]{:S(2)}) collective-permute-start(bf16[32,128]{1,0:T(8,128)(2,1)} %get-tuple-element.80), channel_id=1, source_target_pairs={{0,32},{32,8},{8,40},{40,16},{16,48},{48,24},{24,56},{1,33},{33,9}... | collective-permute-start | bytes 24584 | tf_op jit(solution)/shard_map/ppermute | solution.py:373
  86.1 9.3 %collective-permute-start.5 = (bf16[32,128]{1,0:T(8,128)(2,1)}, bf16[32,128]{1,0:T(8,128)(2,1)}, u32[]{:S(2)}, u32[]{:S(2)}) collective-permute-start(bf16[32,128]{1,0:T(8,128)(2,1)} %get-tuple-element.79), channel_id=1, source_target_pairs={{32,0},{8,32},{40,8},{16,40},{48,16},{24,48},{56,24},{33,1},{9,33}... | collective-permute-start | bytes 24584 | tf_op jit(solution)/shard_map/ppermute | solution.py:374
  89.3 8.3 %collective-permute-start.11 = (bf16[16,128]{1,0:T(8,128)(2,1)S(1)}, bf16[16,128]{1,0:T(8,128)(2,1)S(1)}, u32[]{:S(2)}, u32[]{:S(2)}) collective-permute-start(bf16[16,128]{1,0:T(8,128)(2,1)S(1)} %get-tuple-element.78), channel_id=1, source_target_pairs={{0,32},{32,8},{8,40},{40,16},{16,48},{48,24},{24,56},{1,33},{33,9}... | collective-permute-start | bytes 12296 | tf_op jit(solution)/shard_map/ppermute | solution.py:373
  103.1 6.9 %collective-permute-start.13 = (bf16[416,256]{1,0:T(8,128)(2,1)S(1)}, bf16[416,256]{1,0:T(8,128)(2,1)S(1)}, u32[]{:S(2)}, u32[]{:S(2)}) collective-permute-start(bf16[416,256]{1,0:T(8,128)(2,1)S(1)} %get-tuple-element.62.g0_ref), channel_id=1, source_target_pairs={{0,64},{64,128},{128,192},{192,0},{1,65},{65,129},{129,193},{193,1... | collective-permute-start | bytes 638984 | tf_op jit(solution)/shard_map/ppermute | solution.py:387
  104.3 8.6 %collective-permute-start.14 = (bf16[416,256]{1,0:T(8,128)(2,1)S(1)}, bf16[416,256]{1,0:T(8,128)(2,1)S(1)}, u32[]{:S(2)}, u32[]{:S(2)}) collective-permute-start(bf16[416,256]{1,0:T(8,128)(2,1)S(1)} %get-tuple-element.62.g0_ref), channel_id=1, source_target_pairs={{0,128},{64,192},{128,0},{192,64},{1,129},{65,193},{129,1},{193,65... | collective-permute-start | bytes 638984 | tf_op jit(solution)/shard_map/ppermute | solution.py:387
  105.3 13.1 %collective-permute-start.15 = (bf16[416,256]{1,0:T(8,128)(2,1)S(1)}, bf16[416,256]{1,0:T(8,128)(2,1)S(1)}, u32[]{:S(2)}, u32[]{:S(2)}) collective-permute-start(bf16[416,256]{1,0:T(8,128)(2,1)S(1)} %get-tuple-element.62.g0_ref), channel_id=1, source_target_pairs={{0,192},{64,0},{128,64},{192,128},{1,193},{65,1},{129,65},{193,129... | collective-permute-start | bytes 638984 | tf_op jit(solution)/shard_map/ppermute | solution.py:387
  155.6 37.4 %all-to-all-start.3 = ((bf16[8,432,128]{2,1,0:T(8,128)(2,1)}), bf16[8,432,128]{2,1,0:T(8,128)(2,1)}, u32[]{:S(2)}, u32[]{:S(2)}) async-start(bf16[8,432,128]{2,1,0:T(8,128)(2,1)} %copy-done.6), calls=%async_computation.3 | async-start | bytes 1769472 | tf_op jit(solution)/shard_map/all_to_all | solution.py:379
  169.4 19.1 %collective-permute-start.26 = (bf16[4,512,128]{2,1,0:T(8,128)(2,1)}, bf16[4,512,128]{2,1,0:T(8,128)(2,1)S(1)}, u32[]{:S(2)}, u32[]{:S(2)}) collective-permute-start(bf16[4,512,128]{2,1,0:T(8,128)(2,1)} %get-tuple-element.69), channel_id=1, source_target_pairs={{0,32},{32,0},{1,33},{33,1},{2,34},{34,2},{3,35},{35,3},{4,36},{36... | collective-permute-start | bytes 1572872 | tf_op jit(solution)/shard_map/ppermute | solution.py:524
  170.7 6.7 %collective-permute-start.17 = (bf16[384,128]{1,0:T(8,128)(2,1)}, bf16[384,128]{1,0:T(8,128)(2,1)S(1)}, u32[]{:S(2)}, u32[]{:S(2)}) collective-permute-start(bf16[384,128]{1,0:T(8,128)(2,1)} %copy-done.31), channel_id=1, source_target_pairs={{0,128},{64,192},{128,0},{192,64},{1,129},{65,193},{129,1},{193,65... | collective-permute-start | bytes 294920 | tf_op jit(solution)/shard_map/ppermute | solution.py:387
  170.8 8.5 %collective-permute-start.18 = (bf16[384,128]{1,0:T(8,128)(2,1)}, bf16[384,128]{1,0:T(8,128)(2,1)S(1)}, u32[]{:S(2)}, u32[]{:S(2)}) collective-permute-start(bf16[384,128]{1,0:T(8,128)(2,1)} %copy-done.30), channel_id=1, source_target_pairs={{0,192},{64,0},{128,64},{192,128},{1,193},{65,1},{129,65},{193,129... | collective-permute-start | bytes 294920 | tf_op jit(solution)/shard_map/ppermute | solution.py:387
  180.3 14.5 %collective-permute-start.19 = (bf16[384,128]{1,0:T(8,128)(2,1)S(1)}, bf16[384,128]{1,0:T(8,128)(2,1)S(1)}, u32[]{:S(2)}, u32[]{:S(2)}) collective-permute-start(bf16[384,128]{1,0:T(8,128)(2,1)S(1)} %add_convert_fusion.3), channel_id=1, source_target_pairs={{0,0},{8,64},{16,128},{24,192},{64,8},{72,72},{80,136},{88,200},{1... | collective-permute-start | bytes 294920 | tf_op jit(solution)/shard_map/ppermute | solution.py:364
  189.7 14.2 %collective-permute-start.27 = (bf16[512,128]{1,0:T(8,128)(2,1)S(1)}, bf16[512,128]{1,0:T(8,128)(2,1)S(1)}, u32[]{:S(2)}, u32[]{:S(2)}) collective-permute-start(bf16[512,128]{1,0:T(8,128)(2,1)S(1)} %get-tuple-element.72), channel_id=1, source_target_pairs={{0,8},{8,16},{16,24},{24,0},{1,9},{9,17},{17,25},{25,1},{2,10},{10... | collective-permute-start | bytes 393224 | tf_op jit(solution)/shard_map/ppermute | solution.py:387
  189.8 16.0 %collective-permute-start.28 = (bf16[512,128]{1,0:T(8,128)(2,1)S(1)}, bf16[512,128]{1,0:T(8,128)(2,1)S(1)}, u32[]{:S(2)}, u32[]{:S(2)}) collective-permute-start(bf16[512,128]{1,0:T(8,128)(2,1)S(1)} %get-tuple-element.74), channel_id=1, source_target_pairs={{0,16},{8,24},{16,0},{24,8},{1,17},{9,25},{17,1},{25,9},{2,18},{10... | collective-permute-start | bytes 393224 | tf_op jit(solution)/shard_map/ppermute | solution.py:387
  190.4 15.4 %collective-permute-start.29 = (bf16[512,128]{1,0:T(8,128)(2,1)S(1)}, bf16[512,128]{1,0:T(8,128)(2,1)S(1)}, u32[]{:S(2)}, u32[]{:S(2)}) collective-permute-start(bf16[512,128]{1,0:T(8,128)(2,1)S(1)} %get-tuple-element.73), channel_id=1, source_target_pairs={{0,24},{8,0},{16,8},{24,16},{1,25},{9,1},{17,9},{25,17},{2,26},{10... | collective-permute-start | bytes 393224 | tf_op jit(solution)/shard_map/ppermute | solution.py:387
  196.0 16.2 %collective-permute-start.22 = (f32[40,128]{1,0:T(8,128)S(1)}, f32[40,128]{1,0:T(8,128)S(1)}, u32[]{:S(2)}, u32[]{:S(2)}) collective-permute-start(f32[40,128]{1,0:T(8,128)S(1)} %add.121), channel_id=1, source_target_pairs={{0,0},{8,64},{16,128},{24,192},{64,8},{72,72},{80,136},{88,200},{1... | collective-permute-start | bytes 61448 | tf_op jit(solution)/shard_map/ppermute | solution.py:548
  200.8 11.5 %collective-permute-start.23 = (f32[40,128]{1,0:T(8,128)S(1)}, f32[40,128]{1,0:T(8,128)S(1)}, u32[]{:S(2)}, u32[]{:S(2)}) collective-permute-start(f32[40,128]{1,0:T(8,128)S(1)} %add.121), channel_id=1, source_target_pairs={{0,64},{8,128},{16,192},{24,0},{64,72},{72,136},{80,200},{88,8},{1... | collective-permute-start | bytes 61448 | tf_op jit(solution)/shard_map/ppermute | solution.py:548
  203.9 8.3 %collective-permute-start.24 = (f32[40,128]{1,0:T(8,128)S(1)}, f32[40,128]{1,0:T(8,128)S(1)}, u32[]{:S(2)}, u32[]{:S(2)}) collective-permute-start(f32[40,128]{1,0:T(8,128)S(1)} %add.121), channel_id=1, source_target_pairs={{0,128},{8,192},{16,0},{24,64},{64,136},{72,200},{80,8},{88,72},{1... | collective-permute-start | bytes 61448 | tf_op jit(solution)/shard_map/ppermute | solution.py:548
  205.8 6.4 %collective-permute-start.25 = (f32[40,128]{1,0:T(8,128)S(1)}, f32[40,128]{1,0:T(8,128)S(1)}, u32[]{:S(2)}, u32[]{:S(2)}) collective-permute-start(f32[40,128]{1,0:T(8,128)S(1)} %add.121), channel_id=1, source_target_pairs={{0,192},{8,0},{16,64},{24,128},{64,200},{72,8},{80,72},{88,136},{1... | collective-permute-start | bytes 61448 | tf_op jit(solution)/shard_map/ppermute | solution.py:548
  207.5 10.3 %collective-permute-start.20 = (bf16[384,128]{1,0:T(8,128)(2,1)S(1)}, bf16[384,128]{1,0:T(8,128)(2,1)S(1)}, u32[]{:S(2)}, u32[]{:S(2)}) collective-permute-start(bf16[384,128]{1,0:T(8,128)(2,1)S(1)} %get-tuple-element.61), channel_id=1, source_target_pairs={{0,0},{8,64},{16,128},{24,192},{64,8},{72,72},{80,136},{88,200},{1... | collective-permute-start | bytes 294920 | tf_op jit(solution)/shard_map/ppermute | solution.py:364
  (38 other events, 164.6 us)
Sparse Core Ops, SparseCore 0:
  9.8 35.3 all-gather.1
  124.7 41.1 reduce-scatter.1

commit v5 on v4

--- a/solution.py
+++ b/solution.py
@@ -17,6 +17,8 @@
 QUARTER = COLS * NZ
 WIDTH = QUARTER * NX
 EDGE = 32
+IN = (0, 2 * COLS)
+OUT = (2 * COLS, COLS)
 
 epsilon = 1e-05
 f32 = jnp.float32
@@ -66,18 +68,69 @@
     return out
 
 
-def call(body, out_shape, args, smem=(), scratch=()):
-    specs = [
-        pl.BlockSpec(memory_space=pltpu.SMEM) if i in smem else pl.BlockSpec()
-        for i in range(len(args))
+def call(body, out_shape, args, smem=(), near=(), scratch=(), cuts=()):
+    cuts = dict(cuts)
+    single = not isinstance(out_shape, (list, tuple))
+    outs = [out_shape] if single else list(out_shape)
+    count = len(args)
+    moved = [i for i in range(count) if i not in smem and i not in near]
+    buffers = []
+    for i in moved:
+        dims = args[i].shape
+        if i in cuts:
+            dims = (dims[0], cuts[i][1])
+        buffers.append(pltpu.VMEM(dims, args[i].dtype))
+    for out in outs:
+        buffers.append(pltpu.VMEM(out.shape, out.dtype))
+
+    def whole(*refs):
+        refs = list(refs)
+        inputs, refs = refs[:count], refs[count:]
+        results, refs = refs[: len(outs)], refs[len(outs) :]
+        held, refs = refs[: len(buffers)], refs[len(buffers) :]
+        sems, extra = refs[0], refs[1:]
+        copies = []
+        for place, i in enumerate(moved):
+            source = inputs[i]
+            if i in cuts:
+                source = source.at[:, pl.ds(cuts[i][0], cuts[i][1])]
+            copies.append(pltpu.make_async_copy(source, held[place], sems.at[place]))
+            inputs[i] = held[place]
+        for copy in copies:
+            copy.start()
+        for copy in copies:
+            copy.wait()
+        body(*inputs, *held[len(moved) :], *extra)
+        copies = []
+        for place, result in enumerate(results, len(moved)):
+            copies.append(pltpu.make_async_copy(held[place], result, sems.at[place]))
+        for copy in copies:
+            copy.start()
+        for copy in copies:
+            copy.wait()
+
+    hbm = pl.BlockSpec(memory_space=pltpu.MemorySpace.HBM)
+    spaces = [
+        pltpu.MemorySpace.SMEM
+        if i in smem
+        else (pltpu.MemorySpace.VMEM if i in near else pltpu.MemorySpace.HBM)
+        for i in range(count)
     ]
-    return pl.pallas_call(
-        body,
-        out_shape=out_shape,
-        in_specs=specs,
-        scratch_shapes=list(scratch),
-        compiler_params=pltpu.CompilerParams(vmem_limit_bytes=48 * 1024 * 1024),
-    )(*args)
+    made = pl.pallas_call(
+        whole,
+        out_shape=[pltpu.HBM(out.shape, out.dtype) for out in outs],
+        in_specs=[pl.BlockSpec(memory_space=space) for space in spaces],
+        out_specs=[hbm] * len(outs),
+        scratch_shapes=buffers + [pltpu.SemaphoreType.DMA((len(buffers),))] + list(scratch),
+        compiler_params=pltpu.CompilerParams(vmem_limit_bytes=24 * 1024 * 1024),
+        name=body.__name__,
+    )(
+        *[
+            pltpu.with_memory_space_constraint(arg, pltpu.HBM) if i in moved else arg
+            for i, arg in enumerate(args)
+        ]
+    )
+    return made[0] if single else made
 
 
 def shape(dims, kind):
@@ -100,7 +153,7 @@
     sums = columns_to_rows(total, square).astype(bf16)
     for j, out_ref in enumerate(refs[:NX]):
         start = pl.multiple_of(place_ref[4 + j] * QUARTER, QUARTER)
-        weight = weight_ref[pl.ds(start, QUARTER), 0 : 2 * COLS]
+        weight = weight_ref[pl.ds(start, QUARTER), :]
         out_ref[0:ROWS, :] = dot(left_ref[...], weight, 1, 0).astype(bf16)
         unit = jnp.sum(dot(gain_rows_ref[...], weight, 1, 0), axis=0, keepdims=True)
         out_ref[ROWS : ROWS + 16, :] = stacked_rows(split3(unit)).astype(bf16)
@@ -139,7 +192,7 @@
     total = jnp.zeros((ROWS, QUARTER), f32)
     for j, grad_ref in enumerate((g0_ref, g1_ref, g2_ref, g3_ref)):
         start = pl.multiple_of(place_ref[j] * QUARTER, QUARTER)
-        weight = weight_ref[pl.ds(start, QUARTER), 2 * COLS : 3 * COLS]
+        weight = weight_ref[pl.ds(start, QUARTER), :]
         total = total + dot(grad_ref[...], weight, 1, 1)
     for i in range(NZ):
         out_ref[i] = total[:, i * COLS : (i + 1) * COLS].astype(bf16)
@@ -162,50 +215,16 @@
     return inside == own
 
 
-def fill_wide(wide_ref, gated_ref, low_ref, high_ref):
-    wide_ref[0:EDGE, :] = low_ref[...].astype(f32)
-    wide_ref[EDGE : EDGE + ROWS, :] = gated_ref[...].astype(f32)
-    wide_ref[EDGE + ROWS :, :] = high_ref[...].astype(f32)
-
-
-def forward_kernel(
+def conv_kernel(
     place_ref,
     gated_ref,
+    act_ref,
     low_ref,
     high_ref,
     taps_ref,
-    activated_ref,
-    slope_ref,
-    wide_ref,
-    masked_ref,
-):
-    border = place_ref[0]
-    fill_wide(wide_ref, gated_ref, low_ref, high_ref)
-    bias = taps_ref[K : K + 1, :]
-    for start, count in CHUNKS:
-        here = wide_ref[pl.ds(start - 16 + EDGE, count + 32), :]
-        masked_ref[0 : count + 32, :] = jnp.where(same_clip(border, start, count), here, 0.0)
-        conv = jnp.broadcast_to(bias, (count, COLS))
-        for tap in range(K):
-            conv = conv + taps_ref[tap : tap + 1, :] * masked_ref[1 + tap : 1 + tap + count, :]
-        sig = jax.nn.sigmoid(conv)
-        slope_ref[pl.ds(start + 16, count), :] = sig * (1.0 + conv * (1.0 - sig))
-        if 0 <= start < ROWS:
-            activated_ref[pl.ds(start, count), :] = (conv * sig).astype(bf16)
-
-
-def backward_kernel(
-    place_ref,
-    gated_ref,
-    low_ref,
-    high_ref,
-    act_ref,
-    act_low_ref,
-    act_high_ref,
-    slope_ref,
-    taps_ref,
     pre_ref,
     unit_ref,
+    activated_ref,
     message_ref,
     small_ref,
     wide_ref,
@@ -214,23 +233,35 @@
     sums_ref,
     masked_ref,
     masked_grad_ref,
+    kernel_ref,
 ):
     border = place_ref[0]
-    fill_wide(wide_ref, gated_ref, low_ref, high_ref)
+    total = jnp.zeros((K + 1, COLS), f32)
+    for i in range(3):
+        total = total + taps_ref[pl.ds(ROWS + i * (K + 1), K + 1), :].astype(f32)
+    kernel_ref[...] = total
+    wide_ref[0:EDGE, :] = low_ref[0:EDGE, :].astype(f32)
+    wide_ref[EDGE : EDGE + ROWS, :] = gated_ref[...].astype(f32)
+    wide_ref[EDGE + ROWS :, :] = high_ref[0:EDGE, :].astype(f32)
     sums_ref[...] = jnp.zeros((K + 1, 8, COLS), f32)
+    bias = kernel_ref[K : K + 1, :]
     for start, count in CHUNKS:
+        here = wide_ref[pl.ds(start - 16 + EDGE, count + 32), :]
+        masked_ref[0 : count + 32, :] = jnp.where(same_clip(border, start, count), here, 0.0)
+        conv = jnp.broadcast_to(bias, (count, COLS))
+        for tap in range(K):
+            conv = conv + kernel_ref[tap : tap + 1, :] * masked_ref[1 + tap : 1 + tap + count, :]
+        sig = jax.nn.sigmoid(conv)
         if start < 0:
-            act = act_low_ref[...]
+            act = low_ref[EDGE:, :]
         elif start < ROWS:
             act = act_ref[pl.ds(start, count), :]
         else:
-            act = act_high_ref[...]
-        grad = act.astype(f32) * slope_ref[pl.ds(start + 16, count), :]
-        grad = grad.astype(bf16).astype(f32)
+            act = high_ref[EDGE:, :]
+        grad = (act.astype(f32) * sig * (1.0 + conv * (1.0 - sig))).astype(bf16).astype(f32)
         grad_ref[pl.ds(start + 16, count), :] = grad
         if 0 <= start < ROWS:
-            here = wide_ref[pl.ds(start - 16 + EDGE, count + 32), :]
-            masked_ref[...] = jnp.where(same_clip(border, start, count), here, 0.0)
+            activated_ref[pl.ds(start, count), :] = (conv * sig).astype(bf16)
             for tap in range(K):
                 product = grad * masked_ref[1 + tap : 1 + tap + count, :]
                 sums_ref[tap] += jnp.sum(product.reshape(count // 8, 8, COLS), axis=0)
@@ -242,7 +273,7 @@
         masked_grad_ref[...] = jnp.where(same_clip(border, start, count), here, 0.0)
         glu = jnp.zeros((count, COLS), f32)
         for tap in range(K):
-            glu = glu + taps_ref[tap : tap + 1, :] * masked_grad_ref[31 - tap : 31 - tap + count, :]
+            glu = glu + kernel_ref[tap : tap + 1, :] * masked_grad_ref[31 - tap : 31 - tap + count, :]
         glu_ref[pl.ds(start, count), :] = glu
 
     glu = glu_ref[...]
@@ -272,7 +303,7 @@
     rows = jnp.zeros((16, ROWS), f32)
     for j, grad_ref in enumerate((g0_ref, g1_ref, g2_ref, g3_ref)):
         start = pl.multiple_of(place_ref[j] * QUARTER, QUARTER)
-        weight = weight_ref[pl.ds(start, QUARTER), 0 : 2 * COLS]
+        weight = weight_ref[pl.ds(start, QUARTER), :]
         total = total + dot(grad_ref[0:ROWS, :], weight, 1, 1)
         here = jnp.concatenate(
             [grad_ref[ROWS : ROWS + 16, :], grad_ref[ROWS + 16 : ROWS + 32, 0:128]], axis=1
@@ -321,7 +352,7 @@
         total = jnp.zeros((ROWS, COLS), f32)
         for h in range(NK):
             start = pl.multiple_of(place_ref[4 + j] * QUARTER + h * half, half)
-            weight = weight_ref[pl.ds(start, half), 2 * COLS : 3 * COLS]
+            weight = weight_ref[pl.ds(start, half), :]
             total = total + dot(left_ref[h], weight, 1, 0)
         enc_ref[...] = total.astype(bf16)
     for i in range(NY):
@@ -366,12 +397,12 @@
     )
 
 
-def neighbours(block, width):
+def neighbours(upper, lower):
     place = [k * NY + y for y in range(NY) for k in range(NK)]
     forward = list(zip(place[:-1], place[1:]))
     backward = [(target, source) for source, target in forward]
-    low = lax.ppermute(block[-width:], ("k", "y"), forward)
-    high = lax.ppermute(block[:width], ("k", "y"), backward)
+    low = lax.ppermute(upper, ("k", "y"), forward)
+    high = lax.ppermute(lower, ("k", "y"), backward)
     return low, high
 
 
@@ -389,6 +420,15 @@
 
 def spread(block, axis, count):
     return [block] + [shifted(block, axis, count, j) for j in range(1, count)]
+
+
+def pieces(value):
+    out = []
+    for _ in range(3):
+        piece = lax.reduce_precision(value, 8, 7)
+        out.append(piece.astype(bf16))
+        value = value - piece
+    return jnp.stack(out)
 
 
 def after(value, *others):
@@ -402,11 +442,7 @@
     col_start = (x_index * NZ + lax.axis_index("z")) * COLS
     local_gain = lax.dynamic_slice_in_dim(gain, col_start, COLS, 0)[None]
     quarter_gain = lax.dynamic_slice_in_dim(gain, x_index * QUARTER, QUARTER, 0)[None]
-    high = lax.reduce_precision(quarter_gain, 8, 7)
-    middle = lax.reduce_precision(quarter_gain - high, 8, 7)
-    low = quarter_gain - high - middle
-    gain_rows = jnp.pad(jnp.concatenate([high, middle, low], axis=0), ((0, 13), (0, 0)))
-    gain_rows = gain_rows.astype(bf16)
+    gain_rows = jnp.pad(pieces(quarter_gain)[:, 0], ((0, 13), (0, 0)))
     y_index = lax.axis_index("y")
     steps = jnp.arange(NX, dtype=jnp.int32)
     below = (x_index + NX - steps) % NX
@@ -422,23 +458,26 @@
 
     frames = swap_xy(frames)
     frames_z = gathered(frames, "z", NZ)
-    grad_out = swap_xy(after(grad_out, frames))
+    taps = jnp.concatenate([kernel, bias[None, :]], axis=0)
+    packed = jnp.concatenate([grad_out, pieces(taps).reshape(3 * (K + 1), COLS)], axis=0)
+    packed = swap_xy(after(packed, frames))
+    grad_out = packed[:ROWS]
     grads = spread(grad_out, "x", NX)
-    taps = swap_xy(after(jnp.concatenate([kernel, bias[None, :]], axis=0), grads[1]))
-
+
+    act_parts = call(
+        act_kernel, shape((NZ, ROWS, COLS), bf16), (place, *grads, weights), smem=(0,), near=(1, 2, 3, 4), cuts={5: OUT}
+    )
+    act_moved = exchange(act_parts, "z")
     pre_parts = call(
         project_kernel,
         [shape((ROWS + 48, 2 * COLS), bf16) for _ in range(NX)],
-        (place, frames_z, quarter_gain, gain_rows, weights),
+        (place, after(frames_z, act_parts), quarter_gain, gain_rows, weights),
         smem=(0,),
+        near=(1,),
+        cuts={4: IN},
         scratch=[pltpu.VMEM((ROWS, QUARTER), bf16)],
     )
     pre_moved = [pre_parts[0]] + [shifted(pre_parts[j], "x", NX, j) for j in range(1, NX)]
-    held = lax.optimization_barrier((grads, pre_parts[0]))[0]
-    act_parts = call(
-        act_kernel, shape((NZ, ROWS, COLS), bf16), (place, *held, weights), smem=(0,)
-    )
-    act_grad = call(sum_kernel, shape((ROWS, COLS), bf16), (exchange(act_parts, "z"),))
     pre, gated, unit, stat = call(
         gate_kernel,
         [
@@ -448,37 +487,23 @@
             shape((ROWS, 128), f32),
         ],
         tuple(pre_moved),
-    )
-    gated_low, gated_high = neighbours(gated, EDGE)
-    act_low, act_high = neighbours(act_grad, 16)
-    activated, slope = call(
-        forward_kernel,
-        [shape((ROWS, COLS), bf16), shape((ROWS + 32, COLS), f32)],
-        (border, gated, gated_low, gated_high, taps),
+        near=(1, 2, 3),
+    )
+    act_grad = call(sum_kernel, shape((ROWS, COLS), bf16), (act_moved,), near=(0,))
+    low, high = neighbours(
+        jnp.concatenate([gated[-EDGE:], act_grad[-16:]], axis=0),
+        jnp.concatenate([gated[:EDGE], act_grad[:16]], axis=0),
+    )
+    activated, message, small = call(
+        conv_kernel,
+        [
+            shape((ROWS, COLS), bf16),
+            shape((ROWS + 32, 2 * COLS), bf16),
+            shape((K + 1, COLS), f32),
+        ],
+        (border, gated, act_grad, low, high, packed, pre, unit),
         smem=(0,),
-        scratch=[
-            pltpu.VMEM((ROWS + 2 * EDGE, COLS), f32),
-            pltpu.VMEM((160, COLS), f32),
-        ],
-    )
-    act_z = gathered(activated, "z", NZ)
-    message, small = call(
-        backward_kernel,
-        [shape((ROWS + 32, 2 * COLS), bf16), shape((K + 1, COLS), f32)],
-        (
-            border,
-            gated,
-            gated_low,
-            gated_high,
-            act_grad,
-            act_low,
-            act_high,
-            slope,
-            taps,
-            pre,
-            unit,
-        ),
-        smem=(0,),
+        near=(3, 4),
         scratch=[
             pltpu.VMEM((ROWS + 2 * EDGE, COLS), f32),
             pltpu.VMEM((ROWS + 32, COLS), f32),
@@ -486,15 +511,19 @@
             pltpu.VMEM((K + 1, 8, COLS), f32),
             pltpu.VMEM((160, COLS), f32),
             pltpu.VMEM((160, COLS), f32),
+            pltpu.VMEM((K + 1, COLS), f32),
         ],
     )
+    act_z = gathered(activated, "z", NZ)
 
     vg_grads = spread(message, "x", NX)
     norm_parts = call(
         norm_kernel,
         shape((NZ, ROWS + 48, COLS), bf16),
-        (place, *vg_grads, weights),
+        (place, *vg_grads, after(weights, act_z)),
         smem=(0,),
+        near=(2, 3, 4),
+        cuts={5: IN},
     )
     norm_moved = exchange(norm_parts, "z")
     held = lax.optimization_barrier((vg_grads, norm_parts))[0]
@@ -503,6 +532,7 @@
         shape((NY * QUARTER, 2 * COLS), bf16),
         (place, frames_z, quarter_gain, stat, *held),
         smem=(0,),
+        near=(5, 6, 7),
         scratch=[pltpu.VMEM((ROWS, QUARTER), bf16)],
     )
     in_weight = lax.psum_scatter(
@@ -513,8 +543,10 @@
         out_kernel,
         [shape((ROWS, COLS), bf16) for _ in range(NX)]
         + [shape((NY, QUARTER // NK, COLS), bf16) for _ in range(2)],
-        (place, after(act_z, norm_parts), *grads, weights),
+        (place, act_z, *after(grads, norm_parts), weights),
         smem=(0,),
+        near=(1,),
+        cuts={6: OUT},
         scratch=[
             pltpu.VMEM((NK, ROWS, QUARTER // NK), bf16),
             pltpu.VMEM((ROWS, NY * COLS), bf16),
@@ -535,6 +567,7 @@
         input_kernel,
         [shape((ROWS, COLS), bf16), shape((8, COLS), f32)],
         (norm_moved, frames, grad_out, stat, local_gain),
+        near=(0,),
     )
     input_grad = swap_xy(input_grad)
 
@@ -546,7 +579,7 @@
             (a * NY + b, ((b + shift) % NX) * NY + a) for a in range(NX) for b in range(NY)
         ]
         arrived.append(lax.ppermute(small, ("x", "y"), route))
-    small = sum(arrived)
+    small, input_grad = lax.optimization_barrier((sum(arrived), input_grad))
     return (
         encoded,
         input_grad,

time: 230 us -> 204 us (0.89)
  blocking collectives: 29.9 us -> 0 us
  local copies, waits for them, and re-layouts: 31 us -> 11.2 us
  waiting for transfers between devices: 45.4 us -> 64.2 us
  Pallas kernels: 19.4 us -> 32.8 us
  starting transfers between devices: 79.1 us -> 73.8 us
    all_to_all x1 -> x0, blocking collectives: 29.9 us -> none  [exchange(): return lax.all_to_all(parts, axis, 0, 0, tiled=True)]
    unnamed x73 -> x27, local copies, waits for them, and re-layouts: 24.6 us -> 1.33 us
    all_to_all x3 -> x4, waiting for transfers between devices: 5.71 us -> 20.4 us  [exchange(): return lax.all_to_all(parts, axis, 0, 0, tiled=True)]
    pallas_call x10 -> x9, Pallas kernels: 19.4 us -> 32.8 us  [call(): pl.pallas_call(whole, out_shape=[pltpu.HBM(out.shape, out.dtype) for out...]
    ppermute x5 -> x4, starting transfers between devices: 28.9 us -> 18.1 us  [swap_xy(): lax.ppermute(block, ('x', 'y'), [(a * NY + b, b * NY + a) for a in range(...]
    all_to_all x3 -> x4, starting transfers between devices: 16.9 us -> 26.5 us  [exchange(): return lax.all_to_all(parts, axis, 0, 0, tiled=True)]
    ppermute x4 -> x2, starting transfers between devices: 8.6 us -> 4.31 us  [the longest x1 3.03 us: neighbours(): low = lax.ppermute(upper, ('k', 'y'), forward)]
    ppermute x5 -> x4, waiting for transfers between devices: 17.7 us -> 21 us  [swap_xy(): lax.ppermute(block, ('x', 'y'), [(a * NY + b, b * NY + a) for a in range(...]
  transfers between devices with their start and end apart: 35 -> 33, of which waited for: 14 -> 16; matrix products, arithmetic and copies ran while one was open for 5% -> 5% of each run, Pallas kernels for 5% -> 9%
where the time goes in v5:
time: 204 us; the launch traced here: 203 us
  starting transfers between devices  73.8 us (36%)
  waiting for transfers between devices  64.2 us (31%)
  Pallas kernels  32.8 us (16%)
  between operations  14.5 us (7%)
  local copies, waits for them, and re-layouts  11.2 us (5%)
  other arithmetic  6.46 us (3%)
    pallas_call x9, Pallas kernels, call(): pl.pallas_call(whole, out_shape=[pltpu.HBM(out.shape, out.dtype) for out...  32.8 us
    all_to_all x4, starting transfers between devices, exchange(): return lax.all_to_all(parts, axis, 0, 0, tiled=True)  26.5 us
    ppermute x4, waiting for transfers between devices, swap_xy(): lax.ppermute(block, ('x', 'y'), [(a * NY + b, b * NY + a) for a in range(...  21 us
    ppermute x15, waiting for transfers between devices, shifted(): lax.ppermute(block, axis, [(i, (i + shift) % count) for i in range(count)])  20.8 us
    all_to_all x4, waiting for transfers between devices, exchange(): return lax.all_to_all(parts, axis, 0, 0, tiled=True)  20.4 us
    ppermute x4, starting transfers between devices, swap_xy(): lax.ppermute(block, ('x', 'y'), [(a * NY + b, b * NY + a) for a in range(...  18.1 us
    ppermute x15, starting transfers between devices, shifted(): lax.ppermute(block, axis, [(i, (i + shift) % count) for i in range(count)])  15.3 us
    ppermute x4, starting transfers between devices, shards(): arrived.append(lax.ppermute(small, ('x', 'y'), route))  9.47 us
  transfers between devices with their start and end apart: 33, of which 16 were waited for; matrix products, arithmetic and copies ran while one was open for 5% of the time, Pallas kernels for 9%

profile of v5, /device:TPU:6, one launch (start us, length us, event | category | flops | bytes accessed | tf_op | source)
XLA Modules:
  0.0 202.9 jit_solution(10663291899596352979)
XLA Ops:
  9.1 4.8 %collective-permute-start = (bf16[384,128]{1,0:T(8,128)(2,1)}, bf16[384,128]{1,0:T(8,128)(2,1)S(1)}, u32[]{:S(2)}, u32[]{:S(2)}) collective-permute-start(bf16[384,128]{1,0:T(8,128)(2,1)} %param.8), channel_id=1, source_target_pairs={{0,0},{8,64},{16,128},{24,192},{64,8},{72,72},{80,136},{88,200},{1... | collective-permute-start | bytes 294920 | tf_op jit(solution)/shard_map/ppermute | solution.py:395
  14.0 7.3 %collective-permute-done.refs_1_ = bf16[384,128]{1,0:T(8,128)(2,1)S(1)} collective-permute-done((bf16[384,128]{1,0:T(8,128)(2,1)}, bf16[384,128]{1,0:T(8,128)(2,1)S(1)}, u32[]{:S(2)}, u32[]{:S(2)}) %collective-permute-start) | collective-permute-done | bytes 98336 | tf_op jit(solution)/shard_map/ppermute | solution.py:395
  22.3 8.5 %all-to-all-start = ((bf16[8,384,128]{2,1,0:T(8,128)(2,1)}), bf16[8,384,128]{2,1,0:T(8,128)(2,1)S(1)}, u32[]{:S(2)}, u32[]{:S(2)}) async-start(bf16[8,384,128]{2,1,0:T(8,128)(2,1)} %broadcast_in_dim.8), calls=%async_computation | async-start | bytes 1572864 | tf_op jit(solution)/shard_map/all_to_all | solution.py:410
  30.8 4.8 %collective-permute-start.1 = (bf16[480,128]{1,0:T(8,128)(2,1)S(1)}, bf16[480,128]{1,0:T(8,128)(2,1)S(1)}, u32[]{:S(2)}, u32[]{:S(2)}) collective-permute-start(bf16[480,128]{1,0:T(8,128)(2,1)S(1)} %pad_maximum_fusion.1), channel_id=1, source_target_pairs={{0,0},{8,64},{16,128},{24,192},{64,8},{72,72},{80,136},{88,200},{1... | collective-permute-start | bytes 368648 | tf_op jit(solution)/shard_map/ppermute | solution.py:395
  35.6 6.6 %collective-permute-done.1.refs_5_ = bf16[480,128]{1,0:T(8,128)(2,1)S(1)} collective-permute-done((bf16[480,128]{1,0:T(8,128)(2,1)S(1)}, bf16[480,128]{1,0:T(8,128)(2,1)S(1)}, u32[]{:S(2)}, u32[]{:S(2)}) %collective-permute-start.1) | collective-permute-done | bytes 122912 | tf_op jit(solution)/shard_map/ppermute | solution.py:395
  42.3 2.3 %collective-permute-start.3 = (bf16[384,128]{1,0:T(8,128)(2,1)S(1)}, bf16[384,128]{1,0:T(8,128)(2,1)S(1)}, u32[]{:S(2)}, u32[]{:S(2)}) collective-permute-start(bf16[384,128]{1,0:T(8,128)(2,1)S(1)} %slice.72.refs_1_.refs_2_), channel_id=1, source_target_pairs={{0,128},{64,192},{128,0},{192,64},{1,129},{65,193},{129,1},{193,65... | collective-permute-start | bytes 294920 | tf_op jit(solution)/shard_map/ppermute | solution.py:418
  44.8 2.2 %collective-permute-done.2.refs_2_.refs_3_ = bf16[384,128]{1,0:T(8,128)(2,1)S(1)} collective-permute-done((bf16[384,128]{1,0:T(8,128)(2,1)S(1)}, bf16[384,128]{1,0:T(8,128)(2,1)S(1)}, u32[]{:S(2)}, u32[]{:S(2)}) %collective-permute-start.2) | collective-permute-done | bytes 98336 | tf_op jit(solution)/shard_map/ppermute | solution.py:418
  48.6 1.9 collective-permute-done.4.refs_4_.refs_5_
  50.5 3.7 %act_kernel.1 = bf16[8,384,128]{2,1,0:T(8,128)(2,1)} custom-call(s32[14]{0:T(128)S(1)} %concatenate.49.refs_0_, bf16[384,128]{1,0:T(8,128)(2,1)S(1)} %slice.72.refs_1_.refs_2_, bf16[384,128]{1,0:T(8,128)(2,1)S(1)} %collective-permute-done.2.refs_2_.refs_3_, bf16[384,128]{1,0:T(8,128)(2,1)S(1)} %collective-permute-done.3.refs_3_.refs_4_, ...), custom_call_target="tpu_custom_call" | custom-call | tf_op jit(solution)/shard_map/act_kernel/pallas_call | solution.py:119
  54.2 7.2 %all-to-all-start.1 = ((bf16[8,384,128]{2,1,0:T(8,128)(2,1)}), bf16[8,384,128]{2,1,0:T(8,128)(2,1)S(1)}, u32[]{:S(2)}, u32[]{:S(2)}) async-start(bf16[8,384,128]{2,1,0:T(8,128)(2,1)} %act_kernel.1), calls=%async_computation.1 | async-start | bytes 1572864 | tf_op jit(solution)/shard_map/all_to_all | solution.py:410
  62.8 5.1 %project_kernel.1 = (bf16[432,256]{1,0:T(8,128)(2,1)}, bf16[432,256]{1,0:T(8,128)(2,1)}, bf16[432,256]{1,0:T(8,128)(2,1)}, bf16[432,256]{1,0:T(8,128)(2,1)}) custom-call(s32[14]{0:T(128)S(1)} %concatenate.49.refs_0_, bf16[8,384,128]{2,1,0:T(8,128)(2,1)S(1)} %all-to-all-done.refs_1_, f32[1,1024]{1,0:T(1,128)} %bitcast.27, bf16[16,1024]{1,0:T(8,128)(2,1)} %pad.4.refs_3_, ...), custom_call_target="tpu_custom_call" | custom-call | tf_op jit(solution)/shard_map/project_kernel/pallas_call | solution.py:119
  70.6 3.6 %collective-permute-done.5.refs_1_ = bf16[432,256]{1,0:T(8,128)(2,1)S(1)} collective-permute-done((bf16[432,256]{1,0:T(8,128)(2,1)}, bf16[432,256]{1,0:T(8,128)(2,1)S(1)}, u32[]{:S(2)}, u32[]{:S(2)}) %collective-permute-start.5) | collective-permute-done | bytes 221216 | tf_op jit(solution)/shard_map/ppermute | solution.py:418
  74.2 2.8 %collective-permute-done.6.refs_2_ = bf16[432,256]{1,0:T(8,128)(2,1)S(1)} collective-permute-done((bf16[432,256]{1,0:T(8,128)(2,1)}, bf16[432,256]{1,0:T(8,128)(2,1)S(1)}, u32[]{:S(2)}, u32[]{:S(2)}) %collective-permute-start.6) | collective-permute-done | bytes 221216 | tf_op jit(solution)/shard_map/ppermute | solution.py:418
  77.0 2.3 %collective-permute-done.7.refs_3_ = bf16[432,256]{1,0:T(8,128)(2,1)S(1)} collective-permute-done((bf16[432,256]{1,0:T(8,128)(2,1)}, bf16[432,256]{1,0:T(8,128)(2,1)S(1)}, u32[]{:S(2)}, u32[]{:S(2)}) %collective-permute-start.7) | collective-permute-done | bytes 221216 | tf_op jit(solution)/shard_map/ppermute | solution.py:418
  79.2 3.0 %gate_kernel.1 = (f32[384,256]{1,0:T(8,128)}, bf16[384,128]{1,0:T(8,128)(2,1)}, f32[8,256]{1,0:T(8,128)}, f32[384,128]{1,0:T(8,128)}) custom-call(bf16[432,256]{1,0:T(8,128)(2,1)} %get-tuple-element.42.refs_0_, bf16[432,256]{1,0:T(8,128)(2,1)S(1)} %collective-permute-done.5.refs_1_, bf16[432,256]{1,0:T(8,128)(2,1)S(1)} %collective-permute-done.6.refs_2_, ...), custom_call_target="tpu_custom_call" | custom-call | tf_op jit(solution)/shard_map/gate_kernel/pallas_call | solution.py:119
  85.7 3.0 %collective-permute-start.8 = (bf16[48,128]{1,0:T(8,128)(2,1)S(1)}, bf16[48,128]{1,0:T(8,128)(2,1)S(1)}, u32[]{:S(2)}, u32[]{:S(2)}) collective-permute-start(bf16[48,128]{1,0:T(8,128)(2,1)S(1)} %pad_maximum_fusion.4), channel_id=1, source_target_pairs={{0,32},{32,8},{8,40},{40,16},{16,48},{48,24},{24,56},{1,33},{33,9}... | collective-permute-start | bytes 36872 | tf_op jit(solution)/shard_map/ppermute | solution.py:404
  89.6 4.0 %conv_kernel.1 = (bf16[384,128]{1,0:T(8,128)(2,1)}, bf16[416,256]{1,0:T(8,128)(2,1)}, f32[32,128]{1,0:T(8,128)}) custom-call(s32[1]{0:T(128)} %bitcast.refs_0_, bf16[384,128]{1,0:T(8,128)(2,1)} %get-tuple-element.46.refs_1_, bf16[384,128]{1,0:T(8,128)(2,1)} %sum_kernel.1.refs_2_, bf16[48,128]{1,0:T(8,128)(2,1)S(1)} %collective-permute-done.8.refs_3_, ...), custom_call_target="tpu_custom_call" | custom-call | tf_op jit(solution)/shard_map/conv_kernel/pallas_call | solution.py:119
  95.5 7.2 %all-to-all-start.2 = ((bf16[8,384,128]{2,1,0:T(8,128)(2,1)}), bf16[8,384,128]{2,1,0:T(8,128)(2,1)S(1)}, u32[]{:S(2)}, u32[]{:S(2)}) async-start(bf16[8,384,128]{2,1,0:T(8,128)(2,1)} %broadcast_in_dim.10), calls=%async_computation.2 | async-start | bytes 1572864 | tf_op jit(solution)/shard_map/all_to_all | solution.py:410
  103.6 2.0 collective-permute-start.11
  105.9 20.4 %all-to-all-done.2.refs_1_ = bf16[8,384,128]{2,1,0:T(8,128)(2,1)S(1)} async-done(((bf16[8,384,128]{2,1,0:T(8,128)(2,1)}), bf16[8,384,128]{2,1,0:T(8,128)(2,1)S(1)}, u32[]{:S(2)}, u32[]{:S(2)}) %all-to-all-start.2) | async-done | bytes 786464 | tf_op jit(solution)/shard_map/all_to_all | solution.py:410
  126.4 4.2 %norm_kernel.1 = bf16[8,432,128]{2,1,0:T(8,128)(2,1)} custom-call(s32[14]{0:T(128)S(1)} %concatenate.49.refs_0_, bf16[416,256]{1,0:T(8,128)(2,1)} %get-tuple-element.65.refs_1_.refs_4_, bf16[416,256]{1,0:T(8,128)(2,1)S(1)} %collective-permute-done.10.refs_2_.refs_5_, bf16[416,256]{1,0:T(8,128)(2,1)S(1)} %collective-permute-done.11.refs_3_.refs_6_, ...), custom_call_target="tpu_custom_call" | custom-call | tf_op jit(solution)/shard_map/norm_kernel/pallas_call | solution.py:119
  130.6 4.9 %weight_kernel.1 = bf16[4096,256]{1,0:T(8,128)(2,1)} custom-call(s32[14]{0:T(128)S(1)} %concatenate.49.refs_0_, bf16[8,384,128]{2,1,0:T(8,128)(2,1)} %copy-done, f32[1,1024]{1,0:T(1,128)} %bitcast.28, f32[384,128]{1,0:T(8,128)} %get-tuple-element.61.refs_3_, bf16[416,256]{1,0:T(8,128)(2,1)} %get-tuple-element.65.refs_1_.refs_4_, ...), custom_call_target="tpu_custom_call" | custom-call | tf_op jit(solution)/shard_map/weight_kernel/pallas_call | solution.py:119
  135.5 3.6 %all-to-all-start.3 = ((bf16[8,432,128]{2,1,0:T(8,128)(2,1)}), bf16[8,432,128]{2,1,0:T(8,128)(2,1)S(1)}, u32[]{:S(2)}, u32[]{:S(2)}) async-start(bf16[8,432,128]{2,1,0:T(8,128)(2,1)} %norm_kernel.1), calls=%async_computation.3 | async-start | bytes 1769472 | tf_op jit(solution)/shard_map/all_to_all | solution.py:410
  139.1 4.9 %out_kernel.1 = (bf16[384,128]{1,0:T(8,128)(2,1)}, bf16[384,128]{1,0:T(8,128)(2,1)}, bf16[384,128]{1,0:T(8,128)(2,1)}, bf16[384,128]{1,0:T(8,128)(2,1)}, bf16[4,...) custom-call(s32[14]{0:T(128)S(1)} %concatenate.49.refs_0_, bf16[8,384,128]{2,1,0:T(8,128)(2,1)S(1)} %all-to-all-done.2.refs_1_, ...), custom_call_target="tpu_custom_call" | custom-call | tf_op jit(solution)/shard_map/out_kernel/pallas_call | solution.py:119
  148.3 2.9 %collective-permute-done.13 = bf16[384,128]{1,0:T(8,128)(2,1)S(1)} collective-permute-done((bf16[384,128]{1,0:T(8,128)(2,1)}, bf16[384,128]{1,0:T(8,128)(2,1)S(1)}, u32[]{:S(2)}, u32[]{:S(2)}) %collective-permute-start.13) | collective-permute-done | bytes 98336 | tf_op jit(solution)/shard_map/ppermute | solution.py:418
  155.8 4.3 %collective-permute-start.16 = (bf16[384,128]{1,0:T(8,128)(2,1)S(1)}, bf16[384,128]{1,0:T(8,128)(2,1)S(1)}, u32[]{:S(2)}, u32[]{:S(2)}) collective-permute-start(bf16[384,128]{1,0:T(8,128)(2,1)S(1)} %add_convert_fusion.3), channel_id=1, source_target_pairs={{0,0},{8,64},{16,128},{24,192},{64,8},{72,72},{80,136},{88,200},{1... | collective-permute-start | bytes 294920 | tf_op jit(solution)/shard_map/ppermute | solution.py:395
  162.7 2.8 %collective-permute-start.26 = (bf16[512,128]{1,0:T(8,128)(2,1)S(1)}, bf16[512,128]{1,0:T(8,128)(2,1)S(1)}, u32[]{:S(2)}, u32[]{:S(2)}) collective-permute-start(bf16[512,128]{1,0:T(8,128)(2,1)S(1)} %get-tuple-element.75), channel_id=1, source_target_pairs={{0,24},{8,0},{16,8},{24,16},{1,25},{9,1},{17,9},{25,17},{2,26},{10... | collective-permute-start | bytes 393224 | tf_op jit(solution)/shard_map/ppermute | solution.py:418
  165.4 2.2 %input_kernel.1 = (bf16[384,128]{1,0:T(8,128)(2,1)}, f32[8,128]{1,0:T(8,128)}) custom-call(bf16[8,432,128]{2,1,0:T(8,128)(2,1)S(1)} %all-to-all-done.3.refs_0_, bf16[384,128]{1,0:T(8,128)(2,1)} %copy-done.5, bf16[384,128]{1,0:T(8,128)(2,1)} %copy-done.1, f32[384,128]{1,0:T(8,128)} %get-tuple-element.61.refs_3_, f32[1,128]{1,0:T(1,128)} %dynamic-slice_bitcast_fusion.refs_4_), custom_call_target="tpu_custom_call" | custom-call | tf_op jit(solution)/shard_map/input_kernel/pallas_call | solution.py:119
  169.5 3.5 %collective-permute-start.18 = (f32[40,128]{1,0:T(8,128)S(1)}, f32[40,128]{1,0:T(8,128)S(1)}, u32[]{:S(2)}, u32[]{:S(2)}) collective-permute-start(f32[40,128]{1,0:T(8,128)S(1)} %add.121), channel_id=1, source_target_pairs={{0,0},{8,64},{16,128},{24,192},{64,8},{72,72},{80,136},{88,200},{1... | collective-permute-start | bytes 61448 | tf_op jit(solution)/shard_map/ppermute | solution.py:581
  173.1 3.7 %collective-permute-start.19 = (f32[40,128]{1,0:T(8,128)S(1)}, f32[40,128]{1,0:T(8,128)S(1)}, u32[]{:S(2)}, u32[]{:S(2)}) collective-permute-start(f32[40,128]{1,0:T(8,128)S(1)} %add.121), channel_id=1, source_target_pairs={{0,64},{8,128},{16,192},{24,0},{64,72},{72,136},{80,200},{88,8},{1... | collective-permute-start | bytes 61448 | tf_op jit(solution)/shard_map/ppermute | solution.py:581
  180.7 4.1 %collective-permute-start.22 = (bf16[384,128]{1,0:T(8,128)(2,1)}, bf16[384,128]{1,0:T(8,128)(2,1)S(1)}, u32[]{:S(2)}, u32[]{:S(2)}) collective-permute-start(bf16[384,128]{1,0:T(8,128)(2,1)} %get-tuple-element.63), channel_id=1, source_target_pairs={{0,0},{8,64},{16,128},{24,192},{64,8},{72,72},{80,136},{88,200},{1... | collective-permute-start | bytes 294920 | tf_op jit(solution)/shard_map/ppermute | solution.py:395
  184.9 7.0 %collective-permute-done.22 = bf16[384,128]{1,0:T(8,128)(2,1)S(1)} collective-permute-done((bf16[384,128]{1,0:T(8,128)(2,1)}, bf16[384,128]{1,0:T(8,128)(2,1)S(1)}, u32[]{:S(2)}, u32[]{:S(2)}) %collective-permute-start.22) | collective-permute-done | bytes 98336 | tf_op jit(solution)/shard_map/ppermute | solution.py:395
  (103 shorter events, 37.7 us)
Async XLA Ops:
  7.2 43.3 %all-gather.2.cloned.1.call-start = ((), (), s32[]{:S(2)}) async-start(), calls=%async_computation.5 | async-start | bytes 3538944 | tf_op jit(solution)/shard_map/all_gather | solution.py:455
  9.1 12.1 %collective-permute-start = (bf16[384,128]{1,0:T(8,128)(2,1)}, bf16[384,128]{1,0:T(8,128)(2,1)S(1)}, u32[]{:S(2)}, u32[]{:S(2)}) collective-permute-start(bf16[384,128]{1,0:T(8,128)(2,1)} %param.8), channel_id=1, source_target_pairs={{0,0},{8,64},{16,128},{24,192},{64,8},{72,72},{80,136},{88,200},{1... | collective-permute-start | bytes 294920 | tf_op jit(solution)/shard_map/ppermute | solution.py:395
  22.3 31.9 %all-to-all-start = ((bf16[8,384,128]{2,1,0:T(8,128)(2,1)}), bf16[8,384,128]{2,1,0:T(8,128)(2,1)S(1)}, u32[]{:S(2)}, u32[]{:S(2)}) async-start(bf16[8,384,128]{2,1,0:T(8,128)(2,1)} %broadcast_in_dim.8), calls=%async_computation | async-start | bytes 1572864 | tf_op jit(solution)/shard_map/all_to_all | solution.py:410
  30.8 11.4 %collective-permute-start.1 = (bf16[480,128]{1,0:T(8,128)(2,1)S(1)}, bf16[480,128]{1,0:T(8,128)(2,1)S(1)}, u32[]{:S(2)}, u32[]{:S(2)}) collective-permute-start(bf16[480,128]{1,0:T(8,128)(2,1)S(1)} %pad_maximum_fusion.1), channel_id=1, source_target_pairs={{0,0},{8,64},{16,128},{24,192},{64,8},{72,72},{80,136},{88,200},{1... | collective-permute-start | bytes 368648 | tf_op jit(solution)/shard_map/ppermute | solution.py:395
  42.3 4.7 %collective-permute-start.2 = (bf16[384,128]{1,0:T(8,128)(2,1)S(1)}, bf16[384,128]{1,0:T(8,128)(2,1)S(1)}, u32[]{:S(2)}, u32[]{:S(2)}) collective-permute-start(bf16[384,128]{1,0:T(8,128)(2,1)S(1)} %slice.72.refs_1_.refs_2_), channel_id=1, source_target_pairs={{0,64},{64,128},{128,192},{192,0},{1,65},{65,129},{129,193},{193,1... | collective-permute-start | bytes 294920 | tf_op jit(solution)/shard_map/ppermute | solution.py:418
  42.3 6.2 %collective-permute-start.3 = (bf16[384,128]{1,0:T(8,128)(2,1)S(1)}, bf16[384,128]{1,0:T(8,128)(2,1)S(1)}, u32[]{:S(2)}, u32[]{:S(2)}) collective-permute-start(bf16[384,128]{1,0:T(8,128)(2,1)S(1)} %slice.72.refs_1_.refs_2_), channel_id=1, source_target_pairs={{0,128},{64,192},{128,0},{192,64},{1,129},{65,193},{129,1},{193,65... | collective-permute-start | bytes 294920 | tf_op jit(solution)/shard_map/ppermute | solution.py:418
  44.7 5.8 %collective-permute-start.4 = (bf16[384,128]{1,0:T(8,128)(2,1)S(1)}, bf16[384,128]{1,0:T(8,128)(2,1)S(1)}, u32[]{:S(2)}, u32[]{:S(2)}) collective-permute-start(bf16[384,128]{1,0:T(8,128)(2,1)S(1)} %slice.72.refs_1_.refs_2_), channel_id=1, source_target_pairs={{0,192},{64,0},{128,64},{192,128},{1,193},{65,1},{129,65},{193,129... | collective-permute-start | bytes 294920 | tf_op jit(solution)/shard_map/ppermute | solution.py:418
  54.2 28.8 %all-to-all-start.1 = ((bf16[8,384,128]{2,1,0:T(8,128)(2,1)}), bf16[8,384,128]{2,1,0:T(8,128)(2,1)S(1)}, u32[]{:S(2)}, u32[]{:S(2)}) async-start(bf16[8,384,128]{2,1,0:T(8,128)(2,1)} %act_kernel.1), calls=%async_computation.1 | async-start | bytes 1572864 | tf_op jit(solution)/shard_map/all_to_all | solution.py:410
  68.0 6.2 %collective-permute-start.5 = (bf16[432,256]{1,0:T(8,128)(2,1)}, bf16[432,256]{1,0:T(8,128)(2,1)S(1)}, u32[]{:S(2)}, u32[]{:S(2)}) collective-permute-start(bf16[432,256]{1,0:T(8,128)(2,1)} %get-tuple-element.43), channel_id=1, source_target_pairs={{0,64},{64,128},{128,192},{192,0},{1,65},{65,129},{129,193},{193,1... | collective-permute-start | bytes 663560 | tf_op jit(solution)/shard_map/ppermute | solution.py:418
  69.2 7.8 %collective-permute-start.6 = (bf16[432,256]{1,0:T(8,128)(2,1)}, bf16[432,256]{1,0:T(8,128)(2,1)S(1)}, u32[]{:S(2)}, u32[]{:S(2)}) collective-permute-start(bf16[432,256]{1,0:T(8,128)(2,1)} %get-tuple-element.44), channel_id=1, source_target_pairs={{0,128},{64,192},{128,0},{192,64},{1,129},{65,193},{129,1},{193,65... | collective-permute-start | bytes 663560 | tf_op jit(solution)/shard_map/ppermute | solution.py:418
  70.2 9.1 %collective-permute-start.7 = (bf16[432,256]{1,0:T(8,128)(2,1)}, bf16[432,256]{1,0:T(8,128)(2,1)S(1)}, u32[]{:S(2)}, u32[]{:S(2)}) collective-permute-start(bf16[432,256]{1,0:T(8,128)(2,1)} %get-tuple-element.45), channel_id=1, source_target_pairs={{0,192},{64,0},{128,64},{192,128},{1,193},{65,1},{129,65},{193,129... | collective-permute-start | bytes 663560 | tf_op jit(solution)/shard_map/ppermute | solution.py:418
  84.4 4.3 %collective-permute-start.9 = (bf16[48,128]{1,0:T(8,128)(2,1)S(1)}, bf16[48,128]{1,0:T(8,128)(2,1)S(1)}, u32[]{:S(2)}, u32[]{:S(2)}) collective-permute-start(bf16[48,128]{1,0:T(8,128)(2,1)S(1)} %pad_maximum_fusion.5), channel_id=1, source_target_pairs={{32,0},{8,32},{40,8},{16,40},{48,16},{24,48},{56,24},{33,1},{9,33}... | collective-permute-start | bytes 36872 | tf_op jit(solution)/shard_map/ppermute | solution.py:405
  85.7 3.9 %collective-permute-start.8 = (bf16[48,128]{1,0:T(8,128)(2,1)S(1)}, bf16[48,128]{1,0:T(8,128)(2,1)S(1)}, u32[]{:S(2)}, u32[]{:S(2)}) collective-permute-start(bf16[48,128]{1,0:T(8,128)(2,1)S(1)} %pad_maximum_fusion.4), channel_id=1, source_target_pairs={{0,32},{32,8},{8,40},{40,16},{16,48},{48,24},{24,56},{1,33},{33,9}... | collective-permute-start | bytes 36872 | tf_op jit(solution)/shard_map/ppermute | solution.py:404
  95.5 30.9 %all-to-all-start.2 = ((bf16[8,384,128]{2,1,0:T(8,128)(2,1)}), bf16[8,384,128]{2,1,0:T(8,128)(2,1)S(1)}, u32[]{:S(2)}, u32[]{:S(2)}) async-start(bf16[8,384,128]{2,1,0:T(8,128)(2,1)} %broadcast_in_dim.10), calls=%async_computation.2 | async-start | bytes 1572864 | tf_op jit(solution)/shard_map/all_to_all | solution.py:410
  102.7 90.4 %reduce-scatter.2.cloned.1.call-start = ((), (), s32[]{:S(2)}) async-start(), calls=%async_computation.6 | async-start | bytes 2359296 | tf_op jit(solution)/shard_map/reduce_scatter | solution.py:538
  102.7 23.6 %collective-permute-start.10 = (bf16[416,256]{1,0:T(8,128)(2,1)}, bf16[416,256]{1,0:T(8,128)(2,1)S(1)}, u32[]{:S(2)}, u32[]{:S(2)}) collective-permute-start(bf16[416,256]{1,0:T(8,128)(2,1)} %get-tuple-element.65.refs_1_.refs_4_), channel_id=1, source_target_pairs={{0,64},{64,128},{128,192},{192,0},{1,65},{65,129},{129,193},{193,1... | collective-permute-start | bytes 638984 | tf_op jit(solution)/shard_map/ppermute | solution.py:418
  103.6 22.8 %collective-permute-start.11 = (bf16[416,256]{1,0:T(8,128)(2,1)}, bf16[416,256]{1,0:T(8,128)(2,1)S(1)}, u32[]{:S(2)}, u32[]{:S(2)}) collective-permute-start(bf16[416,256]{1,0:T(8,128)(2,1)} %get-tuple-element.65.refs_1_.refs_4_), channel_id=1, source_target_pairs={{0,128},{64,192},{128,0},{192,64},{1,129},{65,193},{129,1},{193,65... | collective-permute-start | bytes 638984 | tf_op jit(solution)/shard_map/ppermute | solution.py:418
  105.5 20.8 %collective-permute-start.12 = (bf16[416,256]{1,0:T(8,128)(2,1)}, bf16[416,256]{1,0:T(8,128)(2,1)S(1)}, u32[]{:S(2)}, u32[]{:S(2)}) collective-permute-start(bf16[416,256]{1,0:T(8,128)(2,1)} %get-tuple-element.65.refs_1_.refs_4_), channel_id=1, source_target_pairs={{0,192},{64,0},{128,64},{192,128},{1,193},{65,1},{129,65},{193,129... | collective-permute-start | bytes 638984 | tf_op jit(solution)/shard_map/ppermute | solution.py:418
  135.5 29.9 %all-to-all-start.3 = ((bf16[8,432,128]{2,1,0:T(8,128)(2,1)}), bf16[8,432,128]{2,1,0:T(8,128)(2,1)S(1)}, u32[]{:S(2)}, u32[]{:S(2)}) async-start(bf16[8,432,128]{2,1,0:T(8,128)(2,1)} %norm_kernel.1), calls=%async_computation.3 | async-start | bytes 1769472 | tf_op jit(solution)/shard_map/all_to_all | solution.py:410
  144.0 16.1 %collective-permute-start.23 = (bf16[4,512,128]{2,1,0:T(8,128)(2,1)}, bf16[4,512,128]{2,1,0:T(8,128)(2,1)S(1)}, u32[]{:S(2)}, u32[]{:S(2)}) collective-permute-start(bf16[4,512,128]{2,1,0:T(8,128)(2,1)} %get-tuple-element.71), channel_id=1, source_target_pairs={{0,32},{32,0},{1,33},{33,1},{2,34},{34,2},{3,35},{35,3},{4,36},{36... | collective-permute-start | bytes 1572872 | tf_op jit(solution)/shard_map/ppermute | solution.py:556
  145.4 5.8 %collective-permute-start.13 = (bf16[384,128]{1,0:T(8,128)(2,1)}, bf16[384,128]{1,0:T(8,128)(2,1)S(1)}, u32[]{:S(2)}, u32[]{:S(2)}) collective-permute-start(bf16[384,128]{1,0:T(8,128)(2,1)} %get-tuple-element.57), channel_id=1, source_target_pairs={{0,64},{64,128},{128,192},{192,0},{1,65},{65,129},{129,193},{193,1... | collective-permute-start | bytes 294920 | tf_op jit(solution)/shard_map/ppermute | solution.py:418
  146.1 7.0 %collective-permute-start.14 = (bf16[384,128]{1,0:T(8,128)(2,1)}, bf16[384,128]{1,0:T(8,128)(2,1)S(1)}, u32[]{:S(2)}, u32[]{:S(2)}) collective-permute-start(bf16[384,128]{1,0:T(8,128)(2,1)} %get-tuple-element.58), channel_id=1, source_target_pairs={{0,128},{64,192},{128,0},{192,64},{1,129},{65,193},{129,1},{193,65... | collective-permute-start | bytes 294920 | tf_op jit(solution)/shard_map/ppermute | solution.py:418
  148.0 6.8 %collective-permute-start.15 = (bf16[384,128]{1,0:T(8,128)(2,1)}, bf16[384,128]{1,0:T(8,128)(2,1)S(1)}, u32[]{:S(2)}, u32[]{:S(2)}) collective-permute-start(bf16[384,128]{1,0:T(8,128)(2,1)} %get-tuple-element.59), channel_id=1, source_target_pairs={{0,192},{64,0},{128,64},{192,128},{1,193},{65,1},{129,65},{193,129... | collective-permute-start | bytes 294920 | tf_op jit(solution)/shard_map/ppermute | solution.py:418
  155.8 12.7 %collective-permute-start.16 = (bf16[384,128]{1,0:T(8,128)(2,1)S(1)}, bf16[384,128]{1,0:T(8,128)(2,1)S(1)}, u32[]{:S(2)}, u32[]{:S(2)}) collective-permute-start(bf16[384,128]{1,0:T(8,128)(2,1)S(1)} %add_convert_fusion.3), channel_id=1, source_target_pairs={{0,0},{8,64},{16,128},{24,192},{64,8},{72,72},{80,136},{88,200},{1... | collective-permute-start | bytes 294920 | tf_op jit(solution)/shard_map/ppermute | solution.py:395
  161.3 15.5 %collective-permute-start.24 = (bf16[512,128]{1,0:T(8,128)(2,1)S(1)}, bf16[512,128]{1,0:T(8,128)(2,1)S(1)}, u32[]{:S(2)}, u32[]{:S(2)}) collective-permute-start(bf16[512,128]{1,0:T(8,128)(2,1)S(1)} %get-tuple-element.74), channel_id=1, source_target_pairs={{0,8},{8,16},{16,24},{24,0},{1,9},{9,17},{17,25},{25,1},{2,10},{10... | collective-permute-start | bytes 393224 | tf_op jit(solution)/shard_map/ppermute | solution.py:418
  162.7 15.6 %collective-permute-start.25 = (bf16[512,128]{1,0:T(8,128)(2,1)S(1)}, bf16[512,128]{1,0:T(8,128)(2,1)S(1)}, u32[]{:S(2)}, u32[]{:S(2)}) collective-permute-start(bf16[512,128]{1,0:T(8,128)(2,1)S(1)} %get-tuple-element.76), channel_id=1, source_target_pairs={{0,16},{8,24},{16,0},{24,8},{1,17},{9,25},{17,1},{25,9},{2,18},{10... | collective-permute-start | bytes 393224 | tf_op jit(solution)/shard_map/ppermute | solution.py:418
  162.7 16.4 %collective-permute-start.26 = (bf16[512,128]{1,0:T(8,128)(2,1)S(1)}, bf16[512,128]{1,0:T(8,128)(2,1)S(1)}, u32[]{:S(2)}, u32[]{:S(2)}) collective-permute-start(bf16[512,128]{1,0:T(8,128)(2,1)S(1)} %get-tuple-element.75), channel_id=1, source_target_pairs={{0,24},{8,0},{16,8},{24,16},{1,25},{9,1},{17,9},{25,17},{2,26},{10... | collective-permute-start | bytes 393224 | tf_op jit(solution)/shard_map/ppermute | solution.py:418
  169.5 15.3 %collective-permute-start.18 = (f32[40,128]{1,0:T(8,128)S(1)}, f32[40,128]{1,0:T(8,128)S(1)}, u32[]{:S(2)}, u32[]{:S(2)}) collective-permute-start(f32[40,128]{1,0:T(8,128)S(1)} %add.121), channel_id=1, source_target_pairs={{0,0},{8,64},{16,128},{24,192},{64,8},{72,72},{80,136},{88,200},{1... | collective-permute-start | bytes 61448 | tf_op jit(solution)/shard_map/ppermute | solution.py:581
  173.1 11.8 %collective-permute-start.19 = (f32[40,128]{1,0:T(8,128)S(1)}, f32[40,128]{1,0:T(8,128)S(1)}, u32[]{:S(2)}, u32[]{:S(2)}) collective-permute-start(f32[40,128]{1,0:T(8,128)S(1)} %add.121), channel_id=1, source_target_pairs={{0,64},{8,128},{16,192},{24,0},{64,72},{72,136},{80,200},{88,8},{1... | collective-permute-start | bytes 61448 | tf_op jit(solution)/shard_map/ppermute | solution.py:581
  176.8 8.1 %collective-permute-start.20 = (f32[40,128]{1,0:T(8,128)S(1)}, f32[40,128]{1,0:T(8,128)S(1)}, u32[]{:S(2)}, u32[]{:S(2)}) collective-permute-start(f32[40,128]{1,0:T(8,128)S(1)} %add.121), channel_id=1, source_target_pairs={{0,128},{8,192},{16,0},{24,64},{64,136},{72,200},{80,8},{88,72},{1... | collective-permute-start | bytes 61448 | tf_op jit(solution)/shard_map/ppermute | solution.py:581
  178.2 6.7 %collective-permute-start.21 = (f32[40,128]{1,0:T(8,128)S(1)}, f32[40,128]{1,0:T(8,128)S(1)}, u32[]{:S(2)}, u32[]{:S(2)}) collective-permute-start(f32[40,128]{1,0:T(8,128)S(1)} %add.121), channel_id=1, source_target_pairs={{0,192},{8,0},{16,64},{24,128},{64,200},{72,8},{80,72},{88,136},{1... | collective-permute-start | bytes 61448 | tf_op jit(solution)/shard_map/ppermute | solution.py:581
  180.7 11.2 %collective-permute-start.22 = (bf16[384,128]{1,0:T(8,128)(2,1)}, bf16[384,128]{1,0:T(8,128)(2,1)S(1)}, u32[]{:S(2)}, u32[]{:S(2)}) collective-permute-start(bf16[384,128]{1,0:T(8,128)(2,1)} %get-tuple-element.63), channel_id=1, source_target_pairs={{0,0},{8,64},{16,128},{24,192},{64,8},{72,72},{80,136},{88,200},{1... | collective-permute-start | bytes 294920 | tf_op jit(solution)/shard_map/ppermute | solution.py:395
  (13 other events, 356.4 us)
Sparse Core Ops, SparseCore 0:
  9.9 35.8 all-gather.1
  135.7 37.7 reduce-scatter.1

commit v6 on v5

--- a/solution.py
+++ b/solution.py
@@ -17,6 +17,7 @@
 QUARTER = COLS * NZ
 WIDTH = QUARTER * NX
 EDGE = 32
+GATHER_ROWS = 512
 IN = (0, 2 * COLS)
 OUT = (2 * COLS, COLS)
 
@@ -68,7 +69,7 @@
     return out
 
 
-def call(body, out_shape, args, smem=(), near=(), scratch=(), cuts=()):
+def call(body, out_shape, args, smem=(), near=(), late=(), scratch=(), cuts=()):
     cuts = dict(cuts)
     single = not isinstance(out_shape, (list, tuple))
     outs = [out_shape] if single else list(out_shape)
@@ -89,24 +90,35 @@
         results, refs = refs[: len(outs)], refs[len(outs) :]
         held, refs = refs[: len(buffers)], refs[len(buffers) :]
         sems, extra = refs[0], refs[1:]
-        copies = []
+        copies = {}
         for place, i in enumerate(moved):
             source = inputs[i]
             if i in cuts:
                 source = source.at[:, pl.ds(cuts[i][0], cuts[i][1])]
-            copies.append(pltpu.make_async_copy(source, held[place], sems.at[place]))
+            copies[i] = pltpu.make_async_copy(source, held[place], sems.at[place])
             inputs[i] = held[place]
-        for copy in copies:
+        for copy in copies.values():
             copy.start()
-        for copy in copies:
-            copy.wait()
-        body(*inputs, *held[len(moved) :], *extra)
-        copies = []
-        for place, result in enumerate(results, len(moved)):
-            copies.append(pltpu.make_async_copy(held[place], result, sems.at[place]))
-        for copy in copies:
+        for i, copy in copies.items():
+            if i not in late:
+                copy.wait()
+        sent = []
+
+        def send(j, part=None):
+            source, target = held[len(moved) + j], results[j]
+            if part is not None:
+                source, target = source.at[part], target.at[part]
+            copy = pltpu.make_async_copy(source, target, sems.at[len(moved) + len(sent)])
             copy.start()
-        for copy in copies:
+            sent.append((j, copy))
+
+        hooks = (lambda i: copies[i].wait(), send) if late else ()
+        body(*hooks, *inputs, *held[len(moved) :], *extra)
+        already = {j for j, _ in sent}
+        for j in range(len(outs)):
+            if j not in already:
+                send(j)
+        for _, copy in sent:
             copy.wait()
 
     hbm = pl.BlockSpec(memory_space=pltpu.MemorySpace.HBM)
@@ -121,7 +133,7 @@
         out_shape=[pltpu.HBM(out.shape, out.dtype) for out in outs],
         in_specs=[pl.BlockSpec(memory_space=space) for space in spaces],
         out_specs=[hbm] * len(outs),
-        scratch_shapes=buffers + [pltpu.SemaphoreType.DMA((len(buffers),))] + list(scratch),
+        scratch_shapes=buffers + [pltpu.SemaphoreType.DMA((len(moved) + max(len(outs), NZ),))] + list(scratch),
         compiler_params=pltpu.CompilerParams(vmem_limit_bytes=24 * 1024 * 1024),
         name=body.__name__,
     )(
@@ -137,7 +149,7 @@
     return jax.ShapeDtypeStruct(dims, kind)
 
 
-def project_kernel(place_ref, frames_ref, gain_ref, gain_rows_ref, weight_ref, *refs):
+def project_kernel(arrive, send, place_ref, frames_ref, gain_ref, gain_rows_ref, weight_ref, *refs):
     left_ref = refs[NX]
     total = jnp.zeros((ROWS, 1), f32)
     square = jnp.zeros((ROWS, 1), f32)
@@ -151,6 +163,7 @@
         scaled = (frames_ref[i].astype(f32) - mean) * gain_ref[0:1, cut]
         left_ref[:, cut] = scaled.astype(bf16)
     sums = columns_to_rows(total, square).astype(bf16)
+    arrive(4)
     for j, out_ref in enumerate(refs[:NX]):
         start = pl.multiple_of(place_ref[4 + j] * QUARTER, QUARTER)
         weight = weight_ref[pl.ds(start, QUARTER), :]
@@ -160,6 +173,7 @@
         out_ref[ROWS + 16 : ROWS + 32, :] = sums[:, 0:256]
         out_ref[ROWS + 32 : ROWS + 48, 0:128] = sums[:, 256:384]
         out_ref[ROWS + 32 : ROWS + 48, 128:256] = jnp.zeros((16, 128), bf16)
+        send(j)
 
 
 def gate_kernel(p0_ref, p1_ref, p2_ref, p3_ref, pre_ref, gated_ref, unit_ref, stat_ref):
@@ -266,6 +280,7 @@
                 product = grad * masked_ref[1 + tap : 1 + tap + count, :]
                 sums_ref[tap] += jnp.sum(product.reshape(count // 8, 8, COLS), axis=0)
             sums_ref[K] += jnp.sum(grad.reshape(count // 8, 8, COLS), axis=0)
+    activated_ref[ROWS:, :] = jnp.zeros((GATHER_ROWS - ROWS, COLS), bf16)
     small_ref[...] = jnp.sum(sums_ref[...], axis=1)
 
     for start, count in CHUNKS[1:4]:
@@ -298,13 +313,11 @@
     message_ref[ROWS + 16 : ROWS + 32, 128:256] = jnp.zeros((16, 128), bf16)
 
 
-def norm_kernel(place_ref, g0_ref, g1_ref, g2_ref, g3_ref, weight_ref, out_ref):
-    total = jnp.zeros((ROWS, QUARTER), f32)
+def norm_kernel(arrive, send, place_ref, g0_ref, g1_ref, g2_ref, g3_ref, weight_ref, out_ref):
     rows = jnp.zeros((16, ROWS), f32)
-    for j, grad_ref in enumerate((g0_ref, g1_ref, g2_ref, g3_ref)):
-        start = pl.multiple_of(place_ref[j] * QUARTER, QUARTER)
-        weight = weight_ref[pl.ds(start, QUARTER), :]
-        total = total + dot(grad_ref[0:ROWS, :], weight, 1, 1)
+    arrive(1)
+    grads = (g0_ref, g1_ref, g2_ref, g3_ref)
+    for grad_ref in grads:
         here = jnp.concatenate(
             [grad_ref[ROWS : ROWS + 16, :], grad_ref[ROWS + 16 : ROWS + 32, 0:128]], axis=1
         )
@@ -312,10 +325,20 @@
     first = rows[0:1] + rows[1:2] + rows[2:3]
     second = rows[3:4] + rows[4:5] + rows[5:6]
     sums = stacked_rows(split3(first) + split3(second)).astype(bf16)
-    for i in range(NZ):
-        out_ref[i, 0:ROWS, :] = total[:, i * COLS : (i + 1) * COLS].astype(bf16)
-        for j in range(3):
-            out_ref[i, ROWS + 16 * j : ROWS + 16 * j + 16, :] = sums[:, j * 128 : (j + 1) * 128]
+    arrive(5)
+    step = 2 * COLS
+    for part in range(QUARTER // step):
+        total = jnp.zeros((ROWS, step), f32)
+        for j, grad_ref in enumerate(grads):
+            start = pl.multiple_of(place_ref[j] * QUARTER + part * step, step)
+            total = total + dot(grad_ref[0:ROWS, :], weight_ref[pl.ds(start, step), :], 1, 1)
+        for i in (2 * part, 2 * part + 1):
+            cut = (i - 2 * part) * COLS
+            out_ref[i, 0:ROWS, :] = total[:, cut : cut + COLS].astype(bf16)
+            for j in range(3):
+                rows_here = sums[:, j * 128 : (j + 1) * 128]
+                out_ref[i, ROWS + 16 * j : ROWS + 16 * j + 16, :] = rows_here
+            send(0, i)
 
 
 def weight_kernel(
@@ -327,19 +350,34 @@
     g1_ref,
     g2_ref,
     g3_ref,
-    out_ref,
+    kept_ref,
+    given_ref,
     left_ref,
+    right_ref,
 ):
     mean = stat_ref[:, 0:1]
     inv_std = stat_ref[:, 1:2]
+    half = QUARTER // NK
     for i in range(NZ):
         cut = pl.ds(i * COLS, COLS)
         scaled = (frames_ref[i].astype(f32) - mean) * inv_std * gain_ref[0:1, cut]
-        left_ref[:, cut] = scaled.astype(bf16)
-    for j, grad_ref in enumerate((g0_ref, g1_ref, g2_ref, g3_ref)):
-        start = pl.multiple_of(place_ref[j] * QUARTER, QUARTER)
-        out = dot(left_ref[...], grad_ref[0:ROWS, :], 0, 0)
-        out_ref[pl.ds(start, QUARTER), :] = out.astype(bf16)
+        left_ref[i * COLS // half, :, pl.ds(i * COLS % half, COLS)] = scaled.astype(bf16)
+    order_blocks(place_ref, 10, (g0_ref, g1_ref, g2_ref, g3_ref), right_ref, 2 * COLS)
+    core = place_ref[9]
+    for out_ref, which in ((given_ref, 1 - core), (kept_ref, core)):
+        out = dot(left_ref[which], right_ref[...], 0, 0).astype(bf16)
+        for i in range(NY):
+            out_ref[i] = out[:, i * 2 * COLS : (i + 1) * 2 * COLS]
+
+
+def order_blocks(place_ref, base, sources, out_ref, lanes):
+    for i in range(NY):
+        source = place_ref[base + i]
+        for j, block_ref in enumerate(sources):
+
+            @pl.when(source == j)
+            def _(block_ref=block_ref, i=i):
+                out_ref[:, i * lanes : (i + 1) * lanes] = block_ref[0:ROWS, :]
 
 
 def out_kernel(place_ref, act_ref, g0_ref, g1_ref, g2_ref, g3_ref, weight_ref, *refs):
@@ -355,14 +393,7 @@
             weight = weight_ref[pl.ds(start, half), :]
             total = total + dot(left_ref[h], weight, 1, 0)
         enc_ref[...] = total.astype(bf16)
-    for i in range(NY):
-        source = place_ref[10 + i]
-        for j, right_ref in enumerate((g0_ref, g1_ref, g2_ref, g3_ref)):
-
-            @pl.when(source == j)
-            def _(right_ref=right_ref, i=i):
-                grad_ref[:, i * COLS : (i + 1) * COLS] = right_ref[...]
-
+    order_blocks(place_ref, 0, (g0_ref, g1_ref, g2_ref, g3_ref), grad_ref, COLS)
     core = place_ref[9]
     for out_ref, which in ((given_ref, 1 - core), (kept_ref, core)):
         out = dot(left_ref[which], grad_ref[...], 0, 0).astype(bf16)
@@ -422,6 +453,15 @@
     return [block] + [shifted(block, axis, count, j) for j in range(1, count)]
 
 
+def reduced(kept, given):
+    other = lax.ppermute(given, "k", [(0, 1), (1, 0)])
+    both = [(kept[i].astype(f32) + other[i].astype(f32)) for i in range(NY)]
+    total = both[0]
+    for i in range(1, NY):
+        total = total + shifted(both[i].astype(bf16), "y", NY, i).astype(f32)
+    return total
+
+
 def pieces(value):
     out = []
     for _ in range(3):
@@ -460,7 +500,7 @@
     frames_z = gathered(frames, "z", NZ)
     taps = jnp.concatenate([kernel, bias[None, :]], axis=0)
     packed = jnp.concatenate([grad_out, pieces(taps).reshape(3 * (K + 1), COLS)], axis=0)
-    packed = swap_xy(after(packed, frames))
+    packed = swap_xy(packed)
     grad_out = packed[:ROWS]
     grads = spread(grad_out, "x", NX)
 
@@ -474,6 +514,7 @@
         (place, after(frames_z, act_parts), quarter_gain, gain_rows, weights),
         smem=(0,),
         near=(1,),
+        late=(4,),
         cuts={4: IN},
         scratch=[pltpu.VMEM((ROWS, QUARTER), bf16)],
     )
@@ -497,7 +538,7 @@
     activated, message, small = call(
         conv_kernel,
         [
-            shape((ROWS, COLS), bf16),
+            shape((GATHER_ROWS, COLS), bf16),
             shape((ROWS + 32, 2 * COLS), bf16),
             shape((K + 1, COLS), f32),
         ],
@@ -514,30 +555,32 @@
             pltpu.VMEM((K + 1, COLS), f32),
         ],
     )
-    act_z = gathered(activated, "z", NZ)
+    act_z = lax.all_gather(activated, "z", axis=0, tiled=False)
 
     vg_grads = spread(message, "x", NX)
     norm_parts = call(
         norm_kernel,
         shape((NZ, ROWS + 48, COLS), bf16),
-        (place, *vg_grads, after(weights, act_z)),
+        (place, *vg_grads, weights),
         smem=(0,),
         near=(2, 3, 4),
+        late=(1, 5),
         cuts={5: IN},
     )
     norm_moved = exchange(norm_parts, "z")
     held = lax.optimization_barrier((vg_grads, norm_parts))[0]
-    weight_parts = call(
+    kept, given = call(
         weight_kernel,
-        shape((NY * QUARTER, 2 * COLS), bf16),
+        [shape((NY, QUARTER // NK, 2 * COLS), bf16) for _ in range(2)],
         (place, frames_z, quarter_gain, stat, *held),
         smem=(0,),
         near=(5, 6, 7),
-        scratch=[pltpu.VMEM((ROWS, QUARTER), bf16)],
-    )
-    in_weight = lax.psum_scatter(
-        weight_parts, TIME, scatter_dimension=0, tiled=True
-    ).astype(f32)
+        scratch=[
+            pltpu.VMEM((NK, ROWS, QUARTER // NK), bf16),
+            pltpu.VMEM((ROWS, NY * 2 * COLS), bf16),
+        ],
+    )
+    in_weight = reduced(kept, given)
 
     out_parts = call(
         out_kernel,
@@ -545,7 +588,6 @@
         + [shape((NY, QUARTER // NK, COLS), bf16) for _ in range(2)],
         (place, act_z, *after(grads, norm_parts), weights),
         smem=(0,),
-        near=(1,),
         cuts={6: OUT},
         scratch=[
             pltpu.VMEM((NK, ROWS, QUARTER // NK), bf16),
@@ -554,10 +596,10 @@
     )
     kept, given = out_parts[NX:]
     other = lax.ppermute(given, "k", [(0, 1), (1, 0)])
-    both = [(kept[i].astype(f32) + other[i].astype(f32)) for i in range(NY)]
-    grad_out_weight = both[0]
-    for i in range(1, NY):
-        grad_out_weight = grad_out_weight + shifted(both[i].astype(bf16), "y", NY, i).astype(f32)
+    both = (kept.astype(f32) + other.astype(f32)).astype(bf16)
+    grad_out_weight = lax.psum_scatter(
+        both.reshape(NY * QUARTER // NK, COLS), "y", scatter_dimension=0, tiled=True
+    ).astype(f32)
     enc_sum = out_parts[0].astype(f32)
     for j in range(1, NX):
         enc_sum = enc_sum + shifted(out_parts[j], "x", NX, j).astype(f32)
@@ -566,7 +608,7 @@
     input_grad, gain_term = call(
         input_kernel,
         [shape((ROWS, COLS), bf16), shape((8, COLS), f32)],
-        (norm_moved, frames, grad_out, stat, local_gain),
+        (after(norm_moved, *out_parts), frames, grad_out, stat, local_gain),
         near=(0,),
     )
     input_grad = swap_xy(input_grad)

time: 204 us -> 214 us (1.049); the launches traced: 203 us -> 210 us
  waiting for transfers between devices: 64.2 us -> 72.2 us
  local copies, waits for them, and re-layouts: 11.2 us -> 8.46 us
  other arithmetic: 6.46 us -> 8.7 us
    all_to_all x4 -> x3, waiting for transfers between devices: 20.4 us -> 0.01 us  [exchange(): return lax.all_to_all(parts, axis, 0, 0, tiled=True)]
    all_gather x0 -> x1, waiting for transfers between devices: none -> 15.4 us  [shards(): act_z = lax.all_gather(activated, 'z', axis=0, tiled=False)]
    ppermute x15, waiting for transfers between devices: 20.8 us -> 33 us  [shifted(): lax.ppermute(block, axis, [(i, (i + shift) % count) for i in range(count)])]
    all_to_all x4 -> x3, starting transfers between devices: 26.5 us -> 22.6 us  [exchange(): return lax.all_to_all(parts, axis, 0, 0, tiled=True)]
    convert_element_type x1 -> x3, other arithmetic: 1.15 us -> 4.74 us  [the longest x1 2.12 us: shards(): both = (kept.astype(f32) + other.astype(f32)).astype(bf16)]
    ppermute x15, starting transfers between devices: 15.3 us -> 18.3 us  [shifted(): lax.ppermute(block, axis, [(i, (i + shift) % count) for i in range(count)])]
  transfers between devices with their start and end apart: 33 -> 34, of which waited for: 16 -> 17; matrix products, arithmetic and copies ran while one was open for 5% -> 6% of each run, Pallas kernels for 9% -> 13%
where the time goes in v6:
time: 214 us; the launch traced here: 210 us
  starting transfers between devices  73.6 us (34%)
  waiting for transfers between devices  72.2 us (34%)
  Pallas kernels  33.1 us (15%)
  between operations  14.3 us (7%)
  other arithmetic  8.7 us (4%)
  local copies, waits for them, and re-layouts  8.46 us (4%)
    pallas_call x9, Pallas kernels, call(): pl.pallas_call(whole, out_shape=[pltpu.HBM(out.shape, out.dtype) for out...  33.1 us
    ppermute x15, waiting for transfers between devices, shifted(): lax.ppermute(block, axis, [(i, (i + shift) % count) for i in range(count)])  33 us
    ppermute x4, waiting for transfers between devices, swap_xy(): lax.ppermute(block, ('x', 'y'), [(a * NY + b, b * NY + a) for a in range(...  22.9 us
    all_to_all x3, starting transfers between devices, exchange(): return lax.all_to_all(parts, axis, 0, 0, tiled=True)  22.6 us
    ppermute x4, starting transfers between devices, swap_xy(): lax.ppermute(block, ('x', 'y'), [(a * NY + b, b * NY + a) for a in range(...  19.5 us
    ppermute x15, starting transfers between devices, shifted(): lax.ppermute(block, axis, [(i, (i + shift) % count) for i in range(count)])  18.3 us
    all_gather x1, waiting for transfers between devices, shards(): act_z = lax.all_gather(activated, 'z', axis=0, tiled=False)  15.4 us
    ppermute x4, starting transfers between devices, shards(): arrived.append(lax.ppermute(small, ('x', 'y'), route))  8.65 us
  transfers between devices with their start and end apart: 34, of which 17 were waited for; matrix products, arithmetic and copies ran while one was open for 6% of the time, Pallas kernels for 13%

profile of v6, /device:TPU:6, one launch (start us, length us, event | category | flops | bytes accessed | tf_op | source)
XLA Modules:
  0.0 210.3 jit_solution(6814084218984426999)
XLA Ops:
  9.1 4.8 %collective-permute-start = (bf16[384,128]{1,0:T(8,128)(2,1)}, bf16[384,128]{1,0:T(8,128)(2,1)S(1)}, u32[]{:S(2)}, u32[]{:S(2)}) collective-permute-start(bf16[384,128]{1,0:T(8,128)(2,1)} %param.8), channel_id=1, source_target_pairs={{0,0},{8,64},{16,128},{24,192},{64,8},{72,72},{80,136},{88,200},{1... | collective-permute-start | bytes 294920 | tf_op jit(solution)/shard_map/ppermute | solution.py:426
  14.0 7.3 %collective-permute-done.refs_1_ = bf16[384,128]{1,0:T(8,128)(2,1)S(1)} collective-permute-done((bf16[384,128]{1,0:T(8,128)(2,1)}, bf16[384,128]{1,0:T(8,128)(2,1)S(1)}, u32[]{:S(2)}, u32[]{:S(2)}) %collective-permute-start) | collective-permute-done | bytes 98336 | tf_op jit(solution)/shard_map/ppermute | solution.py:426
  22.3 8.5 %all-to-all-start = ((bf16[8,384,128]{2,1,0:T(8,128)(2,1)}), bf16[8,384,128]{2,1,0:T(8,128)(2,1)S(1)}, u32[]{:S(2)}, u32[]{:S(2)}) async-start(bf16[8,384,128]{2,1,0:T(8,128)(2,1)} %broadcast_in_dim.6), calls=%async_computation | async-start | bytes 1572864 | tf_op jit(solution)/shard_map/all_to_all | solution.py:441
  30.8 4.8 %collective-permute-start.1 = (bf16[480,128]{1,0:T(8,128)(2,1)S(1)}, bf16[480,128]{1,0:T(8,128)(2,1)S(1)}, u32[]{:S(2)}, u32[]{:S(2)}) collective-permute-start(bf16[480,128]{1,0:T(8,128)(2,1)S(1)} %pad_maximum_fusion.1), channel_id=1, source_target_pairs={{0,0},{8,64},{16,128},{24,192},{64,8},{72,72},{80,136},{88,200},{1... | collective-permute-start | bytes 368648 | tf_op jit(solution)/shard_map/ppermute | solution.py:426
  35.6 6.6 %collective-permute-done.1.refs_5_ = bf16[480,128]{1,0:T(8,128)(2,1)S(1)} collective-permute-done((bf16[480,128]{1,0:T(8,128)(2,1)S(1)}, bf16[480,128]{1,0:T(8,128)(2,1)S(1)}, u32[]{:S(2)}, u32[]{:S(2)}) %collective-permute-start.1) | collective-permute-done | bytes 122912 | tf_op jit(solution)/shard_map/ppermute | solution.py:426
  42.4 2.3 %collective-permute-start.3 = (bf16[384,128]{1,0:T(8,128)(2,1)S(1)}, bf16[384,128]{1,0:T(8,128)(2,1)S(1)}, u32[]{:S(2)}, u32[]{:S(2)}) collective-permute-start(bf16[384,128]{1,0:T(8,128)(2,1)S(1)} %slice.72.refs_1_.refs_2_), channel_id=1, source_target_pairs={{0,128},{64,192},{128,0},{192,64},{1,129},{65,193},{129,1},{193,65... | collective-permute-start | bytes 294920 | tf_op jit(solution)/shard_map/ppermute | solution.py:449
  50.5 3.7 %act_kernel.1 = bf16[8,384,128]{2,1,0:T(8,128)(2,1)} custom-call(s32[14]{0:T(128)S(1)} %concatenate.49.refs_0_, bf16[384,128]{1,0:T(8,128)(2,1)S(1)} %slice.72.refs_1_.refs_2_, bf16[384,128]{1,0:T(8,128)(2,1)S(1)} %collective-permute-done.2.refs_2_.refs_3_, bf16[384,128]{1,0:T(8,128)(2,1)S(1)} %collective-permute-done.3.refs_3_.refs_4_, ...), custom_call_target="tpu_custom_call" | custom-call | tf_op jit(solution)/shard_map/act_kernel/pallas_call | solution.py:131
  54.3 7.2 %all-to-all-start.1 = ((bf16[8,384,128]{2,1,0:T(8,128)(2,1)}), bf16[8,384,128]{2,1,0:T(8,128)(2,1)S(1)}, u32[]{:S(2)}, u32[]{:S(2)}) async-start(bf16[8,384,128]{2,1,0:T(8,128)(2,1)} %act_kernel.1), calls=%async_computation.1 | async-start | bytes 1572864 | tf_op jit(solution)/shard_map/all_to_all | solution.py:441
  62.9 4.7 %project_kernel.1 = (bf16[432,256]{1,0:T(8,128)(2,1)}, bf16[432,256]{1,0:T(8,128)(2,1)}, bf16[432,256]{1,0:T(8,128)(2,1)}, bf16[432,256]{1,0:T(8,128)(2,1)}) custom-call(s32[14]{0:T(128)S(1)} %concatenate.49.refs_0_, bf16[8,384,128]{2,1,0:T(8,128)(2,1)S(1)} %all-to-all-done.refs_1_, f32[1,1024]{1,0:T(1,128)} %bitcast.31, bf16[16,1024]{1,0:T(8,128)(2,1)} %pad.4.refs_3_, ...), custom_call_target="tpu_custom_call" | custom-call | tf_op jit(solution)/shard_map/project_kernel/pallas_call | solution.py:131
  70.3 3.6 %collective-permute-done.5.refs_1_ = bf16[432,256]{1,0:T(8,128)(2,1)S(1)} collective-permute-done((bf16[432,256]{1,0:T(8,128)(2,1)}, bf16[432,256]{1,0:T(8,128)(2,1)S(1)}, u32[]{:S(2)}, u32[]{:S(2)}) %collective-permute-start.5) | collective-permute-done | bytes 221216 | tf_op jit(solution)/shard_map/ppermute | solution.py:449
  73.9 2.8 %collective-permute-done.6.refs_2_ = bf16[432,256]{1,0:T(8,128)(2,1)S(1)} collective-permute-done((bf16[432,256]{1,0:T(8,128)(2,1)}, bf16[432,256]{1,0:T(8,128)(2,1)S(1)}, u32[]{:S(2)}, u32[]{:S(2)}) %collective-permute-start.6) | collective-permute-done | bytes 221216 | tf_op jit(solution)/shard_map/ppermute | solution.py:449
  76.7 2.3 %collective-permute-done.7.refs_3_ = bf16[432,256]{1,0:T(8,128)(2,1)S(1)} collective-permute-done((bf16[432,256]{1,0:T(8,128)(2,1)}, bf16[432,256]{1,0:T(8,128)(2,1)S(1)}, u32[]{:S(2)}, u32[]{:S(2)}) %collective-permute-start.7) | collective-permute-done | bytes 221216 | tf_op jit(solution)/shard_map/ppermute | solution.py:449
  78.9 3.0 %gate_kernel.1 = (f32[384,256]{1,0:T(8,128)}, bf16[384,128]{1,0:T(8,128)(2,1)}, f32[8,256]{1,0:T(8,128)}, f32[384,128]{1,0:T(8,128)}) custom-call(bf16[432,256]{1,0:T(8,128)(2,1)} %get-tuple-element.42.refs_0_, bf16[432,256]{1,0:T(8,128)(2,1)S(1)} %collective-permute-done.5.refs_1_, bf16[432,256]{1,0:T(8,128)(2,1)S(1)} %collective-permute-done.6.refs_2_, ...), custom_call_target="tpu_custom_call" | custom-call | tf_op jit(solution)/shard_map/gate_kernel/pallas_call | solution.py:131
  85.5 3.0 %collective-permute-start.8 = (bf16[48,128]{1,0:T(8,128)(2,1)S(1)}, bf16[48,128]{1,0:T(8,128)(2,1)S(1)}, u32[]{:S(2)}, u32[]{:S(2)}) collective-permute-start(bf16[48,128]{1,0:T(8,128)(2,1)S(1)} %pad_maximum_fusion.4), channel_id=1, source_target_pairs={{0,32},{32,8},{8,40},{40,16},{16,48},{48,24},{24,56},{1,33},{33,9}... | collective-permute-start | bytes 36872 | tf_op jit(solution)/shard_map/ppermute | solution.py:435
  89.4 4.0 %conv_kernel.1 = (bf16[512,128]{1,0:T(8,128)(2,1)}, bf16[416,256]{1,0:T(8,128)(2,1)}, f32[32,128]{1,0:T(8,128)}) custom-call(s32[1]{0:T(128)} %bitcast.refs_0_, bf16[384,128]{1,0:T(8,128)(2,1)} %get-tuple-element.46.refs_1_, bf16[384,128]{1,0:T(8,128)(2,1)} %sum_kernel.1.refs_2_, bf16[48,128]{1,0:T(8,128)(2,1)S(1)} %collective-permute-done.8.refs_3_, ...), custom_call_target="tpu_custom_call" | custom-call | tf_op jit(solution)/shard_map/conv_kernel/pallas_call | solution.py:131
  96.6 5.3 %collective-permute-done.10.refs_2_.refs_5_ = bf16[416,256]{1,0:T(8,128)(2,1)S(1)} collective-permute-done((bf16[416,256]{1,0:T(8,128)(2,1)}, bf16[416,256]{1,0:T(8,128)(2,1)S(1)}, u32[]{:S(2)}, u32[]{:S(2)}) %collective-permute-start.10) | collective-permute-done | bytes 213024 | tf_op jit(solution)/shard_map/ppermute | solution.py:449
  104.2 4.0 %collective-permute-done.12.refs_4_.refs_7_ = bf16[416,256]{1,0:T(8,128)(2,1)S(1)} collective-permute-done((bf16[416,256]{1,0:T(8,128)(2,1)}, bf16[416,256]{1,0:T(8,128)(2,1)S(1)}, u32[]{:S(2)}, u32[]{:S(2)}) %collective-permute-start.12) | collective-permute-done | bytes 213024 | tf_op jit(solution)/shard_map/ppermute | solution.py:449
  108.1 4.2 %norm_kernel.1 = bf16[8,432,128]{2,1,0:T(8,128)(2,1)} custom-call(s32[14]{0:T(128)S(1)} %concatenate.49.refs_0_, bf16[416,256]{1,0:T(8,128)(2,1)} %get-tuple-element.67.refs_1_.refs_4_, bf16[416,256]{1,0:T(8,128)(2,1)S(1)} %collective-permute-done.10.refs_2_.refs_5_, bf16[416,256]{1,0:T(8,128)(2,1)S(1)} %collective-permute-done.11.refs_3_.refs_6_, ...), custom_call_target="tpu_custom_call" | custom-call | tf_op jit(solution)/shard_map/norm_kernel/pallas_call | solution.py:131
  112.3 6.9 %all-to-all-start.2 = ((bf16[8,432,128]{2,1,0:T(8,128)(2,1)}), bf16[8,432,128]{2,1,0:T(8,128)(2,1)S(1)}, u32[]{:S(2)}, u32[]{:S(2)}) async-start(bf16[8,432,128]{2,1,0:T(8,128)(2,1)} %norm_kernel.1), calls=%async_computation.2 | async-start | bytes 1769472 | tf_op jit(solution)/shard_map/all_to_all | solution.py:441
  119.3 5.0 %weight_kernel.1 = (bf16[4,512,256]{2,1,0:T(8,128)(2,1)}, bf16[4,512,256]{2,1,0:T(8,128)(2,1)}) custom-call(s32[14]{0:T(128)S(1)} %concatenate.49.refs_0_, bf16[8,384,128]{2,1,0:T(8,128)(2,1)} %copy-done, f32[1,1024]{1,0:T(1,128)} %bitcast.32, f32[384,128]{1,0:T(8,128)} %get-tuple-element.63.refs_3_, bf16[416,256]{1,0:T(8,128)(2,1)} %get-tuple-element.67.refs_1_.refs_4_, ...), custom_call_target="tpu_custom_call" | custom-call | tf_op jit(solution)/shard_map/weight_kernel/pallas_call | solution.py:131
  124.4 15.4 %all-gather.6.cloned.1.call-done = bf16[4096,128]{1,0:T(8,128)(2,1)} async-done(((bf16[512,128]{1,0:T(8,128)(2,1)}), bf16[4096,128]{1,0:T(8,128)(2,1)}) %all-gather.6.cloned.1.call-update) | async-done | bytes 1048592 | tf_op jit(solution)/shard_map/all_gather | solution.py:558
  139.9 5.2 %out_kernel.1 = (bf16[384,128]{1,0:T(8,128)(2,1)}, bf16[384,128]{1,0:T(8,128)(2,1)}, bf16[384,128]{1,0:T(8,128)(2,1)}, bf16[384,128]{1,0:T(8,128)(2,1)}, bf16[4,...) custom-call(s32[14]{0:T(128)S(1)} %concatenate.49.refs_0_, bf16[8,512,128]{2,1,0:T(8,128)(2,1)} %bitcast.29, ...), custom_call_target="tpu_custom_call" | custom-call | tf_op jit(solution)/shard_map/out_kernel/pallas_call | solution.py:131
  148.9 4.0 %collective-permute-start.25 = (bf16[512,256]{1,0:T(8,128)(2,1)}, bf16[512,256]{1,0:T(8,128)(2,1)}, u32[]{:S(2)}, u32[]{:S(2)}) collective-permute-start(bf16[512,256]{1,0:T(8,128)(2,1)} %get-tuple-element.78), channel_id=1, source_target_pairs={{0,16},{8,24},{16,0},{24,8},{1,17},{9,25},{17,1},{25,9},{2,18},{10... | collective-permute-start | bytes 786440 | tf_op jit(solution)/shard_map/ppermute | solution.py:449
  153.1 2.3 %input_kernel.1 = (bf16[384,128]{1,0:T(8,128)(2,1)}, f32[8,128]{1,0:T(8,128)}) custom-call(bf16[8,432,128]{2,1,0:T(8,128)(2,1)S(1)} %all-to-all-done.2.refs_0_, bf16[384,128]{1,0:T(8,128)(2,1)} %copy-done.6, bf16[384,128]{1,0:T(8,128)(2,1)} %copy-done.1, f32[384,128]{1,0:T(8,128)} %get-tuple-element.63.refs_3_, f32[1,128]{1,0:T(1,128)} %dynamic-slice_bitcast_fusion.refs_4_), custom_call_target="tpu_custom_call" | custom-call | tf_op jit(solution)/shard_map/input_kernel/pallas_call | solution.py:131
  158.6 6.9 %collective-permute-done.25 = bf16[512,256]{1,0:T(8,128)(2,1)} collective-permute-done((bf16[512,256]{1,0:T(8,128)(2,1)}, bf16[512,256]{1,0:T(8,128)(2,1)}, u32[]{:S(2)}, u32[]{:S(2)}) %collective-permute-start.25) | collective-permute-done | bytes 262176 | tf_op jit(solution)/shard_map/ppermute | solution.py:449
  166.7 3.7 %collective-permute-start.18 = (f32[40,128]{1,0:T(8,128)S(1)}, f32[40,128]{1,0:T(8,128)S(1)}, u32[]{:S(2)}, u32[]{:S(2)}) collective-permute-start(f32[40,128]{1,0:T(8,128)S(1)} %add.124), channel_id=1, source_target_pairs={{0,0},{8,64},{16,128},{24,192},{64,8},{72,72},{80,136},{88,200},{1... | collective-permute-start | bytes 61448 | tf_op jit(solution)/shard_map/ppermute | solution.py:623
  170.4 4.1 %collective-permute-start.19 = (f32[40,128]{1,0:T(8,128)S(1)}, f32[40,128]{1,0:T(8,128)S(1)}, u32[]{:S(2)}, u32[]{:S(2)}) collective-permute-start(f32[40,128]{1,0:T(8,128)S(1)} %add.124), channel_id=1, source_target_pairs={{0,64},{8,128},{16,192},{24,0},{64,72},{72,136},{80,200},{88,8},{1... | collective-permute-start | bytes 61448 | tf_op jit(solution)/shard_map/ppermute | solution.py:623
  176.2 3.1 %collective-permute-start.13 = (bf16[384,128]{1,0:T(8,128)(2,1)S(1)}, bf16[384,128]{1,0:T(8,128)(2,1)S(1)}, u32[]{:S(2)}, u32[]{:S(2)}) collective-permute-start(bf16[384,128]{1,0:T(8,128)(2,1)S(1)} %copy-done.17), channel_id=1, source_target_pairs={{0,64},{64,128},{128,192},{192,0},{1,65},{65,129},{129,193},{193,1... | collective-permute-start | bytes 294920 | tf_op jit(solution)/shard_map/ppermute | solution.py:449
  180.7 5.0 %collective-permute-start.22 = (bf16[384,128]{1,0:T(8,128)(2,1)}, bf16[384,128]{1,0:T(8,128)(2,1)S(1)}, u32[]{:S(2)}, u32[]{:S(2)}) collective-permute-start(bf16[384,128]{1,0:T(8,128)(2,1)} %get-tuple-element.65), channel_id=1, source_target_pairs={{0,0},{8,64},{16,128},{24,192},{64,8},{72,72},{80,136},{88,200},{1... | collective-permute-start | bytes 294920 | tf_op jit(solution)/shard_map/ppermute | solution.py:426
  185.8 5.2 %collective-permute-done.22 = bf16[384,128]{1,0:T(8,128)(2,1)S(1)} collective-permute-done((bf16[384,128]{1,0:T(8,128)(2,1)}, bf16[384,128]{1,0:T(8,128)(2,1)S(1)}, u32[]{:S(2)}, u32[]{:S(2)}) %collective-permute-start.22) | collective-permute-done | bytes 98336 | tf_op jit(solution)/shard_map/ppermute | solution.py:426
  191.0 4.8 %collective-permute-start.16 = (bf16[384,128]{1,0:T(8,128)(2,1)S(1)}, bf16[384,128]{1,0:T(8,128)(2,1)S(1)}, u32[]{:S(2)}, u32[]{:S(2)}) collective-permute-start(bf16[384,128]{1,0:T(8,128)(2,1)S(1)} %add_convert_fusion.4), channel_id=1, source_target_pairs={{0,0},{8,64},{16,128},{24,192},{64,8},{72,72},{80,136},{88,200},{1... | collective-permute-start | bytes 294920 | tf_op jit(solution)/shard_map/ppermute | solution.py:426
  197.0 3.9 %collective-permute-done.16 = bf16[384,128]{1,0:T(8,128)(2,1)S(1)} collective-permute-done((bf16[384,128]{1,0:T(8,128)(2,1)S(1)}, bf16[384,128]{1,0:T(8,128)(2,1)S(1)}, u32[]{:S(2)}, u32[]{:S(2)}) %collective-permute-start.16) | collective-permute-done | bytes 98336 | tf_op jit(solution)/shard_map/ppermute | solution.py:426
  (119 shorter events, 38.3 us)
Async XLA Ops:
  7.2 43.3 %all-gather.4.cloned.1.call-start = ((), (), s32[]{:S(2)}) async-start(), calls=%async_computation.4 | async-start | bytes 3538944 | tf_op jit(solution)/shard_map/all_gather | solution.py:495
  9.1 12.1 %collective-permute-start = (bf16[384,128]{1,0:T(8,128)(2,1)}, bf16[384,128]{1,0:T(8,128)(2,1)S(1)}, u32[]{:S(2)}, u32[]{:S(2)}) collective-permute-start(bf16[384,128]{1,0:T(8,128)(2,1)} %param.8), channel_id=1, source_target_pairs={{0,0},{8,64},{16,128},{24,192},{64,8},{72,72},{80,136},{88,200},{1... | collective-permute-start | bytes 294920 | tf_op jit(solution)/shard_map/ppermute | solution.py:426
  22.3 32.0 %all-to-all-start = ((bf16[8,384,128]{2,1,0:T(8,128)(2,1)}), bf16[8,384,128]{2,1,0:T(8,128)(2,1)S(1)}, u32[]{:S(2)}, u32[]{:S(2)}) async-start(bf16[8,384,128]{2,1,0:T(8,128)(2,1)} %broadcast_in_dim.6), calls=%async_computation | async-start | bytes 1572864 | tf_op jit(solution)/shard_map/all_to_all | solution.py:441
  30.8 11.4 %collective-permute-start.1 = (bf16[480,128]{1,0:T(8,128)(2,1)S(1)}, bf16[480,128]{1,0:T(8,128)(2,1)S(1)}, u32[]{:S(2)}, u32[]{:S(2)}) collective-permute-start(bf16[480,128]{1,0:T(8,128)(2,1)S(1)} %pad_maximum_fusion.1), channel_id=1, source_target_pairs={{0,0},{8,64},{16,128},{24,192},{64,8},{72,72},{80,136},{88,200},{1... | collective-permute-start | bytes 368648 | tf_op jit(solution)/shard_map/ppermute | solution.py:426
  42.3 4.7 %collective-permute-start.2 = (bf16[384,128]{1,0:T(8,128)(2,1)S(1)}, bf16[384,128]{1,0:T(8,128)(2,1)S(1)}, u32[]{:S(2)}, u32[]{:S(2)}) collective-permute-start(bf16[384,128]{1,0:T(8,128)(2,1)S(1)} %slice.72.refs_1_.refs_2_), channel_id=1, source_target_pairs={{0,64},{64,128},{128,192},{192,0},{1,65},{65,129},{129,193},{193,1... | collective-permute-start | bytes 294920 | tf_op jit(solution)/shard_map/ppermute | solution.py:449
  42.4 6.2 %collective-permute-start.3 = (bf16[384,128]{1,0:T(8,128)(2,1)S(1)}, bf16[384,128]{1,0:T(8,128)(2,1)S(1)}, u32[]{:S(2)}, u32[]{:S(2)}) collective-permute-start(bf16[384,128]{1,0:T(8,128)(2,1)S(1)} %slice.72.refs_1_.refs_2_), channel_id=1, source_target_pairs={{0,128},{64,192},{128,0},{192,64},{1,129},{65,193},{129,1},{193,65... | collective-permute-start | bytes 294920 | tf_op jit(solution)/shard_map/ppermute | solution.py:449
  44.7 5.8 %collective-permute-start.4 = (bf16[384,128]{1,0:T(8,128)(2,1)S(1)}, bf16[384,128]{1,0:T(8,128)(2,1)S(1)}, u32[]{:S(2)}, u32[]{:S(2)}) collective-permute-start(bf16[384,128]{1,0:T(8,128)(2,1)S(1)} %slice.72.refs_1_.refs_2_), channel_id=1, source_target_pairs={{0,192},{64,0},{128,64},{192,128},{1,193},{65,1},{129,65},{193,129... | collective-permute-start | bytes 294920 | tf_op jit(solution)/shard_map/ppermute | solution.py:449
  54.3 28.4 %all-to-all-start.1 = ((bf16[8,384,128]{2,1,0:T(8,128)(2,1)}), bf16[8,384,128]{2,1,0:T(8,128)(2,1)S(1)}, u32[]{:S(2)}, u32[]{:S(2)}) async-start(bf16[8,384,128]{2,1,0:T(8,128)(2,1)} %act_kernel.1), calls=%async_computation.1 | async-start | bytes 1572864 | tf_op jit(solution)/shard_map/all_to_all | solution.py:441
  61.5 78.4 %all-gather.6.cloned.1.call-start = ((), (), s32[]{:S(2)}) async-start(), calls=%async_computation.6 | async-start | bytes 1179648 | tf_op jit(solution)/shard_map/all_gather | solution.py:558
  67.7 6.2 %collective-permute-start.5 = (bf16[432,256]{1,0:T(8,128)(2,1)}, bf16[432,256]{1,0:T(8,128)(2,1)S(1)}, u32[]{:S(2)}, u32[]{:S(2)}) collective-permute-start(bf16[432,256]{1,0:T(8,128)(2,1)} %get-tuple-element.43), channel_id=1, source_target_pairs={{0,64},{64,128},{128,192},{192,0},{1,65},{65,129},{129,193},{193,1... | collective-permute-start | bytes 663560 | tf_op jit(solution)/shard_map/ppermute | solution.py:449
  68.9 7.8 %collective-permute-start.6 = (bf16[432,256]{1,0:T(8,128)(2,1)}, bf16[432,256]{1,0:T(8,128)(2,1)S(1)}, u32[]{:S(2)}, u32[]{:S(2)}) collective-permute-start(bf16[432,256]{1,0:T(8,128)(2,1)} %get-tuple-element.44), channel_id=1, source_target_pairs={{0,128},{64,192},{128,0},{192,64},{1,129},{65,193},{129,1},{193,65... | collective-permute-start | bytes 663560 | tf_op jit(solution)/shard_map/ppermute | solution.py:449
  69.8 9.1 %collective-permute-start.7 = (bf16[432,256]{1,0:T(8,128)(2,1)}, bf16[432,256]{1,0:T(8,128)(2,1)S(1)}, u32[]{:S(2)}, u32[]{:S(2)}) collective-permute-start(bf16[432,256]{1,0:T(8,128)(2,1)} %get-tuple-element.45), channel_id=1, source_target_pairs={{0,192},{64,0},{128,64},{192,128},{1,193},{65,1},{129,65},{193,129... | collective-permute-start | bytes 663560 | tf_op jit(solution)/shard_map/ppermute | solution.py:449
  93.5 8.5 %collective-permute-start.10 = (bf16[416,256]{1,0:T(8,128)(2,1)}, bf16[416,256]{1,0:T(8,128)(2,1)S(1)}, u32[]{:S(2)}, u32[]{:S(2)}) collective-permute-start(bf16[416,256]{1,0:T(8,128)(2,1)} %get-tuple-element.67.refs_1_.refs_4_), channel_id=1, source_target_pairs={{0,64},{64,128},{128,192},{192,0},{1,65},{65,129},{129,193},{193,1... | collective-permute-start | bytes 638984 | tf_op jit(solution)/shard_map/ppermute | solution.py:449
  94.3 9.9 %collective-permute-start.11 = (bf16[416,256]{1,0:T(8,128)(2,1)}, bf16[416,256]{1,0:T(8,128)(2,1)S(1)}, u32[]{:S(2)}, u32[]{:S(2)}) collective-permute-start(bf16[416,256]{1,0:T(8,128)(2,1)} %get-tuple-element.67.refs_1_.refs_4_), channel_id=1, source_target_pairs={{0,128},{64,192},{128,0},{192,64},{1,129},{65,193},{129,1},{193,65... | collective-permute-start | bytes 638984 | tf_op jit(solution)/shard_map/ppermute | solution.py:449
  96.5 11.6 %collective-permute-start.12 = (bf16[416,256]{1,0:T(8,128)(2,1)}, bf16[416,256]{1,0:T(8,128)(2,1)S(1)}, u32[]{:S(2)}, u32[]{:S(2)}) collective-permute-start(bf16[416,256]{1,0:T(8,128)(2,1)} %get-tuple-element.67.refs_1_.refs_4_), channel_id=1, source_target_pairs={{0,192},{64,0},{128,64},{192,128},{1,193},{65,1},{129,65},{193,129... | collective-permute-start | bytes 638984 | tf_op jit(solution)/shard_map/ppermute | solution.py:449
  112.3 40.8 %all-to-all-start.2 = ((bf16[8,432,128]{2,1,0:T(8,128)(2,1)}), bf16[8,432,128]{2,1,0:T(8,128)(2,1)S(1)}, u32[]{:S(2)}, u32[]{:S(2)}) async-start(bf16[8,432,128]{2,1,0:T(8,128)(2,1)} %norm_kernel.1), calls=%async_computation.2 | async-start | bytes 1769472 | tf_op jit(solution)/shard_map/all_to_all | solution.py:441
  119.2 81.7 %reduce-scatter.2.cloned.1.call-start = ((), (), s32[]{:S(2)}) async-start(), calls=%async_computation.5 | async-start | bytes 655360 | tf_op jit(solution)/shard_map/reduce_scatter | solution.py:600
  124.3 22.2 %collective-permute-start.23 = (bf16[4,512,256]{2,1,0:T(8,128)(2,1)}, bf16[4,512,256]{2,1,0:T(8,128)(2,1)S(1)}, u32[]{:S(2)}, u32[]{:S(2)}) collective-permute-start(bf16[4,512,256]{2,1,0:T(8,128)(2,1)} %get-tuple-element.72), channel_id=1, source_target_pairs={{0,32},{32,0},{1,33},{33,1},{2,34},{34,2},{3,35},{35,3},{4,36},{36... | collective-permute-start | bytes 3145736 | tf_op jit(solution)/shard_map/ppermute | solution.py:457
  145.1 11.1 %collective-permute-start.27 = (bf16[4,512,128]{2,1,0:T(8,128)(2,1)}, bf16[4,512,128]{2,1,0:T(8,128)(2,1)}, u32[]{:S(2)}, u32[]{:S(2)}) collective-permute-start(bf16[4,512,128]{2,1,0:T(8,128)(2,1)} %get-tuple-element.61), channel_id=1, source_target_pairs={{0,32},{32,0},{1,33},{33,1},{2,34},{34,2},{3,35},{35,3},{4,36},{36... | collective-permute-start | bytes 1572872 | tf_op jit(solution)/shard_map/ppermute | solution.py:598
  147.5 11.1 %collective-permute-start.24 = (bf16[512,256]{1,0:T(8,128)(2,1)}, bf16[512,256]{1,0:T(8,128)(2,1)S(1)}, u32[]{:S(2)}, u32[]{:S(2)}) collective-permute-start(bf16[512,256]{1,0:T(8,128)(2,1)} %get-tuple-element.76), channel_id=1, source_target_pairs={{0,8},{8,16},{16,24},{24,0},{1,9},{9,17},{17,25},{25,1},{2,10},{10... | collective-permute-start | bytes 786440 | tf_op jit(solution)/shard_map/ppermute | solution.py:449
  148.9 16.6 %collective-permute-start.25 = (bf16[512,256]{1,0:T(8,128)(2,1)}, bf16[512,256]{1,0:T(8,128)(2,1)}, u32[]{:S(2)}, u32[]{:S(2)}) collective-permute-start(bf16[512,256]{1,0:T(8,128)(2,1)} %get-tuple-element.78), channel_id=1, source_target_pairs={{0,16},{8,24},{16,0},{24,8},{1,17},{9,25},{17,1},{25,9},{2,18},{10... | collective-permute-start | bytes 786440 | tf_op jit(solution)/shard_map/ppermute | solution.py:449
  152.9 12.6 %collective-permute-start.26 = (bf16[512,256]{1,0:T(8,128)(2,1)}, bf16[512,256]{1,0:T(8,128)(2,1)}, u32[]{:S(2)}, u32[]{:S(2)}) collective-permute-start(bf16[512,256]{1,0:T(8,128)(2,1)} %get-tuple-element.77), channel_id=1, source_target_pairs={{0,24},{8,0},{16,8},{24,16},{1,25},{9,1},{17,9},{25,17},{2,26},{10... | collective-permute-start | bytes 786440 | tf_op jit(solution)/shard_map/ppermute | solution.py:449
  156.2 10.5 %collective-permute-start.17 = (f32[40,128]{1,0:T(8,128)S(1)}, f32[40,128]{1,0:T(8,128)S(1)}, u32[]{:S(2)}, u32[]{:S(2)}) collective-permute-start(f32[40,128]{1,0:T(8,128)S(1)} %constant_dynamic-update-slice_fusion), channel_id=1, source_target_pairs={{0,32},{32,0},{1,33},{33,1},{2,34},{34,2},{3,35},{35,3},{4,36},{36... | collective-permute-start | bytes 61448 | tf_op jit(solution)/shard_map/ppermute | solution.py:617
  166.7 12.6 %collective-permute-start.18 = (f32[40,128]{1,0:T(8,128)S(1)}, f32[40,128]{1,0:T(8,128)S(1)}, u32[]{:S(2)}, u32[]{:S(2)}) collective-permute-start(f32[40,128]{1,0:T(8,128)S(1)} %add.124), channel_id=1, source_target_pairs={{0,0},{8,64},{16,128},{24,192},{64,8},{72,72},{80,136},{88,200},{1... | collective-permute-start | bytes 61448 | tf_op jit(solution)/shard_map/ppermute | solution.py:623
  170.4 9.5 %collective-permute-start.19 = (f32[40,128]{1,0:T(8,128)S(1)}, f32[40,128]{1,0:T(8,128)S(1)}, u32[]{:S(2)}, u32[]{:S(2)}) collective-permute-start(f32[40,128]{1,0:T(8,128)S(1)} %add.124), channel_id=1, source_target_pairs={{0,64},{8,128},{16,192},{24,0},{64,72},{72,136},{80,200},{88,8},{1... | collective-permute-start | bytes 61448 | tf_op jit(solution)/shard_map/ppermute | solution.py:623
  174.6 6.1 %collective-permute-start.20 = (f32[40,128]{1,0:T(8,128)S(1)}, f32[40,128]{1,0:T(8,128)S(1)}, u32[]{:S(2)}, u32[]{:S(2)}) collective-permute-start(f32[40,128]{1,0:T(8,128)S(1)} %add.124), channel_id=1, source_target_pairs={{0,128},{8,192},{16,0},{24,64},{64,136},{72,200},{80,8},{88,72},{1... | collective-permute-start | bytes 61448 | tf_op jit(solution)/shard_map/ppermute | solution.py:623
  175.3 10.5 %collective-permute-start.21 = (f32[40,128]{1,0:T(8,128)S(1)}, f32[40,128]{1,0:T(8,128)S(1)}, u32[]{:S(2)}, u32[]{:S(2)}) collective-permute-start(f32[40,128]{1,0:T(8,128)S(1)} %add.124), channel_id=1, source_target_pairs={{0,192},{8,0},{16,64},{24,128},{64,200},{72,8},{80,72},{88,136},{1... | collective-permute-start | bytes 61448 | tf_op jit(solution)/shard_map/ppermute | solution.py:623
  176.2 14.7 %collective-permute-start.13 = (bf16[384,128]{1,0:T(8,128)(2,1)S(1)}, bf16[384,128]{1,0:T(8,128)(2,1)S(1)}, u32[]{:S(2)}, u32[]{:S(2)}) collective-permute-start(bf16[384,128]{1,0:T(8,128)(2,1)S(1)} %copy-done.17), channel_id=1, source_target_pairs={{0,64},{64,128},{128,192},{192,0},{1,65},{65,129},{129,193},{193,1... | collective-permute-start | bytes 294920 | tf_op jit(solution)/shard_map/ppermute | solution.py:449
  179.3 11.6 %collective-permute-start.14 = (bf16[384,128]{1,0:T(8,128)(2,1)S(1)}, bf16[384,128]{1,0:T(8,128)(2,1)S(1)}, u32[]{:S(2)}, u32[]{:S(2)}) collective-permute-start(bf16[384,128]{1,0:T(8,128)(2,1)S(1)} %copy-done.16), channel_id=1, source_target_pairs={{0,128},{64,192},{128,0},{192,64},{1,129},{65,193},{129,1},{193,65... | collective-permute-start | bytes 294920 | tf_op jit(solution)/shard_map/ppermute | solution.py:449
  180.0 11.0 %collective-permute-start.15 = (bf16[384,128]{1,0:T(8,128)(2,1)S(1)}, bf16[384,128]{1,0:T(8,128)(2,1)S(1)}, u32[]{:S(2)}, u32[]{:S(2)}) collective-permute-start(bf16[384,128]{1,0:T(8,128)(2,1)S(1)} %copy-done.15), channel_id=1, source_target_pairs={{0,192},{64,0},{128,64},{192,128},{1,193},{65,1},{129,65},{193,129... | collective-permute-start | bytes 294920 | tf_op jit(solution)/shard_map/ppermute | solution.py:449
  180.7 10.2 %collective-permute-start.22 = (bf16[384,128]{1,0:T(8,128)(2,1)}, bf16[384,128]{1,0:T(8,128)(2,1)S(1)}, u32[]{:S(2)}, u32[]{:S(2)}) collective-permute-start(bf16[384,128]{1,0:T(8,128)(2,1)} %get-tuple-element.65), channel_id=1, source_target_pairs={{0,0},{8,64},{16,128},{24,192},{64,8},{72,72},{80,136},{88,200},{1... | collective-permute-start | bytes 294920 | tf_op jit(solution)/shard_map/ppermute | solution.py:426
  191.0 9.8 %collective-permute-start.16 = (bf16[384,128]{1,0:T(8,128)(2,1)S(1)}, bf16[384,128]{1,0:T(8,128)(2,1)S(1)}, u32[]{:S(2)}, u32[]{:S(2)}) collective-permute-start(bf16[384,128]{1,0:T(8,128)(2,1)S(1)} %add_convert_fusion.4), channel_id=1, source_target_pairs={{0,0},{8,64},{16,128},{24,192},{64,8},{72,72},{80,136},{88,200},{1... | collective-permute-start | bytes 294920 | tf_op jit(solution)/shard_map/ppermute | solution.py:426
  (20 other events, 442.2 us)
Sparse Core Ops, SparseCore 0:
  9.9 35.8 all-gather.3
  93.6 46.2 all-gather.5
  158.5 23.2 reduce-scatter.1

commit v7 on v6

--- a/solution.py
+++ b/solution.py
@@ -17,7 +17,6 @@
 QUARTER = COLS * NZ
 WIDTH = QUARTER * NX
 EDGE = 32
-GATHER_ROWS = 512
 IN = (0, 2 * COLS)
 OUT = (2 * COLS, COLS)
 
@@ -158,15 +157,16 @@
         total = total + jnp.sum(wide, axis=1, keepdims=True)
         square = square + jnp.sum(wide * wide, axis=1, keepdims=True)
     mean = total / QUARTER
+    arrive(2)
+    arrive(3)
     for i in range(NZ):
         cut = pl.ds(i * COLS, COLS)
         scaled = (frames_ref[i].astype(f32) - mean) * gain_ref[0:1, cut]
         left_ref[:, cut] = scaled.astype(bf16)
     sums = columns_to_rows(total, square).astype(bf16)
-    arrive(4)
     for j, out_ref in enumerate(refs[:NX]):
         start = pl.multiple_of(place_ref[4 + j] * QUARTER, QUARTER)
-        weight = weight_ref[pl.ds(start, QUARTER), :]
+        weight = weight_ref[pl.ds(start, QUARTER), 0 : 2 * COLS]
         out_ref[0:ROWS, :] = dot(left_ref[...], weight, 1, 0).astype(bf16)
         unit = jnp.sum(dot(gain_rows_ref[...], weight, 1, 0), axis=0, keepdims=True)
         out_ref[ROWS : ROWS + 16, :] = stacked_rows(split3(unit)).astype(bf16)
@@ -206,7 +206,7 @@
     total = jnp.zeros((ROWS, QUARTER), f32)
     for j, grad_ref in enumerate((g0_ref, g1_ref, g2_ref, g3_ref)):
         start = pl.multiple_of(place_ref[j] * QUARTER, QUARTER)
-        weight = weight_ref[pl.ds(start, QUARTER), :]
+        weight = weight_ref[pl.ds(start, QUARTER), 2 * COLS : 3 * COLS]
         total = total + dot(grad_ref[...], weight, 1, 1)
     for i in range(NZ):
         out_ref[i] = total[:, i * COLS : (i + 1) * COLS].astype(bf16)
@@ -229,16 +229,57 @@
     return inside == own
 
 
-def conv_kernel(
+def fill_wide(wide_ref, gated_ref, low_ref, high_ref):
+    wide_ref[0:EDGE, :] = low_ref[...].astype(f32)
+    wide_ref[EDGE : EDGE + ROWS, :] = gated_ref[...].astype(f32)
+    wide_ref[EDGE + ROWS :, :] = high_ref[...].astype(f32)
+
+
+def forward_kernel(
     place_ref,
     gated_ref,
-    act_ref,
     low_ref,
     high_ref,
     taps_ref,
+    activated_ref,
+    slope_ref,
+    kernel_ref,
+    wide_ref,
+    masked_ref,
+):
+    border = place_ref[0]
+    total = jnp.zeros((K + 1, COLS), f32)
+    for i in range(3):
+        total = total + taps_ref[pl.ds(ROWS + i * (K + 1), K + 1), :].astype(f32)
+    kernel_ref[...] = total
+    fill_wide(wide_ref, gated_ref, low_ref, high_ref)
+    bias = kernel_ref[K : K + 1, :]
+    for start, count in CHUNKS:
+        here = wide_ref[pl.ds(start - 16 + EDGE, count + 32), :]
+        masked_ref[0 : count + 32, :] = jnp.where(same_clip(border, start, count), here, 0.0)
+        conv = jnp.broadcast_to(bias, (count, COLS))
+        for tap in range(K):
+            conv = conv + kernel_ref[tap : tap + 1, :] * masked_ref[1 + tap : 1 + tap + count, :]
+        sig = jax.nn.sigmoid(conv)
+        slope_ref[pl.ds(start + 16, count), :] = sig * (1.0 + conv * (1.0 - sig))
+        if 0 <= start < ROWS:
+            activated = (conv * sig).astype(bf16)
+            for i in range(NZ):
+                activated_ref[i, pl.ds(start, count), :] = activated
+
+
+def backward_kernel(
+    place_ref,
+    gated_ref,
+    low_ref,
+    high_ref,
+    act_ref,
+    act_low_ref,
+    act_high_ref,
+    slope_ref,
+    taps_ref,
     pre_ref,
     unit_ref,
-    activated_ref,
     message_ref,
     small_ref,
     wide_ref,
@@ -247,40 +288,27 @@
     sums_ref,
     masked_ref,
     masked_grad_ref,
-    kernel_ref,
 ):
     border = place_ref[0]
-    total = jnp.zeros((K + 1, COLS), f32)
-    for i in range(3):
-        total = total + taps_ref[pl.ds(ROWS + i * (K + 1), K + 1), :].astype(f32)
-    kernel_ref[...] = total
-    wide_ref[0:EDGE, :] = low_ref[0:EDGE, :].astype(f32)
-    wide_ref[EDGE : EDGE + ROWS, :] = gated_ref[...].astype(f32)
-    wide_ref[EDGE + ROWS :, :] = high_ref[0:EDGE, :].astype(f32)
+    fill_wide(wide_ref, gated_ref, low_ref, high_ref)
     sums_ref[...] = jnp.zeros((K + 1, 8, COLS), f32)
-    bias = kernel_ref[K : K + 1, :]
     for start, count in CHUNKS:
-        here = wide_ref[pl.ds(start - 16 + EDGE, count + 32), :]
-        masked_ref[0 : count + 32, :] = jnp.where(same_clip(border, start, count), here, 0.0)
-        conv = jnp.broadcast_to(bias, (count, COLS))
-        for tap in range(K):
-            conv = conv + kernel_ref[tap : tap + 1, :] * masked_ref[1 + tap : 1 + tap + count, :]
-        sig = jax.nn.sigmoid(conv)
         if start < 0:
-            act = low_ref[EDGE:, :]
+            act = act_low_ref[...]
         elif start < ROWS:
             act = act_ref[pl.ds(start, count), :]
         else:
-            act = high_ref[EDGE:, :]
-        grad = (act.astype(f32) * sig * (1.0 + conv * (1.0 - sig))).astype(bf16).astype(f32)
+            act = act_high_ref[...]
+        grad = act.astype(f32) * slope_ref[pl.ds(start + 16, count), :]
+        grad = grad.astype(bf16).astype(f32)
         grad_ref[pl.ds(start + 16, count), :] = grad
         if 0 <= start < ROWS:
-            activated_ref[pl.ds(start, count), :] = (conv * sig).astype(bf16)
+            here = wide_ref[pl.ds(start - 16 + EDGE, count + 32), :]
+            masked_ref[...] = jnp.where(same_clip(border, start, count), here, 0.0)
             for tap in range(K):
                 product = grad * masked_ref[1 + tap : 1 + tap + count, :]
                 sums_ref[tap] += jnp.sum(product.reshape(count // 8, 8, COLS), axis=0)
             sums_ref[K] += jnp.sum(grad.reshape(count // 8, 8, COLS), axis=0)
-    activated_ref[ROWS:, :] = jnp.zeros((GATHER_ROWS - ROWS, COLS), bf16)
     small_ref[...] = jnp.sum(sums_ref[...], axis=1)
 
     for start, count in CHUNKS[1:4]:
@@ -288,7 +316,7 @@
         masked_grad_ref[...] = jnp.where(same_clip(border, start, count), here, 0.0)
         glu = jnp.zeros((count, COLS), f32)
         for tap in range(K):
-            glu = glu + kernel_ref[tap : tap + 1, :] * masked_grad_ref[31 - tap : 31 - tap + count, :]
+            glu = glu + taps_ref[tap : tap + 1, :] * masked_grad_ref[31 - tap : 31 - tap + count, :]
         glu_ref[pl.ds(start, count), :] = glu
 
     glu = glu_ref[...]
@@ -325,13 +353,13 @@
     first = rows[0:1] + rows[1:2] + rows[2:3]
     second = rows[3:4] + rows[4:5] + rows[5:6]
     sums = stacked_rows(split3(first) + split3(second)).astype(bf16)
-    arrive(5)
     step = 2 * COLS
     for part in range(QUARTER // step):
         total = jnp.zeros((ROWS, step), f32)
         for j, grad_ref in enumerate(grads):
             start = pl.multiple_of(place_ref[j] * QUARTER + part * step, step)
-            total = total + dot(grad_ref[0:ROWS, :], weight_ref[pl.ds(start, step), :], 1, 1)
+            weight = weight_ref[pl.ds(start, step), 0 : 2 * COLS]
+            total = total + dot(grad_ref[0:ROWS, :], weight, 1, 1)
         for i in (2 * part, 2 * part + 1):
             cut = (i - 2 * part) * COLS
             out_ref[i, 0:ROWS, :] = total[:, cut : cut + COLS].astype(bf16)
@@ -350,24 +378,19 @@
     g1_ref,
     g2_ref,
     g3_ref,
-    kept_ref,
-    given_ref,
+    out_ref,
     left_ref,
-    right_ref,
 ):
     mean = stat_ref[:, 0:1]
     inv_std = stat_ref[:, 1:2]
-    half = QUARTER // NK
     for i in range(NZ):
         cut = pl.ds(i * COLS, COLS)
         scaled = (frames_ref[i].astype(f32) - mean) * inv_std * gain_ref[0:1, cut]
-        left_ref[i * COLS // half, :, pl.ds(i * COLS % half, COLS)] = scaled.astype(bf16)
-    order_blocks(place_ref, 10, (g0_ref, g1_ref, g2_ref, g3_ref), right_ref, 2 * COLS)
-    core = place_ref[9]
-    for out_ref, which in ((given_ref, 1 - core), (kept_ref, core)):
-        out = dot(left_ref[which], right_ref[...], 0, 0).astype(bf16)
-        for i in range(NY):
-            out_ref[i] = out[:, i * 2 * COLS : (i + 1) * 2 * COLS]
+        left_ref[:, cut] = scaled.astype(bf16)
+    for j, grad_ref in enumerate((g0_ref, g1_ref, g2_ref, g3_ref)):
+        start = pl.multiple_of(place_ref[j] * QUARTER, QUARTER)
+        out = dot(left_ref[...], grad_ref[0:ROWS, :], 0, 0)
+        out_ref[pl.ds(start, QUARTER), :] = out.astype(bf16)
 
 
 def order_blocks(place_ref, base, sources, out_ref, lanes):
@@ -390,10 +413,10 @@
         total = jnp.zeros((ROWS, COLS), f32)
         for h in range(NK):
             start = pl.multiple_of(place_ref[4 + j] * QUARTER + h * half, half)
-            weight = weight_ref[pl.ds(start, half), :]
+            weight = weight_ref[pl.ds(start, half), 2 * COLS : 3 * COLS]
             total = total + dot(left_ref[h], weight, 1, 0)
         enc_ref[...] = total.astype(bf16)
-    order_blocks(place_ref, 0, (g0_ref, g1_ref, g2_ref, g3_ref), grad_ref, COLS)
+    order_blocks(place_ref, 10, (g0_ref, g1_ref, g2_ref, g3_ref), grad_ref, COLS)
     core = place_ref[9]
     for out_ref, which in ((given_ref, 1 - core), (kept_ref, core)):
         out = dot(left_ref[which], grad_ref[...], 0, 0).astype(bf16)
@@ -401,7 +424,19 @@
             out_ref[i] = out[:, i * COLS : (i + 1) * COLS]
 
 
-def input_kernel(parts_ref, frames_ref, grad_ref, stat_ref, gain_ref, out_ref, small_ref):
+def input_kernel(
+    parts_ref,
+    frames_ref,
+    grad_ref,
+    stat_ref,
+    gain_ref,
+    e0_ref,
+    e1_ref,
+    e2_ref,
+    e3_ref,
+    out_ref,
+    small_ref,
+):
     normed_grad = jnp.zeros((ROWS, COLS), f32)
     rows = jnp.zeros((16, ROWS), f32)
     for i in range(NZ):
@@ -417,7 +452,11 @@
     centred = (frames_ref[...].astype(f32) - mean) * inv_std
     hat = normed_grad * gain_ref[0:1, :]
     out = grad_ref[...].astype(f32) + inv_std * (hat - first / WIDTH - centred * (second / WIDTH))
-    out_ref[...] = out.astype(bf16)
+    out_ref[:, COLS:] = out.astype(bf16)
+    encoded = frames_ref[...].astype(f32)
+    for part_ref in (e0_ref, e1_ref, e2_ref, e3_ref):
+        encoded = encoded + part_ref[...].astype(f32)
+    out_ref[:, 0:COLS] = encoded.astype(bf16)
     gain_term = jnp.sum(normed_grad * centred, axis=0, keepdims=True)
     small_ref[...] = jnp.broadcast_to(gain_term, (8, COLS))
 
@@ -505,7 +544,7 @@
     grads = spread(grad_out, "x", NX)
 
     act_parts = call(
-        act_kernel, shape((NZ, ROWS, COLS), bf16), (place, *grads, weights), smem=(0,), near=(1, 2, 3, 4), cuts={5: OUT}
+        act_kernel, shape((NZ, ROWS, COLS), bf16), (place, *grads, weights), smem=(0,), near=(1, 2, 3, 4, 5)
     )
     act_moved = exchange(act_parts, "z")
     pre_parts = call(
@@ -513,9 +552,8 @@
         [shape((ROWS + 48, 2 * COLS), bf16) for _ in range(NX)],
         (place, after(frames_z, act_parts), quarter_gain, gain_rows, weights),
         smem=(0,),
-        near=(1,),
-        late=(4,),
-        cuts={4: IN},
+        near=(1, 4),
+        late=(2, 3),
         scratch=[pltpu.VMEM((ROWS, QUARTER), bf16)],
     )
     pre_moved = [pre_parts[0]] + [shifted(pre_parts[j], "x", NX, j) for j in range(1, NX)]
@@ -531,20 +569,42 @@
         near=(1, 2, 3),
     )
     act_grad = call(sum_kernel, shape((ROWS, COLS), bf16), (act_moved,), near=(0,))
-    low, high = neighbours(
-        jnp.concatenate([gated[-EDGE:], act_grad[-16:]], axis=0),
-        jnp.concatenate([gated[:EDGE], act_grad[:16]], axis=0),
-    )
-    activated, message, small = call(
-        conv_kernel,
+    gated_low, gated_high = neighbours(gated[-EDGE:], gated[:EDGE])
+    act_low, act_high = neighbours(act_grad[-16:], act_grad[:16])
+    activated, slope, taps = call(
+        forward_kernel,
         [
-            shape((GATHER_ROWS, COLS), bf16),
-            shape((ROWS + 32, 2 * COLS), bf16),
+            shape((NZ, ROWS, COLS), bf16),
+            shape((ROWS + 32, COLS), f32),
             shape((K + 1, COLS), f32),
         ],
-        (border, gated, act_grad, low, high, packed, pre, unit),
+        (border, gated, gated_low, gated_high, packed),
         smem=(0,),
-        near=(3, 4),
+        near=(2, 3),
+        scratch=[
+            pltpu.VMEM((ROWS + 2 * EDGE, COLS), f32),
+            pltpu.VMEM((160, COLS), f32),
+        ],
+    )
+    act_z = exchange(activated, "z")
+    message, small = call(
+        backward_kernel,
+        [shape((ROWS + 32, 2 * COLS), bf16), shape((K + 1, COLS), f32)],
+        (
+            border,
+            gated,
+            gated_low,
+            gated_high,
+            act_grad,
+            act_low,
+            act_high,
+            slope,
+            taps,
+            pre,
+            unit,
+        ),
+        smem=(0,),
+        near=(2, 3, 5, 6),
         scratch=[
             pltpu.VMEM((ROWS + 2 * EDGE, COLS), f32),
             pltpu.VMEM((ROWS + 32, COLS), f32),
@@ -552,35 +612,31 @@
             pltpu.VMEM((K + 1, 8, COLS), f32),
             pltpu.VMEM((160, COLS), f32),
             pltpu.VMEM((160, COLS), f32),
-            pltpu.VMEM((K + 1, COLS), f32),
         ],
     )
-    act_z = lax.all_gather(activated, "z", axis=0, tiled=False)
 
     vg_grads = spread(message, "x", NX)
     norm_parts = call(
         norm_kernel,
         shape((NZ, ROWS + 48, COLS), bf16),
-        (place, *vg_grads, weights),
+        (place, *vg_grads, after(weights, act_z)),
         smem=(0,),
-        near=(2, 3, 4),
-        late=(1, 5),
-        cuts={5: IN},
+        near=(2, 3, 4, 5),
+        late=(1,),
     )
     norm_moved = exchange(norm_parts, "z")
     held = lax.optimization_barrier((vg_grads, norm_parts))[0]
-    kept, given = call(
+    weight_parts = call(
         weight_kernel,
-        [shape((NY, QUARTER // NK, 2 * COLS), bf16) for _ in range(2)],
+        shape((NY * QUARTER, 2 * COLS), bf16),
         (place, frames_z, quarter_gain, stat, *held),
         smem=(0,),
         near=(5, 6, 7),
-        scratch=[
-            pltpu.VMEM((NK, ROWS, QUARTER // NK), bf16),
-            pltpu.VMEM((ROWS, NY * 2 * COLS), bf16),
-        ],
-    )
-    in_weight = reduced(kept, given)
+        scratch=[pltpu.VMEM((ROWS, QUARTER), bf16)],
+    )
+    in_weight = lax.psum_scatter(
+        weight_parts, TIME, scatter_dimension=0, tiled=True
+    ).astype(f32)
 
     out_parts = call(
         out_kernel,
@@ -588,30 +644,24 @@
         + [shape((NY, QUARTER // NK, COLS), bf16) for _ in range(2)],
         (place, act_z, *after(grads, norm_parts), weights),
         smem=(0,),
-        cuts={6: OUT},
+        near=(1, 6),
         scratch=[
             pltpu.VMEM((NK, ROWS, QUARTER // NK), bf16),
             pltpu.VMEM((ROWS, NY * COLS), bf16),
         ],
     )
-    kept, given = out_parts[NX:]
-    other = lax.ppermute(given, "k", [(0, 1), (1, 0)])
-    both = (kept.astype(f32) + other.astype(f32)).astype(bf16)
-    grad_out_weight = lax.psum_scatter(
-        both.reshape(NY * QUARTER // NK, COLS), "y", scatter_dimension=0, tiled=True
-    ).astype(f32)
-    enc_sum = out_parts[0].astype(f32)
-    for j in range(1, NX):
-        enc_sum = enc_sum + shifted(out_parts[j], "x", NX, j).astype(f32)
-    encoded = swap_xy((frames.astype(f32) + enc_sum).astype(bf16))
-
-    input_grad, gain_term = call(
+    grad_out_weight = reduced(*out_parts[NX:])
+    enc = [out_parts[0]] + [shifted(out_parts[j], "x", NX, j) for j in range(1, NX)]
+
+    results, gain_term = call(
         input_kernel,
-        [shape((ROWS, COLS), bf16), shape((8, COLS), f32)],
-        (after(norm_moved, *out_parts), frames, grad_out, stat, local_gain),
-        near=(0,),
-    )
-    input_grad = swap_xy(input_grad)
+        [shape((ROWS, 2 * COLS), bf16), shape((8, COLS), f32)],
+        (norm_moved, frames, grad_out, stat, local_gain, *enc),
+        near=(0, 6, 7, 8),
+    )
+    results = swap_xy(results)
+    encoded = results[:, :COLS]
+    input_grad = results[:, COLS:]
 
     small = jnp.concatenate([small, gain_term], axis=0)
     small = small + lax.ppermute(small, "k", [(0, 1), (1, 0)])
@@ -621,7 +671,7 @@
             (a * NY + b, ((b + shift) % NX) * NY + a) for a in range(NX) for b in range(NY)
         ]
         arrived.append(lax.ppermute(small, ("x", "y"), route))
-    small, input_grad = lax.optimization_barrier((sum(arrived), input_grad))
+    small = sum(after(arrived, results))
     return (
         encoded,
         input_grad,

time: 214 us -> 204 us (0.953); the launches traced: 210 us -> 203 us
  waiting for transfers between devices: 72.2 us -> 57.2 us
  starting transfers between devices: 73.6 us -> 78.3 us
  other arithmetic: 8.7 us -> 5.48 us
  local copies, waits for them, and re-layouts: 8.46 us -> 11.3 us
  Pallas kernels: 33.1 us -> 35.7 us
    all_to_all x3 -> x4, waiting for transfers between devices: 0.01 us -> 18 us  [exchange(): return lax.all_to_all(parts, axis, 0, 0, tiled=True)]
    all_gather x1 -> x0, waiting for transfers between devices: 15.4 us -> none  [shards(): act_z = lax.all_gather(activated, 'z', axis=0, tiled=False)]
    ppermute x15, waiting for transfers between devices: 33 us -> 18.5 us  [shifted(): lax.ppermute(block, axis, [(i, (i + shift) % count) for i in range(count)])]
    ppermute x4 -> x3, waiting for transfers between devices: 22.9 us -> 13.9 us  [swap_xy(): lax.ppermute(block, ('x', 'y'), [(a * NY + b, b * NY + a) for a in range(...]
    ppermute x4 -> x3, starting transfers between devices: 19.5 us -> 11.5 us  [swap_xy(): lax.ppermute(block, ('x', 'y'), [(a * NY + b, b * NY + a) for a in range(...]
    all_to_all x3 -> x4, starting transfers between devices: 22.6 us -> 29.9 us  [exchange(): return lax.all_to_all(parts, axis, 0, 0, tiled=True)]
    convert_element_type x3 -> x0, other arithmetic: 3.82 us -> none  [the longest x1 2.12 us: shards(): both = (kept.astype(f32) + other.astype(f32)).astype(bf16)]
    ppermute x4, starting transfers between devices: 8.65 us -> 12.4 us  [shards(): arrived.append(lax.ppermute(small, ('x', 'y'), route))]
  transfers between devices with their start and end apart: 34 -> 34, of which waited for: 17 -> 15; matrix products, arithmetic and copies ran while one was open for 6% -> 5% of each run, Pallas kernels for 13% -> 13%
where the time goes in v7:
time: 204 us; the launch traced here: 203 us
  starting transfers between devices  78.3 us (38%)
  waiting for transfers between devices  57.2 us (28%)
  Pallas kernels  35.7 us (18%)
  between operations  14.5 us (7%)
  local copies, waits for them, and re-layouts  11.3 us (6%)
  other arithmetic  5.48 us (3%)
    pallas_call x10, Pallas kernels, call(): pl.pallas_call(whole, out_shape=[pltpu.HBM(out.shape, out.dtype) for out...  35.7 us
    all_to_all x4, starting transfers between devices, exchange(): return lax.all_to_all(parts, axis, 0, 0, tiled=True)  29.9 us
    ppermute x15, waiting for transfers between devices, shifted(): lax.ppermute(block, axis, [(i, (i + shift) % count) for i in range(count)])  18.5 us
    all_to_all x4, waiting for transfers between devices, exchange(): return lax.all_to_all(parts, axis, 0, 0, tiled=True)  18 us
    ppermute x15, starting transfers between devices, shifted(): lax.ppermute(block, axis, [(i, (i + shift) % count) for i in range(count)])  16.6 us
    ppermute x3, waiting for transfers between devices, swap_xy(): lax.ppermute(block, ('x', 'y'), [(a * NY + b, b * NY + a) for a in range(...  13.9 us
    ppermute x4, starting transfers between devices, shards(): arrived.append(lax.ppermute(small, ('x', 'y'), route))  12.4 us
    ppermute x3, starting transfers between devices, swap_xy(): lax.ppermute(block, ('x', 'y'), [(a * NY + b, b * NY + a) for a in range(...  11.5 us
  transfers between devices with their start and end apart: 34, of which 15 were waited for; matrix products, arithmetic and copies ran while one was open for 5% of the time, Pallas kernels for 13%

profile of v7, /device:TPU:6, one launch (start us, length us, event | category | flops | bytes accessed | tf_op | source)
XLA Modules:
  0.0 202.6 jit_solution(6465254497384996302)
XLA Ops:
  9.1 4.8 %collective-permute-start = (bf16[384,128]{1,0:T(8,128)(2,1)}, bf16[384,128]{1,0:T(8,128)(2,1)S(1)}, u32[]{:S(2)}, u32[]{:S(2)}) collective-permute-start(bf16[384,128]{1,0:T(8,128)(2,1)} %param.8), channel_id=1, source_target_pairs={{0,0},{8,64},{16,128},{24,192},{64,8},{72,72},{80,136},{88,200},{1... | collective-permute-start | bytes 294920 | tf_op jit(solution)/shard_map/ppermute | solution.py:465
  14.0 7.3 %collective-permute-done.refs_1_ = bf16[384,128]{1,0:T(8,128)(2,1)S(1)} collective-permute-done((bf16[384,128]{1,0:T(8,128)(2,1)}, bf16[384,128]{1,0:T(8,128)(2,1)S(1)}, u32[]{:S(2)}, u32[]{:S(2)}) %collective-permute-start) | collective-permute-done | bytes 98336 | tf_op jit(solution)/shard_map/ppermute | solution.py:465
  22.9 8.5 %all-to-all-start = ((bf16[8,384,128]{2,1,0:T(8,128)(2,1)}), bf16[8,384,128]{2,1,0:T(8,128)(2,1)}, u32[]{:S(2)}, u32[]{:S(2)}) async-start(bf16[8,384,128]{2,1,0:T(8,128)(2,1)} %broadcast_in_dim.6), calls=%async_computation | async-start | bytes 1572864 | tf_op jit(solution)/shard_map/all_to_all | solution.py:480
  31.5 4.8 %collective-permute-start.1 = (bf16[480,128]{1,0:T(8,128)(2,1)S(1)}, bf16[480,128]{1,0:T(8,128)(2,1)S(1)}, u32[]{:S(2)}, u32[]{:S(2)}) collective-permute-start(bf16[480,128]{1,0:T(8,128)(2,1)S(1)} %pad_maximum_fusion.1), channel_id=1, source_target_pairs={{0,0},{8,64},{16,128},{24,192},{64,8},{72,72},{80,136},{88,200},{1... | collective-permute-start | bytes 368648 | tf_op jit(solution)/shard_map/ppermute | solution.py:465
  36.3 6.6 %collective-permute-done.1.refs_4_ = bf16[480,128]{1,0:T(8,128)(2,1)S(1)} collective-permute-done((bf16[480,128]{1,0:T(8,128)(2,1)S(1)}, bf16[480,128]{1,0:T(8,128)(2,1)S(1)}, u32[]{:S(2)}, u32[]{:S(2)}) %collective-permute-start.1) | collective-permute-done | bytes 122912 | tf_op jit(solution)/shard_map/ppermute | solution.py:465
  43.0 2.3 %collective-permute-start.3 = (bf16[384,128]{1,0:T(8,128)(2,1)S(1)}, bf16[384,128]{1,0:T(8,128)(2,1)S(1)}, u32[]{:S(2)}, u32[]{:S(2)}) collective-permute-start(bf16[384,128]{1,0:T(8,128)(2,1)S(1)} %slice.80.refs_1_.refs_2_), channel_id=1, source_target_pairs={{0,128},{64,192},{128,0},{192,64},{1,129},{65,193},{129,1},{193,65... | collective-permute-start | bytes 294920 | tf_op jit(solution)/shard_map/ppermute | solution.py:488
  45.4 2.2 %collective-permute-done.2.refs_2_.refs_3_ = bf16[384,128]{1,0:T(8,128)(2,1)S(1)} collective-permute-done((bf16[384,128]{1,0:T(8,128)(2,1)S(1)}, bf16[384,128]{1,0:T(8,128)(2,1)S(1)}, u32[]{:S(2)}, u32[]{:S(2)}) %collective-permute-start.2) | collective-permute-done | bytes 98336 | tf_op jit(solution)/shard_map/ppermute | solution.py:488
  53.1 2.5 %act_kernel.1 = bf16[8,384,128]{2,1,0:T(8,128)(2,1)} custom-call(s32[14]{0:T(128)S(1)} %concatenate.43.refs_0_, bf16[384,128]{1,0:T(8,128)(2,1)S(1)} %slice.80.refs_1_.refs_2_, bf16[384,128]{1,0:T(8,128)(2,1)S(1)} %collective-permute-done.2.refs_2_.refs_3_, bf16[384,128]{1,0:T(8,128)(2,1)S(1)} %collective-permute-done.3.refs_3_.refs_4_, ...), custom_call_target="tpu_custom_call" | custom-call | tf_op jit(solution)/shard_map/act_kernel/pallas_call | solution.py:130
  55.6 7.2 %all-to-all-start.1 = ((bf16[8,384,128]{2,1,0:T(8,128)(2,1)}), bf16[8,384,128]{2,1,0:T(8,128)(2,1)}, u32[]{:S(2)}, u32[]{:S(2)}) async-start(bf16[8,384,128]{2,1,0:T(8,128)(2,1)} %act_kernel.1), calls=%async_computation.1 | async-start | bytes 1572864 | tf_op jit(solution)/shard_map/all_to_all | solution.py:480
  64.2 4.2 %project_kernel.1 = (bf16[432,256]{1,0:T(8,128)(2,1)}, bf16[432,256]{1,0:T(8,128)(2,1)}, bf16[432,256]{1,0:T(8,128)(2,1)}, bf16[432,256]{1,0:T(8,128)(2,1)}) custom-call(s32[14]{0:T(128)S(1)} %concatenate.43.refs_0_, bf16[8,384,128]{2,1,0:T(8,128)(2,1)} %all-to-all-done.refs_1_, f32[1,1024]{1,0:T(1,128)} %bitcast.27, bf16[16,1024]{1,0:T(8,128)(2,1)} %pad.4.refs_3_, ...), custom_call_target="tpu_custom_call" | custom-call | tf_op jit(solution)/shard_map/project_kernel/pallas_call | solution.py:130
  71.2 3.6 %collective-permute-done.5.refs_1_ = bf16[432,256]{1,0:T(8,128)(2,1)S(1)} collective-permute-done((bf16[432,256]{1,0:T(8,128)(2,1)}, bf16[432,256]{1,0:T(8,128)(2,1)S(1)}, u32[]{:S(2)}, u32[]{:S(2)}) %collective-permute-start.5) | collective-permute-done | bytes 221216 | tf_op jit(solution)/shard_map/ppermute | solution.py:488
  74.7 2.8 %collective-permute-done.6.refs_2_ = bf16[432,256]{1,0:T(8,128)(2,1)S(1)} collective-permute-done((bf16[432,256]{1,0:T(8,128)(2,1)}, bf16[432,256]{1,0:T(8,128)(2,1)S(1)}, u32[]{:S(2)}, u32[]{:S(2)}) %collective-permute-start.6) | collective-permute-done | bytes 221216 | tf_op jit(solution)/shard_map/ppermute | solution.py:488
  77.5 2.3 %collective-permute-done.7.refs_3_ = bf16[432,256]{1,0:T(8,128)(2,1)S(1)} collective-permute-done((bf16[432,256]{1,0:T(8,128)(2,1)}, bf16[432,256]{1,0:T(8,128)(2,1)S(1)}, u32[]{:S(2)}, u32[]{:S(2)}) %collective-permute-start.7) | collective-permute-done | bytes 221216 | tf_op jit(solution)/shard_map/ppermute | solution.py:488
  79.8 3.0 %gate_kernel.1 = (f32[384,256]{1,0:T(8,128)}, bf16[384,128]{1,0:T(8,128)(2,1)}, f32[8,256]{1,0:T(8,128)}, f32[384,128]{1,0:T(8,128)}) custom-call(bf16[432,256]{1,0:T(8,128)(2,1)} %get-tuple-element.44.refs_0_, bf16[432,256]{1,0:T(8,128)(2,1)S(1)} %collective-permute-done.5.refs_1_, bf16[432,256]{1,0:T(8,128)(2,1)S(1)} %collective-permute-done.6.refs_2_, ...), custom_call_target="tpu_custom_call" | custom-call | tf_op jit(solution)/shard_map/gate_kernel/pallas_call | solution.py:130
  87.9 2.6 %forward_kernel.1 = (bf16[8,384,128]{2,1,0:T(8,128)(2,1)}, f32[416,128]{1,0:T(8,128)}, f32[32,128]{1,0:T(8,128)}) custom-call(s32[1]{0:T(128)} %bitcast.refs_0_, bf16[384,128]{1,0:T(8,128)(2,1)} %get-tuple-element.48.refs_1_, bf16[32,128]{1,0:T(8,128)(2,1)S(1)} %collective-permute-done.8.refs_2_, bf16[32,128]{1,0:T(8,128)(2,1)S(1)} %collective-permute-done.9.refs_3_, ...), custom_call_target="tpu_custom_call" | custom-call | tf_op jit(solution)/shard_map/forward_kernel/pallas_call | solution.py:130
  90.5 7.2 %all-to-all-start.2 = ((bf16[8,384,128]{2,1,0:T(8,128)(2,1)}), bf16[8,384,128]{2,1,0:T(8,128)(2,1)}, u32[]{:S(2)}, u32[]{:S(2)}) async-start(bf16[8,384,128]{2,1,0:T(8,128)(2,1)} %get-tuple-element.54), calls=%async_computation.2 | async-start | bytes 1572864 | tf_op jit(solution)/shard_map/all_to_all | solution.py:480
  100.4 3.9 %collective-permute-start.10 = (bf16[16,128]{1,0:T(8,128)(2,1)S(1)}, bf16[16,128]{1,0:T(8,128)(2,1)S(1)}, u32[]{:S(2)}, u32[]{:S(2)}) collective-permute-start(bf16[16,128]{1,0:T(8,128)(2,1)S(1)} %get-tuple-element.88), channel_id=1, source_target_pairs={{0,32},{32,8},{8,40},{40,16},{16,48},{48,24},{24,56},{1,33},{33,9}... | collective-permute-start | bytes 12296 | tf_op jit(solution)/shard_map/ppermute | solution.py:474
  107.3 3.3 %backward_kernel.1 = (bf16[416,256]{1,0:T(8,128)(2,1)}, f32[32,128]{1,0:T(8,128)}) custom-call(s32[1]{0:T(128)} %bitcast.refs_0_, bf16[384,128]{1,0:T(8,128)(2,1)} %get-tuple-element.48.refs_1_, bf16[32,128]{1,0:T(8,128)(2,1)S(1)} %collective-permute-done.8.refs_2_, bf16[32,128]{1,0:T(8,128)(2,1)S(1)} %collective-permute-done.9.refs_3_, ...), custom_call_target="tpu_custom_call" | custom-call | tf_op jit(solution)/shard_map/backward_kernel/pallas_call | solution.py:130
  113.2 9.0 %all-to-all-done.2.refs_1_ = bf16[8,384,128]{2,1,0:T(8,128)(2,1)} async-done(((bf16[8,384,128]{2,1,0:T(8,128)(2,1)}), bf16[8,384,128]{2,1,0:T(8,128)(2,1)}, u32[]{:S(2)}, u32[]{:S(2)}) %all-to-all-start.2) | async-done | bytes 786464 | tf_op jit(solution)/shard_map/all_to_all | solution.py:480
  122.2 4.1 %collective-permute-done.14.refs_4_.refs_7_ = bf16[416,256]{1,0:T(8,128)(2,1)} collective-permute-done((bf16[416,256]{1,0:T(8,128)(2,1)}, bf16[416,256]{1,0:T(8,128)(2,1)}, u32[]{:S(2)}, u32[]{:S(2)}) %collective-permute-start.14) | collective-permute-done | bytes 213024 | tf_op jit(solution)/shard_map/ppermute | solution.py:488
  126.4 3.9 %norm_kernel.1 = bf16[8,432,128]{2,1,0:T(8,128)(2,1)} custom-call(s32[14]{0:T(128)S(1)} %copy-done.7, bf16[416,256]{1,0:T(8,128)(2,1)} %get-tuple-element.66.refs_1_.refs_4_, bf16[416,256]{1,0:T(8,128)(2,1)S(1)} %collective-permute-done.12.refs_2_.refs_5_, bf16[416,256]{1,0:T(8,128)(2,1)} %collective-permute-done.13.refs_3_.refs_6_, ...), custom_call_target="tpu_custom_call" | custom-call | tf_op jit(solution)/shard_map/norm_kernel/pallas_call | solution.py:130
  130.2 5.5 %weight_kernel.1 = bf16[4096,256]{1,0:T(8,128)(2,1)} custom-call(s32[14]{0:T(128)S(1)} %copy-done.7, bf16[8,384,128]{2,1,0:T(8,128)(2,1)} %all-to-all-done.refs_1_, f32[1,1024]{1,0:T(1,128)} %bitcast.28, f32[384,128]{1,0:T(8,128)} %get-tuple-element.56.refs_3_, bf16[416,256]{1,0:T(8,128)(2,1)} %get-tuple-element.66.refs_1_.refs_4_, ...), custom_call_target="tpu_custom_call" | custom-call | tf_op jit(solution)/shard_map/weight_kernel/pallas_call | solution.py:130
  135.8 7.0 %all-to-all-start.3 = ((bf16[8,432,128]{2,1,0:T(8,128)(2,1)}), bf16[8,432,128]{2,1,0:T(8,128)(2,1)}, u32[]{:S(2)}, u32[]{:S(2)}) async-start(bf16[8,432,128]{2,1,0:T(8,128)(2,1)} %norm_kernel.1), calls=%async_computation.3 | async-start | bytes 1769472 | tf_op jit(solution)/shard_map/all_to_all | solution.py:480
  142.8 5.2 %out_kernel.1 = (bf16[384,128]{1,0:T(8,128)(2,1)}, bf16[384,128]{1,0:T(8,128)(2,1)}, bf16[384,128]{1,0:T(8,128)(2,1)}, bf16[384,128]{1,0:T(8,128)(2,1)}, bf16[4,...) custom-call(s32[14]{0:T(128)S(1)} %copy-done.7, bf16[8,384,128]{2,1,0:T(8,128)(2,1)} %all-to-all-done.2.refs_1_, ...), custom_call_target="tpu_custom_call" | custom-call | tf_op jit(solution)/shard_map/out_kernel/pallas_call | solution.py:130
  152.5 2.4 %collective-permute-start.25 = (bf16[512,128]{1,0:T(8,128)(2,1)S(1)}, bf16[512,128]{1,0:T(8,128)(2,1)S(1)}, u32[]{:S(2)}, u32[]{:S(2)}) collective-permute-start(bf16[512,128]{1,0:T(8,128)(2,1)S(1)} %get-tuple-element.80), channel_id=1, source_target_pairs={{0,8},{8,16},{16,24},{24,0},{1,9},{9,17},{17,25},{25,1},{2,10},{10... | collective-permute-start | bytes 393224 | tf_op jit(solution)/shard_map/ppermute | solution.py:488
  154.9 2.0 collective-permute-start.26
  156.9 2.5 %collective-permute-start.27 = (bf16[512,128]{1,0:T(8,128)(2,1)S(1)}, bf16[512,128]{1,0:T(8,128)(2,1)S(1)}, u32[]{:S(2)}, u32[]{:S(2)}) collective-permute-start(bf16[512,128]{1,0:T(8,128)(2,1)S(1)} %get-tuple-element.81), channel_id=1, source_target_pairs={{0,24},{8,0},{16,8},{24,16},{1,25},{9,1},{17,9},{25,17},{2,26},{10... | collective-permute-start | bytes 393224 | tf_op jit(solution)/shard_map/ppermute | solution.py:488
  159.4 9.0 %all-to-all-done.3.refs_0_ = bf16[8,432,128]{2,1,0:T(8,128)(2,1)} async-done(((bf16[8,432,128]{2,1,0:T(8,128)(2,1)}), bf16[8,432,128]{2,1,0:T(8,128)(2,1)}, u32[]{:S(2)}, u32[]{:S(2)}) %all-to-all-start.3) | async-done | bytes 884768 | tf_op jit(solution)/shard_map/all_to_all | solution.py:480
  168.4 3.7 %input_kernel.1 = (bf16[384,256]{1,0:T(8,128)(2,1)}, f32[8,128]{1,0:T(8,128)}) custom-call(bf16[8,432,128]{2,1,0:T(8,128)(2,1)} %all-to-all-done.3.refs_0_, bf16[384,128]{1,0:T(8,128)(2,1)} %copy-done.9, bf16[384,128]{1,0:T(8,128)(2,1)} %copy-done.2, f32[384,128]{1,0:T(8,128)} %get-tuple-element.56.refs_3_, f32[1,128]{1,0:T(1,128)} %dynamic-slice_bitcast_fusion.refs_4_, ...), custom_call_target="tpu_custom_call" | custom-call | tf_op jit(solution)/shard_map/input_kernel/pallas_call | solution.py:130
  174.7 7.2 %collective-permute-start.20 = (f32[40,128]{1,0:T(8,128)S(1)}, f32[40,128]{1,0:T(8,128)S(1)}, u32[]{:S(2)}, u32[]{:S(2)}) collective-permute-start(f32[40,128]{1,0:T(8,128)S(1)} %add.105), channel_id=1, source_target_pairs={{0,0},{8,64},{16,128},{24,192},{64,8},{72,72},{80,136},{88,200},{1... | collective-permute-start | bytes 61448 | tf_op jit(solution)/shard_map/ppermute | solution.py:673
  181.9 2.1 %collective-permute-start.21 = (f32[40,128]{1,0:T(8,128)S(1)}, f32[40,128]{1,0:T(8,128)S(1)}, u32[]{:S(2)}, u32[]{:S(2)}) collective-permute-start(f32[40,128]{1,0:T(8,128)S(1)} %add.105), channel_id=1, source_target_pairs={{0,64},{8,128},{16,192},{24,0},{64,72},{72,136},{80,200},{88,8},{1... | collective-permute-start | bytes 61448 | tf_op jit(solution)/shard_map/ppermute | solution.py:673
  184.1 3.1 %collective-permute-start.22 = (f32[40,128]{1,0:T(8,128)S(1)}, f32[40,128]{1,0:T(8,128)S(1)}, u32[]{:S(2)}, u32[]{:S(2)}) collective-permute-start(f32[40,128]{1,0:T(8,128)S(1)} %add.105), channel_id=1, source_target_pairs={{0,128},{8,192},{16,0},{24,64},{64,136},{72,200},{80,8},{88,72},{1... | collective-permute-start | bytes 61448 | tf_op jit(solution)/shard_map/ppermute | solution.py:673
  (107 shorter events, 42.5 us)
Async XLA Ops:
  7.2 43.9 %all-gather.2.cloned.1.call-start = ((), (), s32[]{:S(2)}) async-start(), calls=%async_computation.5 | async-start | bytes 3538944 | tf_op jit(solution)/shard_map/all_gather | solution.py:534
  9.1 12.1 %collective-permute-start = (bf16[384,128]{1,0:T(8,128)(2,1)}, bf16[384,128]{1,0:T(8,128)(2,1)S(1)}, u32[]{:S(2)}, u32[]{:S(2)}) collective-permute-start(bf16[384,128]{1,0:T(8,128)(2,1)} %param.8), channel_id=1, source_target_pairs={{0,0},{8,64},{16,128},{24,192},{64,8},{72,72},{80,136},{88,200},{1... | collective-permute-start | bytes 294920 | tf_op jit(solution)/shard_map/ppermute | solution.py:465
  22.9 32.6 %all-to-all-start = ((bf16[8,384,128]{2,1,0:T(8,128)(2,1)}), bf16[8,384,128]{2,1,0:T(8,128)(2,1)}, u32[]{:S(2)}, u32[]{:S(2)}) async-start(bf16[8,384,128]{2,1,0:T(8,128)(2,1)} %broadcast_in_dim.6), calls=%async_computation | async-start | bytes 1572864 | tf_op jit(solution)/shard_map/all_to_all | solution.py:480
  31.5 11.4 %collective-permute-start.1 = (bf16[480,128]{1,0:T(8,128)(2,1)S(1)}, bf16[480,128]{1,0:T(8,128)(2,1)S(1)}, u32[]{:S(2)}, u32[]{:S(2)}) collective-permute-start(bf16[480,128]{1,0:T(8,128)(2,1)S(1)} %pad_maximum_fusion.1), channel_id=1, source_target_pairs={{0,0},{8,64},{16,128},{24,192},{64,8},{72,72},{80,136},{88,200},{1... | collective-permute-start | bytes 368648 | tf_op jit(solution)/shard_map/ppermute | solution.py:465
  42.9 4.7 %collective-permute-start.2 = (bf16[384,128]{1,0:T(8,128)(2,1)S(1)}, bf16[384,128]{1,0:T(8,128)(2,1)S(1)}, u32[]{:S(2)}, u32[]{:S(2)}) collective-permute-start(bf16[384,128]{1,0:T(8,128)(2,1)S(1)} %slice.80.refs_1_.refs_2_), channel_id=1, source_target_pairs={{0,64},{64,128},{128,192},{192,0},{1,65},{65,129},{129,193},{193,1... | collective-permute-start | bytes 294920 | tf_op jit(solution)/shard_map/ppermute | solution.py:488
  43.0 6.2 %collective-permute-start.3 = (bf16[384,128]{1,0:T(8,128)(2,1)S(1)}, bf16[384,128]{1,0:T(8,128)(2,1)S(1)}, u32[]{:S(2)}, u32[]{:S(2)}) collective-permute-start(bf16[384,128]{1,0:T(8,128)(2,1)S(1)} %slice.80.refs_1_.refs_2_), channel_id=1, source_target_pairs={{0,128},{64,192},{128,0},{192,64},{1,129},{65,193},{129,1},{193,65... | collective-permute-start | bytes 294920 | tf_op jit(solution)/shard_map/ppermute | solution.py:488
  45.3 5.8 %collective-permute-start.4 = (bf16[384,128]{1,0:T(8,128)(2,1)S(1)}, bf16[384,128]{1,0:T(8,128)(2,1)S(1)}, u32[]{:S(2)}, u32[]{:S(2)}) collective-permute-start(bf16[384,128]{1,0:T(8,128)(2,1)S(1)} %slice.80.refs_1_.refs_2_), channel_id=1, source_target_pairs={{0,192},{64,0},{128,64},{192,128},{1,193},{65,1},{129,65},{193,129... | collective-permute-start | bytes 294920 | tf_op jit(solution)/shard_map/ppermute | solution.py:488
  55.6 34.9 %all-to-all-start.1 = ((bf16[8,384,128]{2,1,0:T(8,128)(2,1)}), bf16[8,384,128]{2,1,0:T(8,128)(2,1)}, u32[]{:S(2)}, u32[]{:S(2)}) async-start(bf16[8,384,128]{2,1,0:T(8,128)(2,1)} %act_kernel.1), calls=%async_computation.1 | async-start | bytes 1572864 | tf_op jit(solution)/shard_map/all_to_all | solution.py:480
  68.5 6.2 %collective-permute-start.5 = (bf16[432,256]{1,0:T(8,128)(2,1)}, bf16[432,256]{1,0:T(8,128)(2,1)S(1)}, u32[]{:S(2)}, u32[]{:S(2)}) collective-permute-start(bf16[432,256]{1,0:T(8,128)(2,1)} %get-tuple-element.45), channel_id=1, source_target_pairs={{0,64},{64,128},{128,192},{192,0},{1,65},{65,129},{129,193},{193,1... | collective-permute-start | bytes 663560 | tf_op jit(solution)/shard_map/ppermute | solution.py:488
  69.7 7.8 %collective-permute-start.6 = (bf16[432,256]{1,0:T(8,128)(2,1)}, bf16[432,256]{1,0:T(8,128)(2,1)S(1)}, u32[]{:S(2)}, u32[]{:S(2)}) collective-permute-start(bf16[432,256]{1,0:T(8,128)(2,1)} %get-tuple-element.46), channel_id=1, source_target_pairs={{0,128},{64,192},{128,0},{192,64},{1,129},{65,193},{129,1},{193,65... | collective-permute-start | bytes 663560 | tf_op jit(solution)/shard_map/ppermute | solution.py:488
  70.7 9.1 %collective-permute-start.7 = (bf16[432,256]{1,0:T(8,128)(2,1)}, bf16[432,256]{1,0:T(8,128)(2,1)S(1)}, u32[]{:S(2)}, u32[]{:S(2)}) collective-permute-start(bf16[432,256]{1,0:T(8,128)(2,1)} %get-tuple-element.47), channel_id=1, source_target_pairs={{0,192},{64,0},{128,64},{192,128},{1,193},{65,1},{129,65},{193,129... | collective-permute-start | bytes 663560 | tf_op jit(solution)/shard_map/ppermute | solution.py:488
  84.8 3.1 %collective-permute-start.9 = (bf16[32,128]{1,0:T(8,128)(2,1)S(1)}, bf16[32,128]{1,0:T(8,128)(2,1)S(1)}, u32[]{:S(2)}, u32[]{:S(2)}) collective-permute-start(bf16[32,128]{1,0:T(8,128)(2,1)S(1)} %get-tuple-element.89), channel_id=1, source_target_pairs={{32,0},{8,32},{40,8},{16,40},{48,16},{24,48},{56,24},{33,1},{9,33}... | collective-permute-start | bytes 24584 | tf_op jit(solution)/shard_map/ppermute | solution.py:475
  90.5 31.8 %all-to-all-start.2 = ((bf16[8,384,128]{2,1,0:T(8,128)(2,1)}), bf16[8,384,128]{2,1,0:T(8,128)(2,1)}, u32[]{:S(2)}, u32[]{:S(2)}) async-start(bf16[8,384,128]{2,1,0:T(8,128)(2,1)} %get-tuple-element.54), calls=%async_computation.2 | async-start | bytes 1572864 | tf_op jit(solution)/shard_map/all_to_all | solution.py:480
  97.7 96.3 %reduce-scatter.2.cloned.1.call-start = ((), (), s32[]{:S(2)}) async-start(), calls=%async_computation.6 | async-start | bytes 2359296 | tf_op jit(solution)/shard_map/reduce_scatter | solution.py:637
  100.4 5.2 %collective-permute-start.10 = (bf16[16,128]{1,0:T(8,128)(2,1)S(1)}, bf16[16,128]{1,0:T(8,128)(2,1)S(1)}, u32[]{:S(2)}, u32[]{:S(2)}) collective-permute-start(bf16[16,128]{1,0:T(8,128)(2,1)S(1)} %get-tuple-element.88), channel_id=1, source_target_pairs={{0,32},{32,8},{8,40},{40,16},{16,48},{48,24},{24,56},{1,33},{33,9}... | collective-permute-start | bytes 12296 | tf_op jit(solution)/shard_map/ppermute | solution.py:474
  104.2 3.1 %collective-permute-start.11 = (bf16[16,128]{1,0:T(8,128)(2,1)S(1)}, bf16[16,128]{1,0:T(8,128)(2,1)S(1)}, u32[]{:S(2)}, u32[]{:S(2)}) collective-permute-start(bf16[16,128]{1,0:T(8,128)(2,1)S(1)} %get-tuple-element.87), channel_id=1, source_target_pairs={{32,0},{8,32},{40,8},{16,40},{48,16},{24,48},{56,24},{33,1},{9,33}... | collective-permute-start | bytes 12296 | tf_op jit(solution)/shard_map/ppermute | solution.py:475
  110.6 11.6 %collective-permute-start.12 = (bf16[416,256]{1,0:T(8,128)(2,1)}, bf16[416,256]{1,0:T(8,128)(2,1)S(1)}, u32[]{:S(2)}, u32[]{:S(2)}) collective-permute-start(bf16[416,256]{1,0:T(8,128)(2,1)} %get-tuple-element.66.refs_1_.refs_4_), channel_id=1, source_target_pairs={{0,64},{64,128},{128,192},{192,0},{1,65},{65,129},{129,193},{193,1... | collective-permute-start | bytes 638984 | tf_op jit(solution)/shard_map/ppermute | solution.py:488
  111.9 10.3 %collective-permute-start.13 = (bf16[416,256]{1,0:T(8,128)(2,1)}, bf16[416,256]{1,0:T(8,128)(2,1)}, u32[]{:S(2)}, u32[]{:S(2)}) collective-permute-start(bf16[416,256]{1,0:T(8,128)(2,1)} %get-tuple-element.66.refs_1_.refs_4_), channel_id=1, source_target_pairs={{0,128},{64,192},{128,0},{192,64},{1,129},{65,193},{129,1},{193,65... | collective-permute-start | bytes 638984 | tf_op jit(solution)/shard_map/ppermute | solution.py:488
  112.4 14.0 %collective-permute-start.14 = (bf16[416,256]{1,0:T(8,128)(2,1)}, bf16[416,256]{1,0:T(8,128)(2,1)}, u32[]{:S(2)}, u32[]{:S(2)}) collective-permute-start(bf16[416,256]{1,0:T(8,128)(2,1)} %get-tuple-element.66.refs_1_.refs_4_), channel_id=1, source_target_pairs={{0,192},{64,0},{128,64},{192,128},{1,193},{65,1},{129,65},{193,129... | collective-permute-start | bytes 638984 | tf_op jit(solution)/shard_map/ppermute | solution.py:488
  135.8 32.6 %all-to-all-start.3 = ((bf16[8,432,128]{2,1,0:T(8,128)(2,1)}), bf16[8,432,128]{2,1,0:T(8,128)(2,1)}, u32[]{:S(2)}, u32[]{:S(2)}) async-start(bf16[8,432,128]{2,1,0:T(8,128)(2,1)} %norm_kernel.1), calls=%async_computation.3 | async-start | bytes 1769472 | tf_op jit(solution)/shard_map/all_to_all | solution.py:480
  147.9 3.4 %collective-permute-start.24 = (bf16[4,512,128]{2,1,0:T(8,128)(2,1)}, bf16[4,512,128]{2,1,0:T(8,128)(2,1)S(1)}, u32[]{:S(2)}, u32[]{:S(2)}) collective-permute-start(bf16[4,512,128]{2,1,0:T(8,128)(2,1)} %get-tuple-element.77), channel_id=1, source_target_pairs={{0,32},{32,0},{1,33},{33,1},{2,34},{34,2},{3,35},{35,3},{4,36},{36... | collective-permute-start | bytes 1572872 | tf_op jit(solution)/shard_map/ppermute | solution.py:496
  149.3 7.5 %collective-permute-start.15 = (bf16[384,128]{1,0:T(8,128)(2,1)}, bf16[384,128]{1,0:T(8,128)(2,1)S(1)}, u32[]{:S(2)}, u32[]{:S(2)}) collective-permute-start(bf16[384,128]{1,0:T(8,128)(2,1)} %get-tuple-element.62), channel_id=1, source_target_pairs={{0,64},{64,128},{128,192},{192,0},{1,65},{65,129},{129,193},{193,1... | collective-permute-start | bytes 294920 | tf_op jit(solution)/shard_map/ppermute | solution.py:488
  149.5 9.9 %collective-permute-start.16 = (bf16[384,128]{1,0:T(8,128)(2,1)}, bf16[384,128]{1,0:T(8,128)(2,1)S(1)}, u32[]{:S(2)}, u32[]{:S(2)}) collective-permute-start(bf16[384,128]{1,0:T(8,128)(2,1)} %get-tuple-element.63), channel_id=1, source_target_pairs={{0,128},{64,192},{128,0},{192,64},{1,129},{65,193},{129,1},{193,65... | collective-permute-start | bytes 294920 | tf_op jit(solution)/shard_map/ppermute | solution.py:488
  149.9 9.5 %collective-permute-start.17 = (bf16[384,128]{1,0:T(8,128)(2,1)}, bf16[384,128]{1,0:T(8,128)(2,1)S(1)}, u32[]{:S(2)}, u32[]{:S(2)}) collective-permute-start(bf16[384,128]{1,0:T(8,128)(2,1)} %get-tuple-element.64), channel_id=1, source_target_pairs={{0,192},{64,0},{128,64},{192,128},{1,193},{65,1},{129,65},{193,129... | collective-permute-start | bytes 294920 | tf_op jit(solution)/shard_map/ppermute | solution.py:488
  152.5 29.4 %collective-permute-start.25 = (bf16[512,128]{1,0:T(8,128)(2,1)S(1)}, bf16[512,128]{1,0:T(8,128)(2,1)S(1)}, u32[]{:S(2)}, u32[]{:S(2)}) collective-permute-start(bf16[512,128]{1,0:T(8,128)(2,1)S(1)} %get-tuple-element.80), channel_id=1, source_target_pairs={{0,8},{8,16},{16,24},{24,0},{1,9},{9,17},{17,25},{25,1},{2,10},{10... | collective-permute-start | bytes 393224 | tf_op jit(solution)/shard_map/ppermute | solution.py:488
  154.9 29.2 %collective-permute-start.26 = (bf16[512,128]{1,0:T(8,128)(2,1)S(1)}, bf16[512,128]{1,0:T(8,128)(2,1)S(1)}, u32[]{:S(2)}, u32[]{:S(2)}) collective-permute-start(bf16[512,128]{1,0:T(8,128)(2,1)S(1)} %get-tuple-element.82), channel_id=1, source_target_pairs={{0,16},{8,24},{16,0},{24,8},{1,17},{9,25},{17,1},{25,9},{2,18},{10... | collective-permute-start | bytes 393224 | tf_op jit(solution)/shard_map/ppermute | solution.py:488
  156.9 30.3 %collective-permute-start.27 = (bf16[512,128]{1,0:T(8,128)(2,1)S(1)}, bf16[512,128]{1,0:T(8,128)(2,1)S(1)}, u32[]{:S(2)}, u32[]{:S(2)}) collective-permute-start(bf16[512,128]{1,0:T(8,128)(2,1)S(1)} %get-tuple-element.81), channel_id=1, source_target_pairs={{0,24},{8,0},{16,8},{24,16},{1,25},{9,1},{17,9},{25,17},{2,26},{10... | collective-permute-start | bytes 393224 | tf_op jit(solution)/shard_map/ppermute | solution.py:488
  172.7 19.4 %collective-permute-start.18 = (bf16[384,256]{1,0:T(8,128)(2,1)}, bf16[384,256]{1,0:T(8,128)(2,1)S(1)}, u32[]{:S(2)}, u32[]{:S(2)}) collective-permute-start(bf16[384,256]{1,0:T(8,128)(2,1)} %get-tuple-element.65), channel_id=1, source_target_pairs={{0,0},{8,64},{16,128},{24,192},{64,8},{72,72},{80,136},{88,200},{1... | collective-permute-start | bytes 589832 | tf_op jit(solution)/shard_map/ppermute | solution.py:465
  174.7 15.9 %collective-permute-start.20 = (f32[40,128]{1,0:T(8,128)S(1)}, f32[40,128]{1,0:T(8,128)S(1)}, u32[]{:S(2)}, u32[]{:S(2)}) collective-permute-start(f32[40,128]{1,0:T(8,128)S(1)} %add.105), channel_id=1, source_target_pairs={{0,0},{8,64},{16,128},{24,192},{64,8},{72,72},{80,136},{88,200},{1... | collective-permute-start | bytes 61448 | tf_op jit(solution)/shard_map/ppermute | solution.py:673
  181.9 8.6 %collective-permute-start.21 = (f32[40,128]{1,0:T(8,128)S(1)}, f32[40,128]{1,0:T(8,128)S(1)}, u32[]{:S(2)}, u32[]{:S(2)}) collective-permute-start(f32[40,128]{1,0:T(8,128)S(1)} %add.105), channel_id=1, source_target_pairs={{0,64},{8,128},{16,192},{24,0},{64,72},{72,136},{80,200},{88,8},{1... | collective-permute-start | bytes 61448 | tf_op jit(solution)/shard_map/ppermute | solution.py:673
  184.1 6.5 %collective-permute-start.22 = (f32[40,128]{1,0:T(8,128)S(1)}, f32[40,128]{1,0:T(8,128)S(1)}, u32[]{:S(2)}, u32[]{:S(2)}) collective-permute-start(f32[40,128]{1,0:T(8,128)S(1)} %add.105), channel_id=1, source_target_pairs={{0,128},{8,192},{16,0},{24,64},{64,136},{72,200},{80,8},{88,72},{1... | collective-permute-start | bytes 61448 | tf_op jit(solution)/shard_map/ppermute | solution.py:673
  187.1 5.0 %collective-permute-start.23 = (f32[40,128]{1,0:T(8,128)S(1)}, f32[40,128]{1,0:T(8,128)S(1)}, u32[]{:S(2)}, u32[]{:S(2)}) collective-permute-start(f32[40,128]{1,0:T(8,128)S(1)} %add.105), channel_id=1, source_target_pairs={{0,192},{8,0},{16,64},{24,128},{64,200},{72,8},{80,72},{88,136},{1... | collective-permute-start | bytes 61448 | tf_op jit(solution)/shard_map/ppermute | solution.py:673
  (17 other events, 277.3 us)
Sparse Core Ops, SparseCore 0:
  9.9 35.8 all-gather.1
  135.9 40.9 reduce-scatter.1

commit v8 on v6

--- a/solution.py
+++ b/solution.py
@@ -149,7 +149,7 @@
     return jax.ShapeDtypeStruct(dims, kind)
 
 
-def project_kernel(arrive, send, place_ref, frames_ref, gain_ref, gain_rows_ref, weight_ref, *refs):
+def project_kernel(arrive, send, place_ref, frames_ref, gain_ref, weight_ref, *refs):
     left_ref = refs[NX]
     total = jnp.zeros((ROWS, 1), f32)
     square = jnp.zeros((ROWS, 1), f32)
@@ -158,17 +158,19 @@
         total = total + jnp.sum(wide, axis=1, keepdims=True)
         square = square + jnp.sum(wide * wide, axis=1, keepdims=True)
     mean = total / QUARTER
+    arrive(2)
+    gain = gain_ref[...]
+    gain_rows = stacked_rows(split3(gain)).astype(bf16)
     for i in range(NZ):
         cut = pl.ds(i * COLS, COLS)
         scaled = (frames_ref[i].astype(f32) - mean) * gain_ref[0:1, cut]
         left_ref[:, cut] = scaled.astype(bf16)
     sums = columns_to_rows(total, square).astype(bf16)
-    arrive(4)
     for j, out_ref in enumerate(refs[:NX]):
         start = pl.multiple_of(place_ref[4 + j] * QUARTER, QUARTER)
-        weight = weight_ref[pl.ds(start, QUARTER), :]
+        weight = weight_ref[pl.ds(start, QUARTER), 0 : 2 * COLS]
         out_ref[0:ROWS, :] = dot(left_ref[...], weight, 1, 0).astype(bf16)
-        unit = jnp.sum(dot(gain_rows_ref[...], weight, 1, 0), axis=0, keepdims=True)
+        unit = jnp.sum(dot(gain_rows, weight, 1, 0), axis=0, keepdims=True)
         out_ref[ROWS : ROWS + 16, :] = stacked_rows(split3(unit)).astype(bf16)
         out_ref[ROWS + 16 : ROWS + 32, :] = sums[:, 0:256]
         out_ref[ROWS + 32 : ROWS + 48, 0:128] = sums[:, 256:384]
@@ -206,7 +208,7 @@
     total = jnp.zeros((ROWS, QUARTER), f32)
     for j, grad_ref in enumerate((g0_ref, g1_ref, g2_ref, g3_ref)):
         start = pl.multiple_of(place_ref[j] * QUARTER, QUARTER)
-        weight = weight_ref[pl.ds(start, QUARTER), :]
+        weight = weight_ref[pl.ds(start, QUARTER), 2 * COLS : 3 * COLS]
         total = total + dot(grad_ref[...], weight, 1, 1)
     for i in range(NZ):
         out_ref[i] = total[:, i * COLS : (i + 1) * COLS].astype(bf16)
@@ -325,13 +327,13 @@
     first = rows[0:1] + rows[1:2] + rows[2:3]
     second = rows[3:4] + rows[4:5] + rows[5:6]
     sums = stacked_rows(split3(first) + split3(second)).astype(bf16)
-    arrive(5)
     step = 2 * COLS
     for part in range(QUARTER // step):
         total = jnp.zeros((ROWS, step), f32)
         for j, grad_ref in enumerate(grads):
             start = pl.multiple_of(place_ref[j] * QUARTER + part * step, step)
-            total = total + dot(grad_ref[0:ROWS, :], weight_ref[pl.ds(start, step), :], 1, 1)
+            weight = weight_ref[pl.ds(start, step), 0 : 2 * COLS]
+            total = total + dot(grad_ref[0:ROWS, :], weight, 1, 1)
         for i in (2 * part, 2 * part + 1):
             cut = (i - 2 * part) * COLS
             out_ref[i, 0:ROWS, :] = total[:, cut : cut + COLS].astype(bf16)
@@ -380,19 +382,24 @@
                 out_ref[:, i * lanes : (i + 1) * lanes] = block_ref[0:ROWS, :]
 
 
-def out_kernel(place_ref, act_ref, g0_ref, g1_ref, g2_ref, g3_ref, weight_ref, *refs):
-    enc_refs = refs[:NX]
-    kept_ref, given_ref, left_ref, grad_ref = refs[NX:]
+def encode_kernel(arrive, send, place_ref, act_ref, weight_ref, *refs):
+    left_ref = refs[NX]
+    arrive(1)
+    for i in range(NZ):
+        left_ref[:, pl.ds(i * COLS, COLS)] = act_ref[i, 0:ROWS, :]
+    for j, enc_ref in enumerate(refs[:NX]):
+        start = pl.multiple_of(place_ref[4 + j] * QUARTER, QUARTER)
+        weight = weight_ref[pl.ds(start, QUARTER), 2 * COLS : 3 * COLS]
+        enc_ref[...] = dot(left_ref[...], weight, 1, 0).astype(bf16)
+        send(j)
+
+
+def out_kernel(
+    place_ref, act_ref, g0_ref, g1_ref, g2_ref, g3_ref, kept_ref, given_ref, left_ref, grad_ref
+):
     half = QUARTER // NK
     for i in range(NZ):
         left_ref[i * COLS // half, :, pl.ds(i * COLS % half, COLS)] = act_ref[i, 0:ROWS, :]
-    for j, enc_ref in enumerate(enc_refs):
-        total = jnp.zeros((ROWS, COLS), f32)
-        for h in range(NK):
-            start = pl.multiple_of(place_ref[4 + j] * QUARTER + h * half, half)
-            weight = weight_ref[pl.ds(start, half), :]
-            total = total + dot(left_ref[h], weight, 1, 0)
-        enc_ref[...] = total.astype(bf16)
     order_blocks(place_ref, 0, (g0_ref, g1_ref, g2_ref, g3_ref), grad_ref, COLS)
     core = place_ref[9]
     for out_ref, which in ((given_ref, 1 - core), (kept_ref, core)):
@@ -401,7 +408,19 @@
             out_ref[i] = out[:, i * COLS : (i + 1) * COLS]
 
 
-def input_kernel(parts_ref, frames_ref, grad_ref, stat_ref, gain_ref, out_ref, small_ref):
+def input_kernel(
+    parts_ref,
+    frames_ref,
+    grad_ref,
+    stat_ref,
+    gain_ref,
+    e0_ref,
+    e1_ref,
+    e2_ref,
+    e3_ref,
+    out_ref,
+    small_ref,
+):
     normed_grad = jnp.zeros((ROWS, COLS), f32)
     rows = jnp.zeros((16, ROWS), f32)
     for i in range(NZ):
@@ -417,7 +436,11 @@
     centred = (frames_ref[...].astype(f32) - mean) * inv_std
     hat = normed_grad * gain_ref[0:1, :]
     out = grad_ref[...].astype(f32) + inv_std * (hat - first / WIDTH - centred * (second / WIDTH))
-    out_ref[...] = out.astype(bf16)
+    out_ref[:, COLS:] = out.astype(bf16)
+    encoded = frames_ref[...].astype(f32)
+    for part_ref in (e0_ref, e1_ref, e2_ref, e3_ref):
+        encoded = encoded + part_ref[...].astype(f32)
+    out_ref[:, 0:COLS] = encoded.astype(bf16)
     gain_term = jnp.sum(normed_grad * centred, axis=0, keepdims=True)
     small_ref[...] = jnp.broadcast_to(gain_term, (8, COLS))
 
@@ -456,10 +479,11 @@
 def reduced(kept, given):
     other = lax.ppermute(given, "k", [(0, 1), (1, 0)])
     both = [(kept[i].astype(f32) + other[i].astype(f32)) for i in range(NY)]
+    sent = [part.astype(bf16) for part in both[1:]]
     total = both[0]
     for i in range(1, NY):
-        total = total + shifted(both[i].astype(bf16), "y", NY, i).astype(f32)
-    return total
+        total = total + shifted(sent[i - 1], "y", NY, i).astype(f32)
+    return total, sent
 
 
 def pieces(value):
@@ -482,7 +506,6 @@
     col_start = (x_index * NZ + lax.axis_index("z")) * COLS
     local_gain = lax.dynamic_slice_in_dim(gain, col_start, COLS, 0)[None]
     quarter_gain = lax.dynamic_slice_in_dim(gain, x_index * QUARTER, QUARTER, 0)[None]
-    gain_rows = jnp.pad(pieces(quarter_gain)[:, 0], ((0, 13), (0, 0)))
     y_index = lax.axis_index("y")
     steps = jnp.arange(NX, dtype=jnp.int32)
     below = (x_index + NX - steps) % NX
@@ -505,17 +528,16 @@
     grads = spread(grad_out, "x", NX)
 
     act_parts = call(
-        act_kernel, shape((NZ, ROWS, COLS), bf16), (place, *grads, weights), smem=(0,), near=(1, 2, 3, 4), cuts={5: OUT}
+        act_kernel, shape((NZ, ROWS, COLS), bf16), (place, *grads, weights), smem=(0,), near=(1, 2, 3, 4, 5)
     )
     act_moved = exchange(act_parts, "z")
     pre_parts = call(
         project_kernel,
         [shape((ROWS + 48, 2 * COLS), bf16) for _ in range(NX)],
-        (place, after(frames_z, act_parts), quarter_gain, gain_rows, weights),
+        (place, after(frames_z, act_parts), quarter_gain, weights),
         smem=(0,),
-        near=(1,),
-        late=(4,),
-        cuts={4: IN},
+        near=(1, 3),
+        late=(2,),
         scratch=[pltpu.VMEM((ROWS, QUARTER), bf16)],
     )
     pre_moved = [pre_parts[0]] + [shifted(pre_parts[j], "x", NX, j) for j in range(1, NX)]
@@ -563,9 +585,8 @@
         shape((NZ, ROWS + 48, COLS), bf16),
         (place, *vg_grads, weights),
         smem=(0,),
-        near=(2, 3, 4),
-        late=(1, 5),
-        cuts={5: IN},
+        near=(2, 3, 4, 5),
+        late=(1,),
     )
     norm_moved = exchange(norm_parts, "z")
     held = lax.optimization_barrier((vg_grads, norm_parts))[0]
@@ -580,38 +601,43 @@
             pltpu.VMEM((ROWS, NY * 2 * COLS), bf16),
         ],
     )
-    in_weight = reduced(kept, given)
-
-    out_parts = call(
+    in_weight, in_sent = reduced(kept, given)
+
+    enc_parts = call(
+        encode_kernel,
+        [shape((ROWS, COLS), bf16) for _ in range(NX)],
+        (place, act_z, after(weights, in_sent)),
+        smem=(0,),
+        near=(2,),
+        late=(1,),
+        scratch=[pltpu.VMEM((ROWS, QUARTER), bf16)],
+    )
+    enc = [enc_parts[0]] + [shifted(enc_parts[j], "x", NX, j) for j in range(1, NX)]
+    kept, given = call(
         out_kernel,
-        [shape((ROWS, COLS), bf16) for _ in range(NX)]
-        + [shape((NY, QUARTER // NK, COLS), bf16) for _ in range(2)],
-        (place, act_z, *after(grads, norm_parts), weights),
+        [shape((NY, QUARTER // NK, COLS), bf16) for _ in range(2)],
+        (place, after(act_z, enc_parts), *grads),
         smem=(0,),
-        cuts={6: OUT},
         scratch=[
             pltpu.VMEM((NK, ROWS, QUARTER // NK), bf16),
             pltpu.VMEM((ROWS, NY * COLS), bf16),
         ],
     )
-    kept, given = out_parts[NX:]
     other = lax.ppermute(given, "k", [(0, 1), (1, 0)])
     both = (kept.astype(f32) + other.astype(f32)).astype(bf16)
     grad_out_weight = lax.psum_scatter(
         both.reshape(NY * QUARTER // NK, COLS), "y", scatter_dimension=0, tiled=True
     ).astype(f32)
-    enc_sum = out_parts[0].astype(f32)
-    for j in range(1, NX):
-        enc_sum = enc_sum + shifted(out_parts[j], "x", NX, j).astype(f32)
-    encoded = swap_xy((frames.astype(f32) + enc_sum).astype(bf16))
-
-    input_grad, gain_term = call(
+
+    results, gain_term = call(
         input_kernel,
-        [shape((ROWS, COLS), bf16), shape((8, COLS), f32)],
-        (after(norm_moved, *out_parts), frames, grad_out, stat, local_gain),
-        near=(0,),
-    )
-    input_grad = swap_xy(input_grad)
+        [shape((ROWS, 2 * COLS), bf16), shape((8, COLS), f32)],
+        (after(norm_moved, both), frames, grad_out, stat, local_gain, *enc),
+        near=(0, 6, 7, 8),
+    )
+    results = swap_xy(results)
+    encoded = results[:, :COLS]
+    input_grad = results[:, COLS:]
 
     small = jnp.concatenate([small, gain_term], axis=0)
     small = small + lax.ppermute(small, "k", [(0, 1), (1, 0)])
@@ -621,7 +647,7 @@
             (a * NY + b, ((b + shift) % NX) * NY + a) for a in range(NX) for b in range(NY)
         ]
         arrived.append(lax.ppermute(small, ("x", "y"), route))
-    small, input_grad = lax.optimization_barrier((sum(arrived), input_grad))
+    small = sum(after(arrived, results))
     return (
         encoded,
         input_grad,

time: 214 us -> 206 us (0.963); the launches traced: 210 us -> 205 us
  waiting for transfers between devices: 72.2 us -> 65.8 us
  starting transfers between devices: 73.6 us -> 69.2 us
  local copies, waits for them, and re-layouts: 8.46 us -> 11 us
  Pallas kernels: 33.1 us -> 35.3 us
    ppermute x4 -> x3, waiting for transfers between devices: 22.9 us -> 13.9 us  [swap_xy(): lax.ppermute(block, ('x', 'y'), [(a * NY + b, b * NY + a) for a in range(...]
    ppermute x4 -> x3, starting transfers between devices: 19.5 us -> 13.2 us  [swap_xy(): lax.ppermute(block, ('x', 'y'), [(a * NY + b, b * NY + a) for a in range(...]
    ppermute x4, waiting for transfers between devices: 0.01 us -> 4.58 us  [shards(): arrived.append(lax.ppermute(small, ('x', 'y'), route))]
    ppermute x15, waiting for transfers between devices: 33 us -> 29.5 us  [shifted(): lax.ppermute(block, axis, [(i, (i + shift) % count) for i in range(count)])]
    reduce_scatter x1, waiting for transfers between devices: 0.01 us -> 3.43 us  [shards(): lax.psum_scatter(both.reshape(NY * QUARTER // NK, COLS), 'y', scatter_dim...]
    pallas_call x9 -> x10, Pallas kernels: 33.1 us -> 35.3 us  [call(): pl.pallas_call(whole, out_shape=[pltpu.HBM(out.shape, out.dtype) for out...]
  transfers between devices with their start and end apart: 34 -> 33, of which waited for: 17 -> 17; matrix products, arithmetic and copies ran while one was open for 6% -> 7% of each run, Pallas kernels for 13% -> 14%
where the time goes in v8:
time: 206 us; the launch traced here: 205 us
  starting transfers between devices  69.2 us (34%)
  waiting for transfers between devices  65.8 us (32%)
  Pallas kernels  35.3 us (17%)
  between operations  14.2 us (7%)
  local copies, waits for them, and re-layouts  11 us (5%)
  other arithmetic  9.1 us (4%)
    pallas_call x10, Pallas kernels, call(): pl.pallas_call(whole, out_shape=[pltpu.HBM(out.shape, out.dtype) for out...  35.3 us
    ppermute x15, waiting for transfers between devices, shifted(): lax.ppermute(block, axis, [(i, (i + shift) % count) for i in range(count)])  29.5 us
    all_to_all x3, starting transfers between devices, exchange(): return lax.all_to_all(parts, axis, 0, 0, tiled=True)  22.8 us
    ppermute x15, starting transfers between devices, shifted(): lax.ppermute(block, axis, [(i, (i + shift) % count) for i in range(count)])  19.3 us
    ppermute x3, waiting for transfers between devices, swap_xy(): lax.ppermute(block, ('x', 'y'), [(a * NY + b, b * NY + a) for a in range(...  13.9 us
    all_gather x1, waiting for transfers between devices, shards(): act_z = lax.all_gather(activated, 'z', axis=0, tiled=False)  13.5 us
    ppermute x3, starting transfers between devices, swap_xy(): lax.ppermute(block, ('x', 'y'), [(a * NY + b, b * NY + a) for a in range(...  13.2 us
    ppermute x4, starting transfers between devices, shards(): arrived.append(lax.ppermute(small, ('x', 'y'), route))  9.18 us
  transfers between devices with their start and end apart: 33, of which 17 were waited for; matrix products, arithmetic and copies ran while one was open for 7% of the time, Pallas kernels for 14%

profile of v8, /device:TPU:6, one launch (start us, length us, event | category | flops | bytes accessed | tf_op | source)
XLA Modules:
  0.0 204.6 jit_solution(17513674661979505323)
XLA Ops:
  9.1 4.8 %collective-permute-start = (bf16[384,128]{1,0:T(8,128)(2,1)}, bf16[384,128]{1,0:T(8,128)(2,1)S(1)}, u32[]{:S(2)}, u32[]{:S(2)}) collective-permute-start(bf16[384,128]{1,0:T(8,128)(2,1)} %param.8), channel_id=1, source_target_pairs={{0,0},{8,64},{16,128},{24,192},{64,8},{72,72},{80,136},{88,200},{1... | collective-permute-start | bytes 294920 | tf_op jit(solution)/shard_map/ppermute | solution.py:449
  14.0 7.3 %collective-permute-done.refs_1_ = bf16[384,128]{1,0:T(8,128)(2,1)S(1)} collective-permute-done((bf16[384,128]{1,0:T(8,128)(2,1)}, bf16[384,128]{1,0:T(8,128)(2,1)S(1)}, u32[]{:S(2)}, u32[]{:S(2)}) %collective-permute-start) | collective-permute-done | bytes 98336 | tf_op jit(solution)/shard_map/ppermute | solution.py:449
  22.9 8.5 %all-to-all-start = ((bf16[8,384,128]{2,1,0:T(8,128)(2,1)}), bf16[8,384,128]{2,1,0:T(8,128)(2,1)}, u32[]{:S(2)}, u32[]{:S(2)}) async-start(bf16[8,384,128]{2,1,0:T(8,128)(2,1)} %broadcast_in_dim.6), calls=%async_computation | async-start | bytes 1572864 | tf_op jit(solution)/shard_map/all_to_all | solution.py:464
  31.5 4.8 %collective-permute-start.1 = (bf16[480,128]{1,0:T(8,128)(2,1)S(1)}, bf16[480,128]{1,0:T(8,128)(2,1)S(1)}, u32[]{:S(2)}, u32[]{:S(2)}) collective-permute-start(bf16[480,128]{1,0:T(8,128)(2,1)S(1)} %pad_maximum_fusion.1), channel_id=1, source_target_pairs={{0,0},{8,64},{16,128},{24,192},{64,8},{72,72},{80,136},{88,200},{1... | collective-permute-start | bytes 368648 | tf_op jit(solution)/shard_map/ppermute | solution.py:449
  36.3 6.6 %collective-permute-done.1.refs_5_ = bf16[480,128]{1,0:T(8,128)(2,1)S(1)} collective-permute-done((bf16[480,128]{1,0:T(8,128)(2,1)S(1)}, bf16[480,128]{1,0:T(8,128)(2,1)S(1)}, u32[]{:S(2)}, u32[]{:S(2)}) %collective-permute-start.1) | collective-permute-done | bytes 122912 | tf_op jit(solution)/shard_map/ppermute | solution.py:449
  53.1 2.5 %act_kernel.1 = bf16[8,384,128]{2,1,0:T(8,128)(2,1)} custom-call(s32[14]{0:T(128)S(1)} %concatenate.49.refs_0_, bf16[384,128]{1,0:T(8,128)(2,1)S(1)} %slice.80.refs_1_.refs_2_, bf16[384,128]{1,0:T(8,128)(2,1)S(1)} %collective-permute-done.2.refs_2_.refs_3_, bf16[384,128]{1,0:T(8,128)(2,1)S(1)} %collective-permute-done.3.refs_3_.refs_4_, ...), custom_call_target="tpu_custom_call" | custom-call | tf_op jit(solution)/shard_map/act_kernel/pallas_call | solution.py:131
  55.6 7.2 %all-to-all-start.1 = ((bf16[8,384,128]{2,1,0:T(8,128)(2,1)}), bf16[8,384,128]{2,1,0:T(8,128)(2,1)}, u32[]{:S(2)}, u32[]{:S(2)}) async-start(bf16[8,384,128]{2,1,0:T(8,128)(2,1)} %act_kernel.1), calls=%async_computation.1 | async-start | bytes 1572864 | tf_op jit(solution)/shard_map/all_to_all | solution.py:464
  64.1 4.3 %project_kernel.1 = (bf16[432,256]{1,0:T(8,128)(2,1)}, bf16[432,256]{1,0:T(8,128)(2,1)}, bf16[432,256]{1,0:T(8,128)(2,1)}, bf16[432,256]{1,0:T(8,128)(2,1)}) custom-call(s32[14]{0:T(128)S(1)} %concatenate.49.refs_0_, bf16[8,384,128]{2,1,0:T(8,128)(2,1)} %all-to-all-done.refs_1_, f32[1,1024]{1,0:T(1,128)} %bitcast.30, bf16[4096,384]{1,0:T(8,128)(2,1)S(1)} %copy-done.1), custom_call_target="tpu_custom_call" | custom-call | tf_op jit(solution)/shard_map/project_kernel/pallas_call | solution.py:131
  71.1 3.6 %collective-permute-done.5.refs_1_ = bf16[432,256]{1,0:T(8,128)(2,1)S(1)} collective-permute-done((bf16[432,256]{1,0:T(8,128)(2,1)}, bf16[432,256]{1,0:T(8,128)(2,1)S(1)}, u32[]{:S(2)}, u32[]{:S(2)}) %collective-permute-start.5) | collective-permute-done | bytes 221216 | tf_op jit(solution)/shard_map/ppermute | solution.py:472
  74.7 2.8 %collective-permute-done.6.refs_2_ = bf16[432,256]{1,0:T(8,128)(2,1)S(1)} collective-permute-done((bf16[432,256]{1,0:T(8,128)(2,1)}, bf16[432,256]{1,0:T(8,128)(2,1)S(1)}, u32[]{:S(2)}, u32[]{:S(2)}) %collective-permute-start.6) | collective-permute-done | bytes 221216 | tf_op jit(solution)/shard_map/ppermute | solution.py:472
  79.7 3.0 %gate_kernel.1 = (f32[384,256]{1,0:T(8,128)}, bf16[384,128]{1,0:T(8,128)(2,1)}, f32[8,256]{1,0:T(8,128)}, f32[384,128]{1,0:T(8,128)}) custom-call(bf16[432,256]{1,0:T(8,128)(2,1)} %get-tuple-element.42.refs_0_, bf16[432,256]{1,0:T(8,128)(2,1)S(1)} %collective-permute-done.5.refs_1_, bf16[432,256]{1,0:T(8,128)(2,1)S(1)} %collective-permute-done.6.refs_2_, ...), custom_call_target="tpu_custom_call" | custom-call | tf_op jit(solution)/shard_map/gate_kernel/pallas_call | solution.py:131
  87.5 3.0 %collective-permute-start.8 = (bf16[48,128]{1,0:T(8,128)(2,1)S(1)}, bf16[48,128]{1,0:T(8,128)(2,1)S(1)}, u32[]{:S(2)}, u32[]{:S(2)}) collective-permute-start(bf16[48,128]{1,0:T(8,128)(2,1)S(1)} %pad_maximum_fusion.4), channel_id=1, source_target_pairs={{0,32},{32,8},{8,40},{40,16},{16,48},{48,24},{24,56},{1,33},{33,9}... | collective-permute-start | bytes 36872 | tf_op jit(solution)/shard_map/ppermute | solution.py:458
  91.3 4.0 %conv_kernel.1 = (bf16[512,128]{1,0:T(8,128)(2,1)}, bf16[416,256]{1,0:T(8,128)(2,1)}, f32[32,128]{1,0:T(8,128)}) custom-call(s32[1]{0:T(128)} %bitcast.refs_0_, bf16[384,128]{1,0:T(8,128)(2,1)} %get-tuple-element.46.refs_1_, bf16[384,128]{1,0:T(8,128)(2,1)} %sum_kernel.1.refs_2_, bf16[48,128]{1,0:T(8,128)(2,1)S(1)} %collective-permute-done.8.refs_3_, ...), custom_call_target="tpu_custom_call" | custom-call | tf_op jit(solution)/shard_map/conv_kernel/pallas_call | solution.py:131
  98.6 5.3 %collective-permute-done.10.refs_2_.refs_5_ = bf16[416,256]{1,0:T(8,128)(2,1)S(1)} collective-permute-done((bf16[416,256]{1,0:T(8,128)(2,1)}, bf16[416,256]{1,0:T(8,128)(2,1)S(1)}, u32[]{:S(2)}, u32[]{:S(2)}) %collective-permute-start.10) | collective-permute-done | bytes 213024 | tf_op jit(solution)/shard_map/ppermute | solution.py:472
  106.1 3.6 %collective-permute-done.12.refs_4_.refs_7_ = bf16[416,256]{1,0:T(8,128)(2,1)S(1)} collective-permute-done((bf16[416,256]{1,0:T(8,128)(2,1)}, bf16[416,256]{1,0:T(8,128)(2,1)S(1)}, u32[]{:S(2)}, u32[]{:S(2)}) %collective-permute-start.12) | collective-permute-done | bytes 213024 | tf_op jit(solution)/shard_map/ppermute | solution.py:472
  109.7 3.4 %norm_kernel.1 = bf16[8,432,128]{2,1,0:T(8,128)(2,1)} custom-call(s32[14]{0:T(128)S(1)} %concatenate.49.refs_0_, bf16[416,256]{1,0:T(8,128)(2,1)} %get-tuple-element.52.refs_1_.refs_4_, bf16[416,256]{1,0:T(8,128)(2,1)S(1)} %collective-permute-done.10.refs_2_.refs_5_, bf16[416,256]{1,0:T(8,128)(2,1)S(1)} %collective-permute-done.11.refs_3_.refs_6_, ...), custom_call_target="tpu_custom_call" | custom-call | tf_op jit(solution)/shard_map/norm_kernel/pallas_call | solution.py:131
  113.1 5.0 %weight_kernel.1 = (bf16[4,512,256]{2,1,0:T(8,128)(2,1)}, bf16[4,512,256]{2,1,0:T(8,128)(2,1)}) custom-call(s32[14]{0:T(128)S(1)} %concatenate.49.refs_0_, bf16[8,384,128]{2,1,0:T(8,128)(2,1)} %all-to-all-done.refs_1_, f32[1,1024]{1,0:T(1,128)} %bitcast.31, f32[384,128]{1,0:T(8,128)} %get-tuple-element.51.refs_3_, ...), custom_call_target="tpu_custom_call" | custom-call | tf_op jit(solution)/shard_map/weight_kernel/pallas_call | solution.py:131
  118.2 7.2 %all-to-all-start.2 = ((bf16[8,432,128]{2,1,0:T(8,128)(2,1)}), bf16[8,432,128]{2,1,0:T(8,128)(2,1)}, u32[]{:S(2)}, u32[]{:S(2)}) async-start(bf16[8,432,128]{2,1,0:T(8,128)(2,1)} %norm_kernel.1), calls=%async_computation.2 | async-start | bytes 1769472 | tf_op jit(solution)/shard_map/all_to_all | solution.py:464
  125.4 2.3 %fusion.4 = (bf16[512,256]{1,0:T(8,128)(2,1)S(1)}, bf16[512,256]{1,0:T(8,128)(2,1)}, bf16[512,256]{1,0:T(8,128)(2,1)}) fusion(bf16[4,512,256]{2,1,0:T(8,128)(2,1)} %collective-permute-done.13, bf16[4,512,256]{2,1,0:T(8,128)(2,1)} %get-tuple-element.56), kind=kLoop, calls=%fused_computation.10 | loop fusion | flops 1572864 | bytes 2359296 | tf_op jit(solution)/shard_map/convert_element_type | solution.py:482
  127.8 13.5 %all-gather.6.cloned.1.call-done = bf16[4096,128]{1,0:T(8,128)(2,1)} async-done(((bf16[512,128]{1,0:T(8,128)(2,1)}), bf16[4096,128]{1,0:T(8,128)(2,1)}) %all-gather.6.cloned.1.call-update) | async-done | bytes 1048592 | tf_op jit(solution)/shard_map/all_gather | solution.py:580
  141.3 3.5 %encode_kernel.1 = (bf16[384,128]{1,0:T(8,128)(2,1)}, bf16[384,128]{1,0:T(8,128)(2,1)}, bf16[384,128]{1,0:T(8,128)(2,1)}, bf16[384,128]{1,0:T(8,128)(2,1)}) custom-call(s32[14]{0:T(128)S(1)} %concatenate.49.refs_0_, bf16[8,512,128]{2,1,0:T(8,128)(2,1)} %bitcast.26, bf16[4096,384]{1,0:T(8,128)(2,1)S(1)} %copy-done.1), custom_call_target="tpu_custom_call" | custom-call | tf_op jit(solution)/shard_map/encode_kernel/pallas_call | solution.py:131
  144.8 3.9 %out_kernel.1 = (bf16[4,512,128]{2,1,0:T(8,128)(2,1)}, bf16[4,512,128]{2,1,0:T(8,128)(2,1)}) custom-call(s32[14]{0:T(128)S(1)} %concatenate.49.refs_0_, bf16[8,512,128]{2,1,0:T(8,128)(2,1)} %bitcast.27, bf16[384,128]{1,0:T(8,128)(2,1)} %copy-done.2, bf16[384,128]{1,0:T(8,128)(2,1)} %copy-done.3, bf16[384,128]{1,0:T(8,128)(2,1)} %copy-done.4, ...), custom_call_target="tpu_custom_call" | custom-call | tf_op jit(solution)/shard_map/out_kernel/pallas_call | solution.py:131
  150.2 2.5 %collective-permute-start.19 = (bf16[512,256]{1,0:T(8,128)(2,1)}, bf16[512,256]{1,0:T(8,128)(2,1)S(1)}, u32[]{:S(2)}, u32[]{:S(2)}) collective-permute-start(bf16[512,256]{1,0:T(8,128)(2,1)} %get-tuple-element.76), channel_id=1, source_target_pairs={{0,8},{8,16},{16,24},{24,0},{1,9},{9,17},{17,25},{25,1},{2,10},{10... | collective-permute-start | bytes 786440 | tf_op jit(solution)/shard_map/ppermute | solution.py:472
  152.7 3.5 %collective-permute-start.20 = (bf16[512,256]{1,0:T(8,128)(2,1)}, bf16[512,256]{1,0:T(8,128)(2,1)S(1)}, u32[]{:S(2)}, u32[]{:S(2)}) collective-permute-start(bf16[512,256]{1,0:T(8,128)(2,1)} %get-tuple-element.75), channel_id=1, source_target_pairs={{0,16},{8,24},{16,0},{24,8},{1,17},{9,25},{17,1},{25,9},{2,18},{10... | collective-permute-start | bytes 786440 | tf_op jit(solution)/shard_map/ppermute | solution.py:472
  156.2 5.0 %collective-permute-start.16 = (bf16[384,128]{1,0:T(8,128)(2,1)}, bf16[384,128]{1,0:T(8,128)(2,1)S(1)}, u32[]{:S(2)}, u32[]{:S(2)}) collective-permute-start(bf16[384,128]{1,0:T(8,128)(2,1)} %get-tuple-element.61), channel_id=1, source_target_pairs={{0,128},{64,192},{128,0},{192,64},{1,129},{65,193},{129,1},{193,65... | collective-permute-start | bytes 294920 | tf_op jit(solution)/shard_map/ppermute | solution.py:472
  164.6 2.7 %collective-permute-done.17.refs_8_ = bf16[384,128]{1,0:T(8,128)(2,1)S(1)} collective-permute-done((bf16[384,128]{1,0:T(8,128)(2,1)}, bf16[384,128]{1,0:T(8,128)(2,1)S(1)}, u32[]{:S(2)}, u32[]{:S(2)}) %collective-permute-start.17) | collective-permute-done | bytes 98336 | tf_op jit(solution)/shard_map/ppermute | solution.py:472
  167.3 3.6 %input_kernel.1 = (bf16[384,256]{1,0:T(8,128)(2,1)}, f32[8,128]{1,0:T(8,128)}) custom-call(bf16[8,432,128]{2,1,0:T(8,128)(2,1)} %all-to-all-done.2.refs_0_, bf16[384,128]{1,0:T(8,128)(2,1)} %copy-done.7, bf16[384,128]{1,0:T(8,128)(2,1)} %copy-done.2, f32[384,128]{1,0:T(8,128)} %get-tuple-element.51.refs_3_, f32[1,128]{1,0:T(1,128)} %dynamic-slice_bitcast_fusion.refs_4_, ...), custom_call_target="tpu_custom_call" | custom-call | tf_op jit(solution)/shard_map/input_kernel/pallas_call | solution.py:131
  172.8 3.6 %collective-permute-start.18 = (bf16[384,256]{1,0:T(8,128)(2,1)}, bf16[384,256]{1,0:T(8,128)(2,1)S(1)}, u32[]{:S(2)}, u32[]{:S(2)}) collective-permute-start(bf16[384,256]{1,0:T(8,128)(2,1)} %get-tuple-element.67), channel_id=1, source_target_pairs={{0,0},{8,64},{16,128},{24,192},{64,8},{72,72},{80,136},{88,200},{1... | collective-permute-start | bytes 589832 | tf_op jit(solution)/shard_map/ppermute | solution.py:449
  176.5 5.5 %collective-permute-start.23 = (f32[40,128]{1,0:T(8,128)S(1)}, f32[40,128]{1,0:T(8,128)S(1)}, u32[]{:S(2)}, u32[]{:S(2)}) collective-permute-start(f32[40,128]{1,0:T(8,128)S(1)} %add.115), channel_id=1, source_target_pairs={{0,0},{8,64},{16,128},{24,192},{64,8},{72,72},{80,136},{88,200},{1... | collective-permute-start | bytes 61448 | tf_op jit(solution)/shard_map/ppermute | solution.py:649
  182.1 3.0 %collective-permute-start.24 = (f32[40,128]{1,0:T(8,128)S(1)}, f32[40,128]{1,0:T(8,128)S(1)}, u32[]{:S(2)}, u32[]{:S(2)}) collective-permute-start(f32[40,128]{1,0:T(8,128)S(1)} %add.115), channel_id=1, source_target_pairs={{0,64},{8,128},{16,192},{24,0},{64,72},{72,136},{80,200},{88,8},{1... | collective-permute-start | bytes 61448 | tf_op jit(solution)/shard_map/ppermute | solution.py:649
  186.5 4.6 %collective-permute-done.23 = f32[40,128]{1,0:T(8,128)S(1)} collective-permute-done((f32[40,128]{1,0:T(8,128)S(1)}, f32[40,128]{1,0:T(8,128)S(1)}, u32[]{:S(2)}, u32[]{:S(2)}) %collective-permute-start.23) | collective-permute-done | bytes 20512 | tf_op jit(solution)/shard_map/ppermute | solution.py:649
  193.0 3.4 %reduce-scatter.2.cloned.1.call-done = bf16[512,128]{1,0:T(8,128)(2,1)} async-done(((bf16[2048,128]{1,0:T(8,128)(2,1)}), bf16[512,128]{1,0:T(8,128)(2,1)}) %reduce-scatter.2.cloned.1.call-update) | async-done | bytes 131088 | tf_op jit(solution)/shard_map/reduce_scatter | solution.py:628
  (98 shorter events, 42.7 us)
Async XLA Ops:
  7.2 43.9 %all-gather.4.cloned.1.call-start = ((), (), s32[]{:S(2)}) async-start(), calls=%async_computation.4 | async-start | bytes 3538944 | tf_op jit(solution)/shard_map/all_gather | solution.py:518
  9.1 12.1 %collective-permute-start = (bf16[384,128]{1,0:T(8,128)(2,1)}, bf16[384,128]{1,0:T(8,128)(2,1)S(1)}, u32[]{:S(2)}, u32[]{:S(2)}) collective-permute-start(bf16[384,128]{1,0:T(8,128)(2,1)} %param.8), channel_id=1, source_target_pairs={{0,0},{8,64},{16,128},{24,192},{64,8},{72,72},{80,136},{88,200},{1... | collective-permute-start | bytes 294920 | tf_op jit(solution)/shard_map/ppermute | solution.py:449
  22.9 32.6 %all-to-all-start = ((bf16[8,384,128]{2,1,0:T(8,128)(2,1)}), bf16[8,384,128]{2,1,0:T(8,128)(2,1)}, u32[]{:S(2)}, u32[]{:S(2)}) async-start(bf16[8,384,128]{2,1,0:T(8,128)(2,1)} %broadcast_in_dim.6), calls=%async_computation | async-start | bytes 1572864 | tf_op jit(solution)/shard_map/all_to_all | solution.py:464
  31.5 11.4 %collective-permute-start.1 = (bf16[480,128]{1,0:T(8,128)(2,1)S(1)}, bf16[480,128]{1,0:T(8,128)(2,1)S(1)}, u32[]{:S(2)}, u32[]{:S(2)}) collective-permute-start(bf16[480,128]{1,0:T(8,128)(2,1)S(1)} %pad_maximum_fusion.1), channel_id=1, source_target_pairs={{0,0},{8,64},{16,128},{24,192},{64,8},{72,72},{80,136},{88,200},{1... | collective-permute-start | bytes 368648 | tf_op jit(solution)/shard_map/ppermute | solution.py:449
  42.9 4.7 %collective-permute-start.2 = (bf16[384,128]{1,0:T(8,128)(2,1)S(1)}, bf16[384,128]{1,0:T(8,128)(2,1)S(1)}, u32[]{:S(2)}, u32[]{:S(2)}) collective-permute-start(bf16[384,128]{1,0:T(8,128)(2,1)S(1)} %slice.80.refs_1_.refs_2_), channel_id=1, source_target_pairs={{0,64},{64,128},{128,192},{192,0},{1,65},{65,129},{129,193},{193,1... | collective-permute-start | bytes 294920 | tf_op jit(solution)/shard_map/ppermute | solution.py:472
  43.0 6.2 %collective-permute-start.3 = (bf16[384,128]{1,0:T(8,128)(2,1)S(1)}, bf16[384,128]{1,0:T(8,128)(2,1)S(1)}, u32[]{:S(2)}, u32[]{:S(2)}) collective-permute-start(bf16[384,128]{1,0:T(8,128)(2,1)S(1)} %slice.80.refs_1_.refs_2_), channel_id=1, source_target_pairs={{0,128},{64,192},{128,0},{192,64},{1,129},{65,193},{129,1},{193,65... | collective-permute-start | bytes 294920 | tf_op jit(solution)/shard_map/ppermute | solution.py:472
  45.3 5.8 %collective-permute-start.4 = (bf16[384,128]{1,0:T(8,128)(2,1)S(1)}, bf16[384,128]{1,0:T(8,128)(2,1)S(1)}, u32[]{:S(2)}, u32[]{:S(2)}) collective-permute-start(bf16[384,128]{1,0:T(8,128)(2,1)S(1)} %slice.80.refs_1_.refs_2_), channel_id=1, source_target_pairs={{0,192},{64,0},{128,64},{192,128},{1,193},{65,1},{129,65},{193,129... | collective-permute-start | bytes 294920 | tf_op jit(solution)/shard_map/ppermute | solution.py:472
  55.6 27.9 %all-to-all-start.1 = ((bf16[8,384,128]{2,1,0:T(8,128)(2,1)}), bf16[8,384,128]{2,1,0:T(8,128)(2,1)}, u32[]{:S(2)}, u32[]{:S(2)}) async-start(bf16[8,384,128]{2,1,0:T(8,128)(2,1)} %act_kernel.1), calls=%async_computation.1 | async-start | bytes 1572864 | tf_op jit(solution)/shard_map/all_to_all | solution.py:464
  62.8 78.5 %all-gather.6.cloned.1.call-start = ((), (), s32[]{:S(2)}) async-start(), calls=%async_computation.6 | async-start | bytes 1179648 | tf_op jit(solution)/shard_map/all_gather | solution.py:580
  68.5 6.2 %collective-permute-start.5 = (bf16[432,256]{1,0:T(8,128)(2,1)}, bf16[432,256]{1,0:T(8,128)(2,1)S(1)}, u32[]{:S(2)}, u32[]{:S(2)}) collective-permute-start(bf16[432,256]{1,0:T(8,128)(2,1)} %get-tuple-element.43), channel_id=1, source_target_pairs={{0,64},{64,128},{128,192},{192,0},{1,65},{65,129},{129,193},{193,1... | collective-permute-start | bytes 663560 | tf_op jit(solution)/shard_map/ppermute | solution.py:472
  69.7 7.8 %collective-permute-start.6 = (bf16[432,256]{1,0:T(8,128)(2,1)}, bf16[432,256]{1,0:T(8,128)(2,1)S(1)}, u32[]{:S(2)}, u32[]{:S(2)}) collective-permute-start(bf16[432,256]{1,0:T(8,128)(2,1)} %get-tuple-element.44), channel_id=1, source_target_pairs={{0,128},{64,192},{128,0},{192,64},{1,129},{65,193},{129,1},{193,65... | collective-permute-start | bytes 663560 | tf_op jit(solution)/shard_map/ppermute | solution.py:472
  70.7 9.1 %collective-permute-start.7 = (bf16[432,256]{1,0:T(8,128)(2,1)}, bf16[432,256]{1,0:T(8,128)(2,1)S(1)}, u32[]{:S(2)}, u32[]{:S(2)}) collective-permute-start(bf16[432,256]{1,0:T(8,128)(2,1)} %get-tuple-element.45), channel_id=1, source_target_pairs={{0,192},{64,0},{128,64},{192,128},{1,193},{65,1},{129,65},{193,129... | collective-permute-start | bytes 663560 | tf_op jit(solution)/shard_map/ppermute | solution.py:472
  86.2 4.3 %collective-permute-start.9 = (bf16[48,128]{1,0:T(8,128)(2,1)S(1)}, bf16[48,128]{1,0:T(8,128)(2,1)S(1)}, u32[]{:S(2)}, u32[]{:S(2)}) collective-permute-start(bf16[48,128]{1,0:T(8,128)(2,1)S(1)} %pad_maximum_fusion.5), channel_id=1, source_target_pairs={{32,0},{8,32},{40,8},{16,40},{48,16},{24,48},{56,24},{33,1},{9,33}... | collective-permute-start | bytes 36872 | tf_op jit(solution)/shard_map/ppermute | solution.py:459
  95.4 8.5 %collective-permute-start.10 = (bf16[416,256]{1,0:T(8,128)(2,1)}, bf16[416,256]{1,0:T(8,128)(2,1)S(1)}, u32[]{:S(2)}, u32[]{:S(2)}) collective-permute-start(bf16[416,256]{1,0:T(8,128)(2,1)} %get-tuple-element.52.refs_1_.refs_4_), channel_id=1, source_target_pairs={{0,64},{64,128},{128,192},{192,0},{1,65},{65,129},{129,193},{193,1... | collective-permute-start | bytes 638984 | tf_op jit(solution)/shard_map/ppermute | solution.py:472
  96.2 9.9 %collective-permute-start.11 = (bf16[416,256]{1,0:T(8,128)(2,1)}, bf16[416,256]{1,0:T(8,128)(2,1)S(1)}, u32[]{:S(2)}, u32[]{:S(2)}) collective-permute-start(bf16[416,256]{1,0:T(8,128)(2,1)} %get-tuple-element.52.refs_1_.refs_4_), channel_id=1, source_target_pairs={{0,128},{64,192},{128,0},{192,64},{1,129},{65,193},{129,1},{193,65... | collective-permute-start | bytes 638984 | tf_op jit(solution)/shard_map/ppermute | solution.py:472
  97.8 11.9 %collective-permute-start.12 = (bf16[416,256]{1,0:T(8,128)(2,1)}, bf16[416,256]{1,0:T(8,128)(2,1)S(1)}, u32[]{:S(2)}, u32[]{:S(2)}) collective-permute-start(bf16[416,256]{1,0:T(8,128)(2,1)} %get-tuple-element.52.refs_1_.refs_4_), channel_id=1, source_target_pairs={{0,192},{64,0},{128,64},{192,128},{1,193},{65,1},{129,65},{193,129... | collective-permute-start | bytes 638984 | tf_op jit(solution)/shard_map/ppermute | solution.py:472
  118.1 7.3 %collective-permute-start.13 = (bf16[4,512,256]{2,1,0:T(8,128)(2,1)}, bf16[4,512,256]{2,1,0:T(8,128)(2,1)}, u32[]{:S(2)}, u32[]{:S(2)}) collective-permute-start(bf16[4,512,256]{2,1,0:T(8,128)(2,1)} %get-tuple-element.57), channel_id=1, source_target_pairs={{0,32},{32,0},{1,33},{33,1},{2,34},{34,2},{3,35},{35,3},{4,36},{36... | collective-permute-start | bytes 3145736 | tf_op jit(solution)/shard_map/ppermute | solution.py:480
  118.2 45.0 %all-to-all-start.2 = ((bf16[8,432,128]{2,1,0:T(8,128)(2,1)}), bf16[8,432,128]{2,1,0:T(8,128)(2,1)}, u32[]{:S(2)}, u32[]{:S(2)}) async-start(bf16[8,432,128]{2,1,0:T(8,128)(2,1)} %norm_kernel.1), calls=%async_computation.2 | async-start | bytes 1769472 | tf_op jit(solution)/shard_map/all_to_all | solution.py:464
  125.4 71.0 %reduce-scatter.2.cloned.1.call-start = ((), (), s32[]{:S(2)}) async-start(), calls=%async_computation.5 | async-start | bytes 655360 | tf_op jit(solution)/shard_map/reduce_scatter | solution.py:628
  148.8 12.5 %collective-permute-start.14 = (bf16[4,512,128]{2,1,0:T(8,128)(2,1)}, bf16[4,512,128]{2,1,0:T(8,128)(2,1)S(1)}, u32[]{:S(2)}, u32[]{:S(2)}) collective-permute-start(bf16[4,512,128]{2,1,0:T(8,128)(2,1)} %get-tuple-element.65), channel_id=1, source_target_pairs={{0,32},{32,0},{1,33},{33,1},{2,34},{34,2},{3,35},{35,3},{4,36},{36... | collective-permute-start | bytes 1572872 | tf_op jit(solution)/shard_map/ppermute | solution.py:626
  150.1 6.1 %collective-permute-start.15 = (bf16[384,128]{1,0:T(8,128)(2,1)}, bf16[384,128]{1,0:T(8,128)(2,1)S(1)}, u32[]{:S(2)}, u32[]{:S(2)}) collective-permute-start(bf16[384,128]{1,0:T(8,128)(2,1)} %get-tuple-element.60), channel_id=1, source_target_pairs={{0,64},{64,128},{128,192},{192,0},{1,65},{65,129},{129,193},{193,1... | collective-permute-start | bytes 294920 | tf_op jit(solution)/shard_map/ppermute | solution.py:472
  150.2 21.4 %collective-permute-start.19 = (bf16[512,256]{1,0:T(8,128)(2,1)}, bf16[512,256]{1,0:T(8,128)(2,1)S(1)}, u32[]{:S(2)}, u32[]{:S(2)}) collective-permute-start(bf16[512,256]{1,0:T(8,128)(2,1)} %get-tuple-element.76), channel_id=1, source_target_pairs={{0,8},{8,16},{16,24},{24,0},{1,9},{9,17},{17,25},{25,1},{2,10},{10... | collective-permute-start | bytes 786440 | tf_op jit(solution)/shard_map/ppermute | solution.py:472
  152.7 18.9 %collective-permute-start.20 = (bf16[512,256]{1,0:T(8,128)(2,1)}, bf16[512,256]{1,0:T(8,128)(2,1)S(1)}, u32[]{:S(2)}, u32[]{:S(2)}) collective-permute-start(bf16[512,256]{1,0:T(8,128)(2,1)} %get-tuple-element.75), channel_id=1, source_target_pairs={{0,16},{8,24},{16,0},{24,8},{1,17},{9,25},{17,1},{25,9},{2,18},{10... | collective-permute-start | bytes 786440 | tf_op jit(solution)/shard_map/ppermute | solution.py:472
  156.2 15.5 %collective-permute-start.21 = (bf16[512,256]{1,0:T(8,128)(2,1)S(1)}, bf16[512,256]{1,0:T(8,128)(2,1)S(1)}, u32[]{:S(2)}, u32[]{:S(2)}) collective-permute-start(bf16[512,256]{1,0:T(8,128)(2,1)S(1)} %get-tuple-element.74), channel_id=1, source_target_pairs={{0,24},{8,0},{16,8},{24,16},{1,25},{9,1},{17,9},{25,17},{2,26},{10... | collective-permute-start | bytes 786440 | tf_op jit(solution)/shard_map/ppermute | solution.py:472
  156.2 8.4 %collective-permute-start.16 = (bf16[384,128]{1,0:T(8,128)(2,1)}, bf16[384,128]{1,0:T(8,128)(2,1)S(1)}, u32[]{:S(2)}, u32[]{:S(2)}) collective-permute-start(bf16[384,128]{1,0:T(8,128)(2,1)} %get-tuple-element.61), channel_id=1, source_target_pairs={{0,128},{64,192},{128,0},{192,64},{1,129},{65,193},{129,1},{193,65... | collective-permute-start | bytes 294920 | tf_op jit(solution)/shard_map/ppermute | solution.py:472
  161.2 6.0 %collective-permute-start.17 = (bf16[384,128]{1,0:T(8,128)(2,1)}, bf16[384,128]{1,0:T(8,128)(2,1)S(1)}, u32[]{:S(2)}, u32[]{:S(2)}) collective-permute-start(bf16[384,128]{1,0:T(8,128)(2,1)} %get-tuple-element.62), channel_id=1, source_target_pairs={{0,192},{64,0},{128,64},{192,128},{1,193},{65,1},{129,65},{193,129... | collective-permute-start | bytes 294920 | tf_op jit(solution)/shard_map/ppermute | solution.py:472
  171.6 4.9 %collective-permute-start.22 = (f32[40,128]{1,0:T(8,128)S(1)}, f32[40,128]{1,0:T(8,128)S(1)}, u32[]{:S(2)}, u32[]{:S(2)}) collective-permute-start(f32[40,128]{1,0:T(8,128)S(1)} %constant_dynamic-update-slice_fusion), channel_id=1, source_target_pairs={{0,32},{32,0},{1,33},{33,1},{2,34},{34,2},{3,35},{35,3},{4,36},{36... | collective-permute-start | bytes 61448 | tf_op jit(solution)/shard_map/ppermute | solution.py:643
  172.8 18.3 %collective-permute-start.18 = (bf16[384,256]{1,0:T(8,128)(2,1)}, bf16[384,256]{1,0:T(8,128)(2,1)S(1)}, u32[]{:S(2)}, u32[]{:S(2)}) collective-permute-start(bf16[384,256]{1,0:T(8,128)(2,1)} %get-tuple-element.67), channel_id=1, source_target_pairs={{0,0},{8,64},{16,128},{24,192},{64,8},{72,72},{80,136},{88,200},{1... | collective-permute-start | bytes 589832 | tf_op jit(solution)/shard_map/ppermute | solution.py:449
  176.5 14.6 %collective-permute-start.23 = (f32[40,128]{1,0:T(8,128)S(1)}, f32[40,128]{1,0:T(8,128)S(1)}, u32[]{:S(2)}, u32[]{:S(2)}) collective-permute-start(f32[40,128]{1,0:T(8,128)S(1)} %add.115), channel_id=1, source_target_pairs={{0,0},{8,64},{16,128},{24,192},{64,8},{72,72},{80,136},{88,200},{1... | collective-permute-start | bytes 61448 | tf_op jit(solution)/shard_map/ppermute | solution.py:649
  182.1 9.1 %collective-permute-start.24 = (f32[40,128]{1,0:T(8,128)S(1)}, f32[40,128]{1,0:T(8,128)S(1)}, u32[]{:S(2)}, u32[]{:S(2)}) collective-permute-start(f32[40,128]{1,0:T(8,128)S(1)} %add.115), channel_id=1, source_target_pairs={{0,64},{8,128},{16,192},{24,0},{64,72},{72,136},{80,200},{88,8},{1... | collective-permute-start | bytes 61448 | tf_op jit(solution)/shard_map/ppermute | solution.py:649
  185.1 6.1 %collective-permute-start.25 = (f32[40,128]{1,0:T(8,128)S(1)}, f32[40,128]{1,0:T(8,128)S(1)}, u32[]{:S(2)}, u32[]{:S(2)}) collective-permute-start(f32[40,128]{1,0:T(8,128)S(1)} %add.115), channel_id=1, source_target_pairs={{0,128},{8,192},{16,0},{24,64},{64,136},{72,200},{80,8},{88,72},{1... | collective-permute-start | bytes 61448 | tf_op jit(solution)/shard_map/ppermute | solution.py:649
  185.2 6.0 %collective-permute-start.26 = (f32[40,128]{1,0:T(8,128)S(1)}, f32[40,128]{1,0:T(8,128)S(1)}, u32[]{:S(2)}, u32[]{:S(2)}) collective-permute-start(f32[40,128]{1,0:T(8,128)S(1)} %add.115), channel_id=1, source_target_pairs={{0,192},{8,0},{16,64},{24,128},{64,200},{72,8},{80,72},{88,136},{1... | collective-permute-start | bytes 61448 | tf_op jit(solution)/shard_map/ppermute | solution.py:649
  (13 other events, 198.1 us)
Sparse Core Ops, SparseCore 0:
  9.9 35.8 all-gather.3
  95.5 45.7 all-gather.5
  171.7 24.6 reduce-scatter.1

commit v9 on v8

--- a/solution.py
+++ b/solution.py
@@ -17,7 +17,6 @@
 QUARTER = COLS * NZ
 WIDTH = QUARTER * NX
 EDGE = 32
-GATHER_ROWS = 512
 IN = (0, 2 * COLS)
 OUT = (2 * COLS, COLS)
 
@@ -282,7 +281,6 @@
                 product = grad * masked_ref[1 + tap : 1 + tap + count, :]
                 sums_ref[tap] += jnp.sum(product.reshape(count // 8, 8, COLS), axis=0)
             sums_ref[K] += jnp.sum(grad.reshape(count // 8, 8, COLS), axis=0)
-    activated_ref[ROWS:, :] = jnp.zeros((GATHER_ROWS - ROWS, COLS), bf16)
     small_ref[...] = jnp.sum(sums_ref[...], axis=1)
 
     for start, count in CHUNKS[1:4]:
@@ -382,30 +380,32 @@
                 out_ref[:, i * lanes : (i + 1) * lanes] = block_ref[0:ROWS, :]
 
 
-def encode_kernel(arrive, send, place_ref, act_ref, weight_ref, *refs):
-    left_ref = refs[NX]
+def encode_kernel(arrive, send, place_ref, *refs):
+    acts, weight_ref, outs = refs[:NZ], refs[NZ], refs[NZ + 1 :]
     arrive(1)
-    for i in range(NZ):
-        left_ref[:, pl.ds(i * COLS, COLS)] = act_ref[i, 0:ROWS, :]
-    for j, enc_ref in enumerate(refs[:NX]):
-        start = pl.multiple_of(place_ref[4 + j] * QUARTER, QUARTER)
-        weight = weight_ref[pl.ds(start, QUARTER), 2 * COLS : 3 * COLS]
-        enc_ref[...] = dot(left_ref[...], weight, 1, 0).astype(bf16)
+    for j, enc_ref in enumerate(outs):
+        total = jnp.zeros((ROWS, COLS), f32)
+        for i, act_ref in enumerate(acts):
+            start = place_ref[4 + j] * QUARTER + place_ref[14 + i] * COLS
+            weight = weight_ref[pl.ds(pl.multiple_of(start, COLS), COLS), 2 * COLS : 3 * COLS]
+            total = total + dot(act_ref[...], weight, 1, 0)
+        enc_ref[...] = total.astype(bf16)
         send(j)
 
 
-def out_kernel(
-    place_ref, act_ref, g0_ref, g1_ref, g2_ref, g3_ref, kept_ref, given_ref, left_ref, grad_ref
-):
-    half = QUARTER // NK
-    for i in range(NZ):
-        left_ref[i * COLS // half, :, pl.ds(i * COLS % half, COLS)] = act_ref[i, 0:ROWS, :]
-    order_blocks(place_ref, 0, (g0_ref, g1_ref, g2_ref, g3_ref), grad_ref, COLS)
+def out_kernel(place_ref, *refs):
+    acts, grads = refs[:NZ], refs[NZ : NZ + NX]
+    kept_ref, given_ref, left_ref, grad_ref = refs[NZ + NX :]
+    for i, act_ref in enumerate(acts):
+        left_ref[place_ref[14 + i]] = act_ref[...]
+    order_blocks(place_ref, 0, grads, grad_ref, COLS)
     core = place_ref[9]
+    count = NZ // NK
     for out_ref, which in ((given_ref, 1 - core), (kept_ref, core)):
-        out = dot(left_ref[which], grad_ref[...], 0, 0).astype(bf16)
-        for i in range(NY):
-            out_ref[i] = out[:, i * COLS : (i + 1) * COLS]
+        for m in range(count):
+            out = dot(left_ref[which * count + m], grad_ref[...], 0, 0).astype(bf16)
+            for i in range(NY):
+                out_ref[i, m * COLS : (m + 1) * COLS, :] = out[:, i * COLS : (i + 1) * COLS]
 
 
 def input_kernel(
@@ -512,7 +512,8 @@
     above = (x_index + steps) % NX
     distance = (x_index + 2 * NX - (y_index + steps) % NY) % NX
     edges = jnp.stack([LEN - row_start, k_index]).astype(jnp.int32)
-    place = jnp.concatenate([below, above, edges, distance]).astype(jnp.int32)
+    sources = (lax.axis_index("z") + NZ - jnp.arange(NZ, dtype=jnp.int32)) % NZ
+    place = jnp.concatenate([below, above, edges, distance, sources]).astype(jnp.int32)
     border = place[8:9]
 
     weights = lax.all_gather(
@@ -560,7 +561,7 @@
     activated, message, small = call(
         conv_kernel,
         [
-            shape((GATHER_ROWS, COLS), bf16),
+            shape((ROWS, COLS), bf16),
             shape((ROWS + 32, 2 * COLS), bf16),
             shape((K + 1, COLS), f32),
         ],
@@ -577,7 +578,7 @@
             pltpu.VMEM((K + 1, COLS), f32),
         ],
     )
-    act_z = lax.all_gather(activated, "z", axis=0, tiled=False)
+    acts = spread(activated, "z", NZ)
 
     vg_grads = spread(message, "x", NX)
     norm_parts = call(
@@ -589,7 +590,7 @@
         late=(1,),
     )
     norm_moved = exchange(norm_parts, "z")
-    held = lax.optimization_barrier((vg_grads, norm_parts))[0]
+    held = lax.optimization_barrier((vg_grads, norm_parts, acts))[0]
     kept, given = call(
         weight_kernel,
         [shape((NY, QUARTER // NK, 2 * COLS), bf16) for _ in range(2)],
@@ -606,20 +607,20 @@
     enc_parts = call(
         encode_kernel,
         [shape((ROWS, COLS), bf16) for _ in range(NX)],
-        (place, act_z, after(weights, in_sent)),
+        (place, *acts, after(weights, in_sent)),
         smem=(0,),
-        near=(2,),
+        near=(2, 3, 4, 5, 6, 7, 8, 9),
         late=(1,),
-        scratch=[pltpu.VMEM((ROWS, QUARTER), bf16)],
     )
     enc = [enc_parts[0]] + [shifted(enc_parts[j], "x", NX, j) for j in range(1, NX)]
     kept, given = call(
         out_kernel,
         [shape((NY, QUARTER // NK, COLS), bf16) for _ in range(2)],
-        (place, after(act_z, enc_parts), *grads),
+        (place, *acts, *after(grads, enc_parts)),
         smem=(0,),
+        near=(2, 3, 4, 5, 6, 7, 8),
         scratch=[
-            pltpu.VMEM((NK, ROWS, QUARTER // NK), bf16),
+            pltpu.VMEM((NZ, ROWS, COLS), bf16),
             pltpu.VMEM((ROWS, NY * COLS), bf16),
         ],
     )

time: 206 us -> 210 us (1.019)
  starting transfers between devices: 69.2 us -> 87.8 us
  waiting for transfers between devices: 65.8 us -> 47.4 us
  local copies, waits for them, and re-layouts: 11 us -> 14.4 us
    ppermute x15 -> x22, starting transfers between devices: 19.3 us -> 37.5 us  [shifted(): lax.ppermute(block, axis, [(i, (i + shift) % count) for i in range(count)])]
    all_gather x1 -> x0, waiting for transfers between devices: 13.5 us -> none  [shards(): act_z = lax.all_gather(activated, 'z', axis=0, tiled=False)]
    unnamed x25 -> x35, local copies, waits for them, and re-layouts: 2.6 us -> 5.99 us
    ppermute x15 -> x22, waiting for transfers between devices: 29.5 us -> 26.9 us  [shifted(): lax.ppermute(block, axis, [(i, (i + shift) % count) for i in range(count)])]
    ppermute x3, starting transfers between devices: 13.2 us -> 15.7 us  [swap_xy(): lax.ppermute(block, ('x', 'y'), [(a * NY + b, b * NY + a) for a in range(...]
    all_to_all x3, starting transfers between devices: 22.8 us -> 20.7 us  [exchange(): return lax.all_to_all(parts, axis, 0, 0, tiled=True)]
  transfers between devices with their start and end apart: 33 -> 39, of which waited for: 17 -> 20; matrix products, arithmetic and copies ran while one was open for 7% -> 7% of each run, Pallas kernels for 14% -> 11%
where the time goes in v9:
time: 210 us; the launch traced here: 208 us
  starting transfers between devices  87.8 us (42%)
  waiting for transfers between devices  47.4 us (23%)
  Pallas kernels  34.6 us (16%)
  between operations  14.5 us (7%)
  local copies, waits for them, and re-layouts  14.4 us (7%)
  other arithmetic  9.09 us (4%)
    ppermute x22, starting transfers between devices, shifted(): lax.ppermute(block, axis, [(i, (i + shift) % count) for i in range(count)])  37.5 us
    pallas_call x10, Pallas kernels, call(): pl.pallas_call(whole, out_shape=[pltpu.HBM(out.shape, out.dtype) for out...  34.6 us
    ppermute x22, waiting for transfers between devices, shifted(): lax.ppermute(block, axis, [(i, (i + shift) % count) for i in range(count)])  26.9 us
    all_to_all x3, starting transfers between devices, exchange(): return lax.all_to_all(parts, axis, 0, 0, tiled=True)  20.7 us
    ppermute x3, starting transfers between devices, swap_xy(): lax.ppermute(block, ('x', 'y'), [(a * NY + b, b * NY + a) for a in range(...  15.7 us
    ppermute x3, waiting for transfers between devices, swap_xy(): lax.ppermute(block, ('x', 'y'), [(a * NY + b, b * NY + a) for a in range(...  13.9 us
    ppermute x4, starting transfers between devices, shards(): arrived.append(lax.ppermute(small, ('x', 'y'), route))  9.15 us
    unnamed x35, local copies, waits for them, and re-layouts  5.99 us
  transfers between devices with their start and end apart: 39, of which 20 were waited for; matrix products, arithmetic and copies ran while one was open for 7% of the time, Pallas kernels for 11%

profile of v9, /device:TPU:6, one launch (start us, length us, event | category | flops | bytes accessed | tf_op | source)
XLA Modules:
  0.0 207.8 jit_solution(9276785172156417104)
XLA Ops:
  9.1 4.8 %collective-permute-start = (bf16[384,128]{1,0:T(8,128)(2,1)}, bf16[384,128]{1,0:T(8,128)(2,1)S(1)}, u32[]{:S(2)}, u32[]{:S(2)}) collective-permute-start(bf16[384,128]{1,0:T(8,128)(2,1)} %param.8), channel_id=1, source_target_pairs={{0,0},{8,64},{16,128},{24,192},{64,8},{72,72},{80,136},{88,200},{1... | collective-permute-start | bytes 294920 | tf_op jit(solution)/shard_map/ppermute | solution.py:449
  14.0 7.3 %collective-permute-done.refs_1_ = bf16[384,128]{1,0:T(8,128)(2,1)S(1)} collective-permute-done((bf16[384,128]{1,0:T(8,128)(2,1)}, bf16[384,128]{1,0:T(8,128)(2,1)S(1)}, u32[]{:S(2)}, u32[]{:S(2)}) %collective-permute-start) | collective-permute-done | bytes 98336 | tf_op jit(solution)/shard_map/ppermute | solution.py:449
  22.9 8.5 %all-to-all-start = ((bf16[8,384,128]{2,1,0:T(8,128)(2,1)}), bf16[8,384,128]{2,1,0:T(8,128)(2,1)}, u32[]{:S(2)}, u32[]{:S(2)}) async-start(bf16[8,384,128]{2,1,0:T(8,128)(2,1)} %broadcast_in_dim.6), calls=%async_computation | async-start | bytes 1572864 | tf_op jit(solution)/shard_map/all_to_all | solution.py:464
  31.5 4.8 %collective-permute-start.1 = (bf16[480,128]{1,0:T(8,128)(2,1)S(1)}, bf16[480,128]{1,0:T(8,128)(2,1)S(1)}, u32[]{:S(2)}, u32[]{:S(2)}) collective-permute-start(bf16[480,128]{1,0:T(8,128)(2,1)S(1)} %pad_maximum_fusion.1), channel_id=1, source_target_pairs={{0,0},{8,64},{16,128},{24,192},{64,8},{72,72},{80,136},{88,200},{1... | collective-permute-start | bytes 368648 | tf_op jit(solution)/shard_map/ppermute | solution.py:449
  36.3 6.6 %collective-permute-done.1.refs_5_ = bf16[480,128]{1,0:T(8,128)(2,1)S(1)} collective-permute-done((bf16[480,128]{1,0:T(8,128)(2,1)S(1)}, bf16[480,128]{1,0:T(8,128)(2,1)S(1)}, u32[]{:S(2)}, u32[]{:S(2)}) %collective-permute-start.1) | collective-permute-done | bytes 122912 | tf_op jit(solution)/shard_map/ppermute | solution.py:449
  53.1 2.5 %act_kernel.1 = bf16[8,384,128]{2,1,0:T(8,128)(2,1)} custom-call(s32[22]{0:T(128)S(1)} %concatenate.49.refs_0_, bf16[384,128]{1,0:T(8,128)(2,1)S(1)} %slice.80.refs_1_.refs_9_.refs_2_, bf16[384,128]{1,0:T(8,128)(2,1)S(1)} %collective-permute-done.2.refs_2_.refs_10_, bf16[384,128]{1,0:T(8,128)(2,1)S(1)} %collective-permute-done.3.refs_3_.refs_11_, ...), custom_call_target="tpu_custom_call" | custom-call | tf_op jit(solution)/shard_map/act_kernel/pallas_call | solution.py:130
  55.6 7.2 %all-to-all-start.1 = ((bf16[8,384,128]{2,1,0:T(8,128)(2,1)}), bf16[8,384,128]{2,1,0:T(8,128)(2,1)}, u32[]{:S(2)}, u32[]{:S(2)}) async-start(bf16[8,384,128]{2,1,0:T(8,128)(2,1)} %act_kernel.1), calls=%async_computation.1 | async-start | bytes 1572864 | tf_op jit(solution)/shard_map/all_to_all | solution.py:464
  64.0 4.3 %project_kernel.1 = (bf16[432,256]{1,0:T(8,128)(2,1)}, bf16[432,256]{1,0:T(8,128)(2,1)}, bf16[432,256]{1,0:T(8,128)(2,1)}, bf16[432,256]{1,0:T(8,128)(2,1)}) custom-call(s32[22]{0:T(128)S(1)} %concatenate.49.refs_0_, bf16[8,384,128]{2,1,0:T(8,128)(2,1)} %all-to-all-done.refs_1_, f32[1,1024]{1,0:T(1,128)} %bitcast.27, bf16[4096,384]{1,0:T(8,128)(2,1)S(1)} %copy-done.1), custom_call_target="tpu_custom_call" | custom-call | tf_op jit(solution)/shard_map/project_kernel/pallas_call | solution.py:130
  71.1 3.6 %collective-permute-done.5.refs_1_ = bf16[432,256]{1,0:T(8,128)(2,1)S(1)} collective-permute-done((bf16[432,256]{1,0:T(8,128)(2,1)}, bf16[432,256]{1,0:T(8,128)(2,1)S(1)}, u32[]{:S(2)}, u32[]{:S(2)}) %collective-permute-start.5) | collective-permute-done | bytes 221216 | tf_op jit(solution)/shard_map/ppermute | solution.py:472
  74.6 2.8 %collective-permute-done.6.refs_2_ = bf16[432,256]{1,0:T(8,128)(2,1)S(1)} collective-permute-done((bf16[432,256]{1,0:T(8,128)(2,1)}, bf16[432,256]{1,0:T(8,128)(2,1)S(1)}, u32[]{:S(2)}, u32[]{:S(2)}) %collective-permute-start.6) | collective-permute-done | bytes 221216 | tf_op jit(solution)/shard_map/ppermute | solution.py:472
  79.7 3.0 %gate_kernel.1 = (f32[384,256]{1,0:T(8,128)}, bf16[384,128]{1,0:T(8,128)(2,1)}, f32[8,256]{1,0:T(8,128)}, f32[384,128]{1,0:T(8,128)}) custom-call(bf16[432,256]{1,0:T(8,128)(2,1)} %get-tuple-element.45.refs_0_, bf16[432,256]{1,0:T(8,128)(2,1)S(1)} %collective-permute-done.5.refs_1_, bf16[432,256]{1,0:T(8,128)(2,1)S(1)} %collective-permute-done.6.refs_2_, ...), custom_call_target="tpu_custom_call" | custom-call | tf_op jit(solution)/shard_map/gate_kernel/pallas_call | solution.py:130
  87.4 3.0 %collective-permute-start.8 = (bf16[48,128]{1,0:T(8,128)(2,1)S(1)}, bf16[48,128]{1,0:T(8,128)(2,1)S(1)}, u32[]{:S(2)}, u32[]{:S(2)}) collective-permute-start(bf16[48,128]{1,0:T(8,128)(2,1)S(1)} %pad_maximum_fusion.4), channel_id=1, source_target_pairs={{0,32},{32,8},{8,40},{40,16},{16,48},{48,24},{24,56},{1,33},{33,9}... | collective-permute-start | bytes 36872 | tf_op jit(solution)/shard_map/ppermute | solution.py:458
  91.2 4.0 %conv_kernel.1 = (bf16[384,128]{1,0:T(8,128)(2,1)}, bf16[416,256]{1,0:T(8,128)(2,1)}, f32[32,128]{1,0:T(8,128)}) custom-call(s32[1]{0:T(128)} %bitcast.refs_0_, bf16[384,128]{1,0:T(8,128)(2,1)} %get-tuple-element.49.refs_1_, bf16[384,128]{1,0:T(8,128)(2,1)} %sum_kernel.1.refs_2_, bf16[48,128]{1,0:T(8,128)(2,1)S(1)} %collective-permute-done.8.refs_3_, ...), custom_call_target="tpu_custom_call" | custom-call | tf_op jit(solution)/shard_map/conv_kernel/pallas_call | solution.py:130
  100.3 2.4 %collective-permute-start.14 = (bf16[384,128]{1,0:T(8,128)(2,1)}, bf16[384,128]{1,0:T(8,128)(2,1)S(1)}, u32[]{:S(2)}, u32[]{:S(2)}) collective-permute-start(bf16[384,128]{1,0:T(8,128)(2,1)} %get-tuple-element.53.refs_1_), channel_id=1, source_target_pairs={{0,2},{1,3},{2,4},{3,5},{4,6},{5,7},{6,0},{7,1},{8,10},{9,11},{10,... | collective-permute-start | bytes 294920 | tf_op jit(solution)/shard_map/ppermute | solution.py:472
  102.6 2.7 %collective-permute-done.13.refs_2_ = bf16[384,128]{1,0:T(8,128)(2,1)S(1)} collective-permute-done((bf16[384,128]{1,0:T(8,128)(2,1)}, bf16[384,128]{1,0:T(8,128)(2,1)S(1)}, u32[]{:S(2)}, u32[]{:S(2)}) %collective-permute-start.13) | collective-permute-done | bytes 98336 | tf_op jit(solution)/shard_map/ppermute | solution.py:472
  105.3 4.3 %collective-permute-start.15 = (bf16[384,128]{1,0:T(8,128)(2,1)}, bf16[384,128]{1,0:T(8,128)(2,1)S(1)}, u32[]{:S(2)}, u32[]{:S(2)}) collective-permute-start(bf16[384,128]{1,0:T(8,128)(2,1)} %get-tuple-element.53.refs_1_), channel_id=1, source_target_pairs={{0,3},{1,4},{2,5},{3,6},{4,7},{5,0},{6,1},{7,2},{8,11},{9,12},{10,... | collective-permute-start | bytes 294920 | tf_op jit(solution)/shard_map/ppermute | solution.py:472
  109.6 5.0 %collective-permute-start.16 = (bf16[384,128]{1,0:T(8,128)(2,1)}, bf16[384,128]{1,0:T(8,128)(2,1)S(1)}, u32[]{:S(2)}, u32[]{:S(2)}) collective-permute-start(bf16[384,128]{1,0:T(8,128)(2,1)} %get-tuple-element.53.refs_1_), channel_id=1, source_target_pairs={{0,4},{1,5},{2,6},{3,7},{4,0},{5,1},{6,2},{7,3},{8,12},{9,13},{10,... | collective-permute-start | bytes 294920 | tf_op jit(solution)/shard_map/ppermute | solution.py:472
  114.6 4.7 %collective-permute-start.17 = (bf16[384,128]{1,0:T(8,128)(2,1)}, bf16[384,128]{1,0:T(8,128)(2,1)S(1)}, u32[]{:S(2)}, u32[]{:S(2)}) collective-permute-start(bf16[384,128]{1,0:T(8,128)(2,1)} %get-tuple-element.53.refs_1_), channel_id=1, source_target_pairs={{0,5},{1,6},{2,7},{3,0},{4,1},{5,2},{6,3},{7,4},{8,13},{9,14},{10,... | collective-permute-start | bytes 294920 | tf_op jit(solution)/shard_map/ppermute | solution.py:472
  120.0 3.4 %norm_kernel.1 = bf16[8,432,128]{2,1,0:T(8,128)(2,1)} custom-call(s32[22]{0:T(128)S(1)} %concatenate.49.refs_0_, bf16[416,256]{1,0:T(8,128)(2,1)} %get-tuple-element.55.refs_1_.refs_4_, bf16[416,256]{1,0:T(8,128)(2,1)S(1)} %collective-permute-done.10.refs_2_.refs_5_, bf16[416,256]{1,0:T(8,128)(2,1)S(1)} %collective-permute-done.11.refs_3_.refs_6_, ...), custom_call_target="tpu_custom_call" | custom-call | tf_op jit(solution)/shard_map/norm_kernel/pallas_call | solution.py:130
  124.8 3.7 %collective-permute-done.18.refs_7_ = bf16[384,128]{1,0:T(8,128)(2,1)S(1)} collective-permute-done((bf16[384,128]{1,0:T(8,128)(2,1)}, bf16[384,128]{1,0:T(8,128)(2,1)S(1)}, u32[]{:S(2)}, u32[]{:S(2)}) %collective-permute-start.18) | collective-permute-done | bytes 98336 | tf_op jit(solution)/shard_map/ppermute | solution.py:472
  130.0 5.0 %weight_kernel.1 = (bf16[4,512,256]{2,1,0:T(8,128)(2,1)}, bf16[4,512,256]{2,1,0:T(8,128)(2,1)}) custom-call(s32[22]{0:T(128)S(1)} %concatenate.49.refs_0_, bf16[8,384,128]{2,1,0:T(8,128)(2,1)} %all-to-all-done.refs_1_, f32[1,1024]{1,0:T(1,128)} %bitcast.28, f32[384,128]{1,0:T(8,128)} %get-tuple-element.54.refs_3_, ...), custom_call_target="tpu_custom_call" | custom-call | tf_op jit(solution)/shard_map/weight_kernel/pallas_call | solution.py:130
  135.2 5.0 %all-to-all-start.2 = ((bf16[8,432,128]{2,1,0:T(8,128)(2,1)}), bf16[8,432,128]{2,1,0:T(8,128)(2,1)}, u32[]{:S(2)}, u32[]{:S(2)}) async-start(bf16[8,432,128]{2,1,0:T(8,128)(2,1)} %norm_kernel.1), calls=%async_computation.2 | async-start | bytes 1769472 | tf_op jit(solution)/shard_map/all_to_all | solution.py:464
  145.3 3.1 %encode_kernel.1 = (bf16[384,128]{1,0:T(8,128)(2,1)}, bf16[384,128]{1,0:T(8,128)(2,1)}, bf16[384,128]{1,0:T(8,128)(2,1)}, bf16[384,128]{1,0:T(8,128)(2,1)}) custom-call(s32[22]{0:T(128)S(1)} %concatenate.49.refs_0_, bf16[384,128]{1,0:T(8,128)(2,1)} %get-tuple-element.53.refs_1_, bf16[384,128]{1,0:T(8,128)(2,1)S(1)} %collective-permute-done.13.refs_2_, ...), custom_call_target="tpu_custom_call" | custom-call | tf_op jit(solution)/shard_map/encode_kernel/pallas_call | solution.py:130
  148.4 3.7 %out_kernel.1 = (bf16[4,512,128]{2,1,0:T(8,128)(2,1)}, bf16[4,512,128]{2,1,0:T(8,128)(2,1)}) custom-call(s32[22]{0:T(128)S(1)} %concatenate.49.refs_0_, bf16[384,128]{1,0:T(8,128)(2,1)} %get-tuple-element.53.refs_1_, bf16[384,128]{1,0:T(8,128)(2,1)S(1)} %collective-permute-done.13.refs_2_, bf16[384,128]{1,0:T(8,128)(2,1)S(1)} %collective-permute-done.14.refs_3_, ...), custom_call_target="tpu_custom_call" | custom-call | tf_op jit(solution)/shard_map/out_kernel/pallas_call | solution.py:130
  159.2 3.0 %collective-permute-start.27 = (bf16[512,256]{1,0:T(8,128)(2,1)}, bf16[512,256]{1,0:T(8,128)(2,1)S(1)}, u32[]{:S(2)}, u32[]{:S(2)}) collective-permute-start(bf16[512,256]{1,0:T(8,128)(2,1)} %get-tuple-element.81), channel_id=1, source_target_pairs={{0,16},{8,24},{16,0},{24,8},{1,17},{9,25},{17,1},{25,9},{2,18},{10... | collective-permute-start | bytes 786440 | tf_op jit(solution)/shard_map/ppermute | solution.py:472
  162.2 2.6 %collective-permute-start.28 = (bf16[512,256]{1,0:T(8,128)(2,1)}, bf16[512,256]{1,0:T(8,128)(2,1)S(1)}, u32[]{:S(2)}, u32[]{:S(2)}) collective-permute-start(bf16[512,256]{1,0:T(8,128)(2,1)} %get-tuple-element.80), channel_id=1, source_target_pairs={{0,24},{8,0},{16,8},{24,16},{1,25},{9,1},{17,9},{25,17},{2,26},{10... | collective-permute-start | bytes 786440 | tf_op jit(solution)/shard_map/ppermute | solution.py:472
  166.8 3.6 %input_kernel.1 = (bf16[384,256]{1,0:T(8,128)(2,1)}, f32[8,128]{1,0:T(8,128)}) custom-call(bf16[8,432,128]{2,1,0:T(8,128)(2,1)} %all-to-all-done.2.refs_0_, bf16[384,128]{1,0:T(8,128)(2,1)} %copy-done.13, bf16[384,128]{1,0:T(8,128)(2,1)} %copy-done.2, f32[384,128]{1,0:T(8,128)} %get-tuple-element.54.refs_3_, f32[1,128]{1,0:T(1,128)} %dynamic-slice_bitcast_fusion.refs_4_, ...), custom_call_target="tpu_custom_call" | custom-call | tf_op jit(solution)/shard_map/input_kernel/pallas_call | solution.py:130
  171.2 2.7 %collective-permute-done.27 = bf16[512,256]{1,0:T(8,128)(2,1)S(1)} collective-permute-done((bf16[512,256]{1,0:T(8,128)(2,1)}, bf16[512,256]{1,0:T(8,128)(2,1)S(1)}, u32[]{:S(2)}, u32[]{:S(2)}) %collective-permute-start.27) | collective-permute-done | bytes 262176 | tf_op jit(solution)/shard_map/ppermute | solution.py:472
  175.7 6.1 %collective-permute-start.25 = (bf16[384,256]{1,0:T(8,128)(2,1)}, bf16[384,256]{1,0:T(8,128)(2,1)S(1)}, u32[]{:S(2)}, u32[]{:S(2)}) collective-permute-start(bf16[384,256]{1,0:T(8,128)(2,1)} %get-tuple-element.73), channel_id=1, source_target_pairs={{0,0},{8,64},{16,128},{24,192},{64,8},{72,72},{80,136},{88,200},{1... | collective-permute-start | bytes 589832 | tf_op jit(solution)/shard_map/ppermute | solution.py:449
  181.8 3.1 %collective-permute-start.30 = (f32[40,128]{1,0:T(8,128)S(1)}, f32[40,128]{1,0:T(8,128)S(1)}, u32[]{:S(2)}, u32[]{:S(2)}) collective-permute-start(f32[40,128]{1,0:T(8,128)S(1)} %add.126), channel_id=1, source_target_pairs={{0,0},{8,64},{16,128},{24,192},{64,8},{72,72},{80,136},{88,200},{1... | collective-permute-start | bytes 61448 | tf_op jit(solution)/shard_map/ppermute | solution.py:650
  184.9 4.2 %collective-permute-start.31 = (f32[40,128]{1,0:T(8,128)S(1)}, f32[40,128]{1,0:T(8,128)S(1)}, u32[]{:S(2)}, u32[]{:S(2)}) collective-permute-start(f32[40,128]{1,0:T(8,128)S(1)} %add.126), channel_id=1, source_target_pairs={{0,64},{8,128},{16,192},{24,0},{64,72},{72,136},{80,200},{88,8},{1... | collective-permute-start | bytes 61448 | tf_op jit(solution)/shard_map/ppermute | solution.py:650
  192.4 2.6 %collective-permute-done.32 = f32[40,128]{1,0:T(8,128)S(1)} collective-permute-done((f32[40,128]{1,0:T(8,128)S(1)}, f32[40,128]{1,0:T(8,128)S(1)}, u32[]{:S(2)}, u32[]{:S(2)}) %collective-permute-start.32) | collective-permute-done | bytes 20512 | tf_op jit(solution)/shard_map/ppermute | solution.py:650
  (120 shorter events, 59.9 us)
Async XLA Ops:
  7.2 43.9 %all-gather.2.cloned.1.call-start = ((), (), s32[]{:S(2)}) async-start(), calls=%async_computation.4 | async-start | bytes 3538944 | tf_op jit(solution)/shard_map/all_gather | solution.py:519
  9.1 12.1 %collective-permute-start = (bf16[384,128]{1,0:T(8,128)(2,1)}, bf16[384,128]{1,0:T(8,128)(2,1)S(1)}, u32[]{:S(2)}, u32[]{:S(2)}) collective-permute-start(bf16[384,128]{1,0:T(8,128)(2,1)} %param.8), channel_id=1, source_target_pairs={{0,0},{8,64},{16,128},{24,192},{64,8},{72,72},{80,136},{88,200},{1... | collective-permute-start | bytes 294920 | tf_op jit(solution)/shard_map/ppermute | solution.py:449
  22.9 32.6 %all-to-all-start = ((bf16[8,384,128]{2,1,0:T(8,128)(2,1)}), bf16[8,384,128]{2,1,0:T(8,128)(2,1)}, u32[]{:S(2)}, u32[]{:S(2)}) async-start(bf16[8,384,128]{2,1,0:T(8,128)(2,1)} %broadcast_in_dim.6), calls=%async_computation | async-start | bytes 1572864 | tf_op jit(solution)/shard_map/all_to_all | solution.py:464
  31.5 11.4 %collective-permute-start.1 = (bf16[480,128]{1,0:T(8,128)(2,1)S(1)}, bf16[480,128]{1,0:T(8,128)(2,1)S(1)}, u32[]{:S(2)}, u32[]{:S(2)}) collective-permute-start(bf16[480,128]{1,0:T(8,128)(2,1)S(1)} %pad_maximum_fusion.1), channel_id=1, source_target_pairs={{0,0},{8,64},{16,128},{24,192},{64,8},{72,72},{80,136},{88,200},{1... | collective-permute-start | bytes 368648 | tf_op jit(solution)/shard_map/ppermute | solution.py:449
  43.0 6.2 %collective-permute-start.3 = (bf16[384,128]{1,0:T(8,128)(2,1)S(1)}, bf16[384,128]{1,0:T(8,128)(2,1)S(1)}, u32[]{:S(2)}, u32[]{:S(2)}) collective-permute-start(bf16[384,128]{1,0:T(8,128)(2,1)S(1)} %slice.80.refs_1_.refs_9_.refs_2_), channel_id=1, source_target_pairs={{0,128},{64,192},{128,0},{192,64},{1,129},{65,193},{129,1},{193,65... | collective-permute-start | bytes 294920 | tf_op jit(solution)/shard_map/ppermute | solution.py:472
  55.6 27.9 %all-to-all-start.1 = ((bf16[8,384,128]{2,1,0:T(8,128)(2,1)}), bf16[8,384,128]{2,1,0:T(8,128)(2,1)}, u32[]{:S(2)}, u32[]{:S(2)}) async-start(bf16[8,384,128]{2,1,0:T(8,128)(2,1)} %act_kernel.1), calls=%async_computation.1 | async-start | bytes 1572864 | tf_op jit(solution)/shard_map/all_to_all | solution.py:464
  68.4 6.2 %collective-permute-start.5 = (bf16[432,256]{1,0:T(8,128)(2,1)}, bf16[432,256]{1,0:T(8,128)(2,1)S(1)}, u32[]{:S(2)}, u32[]{:S(2)}) collective-permute-start(bf16[432,256]{1,0:T(8,128)(2,1)} %get-tuple-element.46), channel_id=1, source_target_pairs={{0,64},{64,128},{128,192},{192,0},{1,65},{65,129},{129,193},{193,1... | collective-permute-start | bytes 663560 | tf_op jit(solution)/shard_map/ppermute | solution.py:472
  69.7 7.8 %collective-permute-start.6 = (bf16[432,256]{1,0:T(8,128)(2,1)}, bf16[432,256]{1,0:T(8,128)(2,1)S(1)}, u32[]{:S(2)}, u32[]{:S(2)}) collective-permute-start(bf16[432,256]{1,0:T(8,128)(2,1)} %get-tuple-element.47), channel_id=1, source_target_pairs={{0,128},{64,192},{128,0},{192,64},{1,129},{65,193},{129,1},{193,65... | collective-permute-start | bytes 663560 | tf_op jit(solution)/shard_map/ppermute | solution.py:472
  70.6 9.1 %collective-permute-start.7 = (bf16[432,256]{1,0:T(8,128)(2,1)}, bf16[432,256]{1,0:T(8,128)(2,1)S(1)}, u32[]{:S(2)}, u32[]{:S(2)}) collective-permute-start(bf16[432,256]{1,0:T(8,128)(2,1)} %get-tuple-element.48), channel_id=1, source_target_pairs={{0,192},{64,0},{128,64},{192,128},{1,193},{65,1},{129,65},{193,129... | collective-permute-start | bytes 663560 | tf_op jit(solution)/shard_map/ppermute | solution.py:472
  95.3 19.3 %collective-permute-start.10 = (bf16[416,256]{1,0:T(8,128)(2,1)}, bf16[416,256]{1,0:T(8,128)(2,1)S(1)}, u32[]{:S(2)}, u32[]{:S(2)}) collective-permute-start(bf16[416,256]{1,0:T(8,128)(2,1)} %get-tuple-element.55.refs_1_.refs_4_), channel_id=1, source_target_pairs={{0,64},{64,128},{128,192},{192,0},{1,65},{65,129},{129,193},{193,1... | collective-permute-start | bytes 638984 | tf_op jit(solution)/shard_map/ppermute | solution.py:472
  96.1 23.2 %collective-permute-start.11 = (bf16[416,256]{1,0:T(8,128)(2,1)}, bf16[416,256]{1,0:T(8,128)(2,1)S(1)}, u32[]{:S(2)}, u32[]{:S(2)}) collective-permute-start(bf16[416,256]{1,0:T(8,128)(2,1)} %get-tuple-element.55.refs_1_.refs_4_), channel_id=1, source_target_pairs={{0,128},{64,192},{128,0},{192,64},{1,129},{65,193},{129,1},{193,65... | collective-permute-start | bytes 638984 | tf_op jit(solution)/shard_map/ppermute | solution.py:472
  97.8 21.6 %collective-permute-start.12 = (bf16[416,256]{1,0:T(8,128)(2,1)}, bf16[416,256]{1,0:T(8,128)(2,1)S(1)}, u32[]{:S(2)}, u32[]{:S(2)}) collective-permute-start(bf16[416,256]{1,0:T(8,128)(2,1)} %get-tuple-element.55.refs_1_.refs_4_), channel_id=1, source_target_pairs={{0,192},{64,0},{128,64},{192,128},{1,193},{65,1},{129,65},{193,129... | collective-permute-start | bytes 638984 | tf_op jit(solution)/shard_map/ppermute | solution.py:472
  98.5 6.8 %collective-permute-start.13 = (bf16[384,128]{1,0:T(8,128)(2,1)}, bf16[384,128]{1,0:T(8,128)(2,1)S(1)}, u32[]{:S(2)}, u32[]{:S(2)}) collective-permute-start(bf16[384,128]{1,0:T(8,128)(2,1)} %get-tuple-element.53.refs_1_), channel_id=1, source_target_pairs={{0,1},{1,2},{2,3},{3,4},{4,5},{5,6},{6,7},{7,0},{8,9},{9,10},{10,1... | collective-permute-start | bytes 294920 | tf_op jit(solution)/shard_map/ppermute | solution.py:472
  100.3 9.4 %collective-permute-start.14 = (bf16[384,128]{1,0:T(8,128)(2,1)}, bf16[384,128]{1,0:T(8,128)(2,1)S(1)}, u32[]{:S(2)}, u32[]{:S(2)}) collective-permute-start(bf16[384,128]{1,0:T(8,128)(2,1)} %get-tuple-element.53.refs_1_), channel_id=1, source_target_pairs={{0,2},{1,3},{2,4},{3,5},{4,6},{5,7},{6,0},{7,1},{8,10},{9,11},{10,... | collective-permute-start | bytes 294920 | tf_op jit(solution)/shard_map/ppermute | solution.py:472
  105.3 18.1 %collective-permute-start.15 = (bf16[384,128]{1,0:T(8,128)(2,1)}, bf16[384,128]{1,0:T(8,128)(2,1)S(1)}, u32[]{:S(2)}, u32[]{:S(2)}) collective-permute-start(bf16[384,128]{1,0:T(8,128)(2,1)} %get-tuple-element.53.refs_1_), channel_id=1, source_target_pairs={{0,3},{1,4},{2,5},{3,6},{4,7},{5,0},{6,1},{7,2},{8,11},{9,12},{10,... | collective-permute-start | bytes 294920 | tf_op jit(solution)/shard_map/ppermute | solution.py:472
  109.6 13.8 %collective-permute-start.16 = (bf16[384,128]{1,0:T(8,128)(2,1)}, bf16[384,128]{1,0:T(8,128)(2,1)S(1)}, u32[]{:S(2)}, u32[]{:S(2)}) collective-permute-start(bf16[384,128]{1,0:T(8,128)(2,1)} %get-tuple-element.53.refs_1_), channel_id=1, source_target_pairs={{0,4},{1,5},{2,6},{3,7},{4,0},{5,1},{6,2},{7,3},{8,12},{9,13},{10,... | collective-permute-start | bytes 294920 | tf_op jit(solution)/shard_map/ppermute | solution.py:472
  114.6 10.2 %collective-permute-start.17 = (bf16[384,128]{1,0:T(8,128)(2,1)}, bf16[384,128]{1,0:T(8,128)(2,1)S(1)}, u32[]{:S(2)}, u32[]{:S(2)}) collective-permute-start(bf16[384,128]{1,0:T(8,128)(2,1)} %get-tuple-element.53.refs_1_), channel_id=1, source_target_pairs={{0,5},{1,6},{2,7},{3,0},{4,1},{5,2},{6,3},{7,4},{8,13},{9,14},{10,... | collective-permute-start | bytes 294920 | tf_op jit(solution)/shard_map/ppermute | solution.py:472
  119.3 9.2 %collective-permute-start.18 = (bf16[384,128]{1,0:T(8,128)(2,1)}, bf16[384,128]{1,0:T(8,128)(2,1)S(1)}, u32[]{:S(2)}, u32[]{:S(2)}) collective-permute-start(bf16[384,128]{1,0:T(8,128)(2,1)} %get-tuple-element.53.refs_1_), channel_id=1, source_target_pairs={{0,6},{1,7},{2,0},{3,1},{4,2},{5,3},{6,4},{7,5},{8,14},{9,15},{10,... | collective-permute-start | bytes 294920 | tf_op jit(solution)/shard_map/ppermute | solution.py:472
  119.4 10.6 %collective-permute-start.19 = (bf16[384,128]{1,0:T(8,128)(2,1)}, bf16[384,128]{1,0:T(8,128)(2,1)S(1)}, u32[]{:S(2)}, u32[]{:S(2)}) collective-permute-start(bf16[384,128]{1,0:T(8,128)(2,1)} %get-tuple-element.53.refs_1_), channel_id=1, source_target_pairs={{0,7},{1,0},{2,1},{3,2},{4,3},{5,4},{6,5},{7,6},{8,15},{9,8},{10,9... | collective-permute-start | bytes 294920 | tf_op jit(solution)/shard_map/ppermute | solution.py:472
  135.2 31.6 %all-to-all-start.2 = ((bf16[8,432,128]{2,1,0:T(8,128)(2,1)}), bf16[8,432,128]{2,1,0:T(8,128)(2,1)}, u32[]{:S(2)}, u32[]{:S(2)}) async-start(bf16[8,432,128]{2,1,0:T(8,128)(2,1)} %norm_kernel.1), calls=%async_computation.2 | async-start | bytes 1769472 | tf_op jit(solution)/shard_map/all_to_all | solution.py:464
  140.2 59.1 %reduce-scatter.2.cloned.1.call-start = ((), (), s32[]{:S(2)}) async-start(), calls=%async_computation.5 | async-start | bytes 655360 | tf_op jit(solution)/shard_map/reduce_scatter | solution.py:629
  152.1 10.0 %collective-permute-start.21 = (bf16[4,512,128]{2,1,0:T(8,128)(2,1)}, bf16[4,512,128]{2,1,0:T(8,128)(2,1)S(1)}, u32[]{:S(2)}, u32[]{:S(2)}) collective-permute-start(bf16[4,512,128]{2,1,0:T(8,128)(2,1)} %get-tuple-element.71), channel_id=1, source_target_pairs={{0,32},{32,0},{1,33},{33,1},{2,34},{34,2},{3,35},{35,3},{4,36},{36... | collective-permute-start | bytes 1572872 | tf_op jit(solution)/shard_map/ppermute | solution.py:627
  156.7 10.1 %collective-permute-start.23 = (bf16[384,128]{1,0:T(8,128)(2,1)}, bf16[384,128]{1,0:T(8,128)(2,1)S(1)}, u32[]{:S(2)}, u32[]{:S(2)}) collective-permute-start(bf16[384,128]{1,0:T(8,128)(2,1)} %get-tuple-element.64), channel_id=1, source_target_pairs={{0,128},{64,192},{128,0},{192,64},{1,129},{65,193},{129,1},{193,65... | collective-permute-start | bytes 294920 | tf_op jit(solution)/shard_map/ppermute | solution.py:472
  157.7 9.0 %collective-permute-start.24 = (bf16[384,128]{1,0:T(8,128)(2,1)}, bf16[384,128]{1,0:T(8,128)(2,1)S(1)}, u32[]{:S(2)}, u32[]{:S(2)}) collective-permute-start(bf16[384,128]{1,0:T(8,128)(2,1)} %get-tuple-element.65), channel_id=1, source_target_pairs={{0,192},{64,0},{128,64},{192,128},{1,193},{65,1},{129,65},{193,129... | collective-permute-start | bytes 294920 | tf_op jit(solution)/shard_map/ppermute | solution.py:472
  159.2 12.0 %collective-permute-start.26 = (bf16[512,256]{1,0:T(8,128)(2,1)}, bf16[512,256]{1,0:T(8,128)(2,1)S(1)}, u32[]{:S(2)}, u32[]{:S(2)}) collective-permute-start(bf16[512,256]{1,0:T(8,128)(2,1)} %get-tuple-element.82), channel_id=1, source_target_pairs={{0,8},{8,16},{16,24},{24,0},{1,9},{9,17},{17,25},{25,1},{2,10},{10... | collective-permute-start | bytes 786440 | tf_op jit(solution)/shard_map/ppermute | solution.py:472
  159.2 14.7 %collective-permute-start.27 = (bf16[512,256]{1,0:T(8,128)(2,1)}, bf16[512,256]{1,0:T(8,128)(2,1)S(1)}, u32[]{:S(2)}, u32[]{:S(2)}) collective-permute-start(bf16[512,256]{1,0:T(8,128)(2,1)} %get-tuple-element.81), channel_id=1, source_target_pairs={{0,16},{8,24},{16,0},{24,8},{1,17},{9,25},{17,1},{25,9},{2,18},{10... | collective-permute-start | bytes 786440 | tf_op jit(solution)/shard_map/ppermute | solution.py:472
  162.2 12.3 %collective-permute-start.28 = (bf16[512,256]{1,0:T(8,128)(2,1)}, bf16[512,256]{1,0:T(8,128)(2,1)S(1)}, u32[]{:S(2)}, u32[]{:S(2)}) collective-permute-start(bf16[512,256]{1,0:T(8,128)(2,1)} %get-tuple-element.80), channel_id=1, source_target_pairs={{0,24},{8,0},{16,8},{24,16},{1,25},{9,1},{17,9},{25,17},{2,26},{10... | collective-permute-start | bytes 786440 | tf_op jit(solution)/shard_map/ppermute | solution.py:472
  171.1 10.6 %collective-permute-start.29 = (f32[40,128]{1,0:T(8,128)S(1)}, f32[40,128]{1,0:T(8,128)S(1)}, u32[]{:S(2)}, u32[]{:S(2)}) collective-permute-start(f32[40,128]{1,0:T(8,128)S(1)} %constant_dynamic-update-slice_fusion), channel_id=1, source_target_pairs={{0,32},{32,0},{1,33},{33,1},{2,34},{34,2},{3,35},{35,3},{4,36},{36... | collective-permute-start | bytes 61448 | tf_op jit(solution)/shard_map/ppermute | solution.py:644
  175.7 20.3 %collective-permute-start.25 = (bf16[384,256]{1,0:T(8,128)(2,1)}, bf16[384,256]{1,0:T(8,128)(2,1)S(1)}, u32[]{:S(2)}, u32[]{:S(2)}) collective-permute-start(bf16[384,256]{1,0:T(8,128)(2,1)} %get-tuple-element.73), channel_id=1, source_target_pairs={{0,0},{8,64},{16,128},{24,192},{64,8},{72,72},{80,136},{88,200},{1... | collective-permute-start | bytes 589832 | tf_op jit(solution)/shard_map/ppermute | solution.py:449
  181.8 10.3 %collective-permute-start.30 = (f32[40,128]{1,0:T(8,128)S(1)}, f32[40,128]{1,0:T(8,128)S(1)}, u32[]{:S(2)}, u32[]{:S(2)}) collective-permute-start(f32[40,128]{1,0:T(8,128)S(1)} %add.126), channel_id=1, source_target_pairs={{0,0},{8,64},{16,128},{24,192},{64,8},{72,72},{80,136},{88,200},{1... | collective-permute-start | bytes 61448 | tf_op jit(solution)/shard_map/ppermute | solution.py:650
  184.9 7.5 %collective-permute-start.31 = (f32[40,128]{1,0:T(8,128)S(1)}, f32[40,128]{1,0:T(8,128)S(1)}, u32[]{:S(2)}, u32[]{:S(2)}) collective-permute-start(f32[40,128]{1,0:T(8,128)S(1)} %add.126), channel_id=1, source_target_pairs={{0,64},{8,128},{16,192},{24,0},{64,72},{72,136},{80,200},{88,8},{1... | collective-permute-start | bytes 61448 | tf_op jit(solution)/shard_map/ppermute | solution.py:650
  189.1 5.9 %collective-permute-start.32 = (f32[40,128]{1,0:T(8,128)S(1)}, f32[40,128]{1,0:T(8,128)S(1)}, u32[]{:S(2)}, u32[]{:S(2)}) collective-permute-start(f32[40,128]{1,0:T(8,128)S(1)} %add.126), channel_id=1, source_target_pairs={{0,128},{8,192},{16,0},{24,64},{64,136},{72,200},{80,8},{88,72},{1... | collective-permute-start | bytes 61448 | tf_op jit(solution)/shard_map/ppermute | solution.py:650
  (24 other events, 230.3 us)
Sparse Core Ops, SparseCore 0:
  9.9 35.8 all-gather.1
  171.3 28.0 reduce-scatter.1

commit v10 on v8

--- a/solution.py
+++ b/solution.py
@@ -17,7 +17,6 @@
 QUARTER = COLS * NZ
 WIDTH = QUARTER * NX
 EDGE = 32
-GATHER_ROWS = 512
 IN = (0, 2 * COLS)
 OUT = (2 * COLS, COLS)
 
@@ -149,7 +148,7 @@
     return jax.ShapeDtypeStruct(dims, kind)
 
 
-def project_kernel(arrive, send, place_ref, frames_ref, gain_ref, weight_ref, *refs):
+def project_kernel(arrive, send, place_ref, frames_ref, gain_ref, gain_rows_ref, weight_ref, *refs):
     left_ref = refs[NX]
     total = jnp.zeros((ROWS, 1), f32)
     square = jnp.zeros((ROWS, 1), f32)
@@ -159,8 +158,7 @@
         square = square + jnp.sum(wide * wide, axis=1, keepdims=True)
     mean = total / QUARTER
     arrive(2)
-    gain = gain_ref[...]
-    gain_rows = stacked_rows(split3(gain)).astype(bf16)
+    arrive(3)
     for i in range(NZ):
         cut = pl.ds(i * COLS, COLS)
         scaled = (frames_ref[i].astype(f32) - mean) * gain_ref[0:1, cut]
@@ -170,7 +168,7 @@
         start = pl.multiple_of(place_ref[4 + j] * QUARTER, QUARTER)
         weight = weight_ref[pl.ds(start, QUARTER), 0 : 2 * COLS]
         out_ref[0:ROWS, :] = dot(left_ref[...], weight, 1, 0).astype(bf16)
-        unit = jnp.sum(dot(gain_rows, weight, 1, 0), axis=0, keepdims=True)
+        unit = jnp.sum(dot(gain_rows_ref[...], weight, 1, 0), axis=0, keepdims=True)
         out_ref[ROWS : ROWS + 16, :] = stacked_rows(split3(unit)).astype(bf16)
         out_ref[ROWS + 16 : ROWS + 32, :] = sums[:, 0:256]
         out_ref[ROWS + 32 : ROWS + 48, 0:128] = sums[:, 256:384]
@@ -277,12 +275,13 @@
         grad = (act.astype(f32) * sig * (1.0 + conv * (1.0 - sig))).astype(bf16).astype(f32)
         grad_ref[pl.ds(start + 16, count), :] = grad
         if 0 <= start < ROWS:
-            activated_ref[pl.ds(start, count), :] = (conv * sig).astype(bf16)
+            activated = (conv * sig).astype(bf16)
+            for i in range(NZ):
+                activated_ref[i, pl.ds(start, count), :] = activated
             for tap in range(K):
                 product = grad * masked_ref[1 + tap : 1 + tap + count, :]
                 sums_ref[tap] += jnp.sum(product.reshape(count // 8, 8, COLS), axis=0)
             sums_ref[K] += jnp.sum(grad.reshape(count // 8, 8, COLS), axis=0)
-    activated_ref[ROWS:, :] = jnp.zeros((GATHER_ROWS - ROWS, COLS), bf16)
     small_ref[...] = jnp.sum(sums_ref[...], axis=1)
 
     for start, count in CHUNKS[1:4]:
@@ -352,24 +351,19 @@
     g1_ref,
     g2_ref,
     g3_ref,
-    kept_ref,
-    given_ref,
+    out_ref,
     left_ref,
-    right_ref,
 ):
     mean = stat_ref[:, 0:1]
     inv_std = stat_ref[:, 1:2]
-    half = QUARTER // NK
     for i in range(NZ):
         cut = pl.ds(i * COLS, COLS)
         scaled = (frames_ref[i].astype(f32) - mean) * inv_std * gain_ref[0:1, cut]
-        left_ref[i * COLS // half, :, pl.ds(i * COLS % half, COLS)] = scaled.astype(bf16)
-    order_blocks(place_ref, 10, (g0_ref, g1_ref, g2_ref, g3_ref), right_ref, 2 * COLS)
-    core = place_ref[9]
-    for out_ref, which in ((given_ref, 1 - core), (kept_ref, core)):
-        out = dot(left_ref[which], right_ref[...], 0, 0).astype(bf16)
-        for i in range(NY):
-            out_ref[i] = out[:, i * 2 * COLS : (i + 1) * 2 * COLS]
+        left_ref[:, cut] = scaled.astype(bf16)
+    for j, grad_ref in enumerate((g0_ref, g1_ref, g2_ref, g3_ref)):
+        start = pl.multiple_of(place_ref[j] * QUARTER, QUARTER)
+        out = dot(left_ref[...], grad_ref[0:ROWS, :], 0, 0)
+        out_ref[pl.ds(start, QUARTER), :] = out.astype(bf16)
 
 
 def order_blocks(place_ref, base, sources, out_ref, lanes):
@@ -382,25 +376,20 @@
                 out_ref[:, i * lanes : (i + 1) * lanes] = block_ref[0:ROWS, :]
 
 
-def encode_kernel(arrive, send, place_ref, act_ref, weight_ref, *refs):
-    left_ref = refs[NX]
-    arrive(1)
-    for i in range(NZ):
-        left_ref[:, pl.ds(i * COLS, COLS)] = act_ref[i, 0:ROWS, :]
-    for j, enc_ref in enumerate(refs[:NX]):
-        start = pl.multiple_of(place_ref[4 + j] * QUARTER, QUARTER)
-        weight = weight_ref[pl.ds(start, QUARTER), 2 * COLS : 3 * COLS]
-        enc_ref[...] = dot(left_ref[...], weight, 1, 0).astype(bf16)
-        send(j)
-
-
-def out_kernel(
-    place_ref, act_ref, g0_ref, g1_ref, g2_ref, g3_ref, kept_ref, given_ref, left_ref, grad_ref
-):
+def out_kernel(place_ref, act_ref, g0_ref, g1_ref, g2_ref, g3_ref, weight_ref, *refs):
+    enc_refs = refs[:NX]
+    kept_ref, given_ref, left_ref, grad_ref = refs[NX:]
     half = QUARTER // NK
     for i in range(NZ):
         left_ref[i * COLS // half, :, pl.ds(i * COLS % half, COLS)] = act_ref[i, 0:ROWS, :]
-    order_blocks(place_ref, 0, (g0_ref, g1_ref, g2_ref, g3_ref), grad_ref, COLS)
+    for j, enc_ref in enumerate(enc_refs):
+        total = jnp.zeros((ROWS, COLS), f32)
+        for h in range(NK):
+            start = pl.multiple_of(place_ref[4 + j] * QUARTER + h * half, half)
+            weight = weight_ref[pl.ds(start, half), 2 * COLS : 3 * COLS]
+            total = total + dot(left_ref[h], weight, 1, 0)
+        enc_ref[...] = total.astype(bf16)
+    order_blocks(place_ref, 10, (g0_ref, g1_ref, g2_ref, g3_ref), grad_ref, COLS)
     core = place_ref[9]
     for out_ref, which in ((given_ref, 1 - core), (kept_ref, core)):
         out = dot(left_ref[which], grad_ref[...], 0, 0).astype(bf16)
@@ -479,11 +468,10 @@
 def reduced(kept, given):
     other = lax.ppermute(given, "k", [(0, 1), (1, 0)])
     both = [(kept[i].astype(f32) + other[i].astype(f32)) for i in range(NY)]
-    sent = [part.astype(bf16) for part in both[1:]]
     total = both[0]
     for i in range(1, NY):
-        total = total + shifted(sent[i - 1], "y", NY, i).astype(f32)
-    return total, sent
+        total = total + shifted(both[i].astype(bf16), "y", NY, i).astype(f32)
+    return total
 
 
 def pieces(value):
@@ -506,6 +494,7 @@
     col_start = (x_index * NZ + lax.axis_index("z")) * COLS
     local_gain = lax.dynamic_slice_in_dim(gain, col_start, COLS, 0)[None]
     quarter_gain = lax.dynamic_slice_in_dim(gain, x_index * QUARTER, QUARTER, 0)[None]
+    gain_rows = jnp.pad(pieces(quarter_gain)[:, 0], ((0, 13), (0, 0)))
     y_index = lax.axis_index("y")
     steps = jnp.arange(NX, dtype=jnp.int32)
     below = (x_index + NX - steps) % NX
@@ -534,10 +523,10 @@
     pre_parts = call(
         project_kernel,
         [shape((ROWS + 48, 2 * COLS), bf16) for _ in range(NX)],
-        (place, after(frames_z, act_parts), quarter_gain, weights),
+        (place, after(frames_z, act_parts), quarter_gain, gain_rows, weights),
         smem=(0,),
-        near=(1, 3),
-        late=(2,),
+        near=(1, 4),
+        late=(2, 3),
         scratch=[pltpu.VMEM((ROWS, QUARTER), bf16)],
     )
     pre_moved = [pre_parts[0]] + [shifted(pre_parts[j], "x", NX, j) for j in range(1, NX)]
@@ -560,7 +549,7 @@
     activated, message, small = call(
         conv_kernel,
         [
-            shape((GATHER_ROWS, COLS), bf16),
+            shape((NZ, ROWS, COLS), bf16),
             shape((ROWS + 32, 2 * COLS), bf16),
             shape((K + 1, COLS), f32),
         ],
@@ -577,62 +566,50 @@
             pltpu.VMEM((K + 1, COLS), f32),
         ],
     )
-    act_z = lax.all_gather(activated, "z", axis=0, tiled=False)
+    act_z = exchange(activated, "z")
 
     vg_grads = spread(message, "x", NX)
     norm_parts = call(
         norm_kernel,
         shape((NZ, ROWS + 48, COLS), bf16),
-        (place, *vg_grads, weights),
+        (place, *vg_grads, after(weights, act_z)),
         smem=(0,),
         near=(2, 3, 4, 5),
         late=(1,),
     )
     norm_moved = exchange(norm_parts, "z")
     held = lax.optimization_barrier((vg_grads, norm_parts))[0]
-    kept, given = call(
+    weight_parts = call(
         weight_kernel,
-        [shape((NY, QUARTER // NK, 2 * COLS), bf16) for _ in range(2)],
+        shape((NY * QUARTER, 2 * COLS), bf16),
         (place, frames_z, quarter_gain, stat, *held),
         smem=(0,),
         near=(5, 6, 7),
-        scratch=[
-            pltpu.VMEM((NK, ROWS, QUARTER // NK), bf16),
-            pltpu.VMEM((ROWS, NY * 2 * COLS), bf16),
-        ],
-    )
-    in_weight, in_sent = reduced(kept, given)
-
-    enc_parts = call(
-        encode_kernel,
-        [shape((ROWS, COLS), bf16) for _ in range(NX)],
-        (place, act_z, after(weights, in_sent)),
+        scratch=[pltpu.VMEM((ROWS, QUARTER), bf16)],
+    )
+    in_weight = lax.psum_scatter(
+        weight_parts, TIME, scatter_dimension=0, tiled=True
+    ).astype(f32)
+
+    out_parts = call(
+        out_kernel,
+        [shape((ROWS, COLS), bf16) for _ in range(NX)]
+        + [shape((NY, QUARTER // NK, COLS), bf16) for _ in range(2)],
+        (place, act_z, *after(grads, norm_parts), weights),
         smem=(0,),
-        near=(2,),
-        late=(1,),
-        scratch=[pltpu.VMEM((ROWS, QUARTER), bf16)],
-    )
-    enc = [enc_parts[0]] + [shifted(enc_parts[j], "x", NX, j) for j in range(1, NX)]
-    kept, given = call(
-        out_kernel,
-        [shape((NY, QUARTER // NK, COLS), bf16) for _ in range(2)],
-        (place, after(act_z, enc_parts), *grads),
-        smem=(0,),
+        near=(1, 6),
         scratch=[
             pltpu.VMEM((NK, ROWS, QUARTER // NK), bf16),
             pltpu.VMEM((ROWS, NY * COLS), bf16),
         ],
     )
-    other = lax.ppermute(given, "k", [(0, 1), (1, 0)])
-    both = (kept.astype(f32) + other.astype(f32)).astype(bf16)
-    grad_out_weight = lax.psum_scatter(
-        both.reshape(NY * QUARTER // NK, COLS), "y", scatter_dimension=0, tiled=True
-    ).astype(f32)
+    grad_out_weight = reduced(*out_parts[NX:])
+    enc = [out_parts[0]] + [shifted(out_parts[j], "x", NX, j) for j in range(1, NX)]
 
     results, gain_term = call(
         input_kernel,
         [shape((ROWS, 2 * COLS), bf16), shape((8, COLS), f32)],
-        (after(norm_moved, both), frames, grad_out, stat, local_gain, *enc),
+        (norm_moved, frames, grad_out, stat, local_gain, *enc),
         near=(0, 6, 7, 8),
     )
     results = swap_xy(results)

time: 206 us -> 200 us (0.971)
  other arithmetic: 9.1 us -> 5.5 us
  waiting for transfers between devices: 65.8 us -> 63.5 us
    all_to_all x3 -> x4, waiting for transfers between devices: 0.01 us -> 30.6 us  [exchange(): return lax.all_to_all(parts, axis, 0, 0, tiled=True)]
    ppermute x15, waiting for transfers between devices: 29.5 us -> 14.8 us  [shifted(): lax.ppermute(block, axis, [(i, (i + shift) % count) for i in range(count)])]
    all_gather x1 -> x0, waiting for transfers between devices: 13.5 us -> none  [shards(): act_z = lax.all_gather(activated, 'z', axis=0, tiled=False)]
    convert_element_type x3 -> x1, other arithmetic: 5.96 us -> 1.15 us  [reduced(): total = total + shifted(both[i].astype(bf16), 'y', NY, i).astype(f32)]
    all_to_all x3 -> x4, starting transfers between devices: 22.8 us -> 27.1 us  [exchange(): return lax.all_to_all(parts, axis, 0, 0, tiled=True)]
    ppermute x15, starting transfers between devices: 19.3 us -> 15.7 us  [shifted(): lax.ppermute(block, axis, [(i, (i + shift) % count) for i in range(count)])]
    reduce_scatter x1, waiting for transfers between devices: 3.43 us -> 0.01 us  [shards(): lax.psum_scatter(weight_parts, TIME, scatter_dimension=0, tiled=True)]
    ppermute x4, starting transfers between devices: 9.18 us -> 11.4 us  [shards(): arrived.append(lax.ppermute(small, ('x', 'y'), route))]
  transfers between devices with their start and end apart: 33 -> 32, of which waited for: 17 -> 15; matrix products, arithmetic and copies ran while one was open for 7% -> 5% of each run, Pallas kernels for 14% -> 9%
where the time goes in v10:
time: 200 us; the launch traced here: 199 us
  starting transfers between devices  70.6 us (35%)
  waiting for transfers between devices  63.5 us (32%)
  Pallas kernels  33.9 us (17%)
  between operations  14.5 us (7%)
  local copies, waits for them, and re-layouts  11.3 us (6%)
  other arithmetic  5.5 us (3%)
    pallas_call x9, Pallas kernels, call(): pl.pallas_call(whole, out_shape=[pltpu.HBM(out.shape, out.dtype) for out...  33.9 us
    all_to_all x4, waiting for transfers between devices, exchange(): return lax.all_to_all(parts, axis, 0, 0, tiled=True)  30.6 us
    all_to_all x4, starting transfers between devices, exchange(): return lax.all_to_all(parts, axis, 0, 0, tiled=True)  27.1 us
    ppermute x15, starting transfers between devices, shifted(): lax.ppermute(block, axis, [(i, (i + shift) % count) for i in range(count)])  15.7 us
    ppermute x15, waiting for transfers between devices, shifted(): lax.ppermute(block, axis, [(i, (i + shift) % count) for i in range(count)])  14.8 us
    ppermute x3, waiting for transfers between devices, swap_xy(): lax.ppermute(block, ('x', 'y'), [(a * NY + b, b * NY + a) for a in range(...  13.9 us
    ppermute x3, starting transfers between devices, swap_xy(): lax.ppermute(block, ('x', 'y'), [(a * NY + b, b * NY + a) for a in range(...  11.8 us
    ppermute x4, starting transfers between devices, shards(): arrived.append(lax.ppermute(small, ('x', 'y'), route))  11.4 us
  transfers between devices with their start and end apart: 32, of which 15 were waited for; matrix products, arithmetic and copies ran while one was open for 5% of the time, Pallas kernels for 9%

profile of v10, /device:TPU:6, one launch (start us, length us, event | category | flops | bytes accessed | tf_op | source)
XLA Modules:
  0.0 199.3 jit_solution(4003850851020425999)
XLA Ops:
  9.1 4.8 %collective-permute-start = (bf16[384,128]{1,0:T(8,128)(2,1)}, bf16[384,128]{1,0:T(8,128)(2,1)S(1)}, u32[]{:S(2)}, u32[]{:S(2)}) collective-permute-start(bf16[384,128]{1,0:T(8,128)(2,1)} %param.8), channel_id=1, source_target_pairs={{0,0},{8,64},{16,128},{24,192},{64,8},{72,72},{80,136},{88,200},{1... | collective-permute-start | bytes 294920 | tf_op jit(solution)/shard_map/ppermute | solution.py:438
  14.0 7.3 %collective-permute-done.refs_1_ = bf16[384,128]{1,0:T(8,128)(2,1)S(1)} collective-permute-done((bf16[384,128]{1,0:T(8,128)(2,1)}, bf16[384,128]{1,0:T(8,128)(2,1)S(1)}, u32[]{:S(2)}, u32[]{:S(2)}) %collective-permute-start) | collective-permute-done | bytes 98336 | tf_op jit(solution)/shard_map/ppermute | solution.py:438
  22.9 8.5 %all-to-all-start = ((bf16[8,384,128]{2,1,0:T(8,128)(2,1)}), bf16[8,384,128]{2,1,0:T(8,128)(2,1)}, u32[]{:S(2)}, u32[]{:S(2)}) async-start(bf16[8,384,128]{2,1,0:T(8,128)(2,1)} %broadcast_in_dim.6), calls=%async_computation | async-start | bytes 1572864 | tf_op jit(solution)/shard_map/all_to_all | solution.py:453
  31.5 4.8 %collective-permute-start.1 = (bf16[480,128]{1,0:T(8,128)(2,1)S(1)}, bf16[480,128]{1,0:T(8,128)(2,1)S(1)}, u32[]{:S(2)}, u32[]{:S(2)}) collective-permute-start(bf16[480,128]{1,0:T(8,128)(2,1)S(1)} %pad_maximum_fusion.1), channel_id=1, source_target_pairs={{0,0},{8,64},{16,128},{24,192},{64,8},{72,72},{80,136},{88,200},{1... | collective-permute-start | bytes 368648 | tf_op jit(solution)/shard_map/ppermute | solution.py:438
  36.3 6.6 %collective-permute-done.1.refs_5_ = bf16[480,128]{1,0:T(8,128)(2,1)S(1)} collective-permute-done((bf16[480,128]{1,0:T(8,128)(2,1)S(1)}, bf16[480,128]{1,0:T(8,128)(2,1)S(1)}, u32[]{:S(2)}, u32[]{:S(2)}) %collective-permute-start.1) | collective-permute-done | bytes 122912 | tf_op jit(solution)/shard_map/ppermute | solution.py:438
  43.0 2.3 %collective-permute-start.3 = (bf16[384,128]{1,0:T(8,128)(2,1)S(1)}, bf16[384,128]{1,0:T(8,128)(2,1)S(1)}, u32[]{:S(2)}, u32[]{:S(2)}) collective-permute-start(bf16[384,128]{1,0:T(8,128)(2,1)S(1)} %slice.80.refs_1_.refs_2_), channel_id=1, source_target_pairs={{0,128},{64,192},{128,0},{192,64},{1,129},{65,193},{129,1},{193,65... | collective-permute-start | bytes 294920 | tf_op jit(solution)/shard_map/ppermute | solution.py:461
  45.4 2.2 %collective-permute-done.2.refs_2_.refs_3_ = bf16[384,128]{1,0:T(8,128)(2,1)S(1)} collective-permute-done((bf16[384,128]{1,0:T(8,128)(2,1)S(1)}, bf16[384,128]{1,0:T(8,128)(2,1)S(1)}, u32[]{:S(2)}, u32[]{:S(2)}) %collective-permute-start.2) | collective-permute-done | bytes 98336 | tf_op jit(solution)/shard_map/ppermute | solution.py:461
  49.2 1.9 collective-permute-done.4.refs_4_.refs_5_
  53.1 2.5 %act_kernel.1 = bf16[8,384,128]{2,1,0:T(8,128)(2,1)} custom-call(s32[14]{0:T(128)S(1)} %concatenate.49.refs_0_, bf16[384,128]{1,0:T(8,128)(2,1)S(1)} %slice.80.refs_1_.refs_2_, bf16[384,128]{1,0:T(8,128)(2,1)S(1)} %collective-permute-done.2.refs_2_.refs_3_, bf16[384,128]{1,0:T(8,128)(2,1)S(1)} %collective-permute-done.3.refs_3_.refs_4_, ...), custom_call_target="tpu_custom_call" | custom-call | tf_op jit(solution)/shard_map/act_kernel/pallas_call | solution.py:130
  55.6 7.2 %all-to-all-start.1 = ((bf16[8,384,128]{2,1,0:T(8,128)(2,1)}), bf16[8,384,128]{2,1,0:T(8,128)(2,1)}, u32[]{:S(2)}, u32[]{:S(2)}) async-start(bf16[8,384,128]{2,1,0:T(8,128)(2,1)} %act_kernel.1), calls=%async_computation.1 | async-start | bytes 1572864 | tf_op jit(solution)/shard_map/all_to_all | solution.py:453
  64.2 4.3 %project_kernel.1 = (bf16[432,256]{1,0:T(8,128)(2,1)}, bf16[432,256]{1,0:T(8,128)(2,1)}, bf16[432,256]{1,0:T(8,128)(2,1)}, bf16[432,256]{1,0:T(8,128)(2,1)}) custom-call(s32[14]{0:T(128)S(1)} %concatenate.49.refs_0_, bf16[8,384,128]{2,1,0:T(8,128)(2,1)} %all-to-all-done.refs_1_, f32[1,1024]{1,0:T(1,128)} %bitcast.27, bf16[16,1024]{1,0:T(8,128)(2,1)} %pad.4.refs_3_, ...), custom_call_target="tpu_custom_call" | custom-call | tf_op jit(solution)/shard_map/project_kernel/pallas_call | solution.py:130
  71.2 3.6 %collective-permute-done.5.refs_1_ = bf16[432,256]{1,0:T(8,128)(2,1)S(1)} collective-permute-done((bf16[432,256]{1,0:T(8,128)(2,1)}, bf16[432,256]{1,0:T(8,128)(2,1)S(1)}, u32[]{:S(2)}, u32[]{:S(2)}) %collective-permute-start.5) | collective-permute-done | bytes 221216 | tf_op jit(solution)/shard_map/ppermute | solution.py:461
  74.7 2.8 %collective-permute-done.6.refs_2_ = bf16[432,256]{1,0:T(8,128)(2,1)S(1)} collective-permute-done((bf16[432,256]{1,0:T(8,128)(2,1)}, bf16[432,256]{1,0:T(8,128)(2,1)S(1)}, u32[]{:S(2)}, u32[]{:S(2)}) %collective-permute-start.6) | collective-permute-done | bytes 221216 | tf_op jit(solution)/shard_map/ppermute | solution.py:461
  77.5 2.3 %collective-permute-done.7.refs_3_ = bf16[432,256]{1,0:T(8,128)(2,1)S(1)} collective-permute-done((bf16[432,256]{1,0:T(8,128)(2,1)}, bf16[432,256]{1,0:T(8,128)(2,1)S(1)}, u32[]{:S(2)}, u32[]{:S(2)}) %collective-permute-start.7) | collective-permute-done | bytes 221216 | tf_op jit(solution)/shard_map/ppermute | solution.py:461
  79.8 3.0 %gate_kernel.1 = (f32[384,256]{1,0:T(8,128)}, bf16[384,128]{1,0:T(8,128)(2,1)}, f32[8,256]{1,0:T(8,128)}, f32[384,128]{1,0:T(8,128)}) custom-call(bf16[432,256]{1,0:T(8,128)(2,1)} %get-tuple-element.42.refs_0_, bf16[432,256]{1,0:T(8,128)(2,1)S(1)} %collective-permute-done.5.refs_1_, bf16[432,256]{1,0:T(8,128)(2,1)S(1)} %collective-permute-done.6.refs_2_, ...), custom_call_target="tpu_custom_call" | custom-call | tf_op jit(solution)/shard_map/gate_kernel/pallas_call | solution.py:130
  83.5 1.9 sum_kernel.1.refs_2_
  87.5 3.0 %collective-permute-start.8 = (bf16[48,128]{1,0:T(8,128)(2,1)S(1)}, bf16[48,128]{1,0:T(8,128)(2,1)S(1)}, u32[]{:S(2)}, u32[]{:S(2)}) collective-permute-start(bf16[48,128]{1,0:T(8,128)(2,1)S(1)} %pad_maximum_fusion.4), channel_id=1, source_target_pairs={{0,32},{32,8},{8,40},{40,16},{16,48},{48,24},{24,56},{1,33},{33,9}... | collective-permute-start | bytes 36872 | tf_op jit(solution)/shard_map/ppermute | solution.py:447
  91.3 4.1 %conv_kernel.1 = (bf16[8,384,128]{2,1,0:T(8,128)(2,1)}, bf16[416,256]{1,0:T(8,128)(2,1)}, f32[32,128]{1,0:T(8,128)}) custom-call(s32[1]{0:T(128)} %bitcast.refs_0_, bf16[384,128]{1,0:T(8,128)(2,1)} %get-tuple-element.46.refs_1_, bf16[384,128]{1,0:T(8,128)(2,1)} %sum_kernel.1.refs_2_, bf16[48,128]{1,0:T(8,128)(2,1)S(1)} %collective-permute-done.8.refs_3_, ...), custom_call_target="tpu_custom_call" | custom-call | tf_op jit(solution)/shard_map/conv_kernel/pallas_call | solution.py:130
  95.4 7.2 %all-to-all-start.2 = ((bf16[8,384,128]{2,1,0:T(8,128)(2,1)}), bf16[8,384,128]{2,1,0:T(8,128)(2,1)}, u32[]{:S(2)}, u32[]{:S(2)}) async-start(bf16[8,384,128]{2,1,0:T(8,128)(2,1)} %get-tuple-element.50), calls=%async_computation.2 | async-start | bytes 1572864 | tf_op jit(solution)/shard_map/all_to_all | solution.py:453
  105.6 20.8 %all-to-all-done.2.refs_1_ = bf16[8,384,128]{2,1,0:T(8,128)(2,1)} async-done(((bf16[8,384,128]{2,1,0:T(8,128)(2,1)}), bf16[8,384,128]{2,1,0:T(8,128)(2,1)}, u32[]{:S(2)}, u32[]{:S(2)}) %all-to-all-start.2) | async-done | bytes 786464 | tf_op jit(solution)/shard_map/all_to_all | solution.py:453
  126.4 3.9 %norm_kernel.1 = bf16[8,432,128]{2,1,0:T(8,128)(2,1)} custom-call(s32[14]{0:T(128)S(1)} %copy-done.7, bf16[416,256]{1,0:T(8,128)(2,1)} %get-tuple-element.62.refs_1_.refs_4_, bf16[416,256]{1,0:T(8,128)(2,1)S(1)} %collective-permute-done.10.refs_2_.refs_5_, bf16[416,256]{1,0:T(8,128)(2,1)} %collective-permute-done.11.refs_3_.refs_6_, ...), custom_call_target="tpu_custom_call" | custom-call | tf_op jit(solution)/shard_map/norm_kernel/pallas_call | solution.py:130
  130.3 5.5 %weight_kernel.1 = bf16[4096,256]{1,0:T(8,128)(2,1)} custom-call(s32[14]{0:T(128)S(1)} %copy-done.7, bf16[8,384,128]{2,1,0:T(8,128)(2,1)} %all-to-all-done.refs_1_, f32[1,1024]{1,0:T(1,128)} %bitcast.28, f32[384,128]{1,0:T(8,128)} %get-tuple-element.52.refs_3_, bf16[416,256]{1,0:T(8,128)(2,1)} %get-tuple-element.62.refs_1_.refs_4_, ...), custom_call_target="tpu_custom_call" | custom-call | tf_op jit(solution)/shard_map/weight_kernel/pallas_call | solution.py:130
  135.8 4.2 %all-to-all-start.3 = ((bf16[8,432,128]{2,1,0:T(8,128)(2,1)}), bf16[8,432,128]{2,1,0:T(8,128)(2,1)}, u32[]{:S(2)}, u32[]{:S(2)}) async-start(bf16[8,432,128]{2,1,0:T(8,128)(2,1)} %norm_kernel.1), calls=%async_computation.3 | async-start | bytes 1769472 | tf_op jit(solution)/shard_map/all_to_all | solution.py:453
  140.1 5.1 %out_kernel.1 = (bf16[384,128]{1,0:T(8,128)(2,1)}, bf16[384,128]{1,0:T(8,128)(2,1)}, bf16[384,128]{1,0:T(8,128)(2,1)}, bf16[384,128]{1,0:T(8,128)(2,1)}, bf16[4,...) custom-call(s32[14]{0:T(128)S(1)} %copy-done.7, bf16[8,384,128]{2,1,0:T(8,128)(2,1)} %all-to-all-done.2.refs_1_, ...), custom_call_target="tpu_custom_call" | custom-call | tf_op jit(solution)/shard_map/out_kernel/pallas_call | solution.py:130
  151.0 2.5 %collective-permute-start.24 = (bf16[512,128]{1,0:T(8,128)(2,1)S(1)}, bf16[512,128]{1,0:T(8,128)(2,1)S(1)}, u32[]{:S(2)}, u32[]{:S(2)}) collective-permute-start(bf16[512,128]{1,0:T(8,128)(2,1)S(1)} %get-tuple-element.78), channel_id=1, source_target_pairs={{0,16},{8,24},{16,0},{24,8},{1,17},{9,25},{17,1},{25,9},{2,18},{10... | collective-permute-start | bytes 393224 | tf_op jit(solution)/shard_map/ppermute | solution.py:461
  153.5 2.0 collective-permute-start.25
  155.9 9.8 %all-to-all-done.3.refs_0_ = bf16[8,432,128]{2,1,0:T(8,128)(2,1)} async-done(((bf16[8,432,128]{2,1,0:T(8,128)(2,1)}), bf16[8,432,128]{2,1,0:T(8,128)(2,1)}, u32[]{:S(2)}, u32[]{:S(2)}) %all-to-all-start.3) | async-done | bytes 884768 | tf_op jit(solution)/shard_map/all_to_all | solution.py:453
  165.7 3.7 %input_kernel.1 = (bf16[384,256]{1,0:T(8,128)(2,1)}, f32[8,128]{1,0:T(8,128)}) custom-call(bf16[8,432,128]{2,1,0:T(8,128)(2,1)} %all-to-all-done.3.refs_0_, bf16[384,128]{1,0:T(8,128)(2,1)} %copy-done.9, bf16[384,128]{1,0:T(8,128)(2,1)} %copy-done.2, f32[384,128]{1,0:T(8,128)} %get-tuple-element.52.refs_3_, f32[1,128]{1,0:T(1,128)} %dynamic-slice_bitcast_fusion.refs_4_, ...), custom_call_target="tpu_custom_call" | custom-call | tf_op jit(solution)/shard_map/input_kernel/pallas_call | solution.py:130
  170.1 2.2 %collective-permute-start.16 = (bf16[384,256]{1,0:T(8,128)(2,1)}, bf16[384,256]{1,0:T(8,128)(2,1)S(1)}, u32[]{:S(2)}, u32[]{:S(2)}) collective-permute-start(bf16[384,256]{1,0:T(8,128)(2,1)} %get-tuple-element.61), channel_id=1, source_target_pairs={{0,0},{8,64},{16,128},{24,192},{64,8},{72,72},{80,136},{88,200},{1... | collective-permute-start | bytes 589832 | tf_op jit(solution)/shard_map/ppermute | solution.py:438
  172.4 6.9 %collective-permute-start.18 = (f32[40,128]{1,0:T(8,128)S(1)}, f32[40,128]{1,0:T(8,128)S(1)}, u32[]{:S(2)}, u32[]{:S(2)}) collective-permute-start(f32[40,128]{1,0:T(8,128)S(1)} %add.105), channel_id=1, source_target_pairs={{0,0},{8,64},{16,128},{24,192},{64,8},{72,72},{80,136},{88,200},{1... | collective-permute-start | bytes 61448 | tf_op jit(solution)/shard_map/ppermute | solution.py:626
  180.3 3.5 %collective-permute-start.20 = (f32[40,128]{1,0:T(8,128)S(1)}, f32[40,128]{1,0:T(8,128)S(1)}, u32[]{:S(2)}, u32[]{:S(2)}) collective-permute-start(f32[40,128]{1,0:T(8,128)S(1)} %add.105), channel_id=1, source_target_pairs={{0,128},{8,192},{16,0},{24,64},{64,136},{72,200},{80,8},{88,72},{1... | collective-permute-start | bytes 61448 | tf_op jit(solution)/shard_map/ppermute | solution.py:626
  186.8 2.0 %collective-permute-done.21 = f32[40,128]{1,0:T(8,128)S(1)} collective-permute-done((f32[40,128]{1,0:T(8,128)S(1)}, f32[40,128]{1,0:T(8,128)S(1)}, u32[]{:S(2)}, u32[]{:S(2)}) %collective-permute-start.21) | collective-permute-done | bytes 20512 | tf_op jit(solution)/shard_map/ppermute | solution.py:626
  (104 shorter events, 32.4 us)
Async XLA Ops:
  7.2 43.9 %all-gather.2.cloned.1.call-start = ((), (), s32[]{:S(2)}) async-start(), calls=%async_computation.5 | async-start | bytes 3538944 | tf_op jit(solution)/shard_map/all_gather | solution.py:507
  9.1 12.1 %collective-permute-start = (bf16[384,128]{1,0:T(8,128)(2,1)}, bf16[384,128]{1,0:T(8,128)(2,1)S(1)}, u32[]{:S(2)}, u32[]{:S(2)}) collective-permute-start(bf16[384,128]{1,0:T(8,128)(2,1)} %param.8), channel_id=1, source_target_pairs={{0,0},{8,64},{16,128},{24,192},{64,8},{72,72},{80,136},{88,200},{1... | collective-permute-start | bytes 294920 | tf_op jit(solution)/shard_map/ppermute | solution.py:438
  22.9 32.6 %all-to-all-start = ((bf16[8,384,128]{2,1,0:T(8,128)(2,1)}), bf16[8,384,128]{2,1,0:T(8,128)(2,1)}, u32[]{:S(2)}, u32[]{:S(2)}) async-start(bf16[8,384,128]{2,1,0:T(8,128)(2,1)} %broadcast_in_dim.6), calls=%async_computation | async-start | bytes 1572864 | tf_op jit(solution)/shard_map/all_to_all | solution.py:453
  31.5 11.4 %collective-permute-start.1 = (bf16[480,128]{1,0:T(8,128)(2,1)S(1)}, bf16[480,128]{1,0:T(8,128)(2,1)S(1)}, u32[]{:S(2)}, u32[]{:S(2)}) collective-permute-start(bf16[480,128]{1,0:T(8,128)(2,1)S(1)} %pad_maximum_fusion.1), channel_id=1, source_target_pairs={{0,0},{8,64},{16,128},{24,192},{64,8},{72,72},{80,136},{88,200},{1... | collective-permute-start | bytes 368648 | tf_op jit(solution)/shard_map/ppermute | solution.py:438
  42.9 4.7 %collective-permute-start.2 = (bf16[384,128]{1,0:T(8,128)(2,1)S(1)}, bf16[384,128]{1,0:T(8,128)(2,1)S(1)}, u32[]{:S(2)}, u32[]{:S(2)}) collective-permute-start(bf16[384,128]{1,0:T(8,128)(2,1)S(1)} %slice.80.refs_1_.refs_2_), channel_id=1, source_target_pairs={{0,64},{64,128},{128,192},{192,0},{1,65},{65,129},{129,193},{193,1... | collective-permute-start | bytes 294920 | tf_op jit(solution)/shard_map/ppermute | solution.py:461
  43.0 6.2 %collective-permute-start.3 = (bf16[384,128]{1,0:T(8,128)(2,1)S(1)}, bf16[384,128]{1,0:T(8,128)(2,1)S(1)}, u32[]{:S(2)}, u32[]{:S(2)}) collective-permute-start(bf16[384,128]{1,0:T(8,128)(2,1)S(1)} %slice.80.refs_1_.refs_2_), channel_id=1, source_target_pairs={{0,128},{64,192},{128,0},{192,64},{1,129},{65,193},{129,1},{193,65... | collective-permute-start | bytes 294920 | tf_op jit(solution)/shard_map/ppermute | solution.py:461
  45.3 5.8 %collective-permute-start.4 = (bf16[384,128]{1,0:T(8,128)(2,1)S(1)}, bf16[384,128]{1,0:T(8,128)(2,1)S(1)}, u32[]{:S(2)}, u32[]{:S(2)}) collective-permute-start(bf16[384,128]{1,0:T(8,128)(2,1)S(1)} %slice.80.refs_1_.refs_2_), channel_id=1, source_target_pairs={{0,192},{64,0},{128,64},{192,128},{1,193},{65,1},{129,65},{193,129... | collective-permute-start | bytes 294920 | tf_op jit(solution)/shard_map/ppermute | solution.py:461
  55.6 27.9 %all-to-all-start.1 = ((bf16[8,384,128]{2,1,0:T(8,128)(2,1)}), bf16[8,384,128]{2,1,0:T(8,128)(2,1)}, u32[]{:S(2)}, u32[]{:S(2)}) async-start(bf16[8,384,128]{2,1,0:T(8,128)(2,1)} %act_kernel.1), calls=%async_computation.1 | async-start | bytes 1572864 | tf_op jit(solution)/shard_map/all_to_all | solution.py:453
  68.5 6.2 %collective-permute-start.5 = (bf16[432,256]{1,0:T(8,128)(2,1)}, bf16[432,256]{1,0:T(8,128)(2,1)S(1)}, u32[]{:S(2)}, u32[]{:S(2)}) collective-permute-start(bf16[432,256]{1,0:T(8,128)(2,1)} %get-tuple-element.43), channel_id=1, source_target_pairs={{0,64},{64,128},{128,192},{192,0},{1,65},{65,129},{129,193},{193,1... | collective-permute-start | bytes 663560 | tf_op jit(solution)/shard_map/ppermute | solution.py:461
  69.8 7.8 %collective-permute-start.6 = (bf16[432,256]{1,0:T(8,128)(2,1)}, bf16[432,256]{1,0:T(8,128)(2,1)S(1)}, u32[]{:S(2)}, u32[]{:S(2)}) collective-permute-start(bf16[432,256]{1,0:T(8,128)(2,1)} %get-tuple-element.44), channel_id=1, source_target_pairs={{0,128},{64,192},{128,0},{192,64},{1,129},{65,193},{129,1},{193,65... | collective-permute-start | bytes 663560 | tf_op jit(solution)/shard_map/ppermute | solution.py:461
  70.7 9.1 %collective-permute-start.7 = (bf16[432,256]{1,0:T(8,128)(2,1)}, bf16[432,256]{1,0:T(8,128)(2,1)S(1)}, u32[]{:S(2)}, u32[]{:S(2)}) collective-permute-start(bf16[432,256]{1,0:T(8,128)(2,1)} %get-tuple-element.45), channel_id=1, source_target_pairs={{0,192},{64,0},{128,64},{192,128},{1,193},{65,1},{129,65},{193,129... | collective-permute-start | bytes 663560 | tf_op jit(solution)/shard_map/ppermute | solution.py:461
  86.2 4.3 %collective-permute-start.9 = (bf16[48,128]{1,0:T(8,128)(2,1)S(1)}, bf16[48,128]{1,0:T(8,128)(2,1)S(1)}, u32[]{:S(2)}, u32[]{:S(2)}) collective-permute-start(bf16[48,128]{1,0:T(8,128)(2,1)S(1)} %pad_maximum_fusion.5), channel_id=1, source_target_pairs={{32,0},{8,32},{40,8},{16,40},{48,16},{24,48},{56,24},{33,1},{9,33}... | collective-permute-start | bytes 36872 | tf_op jit(solution)/shard_map/ppermute | solution.py:448
  87.5 3.9 %collective-permute-start.8 = (bf16[48,128]{1,0:T(8,128)(2,1)S(1)}, bf16[48,128]{1,0:T(8,128)(2,1)S(1)}, u32[]{:S(2)}, u32[]{:S(2)}) collective-permute-start(bf16[48,128]{1,0:T(8,128)(2,1)S(1)} %pad_maximum_fusion.4), channel_id=1, source_target_pairs={{0,32},{32,8},{8,40},{40,16},{16,48},{48,24},{24,56},{1,33},{33,9}... | collective-permute-start | bytes 36872 | tf_op jit(solution)/shard_map/ppermute | solution.py:447
  95.4 31.0 %all-to-all-start.2 = ((bf16[8,384,128]{2,1,0:T(8,128)(2,1)}), bf16[8,384,128]{2,1,0:T(8,128)(2,1)}, u32[]{:S(2)}, u32[]{:S(2)}) async-start(bf16[8,384,128]{2,1,0:T(8,128)(2,1)} %get-tuple-element.50), calls=%async_computation.2 | async-start | bytes 1572864 | tf_op jit(solution)/shard_map/all_to_all | solution.py:453
  102.6 88.0 %reduce-scatter.2.cloned.1.call-start = ((), (), s32[]{:S(2)}) async-start(), calls=%async_computation.6 | async-start | bytes 2359296 | tf_op jit(solution)/shard_map/reduce_scatter | solution.py:590
  102.7 23.7 %collective-permute-start.10 = (bf16[416,256]{1,0:T(8,128)(2,1)}, bf16[416,256]{1,0:T(8,128)(2,1)S(1)}, u32[]{:S(2)}, u32[]{:S(2)}) collective-permute-start(bf16[416,256]{1,0:T(8,128)(2,1)} %get-tuple-element.62.refs_1_.refs_4_), channel_id=1, source_target_pairs={{0,64},{64,128},{128,192},{192,0},{1,65},{65,129},{129,193},{193,1... | collective-permute-start | bytes 638984 | tf_op jit(solution)/shard_map/ppermute | solution.py:461
  103.5 22.9 %collective-permute-start.11 = (bf16[416,256]{1,0:T(8,128)(2,1)}, bf16[416,256]{1,0:T(8,128)(2,1)}, u32[]{:S(2)}, u32[]{:S(2)}) collective-permute-start(bf16[416,256]{1,0:T(8,128)(2,1)} %get-tuple-element.62.refs_1_.refs_4_), channel_id=1, source_target_pairs={{0,128},{64,192},{128,0},{192,64},{1,129},{65,193},{129,1},{193,65... | collective-permute-start | bytes 638984 | tf_op jit(solution)/shard_map/ppermute | solution.py:461
  104.8 21.7 %collective-permute-start.12 = (bf16[416,256]{1,0:T(8,128)(2,1)}, bf16[416,256]{1,0:T(8,128)(2,1)}, u32[]{:S(2)}, u32[]{:S(2)}) collective-permute-start(bf16[416,256]{1,0:T(8,128)(2,1)} %get-tuple-element.62.refs_1_.refs_4_), channel_id=1, source_target_pairs={{0,192},{64,0},{128,64},{192,128},{1,193},{65,1},{129,65},{193,129... | collective-permute-start | bytes 638984 | tf_op jit(solution)/shard_map/ppermute | solution.py:461
  135.8 29.9 %all-to-all-start.3 = ((bf16[8,432,128]{2,1,0:T(8,128)(2,1)}), bf16[8,432,128]{2,1,0:T(8,128)(2,1)}, u32[]{:S(2)}, u32[]{:S(2)}) async-start(bf16[8,432,128]{2,1,0:T(8,128)(2,1)} %norm_kernel.1), calls=%async_computation.3 | async-start | bytes 1769472 | tf_op jit(solution)/shard_map/all_to_all | solution.py:453
  145.2 4.1 %collective-permute-start.22 = (bf16[4,512,128]{2,1,0:T(8,128)(2,1)}, bf16[4,512,128]{2,1,0:T(8,128)(2,1)S(1)}, u32[]{:S(2)}, u32[]{:S(2)}) collective-permute-start(bf16[4,512,128]{2,1,0:T(8,128)(2,1)} %get-tuple-element.73), channel_id=1, source_target_pairs={{0,32},{32,0},{1,33},{33,1},{2,34},{34,2},{3,35},{35,3},{4,36},{36... | collective-permute-start | bytes 1572872 | tf_op jit(solution)/shard_map/ppermute | solution.py:469
  146.6 6.9 %collective-permute-start.13 = (bf16[384,128]{1,0:T(8,128)(2,1)}, bf16[384,128]{1,0:T(8,128)(2,1)S(1)}, u32[]{:S(2)}, u32[]{:S(2)}) collective-permute-start(bf16[384,128]{1,0:T(8,128)(2,1)} %get-tuple-element.58), channel_id=1, source_target_pairs={{0,64},{64,128},{128,192},{192,0},{1,65},{65,129},{129,193},{193,1... | collective-permute-start | bytes 294920 | tf_op jit(solution)/shard_map/ppermute | solution.py:461
  147.2 8.3 %collective-permute-start.14 = (bf16[384,128]{1,0:T(8,128)(2,1)}, bf16[384,128]{1,0:T(8,128)(2,1)S(1)}, u32[]{:S(2)}, u32[]{:S(2)}) collective-permute-start(bf16[384,128]{1,0:T(8,128)(2,1)} %get-tuple-element.59), channel_id=1, source_target_pairs={{0,128},{64,192},{128,0},{192,64},{1,129},{65,193},{129,1},{193,65... | collective-permute-start | bytes 294920 | tf_op jit(solution)/shard_map/ppermute | solution.py:461
  148.4 7.5 %collective-permute-start.15 = (bf16[384,128]{1,0:T(8,128)(2,1)}, bf16[384,128]{1,0:T(8,128)(2,1)S(1)}, u32[]{:S(2)}, u32[]{:S(2)}) collective-permute-start(bf16[384,128]{1,0:T(8,128)(2,1)} %get-tuple-element.60), channel_id=1, source_target_pairs={{0,192},{64,0},{128,64},{192,128},{1,193},{65,1},{129,65},{193,129... | collective-permute-start | bytes 294920 | tf_op jit(solution)/shard_map/ppermute | solution.py:461
  150.4 28.9 %collective-permute-start.23 = (bf16[512,128]{1,0:T(8,128)(2,1)S(1)}, bf16[512,128]{1,0:T(8,128)(2,1)S(1)}, u32[]{:S(2)}, u32[]{:S(2)}) collective-permute-start(bf16[512,128]{1,0:T(8,128)(2,1)S(1)} %get-tuple-element.76), channel_id=1, source_target_pairs={{0,8},{8,16},{16,24},{24,0},{1,9},{9,17},{17,25},{25,1},{2,10},{10... | collective-permute-start | bytes 393224 | tf_op jit(solution)/shard_map/ppermute | solution.py:461
  151.0 29.2 %collective-permute-start.24 = (bf16[512,128]{1,0:T(8,128)(2,1)S(1)}, bf16[512,128]{1,0:T(8,128)(2,1)S(1)}, u32[]{:S(2)}, u32[]{:S(2)}) collective-permute-start(bf16[512,128]{1,0:T(8,128)(2,1)S(1)} %get-tuple-element.78), channel_id=1, source_target_pairs={{0,16},{8,24},{16,0},{24,8},{1,17},{9,25},{17,1},{25,9},{2,18},{10... | collective-permute-start | bytes 393224 | tf_op jit(solution)/shard_map/ppermute | solution.py:461
  153.5 30.3 %collective-permute-start.25 = (bf16[512,128]{1,0:T(8,128)(2,1)S(1)}, bf16[512,128]{1,0:T(8,128)(2,1)S(1)}, u32[]{:S(2)}, u32[]{:S(2)}) collective-permute-start(bf16[512,128]{1,0:T(8,128)(2,1)S(1)} %get-tuple-element.77), channel_id=1, source_target_pairs={{0,24},{8,0},{16,8},{24,16},{1,25},{9,1},{17,9},{25,17},{2,26},{10... | collective-permute-start | bytes 393224 | tf_op jit(solution)/shard_map/ppermute | solution.py:461
  170.1 2.2 %collective-permute-start.17 = (f32[40,128]{1,0:T(8,128)S(1)}, f32[40,128]{1,0:T(8,128)S(1)}, u32[]{:S(2)}, u32[]{:S(2)}) collective-permute-start(f32[40,128]{1,0:T(8,128)S(1)} %constant_dynamic-update-slice_fusion), channel_id=1, source_target_pairs={{0,32},{32,0},{1,33},{33,1},{2,34},{34,2},{3,35},{35,3},{4,36},{36... | collective-permute-start | bytes 61448 | tf_op jit(solution)/shard_map/ppermute | solution.py:620
  170.1 18.7 %collective-permute-start.16 = (bf16[384,256]{1,0:T(8,128)(2,1)}, bf16[384,256]{1,0:T(8,128)(2,1)S(1)}, u32[]{:S(2)}, u32[]{:S(2)}) collective-permute-start(bf16[384,256]{1,0:T(8,128)(2,1)} %get-tuple-element.61), channel_id=1, source_target_pairs={{0,0},{8,64},{16,128},{24,192},{64,8},{72,72},{80,136},{88,200},{1... | collective-permute-start | bytes 589832 | tf_op jit(solution)/shard_map/ppermute | solution.py:438
  172.4 13.3 %collective-permute-start.18 = (f32[40,128]{1,0:T(8,128)S(1)}, f32[40,128]{1,0:T(8,128)S(1)}, u32[]{:S(2)}, u32[]{:S(2)}) collective-permute-start(f32[40,128]{1,0:T(8,128)S(1)} %add.105), channel_id=1, source_target_pairs={{0,0},{8,64},{16,128},{24,192},{64,8},{72,72},{80,136},{88,200},{1... | collective-permute-start | bytes 61448 | tf_op jit(solution)/shard_map/ppermute | solution.py:626
  179.3 7.5 %collective-permute-start.19 = (f32[40,128]{1,0:T(8,128)S(1)}, f32[40,128]{1,0:T(8,128)S(1)}, u32[]{:S(2)}, u32[]{:S(2)}) collective-permute-start(f32[40,128]{1,0:T(8,128)S(1)} %add.105), channel_id=1, source_target_pairs={{0,64},{8,128},{16,192},{24,0},{64,72},{72,136},{80,200},{88,8},{1... | collective-permute-start | bytes 61448 | tf_op jit(solution)/shard_map/ppermute | solution.py:626
  180.3 6.5 %collective-permute-start.20 = (f32[40,128]{1,0:T(8,128)S(1)}, f32[40,128]{1,0:T(8,128)S(1)}, u32[]{:S(2)}, u32[]{:S(2)}) collective-permute-start(f32[40,128]{1,0:T(8,128)S(1)} %add.105), channel_id=1, source_target_pairs={{0,128},{8,192},{16,0},{24,64},{64,136},{72,200},{80,8},{88,72},{1... | collective-permute-start | bytes 61448 | tf_op jit(solution)/shard_map/ppermute | solution.py:626
  183.8 5.0 %collective-permute-start.21 = (f32[40,128]{1,0:T(8,128)S(1)}, f32[40,128]{1,0:T(8,128)S(1)}, u32[]{:S(2)}, u32[]{:S(2)}) collective-permute-start(f32[40,128]{1,0:T(8,128)S(1)} %add.105), channel_id=1, source_target_pairs={{0,192},{8,0},{16,64},{24,128},{64,200},{72,8},{80,72},{88,136},{1... | collective-permute-start | bytes 61448 | tf_op jit(solution)/shard_map/ppermute | solution.py:626
  (15 other events, 270.2 us)
Sparse Core Ops, SparseCore 0:
  9.9 35.8 all-gather.1
  135.9 36.5 reduce-scatter.1
